TPU v7x, 32 devices: a whole 2x2x4 slice. The times are simulated.
32 devices in a mesh: groups: 2 (over y), tm: 4 (over x, core), tensor: 4 (over z).
Axes of the slice: x: 2, y: 2, z: 4, core: 2. Of those that a mesh axis runs over, the one named last changes fastest.
Arguments:
- start_latent: float32 [256, 128], P(('groups', 'tensor')), parts along dimension 0, may hold values from -6 to 6
- time_index: int32 [8], P(('groups', 'tm')), parts along dimension 0, may hold values from 39 to 998, as said below
- step_weight: int32 [8], P(('groups', 'tm')), parts along dimension 0, may hold values from 1 to 16
- in_weight: bfloat16 [128, 3072], P('tm'), may hold values from -0.5 to 0.5
- mod_weight: bfloat16 [256, 9216], P(None, 'tensor'), may hold values from -0.375 to 0.375
- qkv_weight: bfloat16 [3072, 6144], P(None, 'tensor'), as said below
- out_weight: bfloat16 [2048, 3072], P('tensor'), may hold values from -0.125 to 0.125
- head_weight: bfloat16 [3072, 128], P('tm'), may hold values from -0.109375 to 0.109375
Outputs:
- window_latents: float32 [8, 128, 128], P(('groups', 'tm'), 'tensor'), parts along dimension 0
There are 2 independent parts, one for each index of `groups`. A program takes and returns all parts, laid end to end along the dimension named above; an argument that names none is the same for every part. Nothing has to cross between parts.
Inputs may be any that keep to these rules, and one draw needn't show every extreme that they name: `time_index`: strictly decreasing indices of a 1000-step plan. `qkv_weight`: entries at most 24 / sqrt(3072) in magnitude.
All inputs are finite; a program needn't handle non-finite values.
Results may differ from a plain program's by a relative error of at most 0.0075.
Values may be sent and summed in bfloat16 or wider, within the bound.
No kernel may reach another device: no remote copies, remote signals or barrier semaphores. Data moves between devices by JAX's collectives and lax.ppermute only.
A program may use at most 64 MiB of HBM per device.

v0:
```python
import math

import jax
import jax.numpy as jnp
from jax import lax
from jax.sharding import PartitionSpec as P

D = 3072
HD = 128
ITERS = 2


NORM_EPS = 1e-06
STEP_DIVISOR = 64.0


def carried_in(value, axis, combine, identity):
    devices, index = (lax.axis_size(axis), lax.axis_index(axis))
    everything = lax.all_gather(value, axis)
    start = jnp.broadcast_to(jnp.asarray(identity, value.dtype), value.shape)

    def turn(k, before):
        reached = k < index
        new = combine(before, everything[k])
        return jnp.where(reached, new, before)

    return lax.fori_loop(0, devices, turn, start)


def embedding_of(time_index, width):
    half_width = width // 2
    frequency = jnp.exp(
        -math.log(10000.0) * jnp.arange(half_width).astype(jnp.float32) / half_width
    )
    angles = time_index.astype(jnp.float32)[:, None] * frequency[None, :]
    return jnp.concatenate([jnp.cos(angles), jnp.sin(angles)], axis=1)


def attention(qkv_rows, head_count):
    token_count = qkv_rows.shape[0]
    packed = qkv_rows.reshape(token_count, head_count, 3, HD)
    queries = packed[:, :, 0]
    key_rows = packed[:, :, 1]
    values = packed[:, :, 2]
    block_rows = min(token_count, 512)

    def one_block(block_start):
        scores = jnp.einsum(
            "qhe,khe->hqk", queries, key_rows, preferred_element_type=jnp.float32
        ) * (1.0 / math.sqrt(HD))
        attention_weights = jax.nn.softmax(scores, axis=-1).astype(jnp.bfloat16)
        return jnp.einsum(
            "hqk,khe->qhe", attention_weights, values, preferred_element_type=jnp.float32
        ).astype(jnp.bfloat16)

    block_starts = jnp.arange(token_count // block_rows, dtype=jnp.int32) * block_rows
    blocks_out = lax.map(one_block, block_starts)
    return blocks_out.reshape(token_count, head_count * HD)


def evaluate(latents, shifts, scales, folded, in_weight_all, qkv_weight, head_count):
    widened = jnp.dot(latents, in_weight_all, preferred_element_type=jnp.float32)
    row_mean = jnp.mean(widened, axis=1, keepdims=True)
    centered = widened - row_mean
    spread = jnp.mean(centered * centered, axis=1, keepdims=True)
    normed = (centered * lax.rsqrt(spread + NORM_EPS) * (1.0 + scales) + shifts).astype(
        jnp.bfloat16
    )
    qkv_rows = jnp.dot(normed, qkv_weight, preferred_element_type=jnp.float32).astype(jnp.bfloat16)
    attended = attention(qkv_rows, head_count)
    return (widened, jnp.dot(attended, folded, preferred_element_type=jnp.float32))


def fold_head(out_weight, gate_rows, head_weight_all):
    scaled_out = (out_weight.astype(jnp.float32) * gate_rows[None, :]).astype(jnp.bfloat16)
    return jnp.dot(scaled_out, head_weight_all, preferred_element_type=jnp.float32).astype(
        jnp.bfloat16
    )


def add_terms(earlier, later):
    return earlier + later


def local(
    start_latent,
    time_index,
    step_weight,
    in_weight,
    mod_weight,
    qkv_weight,
    out_weight,
    head_weight,
):
    rows_dev = start_latent.shape[0]
    head_count = qkv_weight.shape[1] // (3 * HD)
    in_weight_all, head_weight_all = (
        lax.all_gather(in_weight, "tm", axis=0, tiled=True),
        lax.all_gather(head_weight, "tm", axis=0, tiled=True),
    )
    embedding = embedding_of(time_index, mod_weight.shape[0]).astype(jnp.bfloat16)
    mod_part = jnp.dot(embedding, mod_weight, preferred_element_type=jnp.float32)
    modulation = lax.all_gather(mod_part, "tensor", axis=1, tiled=True)
    shifts = modulation[:, :D]
    scales = modulation[:, D : 2 * D]
    gate_rows = modulation[:, 2 * D :]
    folded = fold_head(out_weight, gate_rows[0], head_weight_all)
    step_size = step_weight.astype(jnp.float32) / STEP_DIVISOR
    start_all = lax.all_gather(start_latent, "tensor", axis=0, tiled=True)
    row_first = lax.axis_index("tensor") * rows_dev
    guesses = start_all.astype(jnp.bfloat16)[None]
    window_end = start_latent[None]
    for iteration in range(ITERS):
        widened, partial_sum = evaluate(
            guesses[0], shifts[0], scales[0], folded, in_weight_all, qkv_weight, head_count
        )
        widened_list = [widened]
        partials = [partial_sum]
        stacked = jnp.stack(partials, 0)
        residual = jnp.stack(
            [
                jnp.dot(
                    lax.dynamic_slice_in_dim(widened, row_first, rows_dev, 0).astype(jnp.bfloat16),
                    head_weight_all,
                    preferred_element_type=jnp.float32,
                )
                for widened in widened_list
            ],
            0,
        )
        velocity = lax.psum_scatter(stacked, "tensor", scatter_dimension=1, tiled=True) + residual
        drifts = step_size[:, None, None] * velocity
        inclusive = jnp.cumsum(drifts, axis=0)
        earlier = carried_in(inclusive[-1], "tm", add_terms, jnp.zeros_like(inclusive[-1]))
        window_end = start_latent[None] + earlier[None] + inclusive
        if iteration + 1 < ITERS:
            guesses = lax.all_gather(
                (window_end - drifts).astype(jnp.bfloat16), "tensor", axis=1, tiled=True
            )
    return window_end


def solution(mesh):
    return jax.shard_map(
        local,
        mesh=mesh,
        in_specs=(
            P(("groups", "tensor"), None),
            P(("groups", "tm")),
            P(("groups", "tm")),
            P("tm", None),
            P(None, "tensor"),
            P(None, "tensor"),
            P("tensor", None),
            P("tm", None),
        ),
        out_specs=P(("groups", "tm"), "tensor", None),
        check_vma=False,
    )
```

profile of v0, /device:TPU:0, one launch (start us, length us, event | category | flops | bytes accessed | tf_op | source)
XLA Modules:
  0.0 162.6 jit_solution(14899555492809119197)
XLA Ops:
  6.5 10.4 %all_gather.22 = bf16[128,3072]{1,0:T(8,128)(2,1)S(1)} all-gather(bf16[32,3072]{1,0:T(8,128)(2,1)} %param.15), channel_id=1, replica_groups=mesh['groups'=2,'tm'=4,'tensor'=4] {'tm'}, dimensions={0}, use_global_device_ids=true | all-gather | bytes 983040 | tf_op jit(solution)/shard_map/all_gather | solution.py:98
  16.9 0.7 convert.14
  17.7 13.4 %all_gather.21 = bf16[128,128]{1,0:T(8,128)(2,1)S(1)} all-gather(bf16[32,128]{1,0:T(8,128)(2,1)S(1)} %convert.14), channel_id=1, replica_groups=mesh['groups'=2,'tm'=4,'tensor'=4] {'tensor'}, dimensions={0}, use_global_device_ids=true | all-gather | bytes 40960 | tf_op jit(solution)/shard_map/all_gather | solution.py:109
  32.8 13.2 %all-gather.1 = f32[4,1,2304]{2,1,0:T(1,128)S(1)} all-gather(f32[1,1,2304]{2,1,0:T(1,128)S(1)} %convolution_bitcast_fusion), channel_id=2, replica_groups=mesh['groups'=2,'tm'=4,'tensor'=4] {'tensor'}, dimensions={0}, use_global_device_ids=true | all-gather | bytes 46080 | tf_op jit(solution)/shard_map/all_gather | solution.py:103
  46.0 0.6 copy-done.3
  46.6 5.9 %convolution_convert_fusion.1 = bf16[128,1536]{1,0:T(8,128)(2,1)} fusion(bf16[3072,1536]{1,0:T(8,128)(2,1)} %param.17, f32[128,3072]{1,0:T(8,128)S(1)} %get-tuple-element.245, f32[3072]{0:T(1024)S(1)} %bitcast.113, f32[3072]{0:T(1024)S(1)} %bitcast.115, f32[128]{0:T(128)S(1)} %add_rsqrt_fusion.1, f32[128]{0:T(128)S(1)} %broadcast_multiply_fusion.1), kind=kOutput, calls=%fused_computation.9 | convolution fusion | flops 1210122240 | bytes 11428864 | tf_op jit(solution)/shard_map/dot_general | solution.py:69
  52.5 1.9 %copy.27 = bf16[128,1536]{0,1:T(8,128)(2,1)} copy(bf16[128,1536]{1,0:T(8,128)(2,1)} %convolution_convert_fusion.1) | data formatting | bytes 786432 | tf_op jit(solution)/shard_map/convert_element_type | solution.py:69
  54.4 1.9 %convolution_multiply_fusion.1 = f32[4,128,128]{1,2,0:T(8,128)} fusion(bf16[128,4,3,128]{0,3,2,1:T(8,128)(2,1)} %bitcast.107), kind=kOutput, calls=%fused_computation.17 | convolution fusion | flops 16842752 | bytes 524288 | tf_op jit(solution)/shard_map/while/body/eval_jaxpr/qhe,khe->hqk/dot_general | solution.py:48
  56.3 1.3 fusion.36
  57.6 8.4 %all_gather.24 = bf16[3072,128]{1,0:T(8,128)(2,1)S(1)} all-gather(bf16[768,128]{1,0:T(8,128)(2,1)} %param.19), channel_id=1, replica_groups=mesh['groups'=2,'tm'=4,'tensor'=4] {'tm'}, dimensions={0}, use_global_device_ids=true | all-gather | bytes 983040 | tf_op jit(solution)/shard_map/all_gather | solution.py:99
  66.0 2.0 %convolution_convert_fusion.3 = bf16[4,128,128]{2,1,0:T(8,128)(2,1)} fusion(bf16[128,4,3,128]{0,3,2,1:T(8,128)(2,1)} %bitcast.109, f32[4,128]{1,0:T(4,128)S(1)} %fusion.36, f32[4,128,128]{1,2,0:T(8,128)} %convolution_multiply_fusion.1), kind=kOutput, calls=%fused_computation.21 | convolution fusion | flops 17040000 | bytes 788480 | tf_op jit(solution)/shard_map/while/body/eval_jaxpr/hqk,khe->qhe/dot_general | solution.py:52
  68.0 2.9 %fusion.8 = bf16[512,128]{1,0:T(8,128)(2,1)S(1)} fusion(bf16[3072,128]{1,0:T(8,128)(2,1)S(1)} %all_gather.24, bf16[512,3072]{1,0:T(8,128)(2,1)} %param.18, f32[3072]{0:T(1024)S(1)} %bitcast.120), kind=kOutput, calls=%fused_computation.22 | convolution fusion | flops 407437312 | bytes 4075520 | tf_op jit(solution)/shard_map/dot_general | solution.py:76
  70.9 0.6 copy-done.2
  71.6 0.8 convolution_bitcast_fusion.2
  73.2 19.2 %reduce-scatter.3.cloned.1.call-done = f32[1,32,128]{2,1,0:T(8,128)} async-done(((f32[1,128,128]{2,1,0:T(8,128)}), f32[1,32,128]{2,1,0:T(8,128)}) %reduce-scatter.3.cloned.1.call-update) | async-done | bytes 16400 | tf_op jit(solution)/shard_map/reduce_scatter | solution.py:131
  92.4 1.0 fusion.12
  93.3 0.6 copy-done.7
  93.9 5.2 %all_gather.25 = f32[4,32,128]{2,1,0:T(8,128)S(1)} all-gather(f32[1,32,128]{2,1,0:T(8,128)S(1)} %fusion.12), channel_id=1, replica_groups=mesh['groups'=2,'tm'=4,'tensor'=4] {'tm'}, dimensions={0}, use_global_device_ids=true | all-gather | bytes 81920 | tf_op jit(solution)/shard_map/all_gather | solution.py:19
  99.3 0.7 fusion.27
  100.0 13.1 %all_gather.26 = bf16[1,128,128]{2,1,0:T(8,128)(2,1)S(1)} all-gather(bf16[1,32,128]{2,1,0:T(8,128)(2,1)S(1)} %fusion.27), channel_id=1, replica_groups=mesh['groups'=2,'tm'=4,'tensor'=4] {'tensor'}, dimensions={1}, use_global_device_ids=true | all-gather | bytes 40960 | tf_op jit(solution)/shard_map/all_gather | solution.py:137
  113.1 1.6 fusion.37
  115.1 5.9 %convolution_convert_fusion = bf16[128,1536]{1,0:T(8,128)(2,1)} fusion(bf16[3072,1536]{1,0:T(8,128)(2,1)} %param.17, f32[128,3072]{1,0:T(8,128)S(1)} %get-tuple-element.247, f32[128]{0:T(128)S(1)} %add_rsqrt_fusion, f32[128]{0:T(128)S(1)} %broadcast_multiply_fusion, f32[3072]{0:T(1024)S(1)} %bitcast.114, f32[3072]{0:T(1024)S(1)} %bitcast.116), kind=kOutput, calls=%fused_computation.8 | convolution fusion | flops 1210122240 | bytes 11428864 | tf_op jit(solution)/shard_map/dot_general | solution.py:69
  121.0 1.9 %copy.32 = bf16[128,1536]{0,1:T(8,128)(2,1)} copy(bf16[128,1536]{1,0:T(8,128)(2,1)} %convolution_convert_fusion) | data formatting | bytes 786432 | tf_op jit(solution)/shard_map/convert_element_type | solution.py:69
  122.9 1.9 %convolution_multiply_fusion = f32[4,128,128]{1,2,0:T(8,128)} fusion(bf16[128,4,3,128]{0,3,2,1:T(8,128)(2,1)} %bitcast.110), kind=kOutput, calls=%fused_computation.16 | convolution fusion | flops 16842752 | bytes 524288 | tf_op jit(solution)/shard_map/while/body/eval_jaxpr/qhe,khe->hqk/dot_general | solution.py:48
  124.8 1.3 fusion.38
  126.1 2.0 %convolution_convert_fusion.2 = bf16[4,128,128]{2,1,0:T(8,128)(2,1)} fusion(bf16[128,4,3,128]{0,3,2,1:T(8,128)(2,1)} %bitcast.112, f32[4,128]{1,0:T(4,128)S(1)} %fusion.38, f32[4,128,128]{1,2,0:T(8,128)} %convolution_multiply_fusion), kind=kOutput, calls=%fused_computation.20 | convolution fusion | flops 17040000 | bytes 788480 | tf_op jit(solution)/shard_map/while/body/eval_jaxpr/hqk,khe->qhe/dot_general | solution.py:52
  128.0 1.8 %convolution_bitcast_fusion.1 = f32[1,128,128]{2,1,0:T(8,128)} fusion(bf16[128,512]{0,1:T(8,128)(2,1)} %bitcast.119, bf16[512,128]{1,0:T(8,128)(2,1)} %copy-done.2), kind=kOutput, calls=%fused_computation.23 | convolution fusion | flops 16777216 | bytes 327680 | tf_op jit(solution)/shard_map/dot_general | solution.py:71
  129.9 17.6 %reduce-scatter.5.cloned.1.call-done = f32[1,32,128]{2,1,0:T(8,128)} async-done(((f32[1,128,128]{2,1,0:T(8,128)}), f32[1,32,128]{2,1,0:T(8,128)}) %reduce-scatter.5.cloned.1.call-update) | async-done | bytes 16400 | tf_op jit(solution)/shard_map/reduce_scatter | solution.py:131
  147.5 1.0 fusion.10
  148.5 0.6 copy-done.8
  149.1 5.2 %all_gather.27 = f32[4,32,128]{2,1,0:T(8,128)S(1)} all-gather(f32[1,32,128]{2,1,0:T(8,128)S(1)} %fusion.10), channel_id=1, replica_groups=mesh['groups'=2,'tm'=4,'tensor'=4] {'tm'}, dimensions={0}, use_global_device_ids=true | all-gather | bytes 81920 | tf_op jit(solution)/shard_map/all_gather | solution.py:19
  154.4 1.3 bitcast_add_fusion
  (44 shorter events, 1.8 us)
Async XLA Ops:
  6.5 26.0 %copy-start = (bf16[256,2304]{1,0:T(8,128)(2,1)S(1)}, bf16[256,2304]{1,0:T(8,128)(2,1)}, u32[]{:S(2)}) copy-start(bf16[256,2304]{1,0:T(8,128)(2,1)} %param.16) | copy-start | bytes 3538948
  6.5 85.8 %reduce-scatter.3.cloned.1.call-start = ((), (), s32[]{:S(2)}) async-start(), calls=%async_computation.2 | async-start | bytes 81920 | tf_op jit(solution)/shard_map/reduce_scatter | solution.py:131
  16.9 35.6 %copy-start.1 = (bf16[128,3072]{1,0:T(8,128)(2,1)}, bf16[128,3072]{1,0:T(8,128)(2,1)S(1)}, u32[]{:S(2)}) copy-start(bf16[128,3072]{1,0:T(8,128)(2,1)S(1)} %all_gather.22) | copy-start | bytes 2359300
  46.0 0.6 copy-start.3
  46.0 0.6 copy-start.5
  68.0 3.6 %copy-start.9 = (bf16[4,128,128]{2,1,0:T(8,128)(2,1)S(1)}, bf16[4,128,128]{2,1,0:T(8,128)(2,1)}, u32[]{:S(2)}) copy-start(bf16[4,128,128]{2,1,0:T(8,128)(2,1)} %convolution_convert_fusion.3) | copy-start | bytes 393220
  70.9 0.7 copy-start.2
  72.4 75.1 %reduce-scatter.5.cloned.1.call-start = ((), (), s32[]{:S(2)}) async-start(), calls=%async_computation.3 | async-start | bytes 81920 | tf_op jit(solution)/shard_map/reduce_scatter | solution.py:131
  93.3 0.6 copy-start.7
  113.1 1.9 %copy-start.4 = (f32[1,3072]{1,0:T(1,128)S(1)}, f32[1,3072]{1,0:T(1,128)}, u32[]{:S(2)}) copy-start(f32[1,3072]{1,0:T(1,128)} %copy-done.3) | copy-start | bytes 36868
  113.1 1.9 %copy-start.6 = (f32[1,3072]{1,0:T(1,128)S(1)}, f32[1,3072]{1,0:T(1,128)}, u32[]{:S(2)}) copy-start(f32[1,3072]{1,0:T(1,128)} %copy-done.5) | copy-start | bytes 36868
  148.5 0.6 copy-start.8
Sparse Core Ops, SparseCore 0:
  72.6 19.7 reduce-scatter.2
  130.0 17.4 reduce-scatter.4
where the time goes:
time: 163 us
  blocking collectives  68.9 us (42%)
  waiting for transfers between devices  36.8 us (23%)
  matrix products  31.9 us (20%)
  between operations  14.9 us (9%)
  local copies, waits for them, and re-layouts  6.27 us (4%)
  other arithmetic  3.61 us (2%)
    reduce_scatter x2, waiting for transfers between devices, local(): lax.psum_scatter(stacked, 'tensor', scatter_dimension=1, tiled=True)  36.8 us
    all_gather x1, blocking collectives, local(): start_all = lax.all_gather(start_latent, 'tensor', axis=0, tiled=True)  13.4 us
    all_gather x1, blocking collectives, local(): modulation = lax.all_gather(mod_part, 'tensor', axis=1, tiled=True)  13.2 us
    all_gather x1, blocking collectives, local(): lax.all_gather((window_end - drifts).astype(jnp.bfloat16), 'tensor', axis...  13.1 us
    dot_general x2, matrix products, evaluate(): jnp.dot(normed, qkv_weight, preferred_element_type=jnp.float32)  11.8 us
    all_gather x2, blocking collectives, carried_in(): everything = lax.all_gather(value, axis)  10.4 us
    all_gather x1, blocking collectives, local(): lax.all_gather(in_weight, 'tm', axis=0, tiled=True)  10.4 us
    all_gather x1, blocking collectives, local(): lax.all_gather(head_weight, 'tm', axis=0, tiled=True)  8.41 us
  transfers between devices with their start and end apart: 2, of which 2 were waited for; matrix products, arithmetic and copies ran while one was open for 0% of the time, Pallas kernels for 0%

commit v1 on v0

v1 whole, which is shorter than its diff:
```python
import functools
import math

import jax
import jax.numpy as jnp
from jax import lax
from jax.experimental import pallas as pl
from jax.experimental.pallas import tpu as pltpu
from jax.sharding import PartitionSpec as P

HD = 128
LANES = 128
ITERS = 2
NORM_EPS = 1e-06
STEP_DIVISOR = 64.0
F32 = jnp.float32
BF16 = jnp.bfloat16
VMEM = pl.BlockSpec(memory_space=pltpu.VMEM)
SMEM = pl.BlockSpec(memory_space=pltpu.SMEM)


def embedding_of(time_index, width):
    half_width = width // 2
    frequency = jnp.exp(
        -math.log(10000.0) * jnp.arange(half_width).astype(F32) / half_width
    )
    angles = time_index.astype(F32)[:, None] * frequency[None, :]
    return jnp.concatenate([jnp.cos(angles), jnp.sin(angles)], axis=1)


def is_small(axis):
    return lax.axis_size(axis) in (2, 4)


def swap(value, axis, k):
    n = lax.axis_size(axis)
    return lax.ppermute(value, axis, [(i, i ^ k) for i in range(n)])


def gather_parts(value, axis):
    if is_small(axis):
        return [value] + [swap(value, axis, k) for k in range(1, lax.axis_size(axis))]
    return [lax.all_gather(value, axis, axis=0, tiled=True)]


def gather_weight_parts(value, axis):
    n = lax.axis_size(axis)
    if n != 4:
        return gather_parts(value, axis)
    far = swap(value, axis, 2)
    near = swap(value, axis, 1)
    return [value, near, far, swap(far, axis, 1)]


def place(axis, parts, k):
    if parts == 1:
        return 0
    return lax.axis_index(axis) ^ k


def bdot(a, b):
    return jnp.dot(a, b, preferred_element_type=F32)


def bdot_t(a, b):
    return lax.dot_general(a, b, (((1,), (1,)), ((), ())), preferred_element_type=F32)


def split_terms(value, terms):
    out = []
    for _ in range(terms):
        piece = value.astype(BF16)
        out.append(piece)
        value = value - piece.astype(F32)
    return out


def modulation_kernel(emb_ref, weight_ref, start_ref, out_ref):
    rows = start_ref.shape[0]
    result = bdot(jnp.broadcast_to(emb_ref[...], (16, emb_ref.shape[1])), weight_ref[...])
    out_ref[0:rows, :] = start_ref[...]
    for r in range(weight_ref.shape[1] // LANES):
        out_ref[rows + r : rows + r + 1, :] = result[0:1, r * LANES : (r + 1) * LANES]


def attend(x, factors, base, gram, head_count):
    twice = jnp.concatenate([x, x], axis=1)
    thrice = jnp.concatenate([twice, x], axis=1)
    spread = jnp.sum(bdot(thrice, gram[...]) * x.astype(F32), axis=1, keepdims=True)
    scale = lax.rsqrt(jnp.maximum(spread, 0.0) + NORM_EPS)
    outs = []
    for h in range(head_count):
        cols = slice(h * 3 * HD, (h + 1) * 3 * HD)
        qkv = (bdot(twice, factors[:, cols]) * scale + base[0:1, cols]).astype(BF16)
        scores = bdot_t(qkv[:, :HD], qkv[:, HD : 2 * HD]) * (1.0 / math.sqrt(HD))
        top = jnp.max(scores, axis=1, keepdims=True)
        weights = jnp.exp(scores - top)
        weights = weights / jnp.sum(weights, axis=1, keepdims=True)
        outs.append(bdot(weights.astype(BF16), qkv[:, 2 * HD :]).astype(BF16))
    return outs[0] if head_count == 1 else jnp.concatenate(outs, axis=1)


def setup_kernel(nt, nm, rows, head_count, *refs):
    msgs, refs = refs[:nt], refs[nt:]
    inws, refs = refs[:nm], refs[nm:]
    qkv_ref, refs = refs[0], refs[1:]
    factor_ref, base_ref, gram_ref, start_ref, inw_ref, gate_ref, att_ref = refs[:7]
    start_s, mod_s, inw_s, z_s = refs[7:]
    for k in range(nt):
        at = place("tensor", nt, k)
        start_s[at] = msgs[k][0 : start_s.shape[1], :]
        mod_s[at, 0 : msgs[k].shape[0] - start_s.shape[1], :] = msgs[k][start_s.shape[1] :, :]
    for k in range(nm):
        inw_s[place("tm", nm, k)] = inws[k][...]
    channels, width = inw_ref.shape
    chunks = width // LANES
    per = 3 * chunks // nt

    def mod_row(r):
        return mod_s[r // per, r % per : r % per + 1, :]

    inw = inw_s[...].reshape(channels, width)
    inw_ref[...] = inw
    total = jnp.zeros((channels, LANES), F32)
    for c in range(chunks):
        total = total + inw[:, c * LANES : (c + 1) * LANES].astype(F32)
    mean = jnp.sum(total, axis=1, keepdims=True) * (1.0 / width)
    for c in range(chunks):
        cols = slice(c * LANES, (c + 1) * LANES)
        centered = inw[:, cols].astype(F32) - mean
        z_s[0:channels, cols] = (centered * (1.0 + mod_row(chunks + c))).astype(BF16)
        z_s[channels : channels + 16, cols] = jnp.broadcast_to(mod_row(c), (16, LANES)).astype(BF16)
        gate_ref[c : c + 1, :] = mod_row(2 * chunks + c)
    mean_b = jnp.broadcast_to(mean, (channels, channels))
    gram = bdot_t(inw, inw) * (1.0 / width) - mean_b * mean_b.T
    for i, piece in enumerate(split_terms(gram, 3)):
        gram_ref[i * channels : (i + 1) * channels, :] = piece
    start = start_s[...].reshape(start_ref.shape)
    start_ref[...] = start

    block = 3 * HD

    def columns(n, carry):
        at = pl.ds(pl.multiple_of(n * block, block), block)
        result = bdot(z_s[...], qkv_ref[:, at])
        high, low = split_terms(result[0:channels], 2)
        factor_ref[0:channels, at] = high
        factor_ref[channels : 2 * channels, at] = low
        base_ref[:, at] = result[channels : channels + 8]
        return carry

    lax.fori_loop(0, head_count, columns, 0)
    att_ref[...] = attend(start.astype(BF16), factor_ref, base_ref, gram_ref, head_count)


def add_own_rows(result, residual, rows):
    first = lax.axis_index("tensor") * rows
    at = lax.broadcasted_iota(jnp.int32, result.shape, 0)
    return result + jnp.where((at >= first) & (at < first + rows), residual, 0.0)


def step_size(step_ref):
    return step_ref[0].astype(F32) * (1.0 / STEP_DIVISOR)


def fold_kernel(nm, rows, *refs):
    heads, refs = refs[:nm], refs[nm:]
    step_ref, out_w_ref, gate_ref, inw_ref, att_ref, start_ref = refs[:6]
    fold_ref, resid_ref, vel_ref = refs[6:9]
    head_s, s_s = refs[9:]
    for k in range(nm):
        head_s[place("tm", nm, k)] = heads[k][...]
    span, width = out_w_ref.shape
    channels = inw_ref.shape[0]
    for c in range(width // LANES):
        cols = slice(c * LANES, (c + 1) * LANES)
        s_s[0:span, cols] = (out_w_ref[:, cols].astype(F32) * gate_ref[c : c + 1, :]).astype(BF16)
    s_s[span:, :] = inw_ref[...]
    head = head_s[...].reshape(width, head_s.shape[2])
    result = bdot(s_s[...], head)
    folded = result[0:span].astype(BF16)
    fold_ref[...] = folded
    for i, piece in enumerate(split_terms(result[span:], 2)):
        resid_ref[i * channels : (i + 1) * channels, :] = piece
    x = start_ref[...].astype(BF16)
    vel = bdot(att_ref[...], folded)
    residual = bdot(jnp.concatenate([x, x], axis=1), resid_ref[...])
    vel_ref[...] = (add_own_rows(vel, residual, rows) * step_size(step_ref)).astype(vel_ref.dtype)


def iterate_kernel(nparts, rows, head_count, split, *refs):
    parts, refs = refs[:nparts], refs[nparts:]
    step_ref, start_ref, factor_ref, base_ref, gram_ref, fold_ref, resid_ref = refs[:7]
    outs = refs[7:-1]
    vel_s = refs[-1]
    guess = start_ref[...]
    for part in parts:
        guess = guess + part[...].astype(F32)
    x = guess.astype(BF16)
    attended = attend(x, factor_ref, base_ref, gram_ref, head_count)
    vel = bdot(attended, fold_ref[...])
    residual = bdot(jnp.concatenate([x, x], axis=1), resid_ref[...])
    vel = add_own_rows(vel, residual, rows) * step_size(step_ref)
    if not split:
        outs[0][...] = vel.astype(outs[0].dtype)
        return
    vel_s[...] = vel.reshape(vel_s.shape)
    for k in range(len(outs)):
        outs[k][...] = vel_s[lax.axis_index("tensor") ^ k]


def shape_of(shape, dtype):
    return jax.ShapeDtypeStruct(shape, dtype)


PARAMS = pltpu.CompilerParams(vmem_limit_bytes=40 * 2**20)


def call(kernel, name, outs, in_specs, scratch, *args):
    return pl.pallas_call(
        kernel,
        name=name,
        out_shape=outs,
        in_specs=in_specs,
        out_specs=[VMEM] * len(outs),
        scratch_shapes=scratch,
        compiler_params=PARAMS,
    )(*args)


def sum_earlier(parts, inclusive):
    me = lax.axis_index("tm")
    total = parts[0].astype(F32) if inclusive else jnp.zeros(parts[0].shape, F32)
    for k in range(1, len(parts)):
        total = total + jnp.where((me ^ k) < me, parts[k].astype(F32), 0.0)
    return total


def earlier_sum(value, inclusive):
    if is_small("tm"):
        return sum_earlier(gather_parts(value, "tm"), inclusive)
    everything = lax.all_gather(value, "tm").astype(F32)
    index = jnp.arange(everything.shape[0]).reshape((-1,) + (1,) * value.ndim)
    me = lax.axis_index("tm")
    keep = index <= me if inclusive else index < me
    return jnp.sum(jnp.where(keep, everything, 0.0), axis=0)


def local(
    start_latent,
    time_index,
    step_weight,
    in_weight,
    mod_weight,
    qkv_weight,
    out_weight,
    head_weight,
):
    rows, channels = start_latent.shape
    n_tensor = lax.axis_size("tensor")
    tokens = rows * n_tensor
    width = in_weight.shape[1]
    chunks = width // LANES
    head_count = qkv_weight.shape[1] // (3 * HD)
    span = out_weight.shape[0]

    inw_parts = gather_weight_parts(in_weight, "tm")
    embedding = embedding_of(time_index, mod_weight.shape[0]).astype(BF16)
    small = is_small("tensor") and mod_weight.shape[1] % LANES == 0
    if small:
        mod_rows = mod_weight.shape[1] // LANES
        message = call(
            modulation_kernel,
            "modulation",
            [shape_of((rows + mod_rows, LANES), F32)],
            [VMEM] * 3,
            [],
            embedding,
            mod_weight,
            start_latent,
        )[0]
        messages = gather_parts(message, "tensor")
        block_rows = rows
    else:
        mod_part = jnp.dot(embedding, mod_weight, preferred_element_type=F32)
        modulation = lax.all_gather(mod_part, "tensor", axis=1, tiled=True)
        start_all = lax.all_gather(start_latent, "tensor", axis=0, tiled=True)
        messages = [jnp.concatenate([start_all, modulation.reshape(-1, LANES)], axis=0)]
        block_rows = tokens
    nt, nm = len(messages), len(inw_parts)
    mod_rows = messages[0].shape[0] - block_rows
    padded = -(-mod_rows // 8) * 8
    factor, base, gram, start_all, inw_all, gate, attended = call(
        functools.partial(setup_kernel, nt, nm, rows, head_count),
        "setup",
        [
            shape_of((2 * channels, qkv_weight.shape[1]), BF16),
            shape_of((8, qkv_weight.shape[1]), F32),
            shape_of((3 * channels, channels), BF16),
            shape_of((tokens, channels), F32),
            shape_of((channels, width), BF16),
            shape_of((chunks, LANES), F32),
            shape_of((tokens, head_count * HD), BF16),
        ],
        [VMEM] * (nt + nm + 1),
        [
            pltpu.VMEM((nt, block_rows, channels), F32),
            pltpu.VMEM((nt, padded, LANES), F32),
            pltpu.VMEM((nm, channels // nm, width), BF16),
            pltpu.VMEM((channels + 16, width), BF16),
        ],
        *messages,
        *inw_parts,
        qkv_weight,
    )
    head_parts = gather_weight_parts(head_weight, "tm")
    folded, resid, vel = call(
        functools.partial(fold_kernel, nm, rows),
        "fold",
        [
            shape_of((span, channels), BF16),
            shape_of((2 * channels, channels), BF16),
            shape_of((tokens, channels), BF16),
        ],
        [VMEM] * nm + [SMEM] + [VMEM] * 5,
        [
            pltpu.VMEM((nm, width // nm, channels), BF16),
            pltpu.VMEM((span + channels, width), BF16),
        ],
        *head_parts,
        step_weight,
        out_weight,
        gate,
        inw_all,
        attended,
        start_all,
    )
    small = is_small("tensor")
    for iteration in range(1, ITERS):
        last = iteration + 1 == ITERS
        earlier = earlier_sum(vel, False)
        if small:
            pieces = gather_parts(earlier.astype(BF16), "tensor")
        else:
            pieces = [lax.psum(earlier, "tensor")]
        split = last and small
        if split:
            outs = [shape_of((rows, channels), F32)] * n_tensor
        else:
            outs = [shape_of((tokens, channels), F32 if last else BF16)]
        vels = call(
            functools.partial(iterate_kernel, len(pieces), rows, head_count, split),
            "iterate",
            outs,
            [VMEM] * len(pieces) + [SMEM] + [VMEM] * 6,
            [pltpu.VMEM((n_tensor, rows, channels), F32)],
            *pieces,
            step_weight,
            start_all,
            factor,
            base,
            gram,
            folded,
            resid,
        )
        vel = vels[0]
    if small:
        drift = vels[0]
        for k in range(1, n_tensor):
            drift = drift + swap(vels[k], "tensor", k)
    else:
        drift = lax.psum_scatter(vel, "tensor", scatter_dimension=0, tiled=True)
    return (start_latent + earlier_sum(drift, True))[None]


def solution(mesh):
    return jax.shard_map(
        local,
        mesh=mesh,
        in_specs=(
            P(("groups", "tensor"), None),
            P(("groups", "tm")),
            P(("groups", "tm")),
            P("tm", None),
            P(None, "tensor"),
            P(None, "tensor"),
            P("tensor", None),
            P("tm", None),
        ),
        out_specs=P(("groups", "tm"), "tensor", None),
        check_vma=False,
    )
```

time: 163 us -> 69 us (0.42)
  blocking collectives: 68.9 us -> 0 us
  matrix products: 31.9 us -> 0 us
  starting transfers between devices: 0.04 us -> 25.2 us
  between operations: 14.9 us -> 1.44 us
  waiting for transfers between devices: 36.8 us -> 26 us
  Pallas kernels: 0 us -> 8.7 us
  other arithmetic: 3.61 us -> 0.7 us
    all_gather x7 -> x0, blocking collectives: 68.9 us -> none  [the longest x1 13.4 us: local(): start_all = lax.all_gather(start_latent, 'tensor', axis=0, tiled=True)]
    reduce_scatter x2 -> x0, waiting for transfers between devices: 36.8 us -> none  [local(): lax.psum_scatter(stacked, 'tensor', scatter_dimension=1, tiled=True)]
    dot_general x14 -> x0, matrix products: 29.4 us -> none  [the longest x2 11.8 us: evaluate(): jnp.dot(normed, qkv_weight, preferred_element_type=jnp.float32)]
    ppermute x0 -> x21, waiting for transfers between devices: none -> 26 us  [swap(): return lax.ppermute(value, axis, [(i, i ^ k) for i in range(n)])]
    ppermute x0 -> x21, starting transfers between devices: none -> 25.2 us  [swap(): return lax.ppermute(value, axis, [(i, i ^ k) for i in range(n)])]
    pallas_call x0 -> x4, Pallas kernels: none -> 8.7 us  [call(): pl.pallas_call(kernel, name=name, out_shape=outs, in_specs=in_specs, out_...]
    unnamed x20 -> x14, local copies, waits for them, and re-layouts: 2.45 us -> 6.6 us
    convert_element_type x2 -> x0, local copies, waits for them, and re-layouts: 3.82 us -> none  [evaluate(): jnp.dot(normed, qkv_weight, preferred_element_type=jnp.float32)]
  transfers between devices with their start and end apart: 2 -> 21, of which waited for: 2 -> 13; matrix products, arithmetic and copies ran while one was open for 0% -> 0% of each run, Pallas kernels for 0% -> 7%
where the time goes in v1:
time: 69 us; the launch traced here: 68.7 us
  waiting for transfers between devices  26 us (38%)
  starting transfers between devices  25.2 us (37%)
  Pallas kernels  8.7 us (13%)
  local copies, waits for them, and re-layouts  6.6 us (10%)
  between operations  1.44 us (2%)
  other arithmetic  0.7 us (1%)
    ppermute x21, waiting for transfers between devices, swap(): return lax.ppermute(value, axis, [(i, i ^ k) for i in range(n)])  26 us
    ppermute x21, starting transfers between devices, swap(): return lax.ppermute(value, axis, [(i, i ^ k) for i in range(n)])  25.2 us
    pallas_call x4, Pallas kernels, call(): pl.pallas_call(kernel, name=name, out_shape=outs, in_specs=in_specs, out_...  8.7 us
    unnamed x14, local copies, waits for them, and re-layouts  6.6 us
  transfers between devices with their start and end apart: 21, of which 13 were waited for; matrix products, arithmetic and copies ran while one was open for 0% of the time, Pallas kernels for 7%

profile of v1, /device:TPU:0, one launch (start us, length us, event | category | flops | bytes accessed | tf_op | source)
XLA Modules:
  0.0 68.7 jit_solution(167746063793941614)
XLA Ops:
  0.0 3.0 %collective-permute-start.7 = (bf16[32,3072]{1,0:T(8,128)(2,1)}, bf16[32,3072]{1,0:T(8,128)(2,1)S(1)}, u32[]{:S(2)}, u32[]{:S(2)}) collective-permute-start(bf16[32,3072]{1,0:T(8,128)(2,1)} %refs_4_.3), channel_id=1, source_target_pairs={{0,8},{4,12},{8,0},{12,4},{1,9},{5,13},{9,1},{13,5},{2,10},{6,14},... | collective-permute-start | bytes 589832 | tf_op jit(solution)/shard_map/ppermute | solution.py:37
  3.0 0.5 collective-permute-start
  4.2 4.8 %collective-permute-done.7.refs_6_ = bf16[32,3072]{1,0:T(8,128)(2,1)S(1)} collective-permute-done((bf16[32,3072]{1,0:T(8,128)(2,1)}, bf16[32,3072]{1,0:T(8,128)(2,1)S(1)}, u32[]{:S(2)}, u32[]{:S(2)}) %collective-permute-start.7) | collective-permute-done | bytes 196640 | tf_op jit(solution)/shard_map/ppermute | solution.py:37
  8.9 3.4 %collective-permute-done.1.refs_2_ = bf16[768,128]{1,0:T(8,128)(2,1)S(1)} collective-permute-done((bf16[768,128]{1,0:T(8,128)(2,1)}, bf16[768,128]{1,0:T(8,128)(2,1)S(1)}, u32[]{:S(2)}, u32[]{:S(2)}) %collective-permute-start.1) | collective-permute-done | bytes 196640 | tf_op jit(solution)/shard_map/ppermute | solution.py:37
  12.4 1.3 %copy-done.2 = bf16[256,2304]{1,0:T(8,128)(2,1)S(1)} copy-done((bf16[256,2304]{1,0:T(8,128)(2,1)S(1)}, bf16[256,2304]{1,0:T(8,128)(2,1)}, u32[]{:S(2)}) %copy-start.2) | copy-done | bytes 1179672
  13.6 0.7 %copy-done.5 = f32[32,128]{1,0:T(8,128)S(1)} copy-done((f32[32,128]{1,0:T(8,128)S(1)}, f32[32,128]{1,0:T(8,128)}, u32[]{:S(2)}) %copy-start.5) | copy-done | bytes 16408
  14.6 1.9 %collective-permute-start.3 = (f32[50,128]{1,0:T(8,128)S(1)}, f32[50,128]{1,0:T(8,128)S(1)}, u32[]{:S(2)}, u32[]{:S(2)}) collective-permute-start(f32[50,128]{1,0:T(8,128)S(1)} %modulation.1.refs_0_), channel_id=1, source_target_pairs={{0,1},{1,0},{2,3},{3,2},{4,5},{5,4},{6,7},{7,6},{8,9},{9,8},{10,11... | collective-permute-start | bytes 76808 | tf_op jit(solution)/shard_map/ppermute | solution.py:37
  16.5 2.0 %collective-permute-done.3.refs_1_ = f32[50,128]{1,0:T(8,128)S(1)} collective-permute-done((f32[50,128]{1,0:T(8,128)S(1)}, f32[50,128]{1,0:T(8,128)S(1)}, u32[]{:S(2)}, u32[]{:S(2)}) %collective-permute-start.3) | collective-permute-done | bytes 25632 | tf_op jit(solution)/shard_map/ppermute | solution.py:37
  18.5 2.8 %collective-permute-start.4 = (f32[50,128]{1,0:T(8,128)S(1)}, f32[50,128]{1,0:T(8,128)S(1)}, u32[]{:S(2)}, u32[]{:S(2)}) collective-permute-start(f32[50,128]{1,0:T(8,128)S(1)} %modulation.1.refs_0_), channel_id=1, source_target_pairs={{0,2},{1,3},{2,0},{3,1},{4,6},{5,7},{6,4},{7,5},{8,10},{9,11},{10,... | collective-permute-start | bytes 76808 | tf_op jit(solution)/shard_map/ppermute | solution.py:37
  21.4 1.9 %collective-permute-done.4.refs_2_ = f32[50,128]{1,0:T(8,128)S(1)} collective-permute-done((f32[50,128]{1,0:T(8,128)S(1)}, f32[50,128]{1,0:T(8,128)S(1)}, u32[]{:S(2)}, u32[]{:S(2)}) %collective-permute-start.4) | collective-permute-done | bytes 25632 | tf_op jit(solution)/shard_map/ppermute | solution.py:37
  23.3 4.0 %collective-permute-start.5 = (f32[50,128]{1,0:T(8,128)S(1)}, f32[50,128]{1,0:T(8,128)S(1)}, u32[]{:S(2)}, u32[]{:S(2)}) collective-permute-start(f32[50,128]{1,0:T(8,128)S(1)} %modulation.1.refs_0_), channel_id=1, source_target_pairs={{0,3},{1,2},{2,1},{3,0},{4,7},{5,6},{6,5},{7,4},{8,11},{9,10},{10,... | collective-permute-start | bytes 76808 | tf_op jit(solution)/shard_map/ppermute | solution.py:37
  28.0 1.2 %collective-permute-done.5.refs_3_ = f32[50,128]{1,0:T(8,128)S(1)} collective-permute-done((f32[50,128]{1,0:T(8,128)S(1)}, f32[50,128]{1,0:T(8,128)S(1)}, u32[]{:S(2)}, u32[]{:S(2)}) %collective-permute-start.5) | collective-permute-done | bytes 25632 | tf_op jit(solution)/shard_map/ppermute | solution.py:37
  29.2 3.7 %copy-done = bf16[3072,1536]{1,0:T(8,128)(2,1)S(1)} copy-done((bf16[3072,1536]{1,0:T(8,128)(2,1)S(1)}, bf16[3072,1536]{1,0:T(8,128)(2,1)}, u32[]{:S(2)}) %copy-start) | copy-done | bytes 9437208
  32.9 0.9 %copy-done.4 = bf16[32,3072]{1,0:T(8,128)(2,1)S(1)} copy-done((bf16[32,3072]{1,0:T(8,128)(2,1)S(1)}, bf16[32,3072]{1,0:T(8,128)(2,1)}, u32[]{:S(2)}) %copy-start.4) | copy-done | bytes 196632
  33.8 4.9 %setup.1 = (bf16[256,1536]{1,0:T(8,128)(2,1)S(1)}, f32[8,1536]{1,0:T(8,128)S(1)}, bf16[384,128]{1,0:T(8,128)(2,1)S(1)}, f32[128,128]{1,0:T(8,128)S(1)}, bf16[128...) custom-call(f32[50,128]{1,0:T(8,128)S(1)} %modulation.1.refs_0_, ...), custom_call_target="tpu_custom_call" | custom-call | tf_op jit(solution)/shard_map/setup/pallas_call | solution.py:220
  38.7 1.6 %fold.1 = (bf16[512,128]{1,0:T(8,128)(2,1)S(1)}, bf16[256,128]{1,0:T(8,128)(2,1)S(1)}, bf16[128,128]{1,0:T(8,128)(2,1)S(1)}) custom-call(bf16[768,128]{1,0:T(8,128)(2,1)S(1)} %copy-done.3, bf16[768,128]{1,0:T(8,128)(2,1)S(1)} %collective-permute-done.refs_1_, bf16[768,128]{1,0:T(8,128)(2,1)S(1)} %collective-permute-done.1.refs_2_, ...), custom_call_target="tpu_custom_call" | custom-call | tf_op jit(solution)/shard_map/fold/pallas_call | solution.py:220
  40.3 1.6 %collective-permute-start.10 = (bf16[128,128]{1,0:T(8,128)(2,1)S(1)}, bf16[128,128]{1,0:T(8,128)(2,1)S(1)}, u32[]{:S(2)}, u32[]{:S(2)}) collective-permute-start(bf16[128,128]{1,0:T(8,128)(2,1)S(1)} %get-tuple-element.23), channel_id=1, source_target_pairs={{0,8},{4,12},{8,0},{12,4},{1,9},{5,13},{9,1},{13,5},{2,10},{6,14},... | collective-permute-start | bytes 98312 | tf_op jit(solution)/shard_map/ppermute | solution.py:37
  41.9 0.6 collective-permute-start.9
  42.5 1.8 %collective-permute-done.10 = bf16[128,128]{1,0:T(8,128)(2,1)S(1)} collective-permute-done((bf16[128,128]{1,0:T(8,128)(2,1)S(1)}, bf16[128,128]{1,0:T(8,128)(2,1)S(1)}, u32[]{:S(2)}, u32[]{:S(2)}) %collective-permute-start.10) | collective-permute-done | bytes 32800 | tf_op jit(solution)/shard_map/ppermute | solution.py:37
  44.3 0.9 %collective-permute-done.11 = bf16[128,128]{1,0:T(8,128)(2,1)S(1)} collective-permute-done((bf16[128,128]{1,0:T(8,128)(2,1)S(1)}, bf16[128,128]{1,0:T(8,128)(2,1)S(1)}, u32[]{:S(2)}, u32[]{:S(2)}) %collective-permute-start.11) | collective-permute-done | bytes 32800 | tf_op jit(solution)/shard_map/ppermute | solution.py:37
  45.4 4.3 %collective-permute-start.13 = (bf16[128,128]{1,0:T(8,128)(2,1)S(1)}, bf16[128,128]{1,0:T(8,128)(2,1)S(1)}, u32[]{:S(2)}, u32[]{:S(2)}) collective-permute-start(bf16[128,128]{1,0:T(8,128)(2,1)S(1)} %add_convert_fusion.refs_0_), channel_id=1, source_target_pairs={{0,2},{1,3},{2,0},{3,1},{4,6},{5,7},{6,4},{7,5},{8,10},{9,11},{10,... | collective-permute-start | bytes 98312 | tf_op jit(solution)/shard_map/ppermute | solution.py:37
  49.7 2.2 %collective-permute-done.13.refs_2_ = bf16[128,128]{1,0:T(8,128)(2,1)S(1)} collective-permute-done((bf16[128,128]{1,0:T(8,128)(2,1)S(1)}, bf16[128,128]{1,0:T(8,128)(2,1)S(1)}, u32[]{:S(2)}, u32[]{:S(2)}) %collective-permute-start.13) | collective-permute-done | bytes 32800 | tf_op jit(solution)/shard_map/ppermute | solution.py:37
  51.9 3.5 %collective-permute-done.14.refs_3_ = bf16[128,128]{1,0:T(8,128)(2,1)S(1)} collective-permute-done((bf16[128,128]{1,0:T(8,128)(2,1)S(1)}, bf16[128,128]{1,0:T(8,128)(2,1)S(1)}, u32[]{:S(2)}, u32[]{:S(2)}) %collective-permute-start.14) | collective-permute-done | bytes 32800 | tf_op jit(solution)/shard_map/ppermute | solution.py:37
  55.4 2.0 %iterate.1 = (f32[32,128]{1,0:T(8,128)S(1)}, f32[32,128]{1,0:T(8,128)S(1)}, f32[32,128]{1,0:T(8,128)S(1)}, f32[32,128]{1,0:T(8,128)S(1)}) custom-call(bf16[128,128]{1,0:T(8,128)(2,1)S(1)} %add_convert_fusion.refs_0_, bf16[128,128]{1,0:T(8,128)(2,1)S(1)} %collective-permute-done.12.refs_1_, bf16[128,128]{1,0:T(8,128)(2,1)S(1)} %collective-permute-done.13.refs_2_, ...), custom_call_target="tpu_custom_call" | custom-call | tf_op jit(solution)/shard_map/iterate/pallas_call | solution.py:220
  57.5 0.9 %collective-permute-start.16 = (f32[32,128]{1,0:T(8,128)S(1)}, f32[32,128]{1,0:T(8,128)S(1)}, u32[]{:S(2)}, u32[]{:S(2)}) collective-permute-start(f32[32,128]{1,0:T(8,128)S(1)} %get-tuple-element.31), channel_id=1, source_target_pairs={{0,2},{1,3},{2,0},{3,1},{4,6},{5,7},{6,4},{7,5},{8,10},{9,11},{10,... | collective-permute-start | bytes 49160 | tf_op jit(solution)/shard_map/ppermute | solution.py:37
  58.4 3.5 %collective-permute-start.17 = (f32[32,128]{1,0:T(8,128)S(1)}, f32[32,128]{1,0:T(8,128)S(1)}, u32[]{:S(2)}, u32[]{:S(2)}) collective-permute-start(f32[32,128]{1,0:T(8,128)S(1)} %get-tuple-element.32), channel_id=1, source_target_pairs={{0,3},{1,2},{2,1},{3,0},{4,7},{5,6},{6,5},{7,4},{8,11},{9,10},{10,... | collective-permute-start | bytes 49160 | tf_op jit(solution)/shard_map/ppermute | solution.py:37
  61.9 0.3 collective-permute-done.16
  62.2 1.7 %collective-permute-done.17 = f32[32,128]{1,0:T(8,128)S(1)} collective-permute-done((f32[32,128]{1,0:T(8,128)S(1)}, f32[32,128]{1,0:T(8,128)S(1)}, u32[]{:S(2)}, u32[]{:S(2)}) %collective-permute-start.17) | collective-permute-done | bytes 16416 | tf_op jit(solution)/shard_map/ppermute | solution.py:37
  63.9 1.0 %collective-permute-start.19 = (f32[32,128]{1,0:T(8,128)S(1)}, f32[32,128]{1,0:T(8,128)S(1)}, u32[]{:S(2)}, u32[]{:S(2)}) collective-permute-start(f32[32,128]{1,0:T(8,128)S(1)} %add_add_fusion), channel_id=1, source_target_pairs={{0,8},{4,12},{8,0},{12,4},{1,9},{5,13},{9,1},{13,5},{2,10},{6,14},... | collective-permute-start | bytes 49160 | tf_op jit(solution)/shard_map/ppermute | solution.py:37
  64.9 0.9 %collective-permute-start.20 = (f32[32,128]{1,0:T(8,128)S(1)}, f32[32,128]{1,0:T(8,128)S(1)}, u32[]{:S(2)}, u32[]{:S(2)}) collective-permute-start(f32[32,128]{1,0:T(8,128)S(1)} %add_add_fusion), channel_id=1, source_target_pairs={{0,12},{4,8},{8,4},{12,0},{1,13},{5,9},{9,5},{13,1},{2,14},{6,10},... | collective-permute-start | bytes 49160 | tf_op jit(solution)/shard_map/ppermute | solution.py:37
  65.8 1.9 %collective-permute-done.19 = f32[32,128]{1,0:T(8,128)S(1)} collective-permute-done((f32[32,128]{1,0:T(8,128)S(1)}, f32[32,128]{1,0:T(8,128)S(1)}, u32[]{:S(2)}, u32[]{:S(2)}) %collective-permute-start.19) | collective-permute-done | bytes 16416 | tf_op jit(solution)/shard_map/ppermute | solution.py:37
  68.1 0.6 add_bitcast_fusion
  (33 shorter events, 0.9 us)
Async XLA Ops:
  0.0 8.9 %collective-permute-start.7 = (bf16[32,3072]{1,0:T(8,128)(2,1)}, bf16[32,3072]{1,0:T(8,128)(2,1)S(1)}, u32[]{:S(2)}, u32[]{:S(2)}) collective-permute-start(bf16[32,3072]{1,0:T(8,128)(2,1)} %refs_4_.3), channel_id=1, source_target_pairs={{0,8},{4,12},{8,0},{12,4},{1,9},{5,13},{9,1},{13,5},{2,10},{6,14},... | collective-permute-start | bytes 589832 | tf_op jit(solution)/shard_map/ppermute | solution.py:37
  3.0 9.3 %collective-permute-start.1 = (bf16[768,128]{1,0:T(8,128)(2,1)}, bf16[768,128]{1,0:T(8,128)(2,1)S(1)}, u32[]{:S(2)}, u32[]{:S(2)}) collective-permute-start(bf16[768,128]{1,0:T(8,128)(2,1)} %refs_0_.1), channel_id=1, source_target_pairs={{0,8},{4,12},{8,0},{12,4},{1,9},{5,13},{9,1},{13,5},{2,10},{6,14},... | collective-permute-start | bytes 589832 | tf_op jit(solution)/shard_map/ppermute | solution.py:37
  3.0 26.2 %collective-permute-start.6 = (bf16[32,3072]{1,0:T(8,128)(2,1)}, bf16[32,3072]{1,0:T(8,128)(2,1)S(1)}, u32[]{:S(2)}, u32[]{:S(2)}) collective-permute-start(bf16[32,3072]{1,0:T(8,128)(2,1)} %refs_4_.3), channel_id=1, source_target_pairs={{0,4},{4,0},{8,12},{12,8},{1,5},{5,1},{9,13},{13,9},{2,6},{6,2},{1... | collective-permute-start | bytes 589832 | tf_op jit(solution)/shard_map/ppermute | solution.py:37
  3.0 35.7 %collective-permute-start = (bf16[768,128]{1,0:T(8,128)(2,1)}, bf16[768,128]{1,0:T(8,128)(2,1)S(1)}, u32[]{:S(2)}, u32[]{:S(2)}) collective-permute-start(bf16[768,128]{1,0:T(8,128)(2,1)} %refs_0_.1), channel_id=1, source_target_pairs={{0,4},{4,0},{8,12},{12,8},{1,5},{5,1},{9,13},{13,9},{2,6},{6,2},{1... | collective-permute-start | bytes 589832 | tf_op jit(solution)/shard_map/ppermute | solution.py:37
  8.9 20.3 %collective-permute-start.8 = (bf16[32,3072]{1,0:T(8,128)(2,1)S(1)}, bf16[32,3072]{1,0:T(8,128)(2,1)S(1)}, u32[]{:S(2)}, u32[]{:S(2)}) collective-permute-start(bf16[32,3072]{1,0:T(8,128)(2,1)S(1)} %collective-permute-done.7.refs_6_), channel_id=1, source_target_pairs={{0,4},{4,0},{8,12},{12,8},{1,5},{5,1},{9,13},{13,9},{2,6},{6,2},{1... | collective-permute-start | bytes 589832 | tf_op jit(solution)/shard_map/ppermute | solution.py:37
  12.3 26.4 %collective-permute-start.2 = (bf16[768,128]{1,0:T(8,128)(2,1)S(1)}, bf16[768,128]{1,0:T(8,128)(2,1)S(1)}, u32[]{:S(2)}, u32[]{:S(2)}) collective-permute-start(bf16[768,128]{1,0:T(8,128)(2,1)S(1)} %collective-permute-done.1.refs_2_), channel_id=1, source_target_pairs={{0,4},{4,0},{8,12},{12,8},{1,5},{5,1},{9,13},{13,9},{2,6},{6,2},{1... | collective-permute-start | bytes 589832 | tf_op jit(solution)/shard_map/ppermute | solution.py:37
  12.4 1.3 %copy-start.2 = (bf16[256,2304]{1,0:T(8,128)(2,1)S(1)}, bf16[256,2304]{1,0:T(8,128)(2,1)}, u32[]{:S(2)}) copy-start(bf16[256,2304]{1,0:T(8,128)(2,1)} %weight_ref.1) | copy-start | bytes 3538948
  13.6 0.7 %copy-start.5 = (f32[32,128]{1,0:T(8,128)S(1)}, f32[32,128]{1,0:T(8,128)}, u32[]{:S(2)}) copy-start(f32[32,128]{1,0:T(8,128)} %start_ref.1) | copy-start | bytes 49156
  14.6 3.9 %collective-permute-start.3 = (f32[50,128]{1,0:T(8,128)S(1)}, f32[50,128]{1,0:T(8,128)S(1)}, u32[]{:S(2)}, u32[]{:S(2)}) collective-permute-start(f32[50,128]{1,0:T(8,128)S(1)} %modulation.1.refs_0_), channel_id=1, source_target_pairs={{0,1},{1,0},{2,3},{3,2},{4,5},{5,4},{6,7},{7,6},{8,9},{9,8},{10,11... | collective-permute-start | bytes 76808 | tf_op jit(solution)/shard_map/ppermute | solution.py:37
  18.5 4.8 %collective-permute-start.4 = (f32[50,128]{1,0:T(8,128)S(1)}, f32[50,128]{1,0:T(8,128)S(1)}, u32[]{:S(2)}, u32[]{:S(2)}) collective-permute-start(f32[50,128]{1,0:T(8,128)S(1)} %modulation.1.refs_0_), channel_id=1, source_target_pairs={{0,2},{1,3},{2,0},{3,1},{4,6},{5,7},{6,4},{7,5},{8,10},{9,11},{10,... | collective-permute-start | bytes 76808 | tf_op jit(solution)/shard_map/ppermute | solution.py:37
  23.3 5.9 %collective-permute-start.5 = (f32[50,128]{1,0:T(8,128)S(1)}, f32[50,128]{1,0:T(8,128)S(1)}, u32[]{:S(2)}, u32[]{:S(2)}) collective-permute-start(f32[50,128]{1,0:T(8,128)S(1)} %modulation.1.refs_0_), channel_id=1, source_target_pairs={{0,3},{1,2},{2,1},{3,0},{4,7},{5,6},{6,5},{7,4},{8,11},{9,10},{10,... | collective-permute-start | bytes 76808 | tf_op jit(solution)/shard_map/ppermute | solution.py:37
  29.2 3.7 %copy-start = (bf16[3072,1536]{1,0:T(8,128)(2,1)S(1)}, bf16[3072,1536]{1,0:T(8,128)(2,1)}, u32[]{:S(2)}) copy-start(bf16[3072,1536]{1,0:T(8,128)(2,1)} %refs_8_.1) | copy-start | bytes 28311556
  32.9 0.9 %copy-start.4 = (bf16[32,3072]{1,0:T(8,128)(2,1)S(1)}, bf16[32,3072]{1,0:T(8,128)(2,1)}, u32[]{:S(2)}) copy-start(bf16[32,3072]{1,0:T(8,128)(2,1)} %refs_4_.3) | copy-start | bytes 589828
  33.8 4.9 %copy-start.1 = (bf16[512,3072]{1,0:T(8,128)(2,1)S(1)}, bf16[512,3072]{1,0:T(8,128)(2,1)}, u32[]{:S(2)}) copy-start(bf16[512,3072]{1,0:T(8,128)(2,1)} %refs_5_.1) | copy-start | bytes 9437188
  33.8 4.9 %copy-start.3 = (bf16[768,128]{1,0:T(8,128)(2,1)S(1)}, bf16[768,128]{1,0:T(8,128)(2,1)}, u32[]{:S(2)}) copy-start(bf16[768,128]{1,0:T(8,128)(2,1)} %refs_0_.1) | copy-start | bytes 589828
  38.7 29.3 %copy-start.6 = (f32[32,128]{1,0:T(8,128)S(1)}, f32[32,128]{1,0:T(8,128)}, u32[]{:S(2)}) copy-start(f32[32,128]{1,0:T(8,128)} %start_ref.1) | copy-start | bytes 49156
  40.3 4.0 %collective-permute-start.10 = (bf16[128,128]{1,0:T(8,128)(2,1)S(1)}, bf16[128,128]{1,0:T(8,128)(2,1)S(1)}, u32[]{:S(2)}, u32[]{:S(2)}) collective-permute-start(bf16[128,128]{1,0:T(8,128)(2,1)S(1)} %get-tuple-element.23), channel_id=1, source_target_pairs={{0,8},{4,12},{8,0},{12,4},{1,9},{5,13},{9,1},{13,5},{2,10},{6,14},... | collective-permute-start | bytes 98312 | tf_op jit(solution)/shard_map/ppermute | solution.py:37
  41.9 3.3 %collective-permute-start.11 = (bf16[128,128]{1,0:T(8,128)(2,1)S(1)}, bf16[128,128]{1,0:T(8,128)(2,1)S(1)}, u32[]{:S(2)}, u32[]{:S(2)}) collective-permute-start(bf16[128,128]{1,0:T(8,128)(2,1)S(1)} %get-tuple-element.23), channel_id=1, source_target_pairs={{0,12},{4,8},{8,4},{12,0},{1,13},{5,9},{9,5},{13,1},{2,14},{6,10},... | collective-permute-start | bytes 98312 | tf_op jit(solution)/shard_map/ppermute | solution.py:37
  41.9 3.3 %collective-permute-start.9 = (bf16[128,128]{1,0:T(8,128)(2,1)S(1)}, bf16[128,128]{1,0:T(8,128)(2,1)S(1)}, u32[]{:S(2)}, u32[]{:S(2)}) collective-permute-start(bf16[128,128]{1,0:T(8,128)(2,1)S(1)} %get-tuple-element.23), channel_id=1, source_target_pairs={{0,4},{4,0},{8,12},{12,8},{1,5},{5,1},{9,13},{13,9},{2,6},{6,2},{1... | collective-permute-start | bytes 98312 | tf_op jit(solution)/shard_map/ppermute | solution.py:37
  45.3 4.5 %collective-permute-start.12 = (bf16[128,128]{1,0:T(8,128)(2,1)S(1)}, bf16[128,128]{1,0:T(8,128)(2,1)S(1)}, u32[]{:S(2)}, u32[]{:S(2)}) collective-permute-start(bf16[128,128]{1,0:T(8,128)(2,1)S(1)} %add_convert_fusion.refs_0_), channel_id=1, source_target_pairs={{0,1},{1,0},{2,3},{3,2},{4,5},{5,4},{6,7},{7,6},{8,9},{9,8},{10,11... | collective-permute-start | bytes 98312 | tf_op jit(solution)/shard_map/ppermute | solution.py:37
  45.4 6.6 %collective-permute-start.13 = (bf16[128,128]{1,0:T(8,128)(2,1)S(1)}, bf16[128,128]{1,0:T(8,128)(2,1)S(1)}, u32[]{:S(2)}, u32[]{:S(2)}) collective-permute-start(bf16[128,128]{1,0:T(8,128)(2,1)S(1)} %add_convert_fusion.refs_0_), channel_id=1, source_target_pairs={{0,2},{1,3},{2,0},{3,1},{4,6},{5,7},{6,4},{7,5},{8,10},{9,11},{10,... | collective-permute-start | bytes 98312 | tf_op jit(solution)/shard_map/ppermute | solution.py:37
  49.7 5.7 %collective-permute-start.14 = (bf16[128,128]{1,0:T(8,128)(2,1)S(1)}, bf16[128,128]{1,0:T(8,128)(2,1)S(1)}, u32[]{:S(2)}, u32[]{:S(2)}) collective-permute-start(bf16[128,128]{1,0:T(8,128)(2,1)S(1)} %add_convert_fusion.refs_0_), channel_id=1, source_target_pairs={{0,3},{1,2},{2,1},{3,0},{4,7},{5,6},{6,5},{7,4},{8,11},{9,10},{10,... | collective-permute-start | bytes 98312 | tf_op jit(solution)/shard_map/ppermute | solution.py:37
  57.4 4.5 %collective-permute-start.15 = (f32[32,128]{1,0:T(8,128)S(1)}, f32[32,128]{1,0:T(8,128)S(1)}, u32[]{:S(2)}, u32[]{:S(2)}) collective-permute-start(f32[32,128]{1,0:T(8,128)S(1)} %get-tuple-element.30), channel_id=1, source_target_pairs={{0,1},{1,0},{2,3},{3,2},{4,5},{5,4},{6,7},{7,6},{8,9},{9,8},{10,11... | collective-permute-start | bytes 49160 | tf_op jit(solution)/shard_map/ppermute | solution.py:37
  57.5 4.7 %collective-permute-start.16 = (f32[32,128]{1,0:T(8,128)S(1)}, f32[32,128]{1,0:T(8,128)S(1)}, u32[]{:S(2)}, u32[]{:S(2)}) collective-permute-start(f32[32,128]{1,0:T(8,128)S(1)} %get-tuple-element.31), channel_id=1, source_target_pairs={{0,2},{1,3},{2,0},{3,1},{4,6},{5,7},{6,4},{7,5},{8,10},{9,11},{10,... | collective-permute-start | bytes 49160 | tf_op jit(solution)/shard_map/ppermute | solution.py:37
  58.4 5.5 %collective-permute-start.17 = (f32[32,128]{1,0:T(8,128)S(1)}, f32[32,128]{1,0:T(8,128)S(1)}, u32[]{:S(2)}, u32[]{:S(2)}) collective-permute-start(f32[32,128]{1,0:T(8,128)S(1)} %get-tuple-element.32), channel_id=1, source_target_pairs={{0,3},{1,2},{2,1},{3,0},{4,7},{5,6},{6,5},{7,4},{8,11},{9,10},{10,... | collective-permute-start | bytes 49160 | tf_op jit(solution)/shard_map/ppermute | solution.py:37
  63.9 1.9 %collective-permute-start.18 = (f32[32,128]{1,0:T(8,128)S(1)}, f32[32,128]{1,0:T(8,128)S(1)}, u32[]{:S(2)}, u32[]{:S(2)}) collective-permute-start(f32[32,128]{1,0:T(8,128)S(1)} %add_add_fusion), channel_id=1, source_target_pairs={{0,4},{4,0},{8,12},{12,8},{1,5},{5,1},{9,13},{13,9},{2,6},{6,2},{1... | collective-permute-start | bytes 49160 | tf_op jit(solution)/shard_map/ppermute | solution.py:37
  63.9 3.8 %collective-permute-start.19 = (f32[32,128]{1,0:T(8,128)S(1)}, f32[32,128]{1,0:T(8,128)S(1)}, u32[]{:S(2)}, u32[]{:S(2)}) collective-permute-start(f32[32,128]{1,0:T(8,128)S(1)} %add_add_fusion), channel_id=1, source_target_pairs={{0,8},{4,12},{8,0},{12,4},{1,9},{5,13},{9,1},{13,5},{2,10},{6,14},... | collective-permute-start | bytes 49160 | tf_op jit(solution)/shard_map/ppermute | solution.py:37
  64.9 3.2 %collective-permute-start.20 = (f32[32,128]{1,0:T(8,128)S(1)}, f32[32,128]{1,0:T(8,128)S(1)}, u32[]{:S(2)}, u32[]{:S(2)}) collective-permute-start(f32[32,128]{1,0:T(8,128)S(1)} %add_add_fusion), channel_id=1, source_target_pairs={{0,12},{4,8},{8,4},{12,0},{1,13},{5,9},{9,5},{13,1},{2,14},{6,10},... | collective-permute-start | bytes 49160 | tf_op jit(solution)/shard_map/ppermute | solution.py:37

commit v2 on v1

--- a/solution.py
+++ b/solution.py
@@ -7,6 +7,7 @@
 from jax.experimental import pallas as pl
 from jax.experimental.pallas import tpu as pltpu
 from jax.sharding import PartitionSpec as P
+
 
 HD = 128
 LANES = 128
@@ -75,12 +76,35 @@
     return out
 
 
-def modulation_kernel(emb_ref, weight_ref, start_ref, out_ref):
+def modulation_kernel(emb_ref, weight_hbm, start_hbm, out_ref, weight_ref, start_ref, sems):
     rows = start_ref.shape[0]
+    copies = [
+        pltpu.make_async_copy(weight_hbm, weight_ref, sems.at[0]),
+        pltpu.make_async_copy(start_hbm, start_ref, sems.at[1]),
+    ]
+    for copy in copies:
+        copy.start()
+    for copy in copies:
+        copy.wait()
     result = bdot(jnp.broadcast_to(emb_ref[...], (16, emb_ref.shape[1])), weight_ref[...])
     out_ref[0:rows, :] = start_ref[...]
     for r in range(weight_ref.shape[1] // LANES):
         out_ref[rows + r : rows + r + 1, :] = result[0:1, r * LANES : (r + 1) * LANES]
+
+
+def load_kernel(source, out_ref, sems):
+    n = sems.shape[0]
+    rows = source.shape[0] // n
+    copies = [
+        pltpu.make_async_copy(
+            source.at[pl.ds(i * rows, rows)], out_ref.at[pl.ds(i * rows, rows)], sems.at[i]
+        )
+        for i in range(n)
+    ]
+    for copy in copies:
+        copy.start()
+    for copy in copies:
+        copy.wait()
 
 
 def attend(x, factors, base, gram, head_count):
@@ -100,12 +124,12 @@
     return outs[0] if head_count == 1 else jnp.concatenate(outs, axis=1)
 
 
-def setup_kernel(nt, nm, rows, head_count, *refs):
+def setup_kernel(nt, nm, head_count, *refs):
     msgs, refs = refs[:nt], refs[nt:]
     inws, refs = refs[:nm], refs[nm:]
     qkv_ref, refs = refs[0], refs[1:]
-    factor_ref, base_ref, gram_ref, start_ref, inw_ref, gate_ref, att_ref = refs[:7]
-    start_s, mod_s, inw_s, z_s = refs[7:]
+    factor_ref, base_ref, gram_ref, start_ref, inw_ref, gate_ref = refs[:6]
+    start_s, mod_s, inw_s, z_s = refs[6:]
     for k in range(nt):
         at = place("tensor", nt, k)
         start_s[at] = msgs[k][0 : start_s.shape[1], :]
@@ -150,7 +174,11 @@
         return carry
 
     lax.fori_loop(0, head_count, columns, 0)
-    att_ref[...] = attend(start.astype(BF16), factor_ref, base_ref, gram_ref, head_count)
+
+
+def attend_kernel(head_count, start_ref, factor_ref, base_ref, gram_ref, out_ref):
+    x = start_ref[...].astype(BF16)
+    out_ref[...] = attend(x, factor_ref, base_ref, gram_ref, head_count)
 
 
 def add_own_rows(result, residual, rows):
@@ -213,18 +241,15 @@
     return jax.ShapeDtypeStruct(shape, dtype)
 
 
-PARAMS = pltpu.CompilerParams(vmem_limit_bytes=40 * 2**20)
-
-
-def call(kernel, name, outs, in_specs, scratch, *args):
+def call(kernel, outs, in_specs, scratch, *args, cost=4 * 2**20, limit=8):
     return pl.pallas_call(
         kernel,
-        name=name,
         out_shape=outs,
         in_specs=in_specs,
         out_specs=[VMEM] * len(outs),
         scratch_shapes=scratch,
-        compiler_params=PARAMS,
+        compiler_params=pltpu.CompilerParams(vmem_limit_bytes=limit * 2**20),
+        cost_estimate=pl.CostEstimate(flops=0, bytes_accessed=cost, transcendentals=0),
     )(*args)
 
 
@@ -271,13 +296,17 @@
         mod_rows = mod_weight.shape[1] // LANES
         message = call(
             modulation_kernel,
-            "modulation",
             [shape_of((rows + mod_rows, LANES), F32)],
-            [VMEM] * 3,
-            [],
+            [VMEM] + [pl.BlockSpec(memory_space=pltpu.HBM)] * 2,
+            [
+                pltpu.VMEM(mod_weight.shape, BF16),
+                pltpu.VMEM(start_latent.shape, F32),
+                pltpu.SemaphoreType.DMA((2,)),
+            ],
             embedding,
             mod_weight,
             start_latent,
+            limit=62,
         )[0]
         messages = gather_parts(message, "tensor")
         block_rows = rows
@@ -288,11 +317,18 @@
         messages = [jnp.concatenate([start_all, modulation.reshape(-1, LANES)], axis=0)]
         block_rows = tokens
     nt, nm = len(messages), len(inw_parts)
+    qkv_near = call(
+        load_kernel,
+        [shape_of(qkv_weight.shape, BF16)],
+        [pl.BlockSpec(memory_space=pltpu.HBM)],
+        [pltpu.SemaphoreType.DMA((4,))],
+        qkv_weight,
+        limit=40,
+    )[0]
     mod_rows = messages[0].shape[0] - block_rows
     padded = -(-mod_rows // 8) * 8
-    factor, base, gram, start_all, inw_all, gate, attended = call(
-        functools.partial(setup_kernel, nt, nm, rows, head_count),
-        "setup",
+    factor, base, gram, start_all, inw_all, gate = call(
+        functools.partial(setup_kernel, nt, nm, head_count),
         [
             shape_of((2 * channels, qkv_weight.shape[1]), BF16),
             shape_of((8, qkv_weight.shape[1]), F32),
@@ -300,7 +336,6 @@
             shape_of((tokens, channels), F32),
             shape_of((channels, width), BF16),
             shape_of((chunks, LANES), F32),
-            shape_of((tokens, head_count * HD), BF16),
         ],
         [VMEM] * (nt + nm + 1),
         [
@@ -311,12 +346,22 @@
         ],
         *messages,
         *inw_parts,
-        qkv_weight,
+        qkv_near,
+        limit=24,
     )
+    attended = call(
+        functools.partial(attend_kernel, head_count),
+        [shape_of((tokens, head_count * HD), BF16)],
+        [VMEM] * 4,
+        [],
+        start_all,
+        factor,
+        base,
+        gram,
+    )[0]
     head_parts = gather_weight_parts(head_weight, "tm")
     folded, resid, vel = call(
         functools.partial(fold_kernel, nm, rows),
-        "fold",
         [
             shape_of((span, channels), BF16),
             shape_of((2 * channels, channels), BF16),
@@ -334,6 +379,7 @@
         inw_all,
         attended,
         start_all,
+        limit=24,
     )
     small = is_small("tensor")
     for iteration in range(1, ITERS):
@@ -350,7 +396,6 @@
             outs = [shape_of((tokens, channels), F32 if last else BF16)]
         vels = call(
             functools.partial(iterate_kernel, len(pieces), rows, head_count, split),
-            "iterate",
             outs,
             [VMEM] * len(pieces) + [SMEM] + [VMEM] * 6,
             [pltpu.VMEM((n_tensor, rows, channels), F32)],

time: 69 us -> 68.4 us (level)
  local copies, waits for them, and re-layouts: 6.6 us -> 0.03 us
  Pallas kernels: 8.7 us -> 15.1 us
  waiting for transfers between devices: 26 us -> 24.9 us
    unnamed x14 -> x10, local copies, waits for them, and re-layouts: 6.6 us -> 0.03 us
    pallas_call x4 -> x6, Pallas kernels: 8.7 us -> 15.1 us  [call(): pl.pallas_call(kernel, out_shape=outs, in_specs=in_specs, out_specs=[VMEM...]
    ppermute x21, waiting for transfers between devices: 26 us -> 24.9 us  [swap(): return lax.ppermute(value, axis, [(i, i ^ k) for i in range(n)])]
  transfers between devices with their start and end apart: 21 -> 21, of which waited for: 13 -> 12; matrix products, arithmetic and copies ran while one was open for 0% -> 1% of each run, Pallas kernels for 7% -> 17%
where the time goes in v2:
time: 68.4 us; the launch traced here: 68.2 us
  starting transfers between devices  25.2 us (37%)
  waiting for transfers between devices  24.9 us (36%)
  Pallas kernels  15.1 us (22%)
  between operations  1.65 us (2%)
  other arithmetic  1.27 us (2%)
    ppermute x21, starting transfers between devices, swap(): return lax.ppermute(value, axis, [(i, i ^ k) for i in range(n)])  25.2 us
    ppermute x21, waiting for transfers between devices, swap(): return lax.ppermute(value, axis, [(i, i ^ k) for i in range(n)])  24.9 us
    pallas_call x6, Pallas kernels, call(): pl.pallas_call(kernel, out_shape=outs, in_specs=in_specs, out_specs=[VMEM...  15.1 us
  transfers between devices with their start and end apart: 21, of which 12 were waited for; matrix products, arithmetic and copies ran while one was open for 1% of the time, Pallas kernels for 17%

profile of v2, /device:TPU:0, one launch (start us, length us, event | category | flops | bytes accessed | tf_op | source)
XLA Modules:
  0.0 68.2 jit_solution(5631185531329281921)
XLA Ops:
  0.0 3.0 %collective-permute-start.7 = (bf16[32,3072]{1,0:T(8,128)(2,1)}, bf16[32,3072]{1,0:T(8,128)(2,1)S(1)}, u32[]{:S(2)}, u32[]{:S(2)}) collective-permute-start(bf16[32,3072]{1,0:T(8,128)(2,1)} %refs_4_.3), channel_id=1, source_target_pairs={{0,8},{4,12},{8,0},{12,4},{1,9},{5,13},{9,1},{13,5},{2,10},{6,14},... | collective-permute-start | bytes 589832 | tf_op jit(solution)/shard_map/ppermute | solution.py:38
  3.0 0.5 collective-permute-start
  4.2 4.8 %collective-permute-done.7.refs_6_ = bf16[32,3072]{1,0:T(8,128)(2,1)S(1)} collective-permute-done((bf16[32,3072]{1,0:T(8,128)(2,1)}, bf16[32,3072]{1,0:T(8,128)(2,1)S(1)}, u32[]{:S(2)}, u32[]{:S(2)}) %collective-permute-start.7) | collective-permute-done | bytes 196640 | tf_op jit(solution)/shard_map/ppermute | solution.py:38
  8.9 3.4 %collective-permute-done.1.refs_2_ = bf16[768,128]{1,0:T(8,128)(2,1)S(1)} collective-permute-done((bf16[768,128]{1,0:T(8,128)(2,1)}, bf16[768,128]{1,0:T(8,128)(2,1)S(1)}, u32[]{:S(2)}, u32[]{:S(2)}) %collective-permute-start.1) | collective-permute-done | bytes 196640 | tf_op jit(solution)/shard_map/ppermute | solution.py:38
  12.3 0.6 pad_maximum_fusion.emb_ref
  12.9 2.8 %shard_map.82.refs_0_ = f32[50,128]{1,0:T(8,128)} custom-call(bf16[1,256]{1,0:T(2,128)(2,1)} %pad_maximum_fusion.emb_ref, bf16[256,2304]{1,0:T(8,128)(2,1)} %weight_hbm.1, f32[32,128]{1,0:T(8,128)} %start_hbm.1), custom_call_target="tpu_custom_call" | custom-call | bytes 4194304 | tf_op jit(solution)/shard_map/pallas_call | solution.py:245
  15.8 1.9 %collective-permute-start.3 = (f32[50,128]{1,0:T(8,128)}, f32[50,128]{1,0:T(8,128)S(1)}, u32[]{:S(2)}, u32[]{:S(2)}) collective-permute-start(f32[50,128]{1,0:T(8,128)} %shard_map.82.refs_0_), channel_id=1, source_target_pairs={{0,1},{1,0},{2,3},{3,2},{4,5},{5,4},{6,7},{7,6},{8,9},{9,8},{10,11... | collective-permute-start | bytes 76808 | tf_op jit(solution)/shard_map/ppermute | solution.py:38
  17.7 2.3 %collective-permute-done.3.refs_1_ = f32[50,128]{1,0:T(8,128)S(1)} collective-permute-done((f32[50,128]{1,0:T(8,128)}, f32[50,128]{1,0:T(8,128)S(1)}, u32[]{:S(2)}, u32[]{:S(2)}) %collective-permute-start.3) | collective-permute-done | bytes 25632 | tf_op jit(solution)/shard_map/ppermute | solution.py:38
  19.9 2.8 %collective-permute-start.4 = (f32[50,128]{1,0:T(8,128)}, f32[50,128]{1,0:T(8,128)S(1)}, u32[]{:S(2)}, u32[]{:S(2)}) collective-permute-start(f32[50,128]{1,0:T(8,128)} %shard_map.82.refs_0_), channel_id=1, source_target_pairs={{0,2},{1,3},{2,0},{3,1},{4,6},{5,7},{6,4},{7,5},{8,10},{9,11},{10,... | collective-permute-start | bytes 76808 | tf_op jit(solution)/shard_map/ppermute | solution.py:38
  22.8 2.1 %collective-permute-done.4.refs_2_ = f32[50,128]{1,0:T(8,128)S(1)} collective-permute-done((f32[50,128]{1,0:T(8,128)}, f32[50,128]{1,0:T(8,128)S(1)}, u32[]{:S(2)}, u32[]{:S(2)}) %collective-permute-start.4) | collective-permute-done | bytes 25632 | tf_op jit(solution)/shard_map/ppermute | solution.py:38
  24.9 4.0 %collective-permute-start.5 = (f32[50,128]{1,0:T(8,128)}, f32[50,128]{1,0:T(8,128)S(1)}, u32[]{:S(2)}, u32[]{:S(2)}) collective-permute-start(f32[50,128]{1,0:T(8,128)} %shard_map.82.refs_0_), channel_id=1, source_target_pairs={{0,3},{1,2},{2,1},{3,0},{4,7},{5,6},{6,5},{7,4},{8,11},{9,10},{10,... | collective-permute-start | bytes 76808 | tf_op jit(solution)/shard_map/ppermute | solution.py:38
  29.0 3.8 %shard_map.83.refs_8_ = bf16[3072,1536]{1,0:T(8,128)(2,1)S(1)} custom-call(bf16[3072,1536]{1,0:T(8,128)(2,1)} %source.1), custom_call_target="tpu_custom_call" | custom-call | bytes 4194304 | tf_op jit(solution)/shard_map/pallas_call | solution.py:245
  33.7 3.2 %shard_map.84 = (bf16[256,1536]{1,0:T(8,128)(2,1)S(1)}, f32[8,1536]{1,0:T(8,128)S(1)}, bf16[384,128]{1,0:T(8,128)(2,1)S(1)}, f32[128,128]{1,0:T(8,128)S(1)}, bf1...) custom-call(f32[50,128]{1,0:T(8,128)S(1)} %copy-done.3, f32[50,128]{1,0:T(8,128)S(1)} %collective-permute-done.3.refs_1_, ...), custom_call_target="tpu_custom_call" | custom-call | bytes 4194304 | tf_op jit(solution)/shard_map/pallas_call | solution.py:245
  36.9 1.7 %shard_map.85.refs_8_ = bf16[128,512]{1,0:T(8,128)(2,1)S(1)} custom-call(f32[128,128]{1,0:T(8,128)S(1)} %get-tuple-element.20.start_ref.refs_9_.refs_5_, bf16[256,1536]{1,0:T(8,128)(2,1)S(1)} %get-tuple-element.21.factor_ref.refs_6_, f32[8,1536]{1,0:T(8,128)S(1)} %get-tuple-element.22.base_ref.refs_7_, bf16[384,128]{1,0:T(8,128)(2,1)S(1)} %get-tuple-element.23.gram_ref.refs_8_), custom_call_target="tpu_custom_call" | custom-call | bytes 4194304 | tf_op jit(solution)/shard_map/pallas_call | solution.py:245
  38.6 1.6 %shard_map.86 = (bf16[512,128]{1,0:T(8,128)(2,1)S(1)}, bf16[256,128]{1,0:T(8,128)(2,1)S(1)}, bf16[128,128]{1,0:T(8,128)(2,1)S(1)}) custom-call(bf16[768,128]{1,0:T(8,128)(2,1)S(1)} %copy-done.1, bf16[768,128]{1,0:T(8,128)(2,1)S(1)} %collective-permute-done.refs_1_, bf16[768,128]{1,0:T(8,128)(2,1)S(1)} %collective-permute-done.1.refs_2_, ...), custom_call_target="tpu_custom_call" | custom-call | bytes 4194304 | tf_op jit(solution)/shard_map/pallas_call | solution.py:245
  40.2 1.6 %collective-permute-start.10 = (bf16[128,128]{1,0:T(8,128)(2,1)S(1)}, bf16[128,128]{1,0:T(8,128)(2,1)S(1)}, u32[]{:S(2)}, u32[]{:S(2)}) collective-permute-start(bf16[128,128]{1,0:T(8,128)(2,1)S(1)} %get-tuple-element.24), channel_id=1, source_target_pairs={{0,8},{4,12},{8,0},{12,4},{1,9},{5,13},{9,1},{13,5},{2,10},{6,14},... | collective-permute-start | bytes 98312 | tf_op jit(solution)/shard_map/ppermute | solution.py:38
  41.8 0.6 collective-permute-start.9
  42.4 1.8 %collective-permute-done.10 = bf16[128,128]{1,0:T(8,128)(2,1)S(1)} collective-permute-done((bf16[128,128]{1,0:T(8,128)(2,1)S(1)}, bf16[128,128]{1,0:T(8,128)(2,1)S(1)}, u32[]{:S(2)}, u32[]{:S(2)}) %collective-permute-start.10) | collective-permute-done | bytes 32800 | tf_op jit(solution)/shard_map/ppermute | solution.py:38
  44.2 0.9 %collective-permute-done.11 = bf16[128,128]{1,0:T(8,128)(2,1)S(1)} collective-permute-done((bf16[128,128]{1,0:T(8,128)(2,1)S(1)}, bf16[128,128]{1,0:T(8,128)(2,1)S(1)}, u32[]{:S(2)}, u32[]{:S(2)}) %collective-permute-start.11) | collective-permute-done | bytes 32800 | tf_op jit(solution)/shard_map/ppermute | solution.py:38
  45.2 1.8 %collective-permute-start.13 = (bf16[128,128]{1,0:T(8,128)(2,1)S(1)}, bf16[128,128]{1,0:T(8,128)(2,1)S(1)}, u32[]{:S(2)}, u32[]{:S(2)}) collective-permute-start(bf16[128,128]{1,0:T(8,128)(2,1)S(1)} %add_convert_fusion.refs_0_), channel_id=1, source_target_pairs={{0,2},{1,3},{2,0},{3,1},{4,6},{5,7},{6,4},{7,5},{8,10},{9,11},{10,... | collective-permute-start | bytes 98312 | tf_op jit(solution)/shard_map/ppermute | solution.py:38
  47.0 2.6 %collective-permute-start.14 = (bf16[128,128]{1,0:T(8,128)(2,1)S(1)}, bf16[128,128]{1,0:T(8,128)(2,1)S(1)}, u32[]{:S(2)}, u32[]{:S(2)}) collective-permute-start(bf16[128,128]{1,0:T(8,128)(2,1)S(1)} %add_convert_fusion.refs_0_), channel_id=1, source_target_pairs={{0,3},{1,2},{2,1},{3,0},{4,7},{5,6},{6,5},{7,4},{8,11},{9,10},{10,... | collective-permute-start | bytes 98312 | tf_op jit(solution)/shard_map/ppermute | solution.py:38
  49.6 0.5 collective-permute-done.13.refs_2_
  50.1 2.6 %collective-permute-done.14.refs_3_ = bf16[128,128]{1,0:T(8,128)(2,1)S(1)} collective-permute-done((bf16[128,128]{1,0:T(8,128)(2,1)S(1)}, bf16[128,128]{1,0:T(8,128)(2,1)S(1)}, u32[]{:S(2)}, u32[]{:S(2)}) %collective-permute-start.14) | collective-permute-done | bytes 32800 | tf_op jit(solution)/shard_map/ppermute | solution.py:38
  52.7 2.0 %shard_map.87 = (f32[32,128]{1,0:T(8,128)S(1)}, f32[32,128]{1,0:T(8,128)S(1)}, f32[32,128]{1,0:T(8,128)S(1)}, f32[32,128]{1,0:T(8,128)S(1)}) custom-call(bf16[128,128]{1,0:T(8,128)(2,1)S(1)} %add_convert_fusion.refs_0_, bf16[128,128]{1,0:T(8,128)(2,1)S(1)} %collective-permute-done.12.refs_1_, bf16[128,128]{1,0:T(8,128)(2,1)S(1)} %collective-permute-done.13.refs_2_, ...), custom_call_target="tpu_custom_call" | custom-call | bytes 4194304 | tf_op jit(solution)/shard_map/pallas_call | solution.py:245
  54.7 3.2 %collective-permute-start.16 = (f32[32,128]{1,0:T(8,128)S(1)}, f32[32,128]{1,0:T(8,128)S(1)}, u32[]{:S(2)}, u32[]{:S(2)}) collective-permute-start(f32[32,128]{1,0:T(8,128)S(1)} %get-tuple-element.29), channel_id=1, source_target_pairs={{0,2},{1,3},{2,0},{3,1},{4,6},{5,7},{6,4},{7,5},{8,10},{9,11},{10,... | collective-permute-start | bytes 49160 | tf_op jit(solution)/shard_map/ppermute | solution.py:38
  57.9 1.2 %collective-permute-start.17 = (f32[32,128]{1,0:T(8,128)S(1)}, f32[32,128]{1,0:T(8,128)S(1)}, u32[]{:S(2)}, u32[]{:S(2)}) collective-permute-start(f32[32,128]{1,0:T(8,128)S(1)} %get-tuple-element.30), channel_id=1, source_target_pairs={{0,3},{1,2},{2,1},{3,0},{4,7},{5,6},{6,5},{7,4},{8,11},{9,10},{10,... | collective-permute-start | bytes 49160 | tf_op jit(solution)/shard_map/ppermute | solution.py:38
  59.1 0.6 collective-permute-done.16
  59.7 3.8 %collective-permute-done.17 = f32[32,128]{1,0:T(8,128)S(1)} collective-permute-done((f32[32,128]{1,0:T(8,128)S(1)}, f32[32,128]{1,0:T(8,128)S(1)}, u32[]{:S(2)}, u32[]{:S(2)}) %collective-permute-start.17) | collective-permute-done | bytes 16416 | tf_op jit(solution)/shard_map/ppermute | solution.py:38
  63.5 1.0 %collective-permute-start.19 = (f32[32,128]{1,0:T(8,128)S(1)}, f32[32,128]{1,0:T(8,128)S(1)}, u32[]{:S(2)}, u32[]{:S(2)}) collective-permute-start(f32[32,128]{1,0:T(8,128)S(1)} %add_add_fusion), channel_id=1, source_target_pairs={{0,8},{4,12},{8,0},{12,4},{1,9},{5,13},{9,1},{13,5},{2,10},{6,14},... | collective-permute-start | bytes 49160 | tf_op jit(solution)/shard_map/ppermute | solution.py:38
  64.4 0.9 %collective-permute-start.20 = (f32[32,128]{1,0:T(8,128)S(1)}, f32[32,128]{1,0:T(8,128)S(1)}, u32[]{:S(2)}, u32[]{:S(2)}) collective-permute-start(f32[32,128]{1,0:T(8,128)S(1)} %add_add_fusion), channel_id=1, source_target_pairs={{0,12},{4,8},{8,4},{12,0},{1,13},{5,9},{9,5},{13,1},{2,14},{6,10},... | collective-permute-start | bytes 49160 | tf_op jit(solution)/shard_map/ppermute | solution.py:38
  65.3 1.9 %collective-permute-done.19 = f32[32,128]{1,0:T(8,128)S(1)} collective-permute-done((f32[32,128]{1,0:T(8,128)S(1)}, f32[32,128]{1,0:T(8,128)S(1)}, u32[]{:S(2)}, u32[]{:S(2)}) %collective-permute-start.19) | collective-permute-done | bytes 16416 | tf_op jit(solution)/shard_map/ppermute | solution.py:38
  67.6 0.6 add_bitcast_fusion
  (31 shorter events, 0.6 us)
Async XLA Ops:
  0.0 8.9 %collective-permute-start.7 = (bf16[32,3072]{1,0:T(8,128)(2,1)}, bf16[32,3072]{1,0:T(8,128)(2,1)S(1)}, u32[]{:S(2)}, u32[]{:S(2)}) collective-permute-start(bf16[32,3072]{1,0:T(8,128)(2,1)} %refs_4_.3), channel_id=1, source_target_pairs={{0,8},{4,12},{8,0},{12,4},{1,9},{5,13},{9,1},{13,5},{2,10},{6,14},... | collective-permute-start | bytes 589832 | tf_op jit(solution)/shard_map/ppermute | solution.py:38
  3.0 9.3 %collective-permute-start.1 = (bf16[768,128]{1,0:T(8,128)(2,1)}, bf16[768,128]{1,0:T(8,128)(2,1)S(1)}, u32[]{:S(2)}, u32[]{:S(2)}) collective-permute-start(bf16[768,128]{1,0:T(8,128)(2,1)} %refs_0_.1), channel_id=1, source_target_pairs={{0,8},{4,12},{8,0},{12,4},{1,9},{5,13},{9,1},{13,5},{2,10},{6,14},... | collective-permute-start | bytes 589832 | tf_op jit(solution)/shard_map/ppermute | solution.py:38
  3.0 30.6 %collective-permute-start.6 = (bf16[32,3072]{1,0:T(8,128)(2,1)}, bf16[32,3072]{1,0:T(8,128)(2,1)S(1)}, u32[]{:S(2)}, u32[]{:S(2)}) collective-permute-start(bf16[32,3072]{1,0:T(8,128)(2,1)} %refs_4_.3), channel_id=1, source_target_pairs={{0,4},{4,0},{8,12},{12,8},{1,5},{5,1},{9,13},{13,9},{2,6},{6,2},{1... | collective-permute-start | bytes 589832 | tf_op jit(solution)/shard_map/ppermute | solution.py:38
  3.0 35.6 %collective-permute-start = (bf16[768,128]{1,0:T(8,128)(2,1)}, bf16[768,128]{1,0:T(8,128)(2,1)S(1)}, u32[]{:S(2)}, u32[]{:S(2)}) collective-permute-start(bf16[768,128]{1,0:T(8,128)(2,1)} %refs_0_.1), channel_id=1, source_target_pairs={{0,4},{4,0},{8,12},{12,8},{1,5},{5,1},{9,13},{13,9},{2,6},{6,2},{1... | collective-permute-start | bytes 589832 | tf_op jit(solution)/shard_map/ppermute | solution.py:38
  8.9 24.7 %collective-permute-start.8 = (bf16[32,3072]{1,0:T(8,128)(2,1)S(1)}, bf16[32,3072]{1,0:T(8,128)(2,1)S(1)}, u32[]{:S(2)}, u32[]{:S(2)}) collective-permute-start(bf16[32,3072]{1,0:T(8,128)(2,1)S(1)} %collective-permute-done.7.refs_6_), channel_id=1, source_target_pairs={{0,4},{4,0},{8,12},{12,8},{1,5},{5,1},{9,13},{13,9},{2,6},{6,2},{1... | collective-permute-start | bytes 589832 | tf_op jit(solution)/shard_map/ppermute | solution.py:38
  12.3 26.3 %collective-permute-start.2 = (bf16[768,128]{1,0:T(8,128)(2,1)S(1)}, bf16[768,128]{1,0:T(8,128)(2,1)S(1)}, u32[]{:S(2)}, u32[]{:S(2)}) collective-permute-start(bf16[768,128]{1,0:T(8,128)(2,1)S(1)} %collective-permute-done.1.refs_2_), channel_id=1, source_target_pairs={{0,4},{4,0},{8,12},{12,8},{1,5},{5,1},{9,13},{13,9},{2,6},{6,2},{1... | collective-permute-start | bytes 589832 | tf_op jit(solution)/shard_map/ppermute | solution.py:38
  15.8 17.9 %copy-start.2 = (bf16[32,3072]{1,0:T(8,128)(2,1)S(1)}, bf16[32,3072]{1,0:T(8,128)(2,1)}, u32[]{:S(2)}) copy-start(bf16[32,3072]{1,0:T(8,128)(2,1)} %refs_4_.3) | copy-start | bytes 589828
  15.8 17.9 %copy-start.3 = (f32[50,128]{1,0:T(8,128)S(1)}, f32[50,128]{1,0:T(8,128)}, u32[]{:S(2)}) copy-start(f32[50,128]{1,0:T(8,128)} %shard_map.82.refs_0_) | copy-start | bytes 76804
  15.8 4.1 %collective-permute-start.3 = (f32[50,128]{1,0:T(8,128)}, f32[50,128]{1,0:T(8,128)S(1)}, u32[]{:S(2)}, u32[]{:S(2)}) collective-permute-start(f32[50,128]{1,0:T(8,128)} %shard_map.82.refs_0_), channel_id=1, source_target_pairs={{0,1},{1,0},{2,3},{3,2},{4,5},{5,4},{6,7},{7,6},{8,9},{9,8},{10,11... | collective-permute-start | bytes 76808 | tf_op jit(solution)/shard_map/ppermute | solution.py:38
  19.9 5.0 %collective-permute-start.4 = (f32[50,128]{1,0:T(8,128)}, f32[50,128]{1,0:T(8,128)S(1)}, u32[]{:S(2)}, u32[]{:S(2)}) collective-permute-start(f32[50,128]{1,0:T(8,128)} %shard_map.82.refs_0_), channel_id=1, source_target_pairs={{0,2},{1,3},{2,0},{3,1},{4,6},{5,7},{6,4},{7,5},{8,10},{9,11},{10,... | collective-permute-start | bytes 76808 | tf_op jit(solution)/shard_map/ppermute | solution.py:38
  24.9 8.7 %collective-permute-start.5 = (f32[50,128]{1,0:T(8,128)}, f32[50,128]{1,0:T(8,128)S(1)}, u32[]{:S(2)}, u32[]{:S(2)}) collective-permute-start(f32[50,128]{1,0:T(8,128)} %shard_map.82.refs_0_), channel_id=1, source_target_pairs={{0,3},{1,2},{2,1},{3,0},{4,7},{5,6},{6,5},{7,4},{8,11},{9,10},{10,... | collective-permute-start | bytes 76808 | tf_op jit(solution)/shard_map/ppermute | solution.py:38
  32.8 5.8 %copy-start = (bf16[512,3072]{1,0:T(8,128)(2,1)S(1)}, bf16[512,3072]{1,0:T(8,128)(2,1)}, u32[]{:S(2)}) copy-start(bf16[512,3072]{1,0:T(8,128)(2,1)} %refs_5_.1) | copy-start | bytes 9437188
  32.8 5.8 %copy-start.1 = (bf16[768,128]{1,0:T(8,128)(2,1)S(1)}, bf16[768,128]{1,0:T(8,128)(2,1)}, u32[]{:S(2)}) copy-start(bf16[768,128]{1,0:T(8,128)(2,1)} %refs_0_.1) | copy-start | bytes 589828
  32.8 34.8 %copy-start.4 = (f32[32,128]{1,0:T(8,128)S(1)}, f32[32,128]{1,0:T(8,128)}, u32[]{:S(2)}) copy-start(f32[32,128]{1,0:T(8,128)} %start_hbm.1) | copy-start | bytes 49156
  40.2 4.0 %collective-permute-start.10 = (bf16[128,128]{1,0:T(8,128)(2,1)S(1)}, bf16[128,128]{1,0:T(8,128)(2,1)S(1)}, u32[]{:S(2)}, u32[]{:S(2)}) collective-permute-start(bf16[128,128]{1,0:T(8,128)(2,1)S(1)} %get-tuple-element.24), channel_id=1, source_target_pairs={{0,8},{4,12},{8,0},{12,4},{1,9},{5,13},{9,1},{13,5},{2,10},{6,14},... | collective-permute-start | bytes 98312 | tf_op jit(solution)/shard_map/ppermute | solution.py:38
  41.8 3.3 %collective-permute-start.11 = (bf16[128,128]{1,0:T(8,128)(2,1)S(1)}, bf16[128,128]{1,0:T(8,128)(2,1)S(1)}, u32[]{:S(2)}, u32[]{:S(2)}) collective-permute-start(bf16[128,128]{1,0:T(8,128)(2,1)S(1)} %get-tuple-element.24), channel_id=1, source_target_pairs={{0,12},{4,8},{8,4},{12,0},{1,13},{5,9},{9,5},{13,1},{2,14},{6,10},... | collective-permute-start | bytes 98312 | tf_op jit(solution)/shard_map/ppermute | solution.py:38
  41.8 3.3 %collective-permute-start.9 = (bf16[128,128]{1,0:T(8,128)(2,1)S(1)}, bf16[128,128]{1,0:T(8,128)(2,1)S(1)}, u32[]{:S(2)}, u32[]{:S(2)}) collective-permute-start(bf16[128,128]{1,0:T(8,128)(2,1)S(1)} %get-tuple-element.24), channel_id=1, source_target_pairs={{0,4},{4,0},{8,12},{12,8},{1,5},{5,1},{9,13},{13,9},{2,6},{6,2},{1... | collective-permute-start | bytes 98312 | tf_op jit(solution)/shard_map/ppermute | solution.py:38
  45.1 4.5 %collective-permute-start.12 = (bf16[128,128]{1,0:T(8,128)(2,1)S(1)}, bf16[128,128]{1,0:T(8,128)(2,1)S(1)}, u32[]{:S(2)}, u32[]{:S(2)}) collective-permute-start(bf16[128,128]{1,0:T(8,128)(2,1)S(1)} %add_convert_fusion.refs_0_), channel_id=1, source_target_pairs={{0,1},{1,0},{2,3},{3,2},{4,5},{5,4},{6,7},{7,6},{8,9},{9,8},{10,11... | collective-permute-start | bytes 98312 | tf_op jit(solution)/shard_map/ppermute | solution.py:38
  45.2 4.9 %collective-permute-start.13 = (bf16[128,128]{1,0:T(8,128)(2,1)S(1)}, bf16[128,128]{1,0:T(8,128)(2,1)S(1)}, u32[]{:S(2)}, u32[]{:S(2)}) collective-permute-start(bf16[128,128]{1,0:T(8,128)(2,1)S(1)} %add_convert_fusion.refs_0_), channel_id=1, source_target_pairs={{0,2},{1,3},{2,0},{3,1},{4,6},{5,7},{6,4},{7,5},{8,10},{9,11},{10,... | collective-permute-start | bytes 98312 | tf_op jit(solution)/shard_map/ppermute | solution.py:38
  47.0 5.7 %collective-permute-start.14 = (bf16[128,128]{1,0:T(8,128)(2,1)S(1)}, bf16[128,128]{1,0:T(8,128)(2,1)S(1)}, u32[]{:S(2)}, u32[]{:S(2)}) collective-permute-start(bf16[128,128]{1,0:T(8,128)(2,1)S(1)} %add_convert_fusion.refs_0_), channel_id=1, source_target_pairs={{0,3},{1,2},{2,1},{3,0},{4,7},{5,6},{6,5},{7,4},{8,11},{9,10},{10,... | collective-permute-start | bytes 98312 | tf_op jit(solution)/shard_map/ppermute | solution.py:38
  54.7 4.5 %collective-permute-start.15 = (f32[32,128]{1,0:T(8,128)S(1)}, f32[32,128]{1,0:T(8,128)S(1)}, u32[]{:S(2)}, u32[]{:S(2)}) collective-permute-start(f32[32,128]{1,0:T(8,128)S(1)} %get-tuple-element.28), channel_id=1, source_target_pairs={{0,1},{1,0},{2,3},{3,2},{4,5},{5,4},{6,7},{7,6},{8,9},{9,8},{10,11... | collective-permute-start | bytes 49160 | tf_op jit(solution)/shard_map/ppermute | solution.py:38
  54.7 4.9 %collective-permute-start.16 = (f32[32,128]{1,0:T(8,128)S(1)}, f32[32,128]{1,0:T(8,128)S(1)}, u32[]{:S(2)}, u32[]{:S(2)}) collective-permute-start(f32[32,128]{1,0:T(8,128)S(1)} %get-tuple-element.29), channel_id=1, source_target_pairs={{0,2},{1,3},{2,0},{3,1},{4,6},{5,7},{6,4},{7,5},{8,10},{9,11},{10,... | collective-permute-start | bytes 49160 | tf_op jit(solution)/shard_map/ppermute | solution.py:38
  57.9 5.5 %collective-permute-start.17 = (f32[32,128]{1,0:T(8,128)S(1)}, f32[32,128]{1,0:T(8,128)S(1)}, u32[]{:S(2)}, u32[]{:S(2)}) collective-permute-start(f32[32,128]{1,0:T(8,128)S(1)} %get-tuple-element.30), channel_id=1, source_target_pairs={{0,3},{1,2},{2,1},{3,0},{4,7},{5,6},{6,5},{7,4},{8,11},{9,10},{10,... | collective-permute-start | bytes 49160 | tf_op jit(solution)/shard_map/ppermute | solution.py:38
  63.5 1.9 %collective-permute-start.18 = (f32[32,128]{1,0:T(8,128)S(1)}, f32[32,128]{1,0:T(8,128)S(1)}, u32[]{:S(2)}, u32[]{:S(2)}) collective-permute-start(f32[32,128]{1,0:T(8,128)S(1)} %add_add_fusion), channel_id=1, source_target_pairs={{0,4},{4,0},{8,12},{12,8},{1,5},{5,1},{9,13},{13,9},{2,6},{6,2},{1... | collective-permute-start | bytes 49160 | tf_op jit(solution)/shard_map/ppermute | solution.py:38
  63.5 3.8 %collective-permute-start.19 = (f32[32,128]{1,0:T(8,128)S(1)}, f32[32,128]{1,0:T(8,128)S(1)}, u32[]{:S(2)}, u32[]{:S(2)}) collective-permute-start(f32[32,128]{1,0:T(8,128)S(1)} %add_add_fusion), channel_id=1, source_target_pairs={{0,8},{4,12},{8,0},{12,4},{1,9},{5,13},{9,1},{13,5},{2,10},{6,14},... | collective-permute-start | bytes 49160 | tf_op jit(solution)/shard_map/ppermute | solution.py:38
  64.4 3.2 %collective-permute-start.20 = (f32[32,128]{1,0:T(8,128)S(1)}, f32[32,128]{1,0:T(8,128)S(1)}, u32[]{:S(2)}, u32[]{:S(2)}) collective-permute-start(f32[32,128]{1,0:T(8,128)S(1)} %add_add_fusion), channel_id=1, source_target_pairs={{0,12},{4,8},{8,4},{12,0},{1,13},{5,9},{9,5},{13,1},{2,14},{6,10},... | collective-permute-start | bytes 49160 | tf_op jit(solution)/shard_map/ppermute | solution.py:38

commit v3 on v1

--- a/solution.py
+++ b/solution.py
@@ -7,6 +7,7 @@
 from jax.experimental import pallas as pl
 from jax.experimental.pallas import tpu as pltpu
 from jax.sharding import PartitionSpec as P
+
 
 HD = 128
 LANES = 128
@@ -17,6 +18,7 @@
 BF16 = jnp.bfloat16
 VMEM = pl.BlockSpec(memory_space=pltpu.VMEM)
 SMEM = pl.BlockSpec(memory_space=pltpu.SMEM)
+HBM = pl.BlockSpec(memory_space=pltpu.HBM)
 
 
 def embedding_of(time_index, width):
@@ -75,9 +77,31 @@
     return out
 
 
-def modulation_kernel(emb_ref, weight_ref, start_ref, out_ref):
+def run_copies(copies):
+    for copy in copies:
+        copy.start()
+    return copies
+
+
+def wait_copies(copies):
+    for copy in copies:
+        copy.wait()
+
+
+def modulation_kernel(time_ref, weight_hbm, start_hbm, out_ref, weight_ref, start_ref, sems):
     rows = start_ref.shape[0]
-    result = bdot(jnp.broadcast_to(emb_ref[...], (16, emb_ref.shape[1])), weight_ref[...])
+    half = weight_ref.shape[0] // 2
+    copies = run_copies(
+        [
+            pltpu.make_async_copy(weight_hbm, weight_ref, sems.at[0]),
+            pltpu.make_async_copy(start_hbm, start_ref, sems.at[1]),
+        ]
+    )
+    index = lax.broadcasted_iota(jnp.int32, (16, half), 1).astype(F32)
+    angles = time_ref[0].astype(F32) * jnp.exp(-math.log(10000.0) * index / half)
+    embedding = jnp.concatenate([jnp.cos(angles), jnp.sin(angles)], axis=1).astype(BF16)
+    wait_copies(copies)
+    result = bdot(embedding, weight_ref[...])
     out_ref[0:rows, :] = start_ref[...]
     for r in range(weight_ref.shape[1] // LANES):
         out_ref[rows + r : rows + r + 1, :] = result[0:1, r * LANES : (r + 1) * LANES]
@@ -86,31 +110,52 @@
 def attend(x, factors, base, gram, head_count):
     twice = jnp.concatenate([x, x], axis=1)
     thrice = jnp.concatenate([twice, x], axis=1)
-    spread = jnp.sum(bdot(thrice, gram[...]) * x.astype(F32), axis=1, keepdims=True)
+    heads = [slice(h * 3 * HD, (h + 1) * 3 * HD) for h in range(head_count)]
+    quadratic = bdot(thrice, gram[...])
+    raw = [bdot(twice, factors[:, cols]) for cols in heads]
+    spread = jnp.sum(quadratic * x.astype(F32), axis=1, keepdims=True)
     scale = lax.rsqrt(jnp.maximum(spread, 0.0) + NORM_EPS)
-    outs = []
-    for h in range(head_count):
-        cols = slice(h * 3 * HD, (h + 1) * 3 * HD)
-        qkv = (bdot(twice, factors[:, cols]) * scale + base[0:1, cols]).astype(BF16)
-        scores = bdot_t(qkv[:, :HD], qkv[:, HD : 2 * HD]) * (1.0 / math.sqrt(HD))
-        top = jnp.max(scores, axis=1, keepdims=True)
-        weights = jnp.exp(scores - top)
-        weights = weights / jnp.sum(weights, axis=1, keepdims=True)
-        outs.append(bdot(weights.astype(BF16), qkv[:, 2 * HD :]).astype(BF16))
+    qkv = [(r * scale + base[0:1, cols]).astype(BF16) for r, cols in zip(raw, heads)]
+    scores = [bdot_t(p[:, :HD], p[:, HD : 2 * HD]) * (1.0 / math.sqrt(HD)) for p in qkv]
+    tops = [jnp.max(s, axis=1, keepdims=True) for s in scores]
+    weights = [jnp.exp(s - t) for s, t in zip(scores, tops)]
+    sums = [jnp.sum(w, axis=1, keepdims=True) for w in weights]
+    probs = [(w / n).astype(BF16) for w, n in zip(weights, sums)]
+    outs = [bdot(w, p[:, 2 * HD :]).astype(BF16) for w, p in zip(probs, qkv)]
     return outs[0] if head_count == 1 else jnp.concatenate(outs, axis=1)
 
 
-def setup_kernel(nt, nm, rows, head_count, *refs):
+def setup_kernel(nt, nm, head_count, *refs):
     msgs, refs = refs[:nt], refs[nt:]
     inws, refs = refs[:nm], refs[nm:]
-    qkv_ref, refs = refs[0], refs[1:]
-    factor_ref, base_ref, gram_ref, start_ref, inw_ref, gate_ref, att_ref = refs[:7]
-    start_s, mod_s, inw_s, z_s = refs[7:]
-    for k in range(nt):
+    qkv_hbm, out_w_hbm, refs = refs[0], refs[1], refs[2:]
+    factor_ref, base_ref, gram_ref, start_ref, inw_ref, gate_ref, out_w_ref = refs[:7]
+    start_s, mod_s, inw_s, z_s, qkv_s, sems = refs[7:]
+    block = 3 * HD
+    own = run_copies(
+        [
+            pltpu.make_async_copy(
+                inws[0], inw_s.at[place("tm", nm, 0)], sems.at[head_count + 1]
+            )
+        ]
+    )
+    copies = run_copies(
+        [
+            pltpu.make_async_copy(
+                qkv_hbm.at[:, pl.ds(h * block, block)],
+                qkv_s.at[:, pl.ds(h * block, block)],
+                sems.at[h],
+            )
+            for h in range(head_count)
+        ]
+        + [pltpu.make_async_copy(out_w_hbm, out_w_ref, sems.at[head_count])]
+    )
+    wait_copies(own)
+    for k, msg in enumerate(msgs):
         at = place("tensor", nt, k)
-        start_s[at] = msgs[k][0 : start_s.shape[1], :]
-        mod_s[at, 0 : msgs[k].shape[0] - start_s.shape[1], :] = msgs[k][start_s.shape[1] :, :]
-    for k in range(nm):
+        start_s[at] = msg[0 : start_s.shape[1], :]
+        mod_s[at, 0 : msg.shape[0] - start_s.shape[1], :] = msg[start_s.shape[1] :, :]
+    for k in range(1, nm):
         inw_s[place("tm", nm, k)] = inws[k][...]
     channels, width = inw_ref.shape
     chunks = width // LANES
@@ -138,19 +183,24 @@
     start = start_s[...].reshape(start_ref.shape)
     start_ref[...] = start
 
-    block = 3 * HD
-
-    def columns(n, carry):
-        at = pl.ds(pl.multiple_of(n * block, block), block)
-        result = bdot(z_s[...], qkv_ref[:, at])
+    for h in range(head_count):
+        at = slice(h * block, (h + 1) * block)
+        copies[h].wait()
+        result = bdot(z_s[...], qkv_s[:, at])
         high, low = split_terms(result[0:channels], 2)
         factor_ref[0:channels, at] = high
         factor_ref[channels : 2 * channels, at] = low
         base_ref[:, at] = result[channels : channels + 8]
-        return carry
-
-    lax.fori_loop(0, head_count, columns, 0)
-    att_ref[...] = attend(start.astype(BF16), factor_ref, base_ref, gram_ref, head_count)
+    copies[head_count].wait()
+
+
+def attend_kernel(head_count, *refs):
+    start_ref, factor_ref, base_ref, gram_ref, out_w_ref, gate_ref, att_ref, scaled_ref = refs
+    x = start_ref[...].astype(BF16)
+    att_ref[...] = attend(x, factor_ref, base_ref, gram_ref, head_count)
+    for c in range(out_w_ref.shape[1] // LANES):
+        cols = slice(c * LANES, (c + 1) * LANES)
+        scaled_ref[:, cols] = (out_w_ref[:, cols].astype(F32) * gate_ref[c : c + 1, :]).astype(BF16)
 
 
 def add_own_rows(result, residual, rows):
@@ -165,23 +215,18 @@
 
 def fold_kernel(nm, rows, *refs):
     heads, refs = refs[:nm], refs[nm:]
-    step_ref, out_w_ref, gate_ref, inw_ref, att_ref, start_ref = refs[:6]
-    fold_ref, resid_ref, vel_ref = refs[6:9]
-    head_s, s_s = refs[9:]
+    step_ref, scaled_ref, inw_ref, att_ref, start_ref = refs[:5]
+    fold_ref, resid_ref, vel_ref, head_s = refs[5:]
     for k in range(nm):
         head_s[place("tm", nm, k)] = heads[k][...]
-    span, width = out_w_ref.shape
+    _, width = scaled_ref.shape
     channels = inw_ref.shape[0]
-    for c in range(width // LANES):
-        cols = slice(c * LANES, (c + 1) * LANES)
-        s_s[0:span, cols] = (out_w_ref[:, cols].astype(F32) * gate_ref[c : c + 1, :]).astype(BF16)
-    s_s[span:, :] = inw_ref[...]
     head = head_s[...].reshape(width, head_s.shape[2])
-    result = bdot(s_s[...], head)
-    folded = result[0:span].astype(BF16)
+    resid = bdot(inw_ref[...], head)
+    folded = bdot(scaled_ref[...], head).astype(BF16)
     fold_ref[...] = folded
-    for i, piece in enumerate(split_terms(result[span:], 2)):
-        resid_ref[i * channels : (i + 1) * channels, :] = piece
+    for i, term in enumerate(split_terms(resid, 2)):
+        resid_ref[i * channels : (i + 1) * channels, :] = term
     x = start_ref[...].astype(BF16)
     vel = bdot(att_ref[...], folded)
     residual = bdot(jnp.concatenate([x, x], axis=1), resid_ref[...])
@@ -213,18 +258,19 @@
     return jax.ShapeDtypeStruct(shape, dtype)
 
 
-PARAMS = pltpu.CompilerParams(vmem_limit_bytes=40 * 2**20)
-
-
-def call(kernel, name, outs, in_specs, scratch, *args):
+def call(kernel, outs, in_specs, scratch, *args, cost=4 * 2**20, limit=8):
+    args = [
+        pltpu.with_memory_space_constraint(arg, pltpu.HBM) if spec is HBM else arg
+        for arg, spec in zip(args, in_specs)
+    ]
     return pl.pallas_call(
         kernel,
-        name=name,
         out_shape=outs,
         in_specs=in_specs,
         out_specs=[VMEM] * len(outs),
         scratch_shapes=scratch,
-        compiler_params=PARAMS,
+        compiler_params=pltpu.CompilerParams(vmem_limit_bytes=limit * 2**20),
+        cost_estimate=pl.CostEstimate(flops=0, bytes_accessed=cost, transcendentals=0),
     )(*args)
 
 
@@ -265,23 +311,27 @@
     span = out_weight.shape[0]
 
     inw_parts = gather_weight_parts(in_weight, "tm")
-    embedding = embedding_of(time_index, mod_weight.shape[0]).astype(BF16)
     small = is_small("tensor") and mod_weight.shape[1] % LANES == 0
     if small:
         mod_rows = mod_weight.shape[1] // LANES
         message = call(
             modulation_kernel,
-            "modulation",
             [shape_of((rows + mod_rows, LANES), F32)],
-            [VMEM] * 3,
-            [],
-            embedding,
+            [SMEM, HBM, HBM],
+            [
+                pltpu.VMEM(mod_weight.shape, BF16),
+                pltpu.VMEM(start_latent.shape, F32),
+                pltpu.SemaphoreType.DMA((2,)),
+            ],
+            time_index,
             mod_weight,
             start_latent,
+            limit=8,
         )[0]
         messages = gather_parts(message, "tensor")
         block_rows = rows
     else:
+        embedding = embedding_of(time_index, mod_weight.shape[0]).astype(BF16)
         mod_part = jnp.dot(embedding, mod_weight, preferred_element_type=F32)
         modulation = lax.all_gather(mod_part, "tensor", axis=1, tiled=True)
         start_all = lax.all_gather(start_latent, "tensor", axis=0, tiled=True)
@@ -290,9 +340,8 @@
     nt, nm = len(messages), len(inw_parts)
     mod_rows = messages[0].shape[0] - block_rows
     padded = -(-mod_rows // 8) * 8
-    factor, base, gram, start_all, inw_all, gate, attended = call(
-        functools.partial(setup_kernel, nt, nm, rows, head_count),
-        "setup",
+    factor, base, gram, start_all, inw_all, gate, out_near = call(
+        functools.partial(setup_kernel, nt, nm, head_count),
         [
             shape_of((2 * channels, qkv_weight.shape[1]), BF16),
             shape_of((8, qkv_weight.shape[1]), F32),
@@ -300,40 +349,53 @@
             shape_of((tokens, channels), F32),
             shape_of((channels, width), BF16),
             shape_of((chunks, LANES), F32),
-            shape_of((tokens, head_count * HD), BF16),
+            shape_of(out_weight.shape, BF16),
         ],
-        [VMEM] * (nt + nm + 1),
+        [VMEM] * nt + [HBM] + [VMEM] * (nm - 1) + [HBM, HBM],
         [
             pltpu.VMEM((nt, block_rows, channels), F32),
             pltpu.VMEM((nt, padded, LANES), F32),
             pltpu.VMEM((nm, channels // nm, width), BF16),
             pltpu.VMEM((channels + 16, width), BF16),
+            pltpu.VMEM(qkv_weight.shape, BF16),
+            pltpu.SemaphoreType.DMA((head_count + 2,)),
         ],
         *messages,
         *inw_parts,
         qkv_weight,
+        out_weight,
+        limit=32,
+    )
+    attended, scaled = call(
+        functools.partial(attend_kernel, head_count),
+        [shape_of((tokens, head_count * HD), BF16), shape_of(out_weight.shape, BF16)],
+        [VMEM] * 6,
+        [],
+        start_all,
+        factor,
+        base,
+        gram,
+        out_near,
+        gate,
+        limit=16,
     )
     head_parts = gather_weight_parts(head_weight, "tm")
     folded, resid, vel = call(
         functools.partial(fold_kernel, nm, rows),
-        "fold",
         [
             shape_of((span, channels), BF16),
             shape_of((2 * channels, channels), BF16),
             shape_of((tokens, channels), BF16),
         ],
-        [VMEM] * nm + [SMEM] + [VMEM] * 5,
-        [
-            pltpu.VMEM((nm, width // nm, channels), BF16),
-            pltpu.VMEM((span + channels, width), BF16),
-        ],
+        [VMEM] * nm + [SMEM] + [VMEM] * 4,
+        [pltpu.VMEM((nm, width // nm, channels), BF16)],
         *head_parts,
         step_weight,
-        out_weight,
-        gate,
+        scaled,
         inw_all,
         attended,
         start_all,
+        limit=24,
     )
     small = is_small("tensor")
     for iteration in range(1, ITERS):
@@ -350,7 +412,6 @@
             outs = [shape_of((tokens, channels), F32 if last else BF16)]
         vels = call(
             functools.partial(iterate_kernel, len(pieces), rows, head_count, split),
-            "iterate",
             outs,
             [VMEM] * len(pieces) + [SMEM] + [VMEM] * 6,
             [pltpu.VMEM((n_tensor, rows, channels), F32)],

time: 69 us -> 65.2 us (0.945)
  local copies, waits for them, and re-layouts: 6.6 us -> 0.01 us
  Pallas kernels: 8.7 us -> 11 us
  waiting for transfers between devices: 26 us -> 26.7 us
    unnamed x14 -> x4, local copies, waits for them, and re-layouts: 6.6 us -> 0.01 us
    pallas_call x4 -> x5, Pallas kernels: 8.7 us -> 11 us  [call(): pl.pallas_call(kernel, out_shape=outs, in_specs=in_specs, out_specs=[VMEM...]
  transfers between devices with their start and end apart: 21 -> 21, of which waited for: 13 -> 13; matrix products, arithmetic and copies ran while one was open for 0% -> 0% of each run, Pallas kernels for 7% -> 13%
where the time goes in v3:
time: 65.2 us; the launch traced here: 65.1 us
  waiting for transfers between devices  26.7 us (41%)
  starting transfers between devices  25.2 us (39%)
  Pallas kernels  11 us (17%)
  between operations  1.43 us (2%)
    ppermute x21, waiting for transfers between devices, swap(): return lax.ppermute(value, axis, [(i, i ^ k) for i in range(n)])  26.7 us
    ppermute x21, starting transfers between devices, swap(): return lax.ppermute(value, axis, [(i, i ^ k) for i in range(n)])  25.2 us
    pallas_call x5, Pallas kernels, call(): pl.pallas_call(kernel, out_shape=outs, in_specs=in_specs, out_specs=[VMEM...  11 us
  transfers between devices with their start and end apart: 21, of which 13 were waited for; matrix products, arithmetic and copies ran while one was open for 0% of the time, Pallas kernels for 13%

profile of v3, /device:TPU:0, one launch (start us, length us, event | category | flops | bytes accessed | tf_op | source)
XLA Modules:
  0.0 65.1 jit_solution(10965939045336610900)
XLA Ops:
  0.0 3.0 %collective-permute-start.7 = (bf16[32,3072]{1,0:T(8,128)(2,1)}, bf16[32,3072]{1,0:T(8,128)(2,1)S(1)}, u32[]{:S(2)}, u32[]{:S(2)}) collective-permute-start(bf16[32,3072]{1,0:T(8,128)(2,1)} %refs_4_.3), channel_id=1, source_target_pairs={{0,8},{4,12},{8,0},{12,4},{1,9},{5,13},{9,1},{13,5},{2,10},{6,14},... | collective-permute-start | bytes 589832 | tf_op jit(solution)/shard_map/ppermute | solution.py:39
  3.0 5.9 %collective-permute-done.7.refs_6_ = bf16[32,3072]{1,0:T(8,128)(2,1)S(1)} collective-permute-done((bf16[32,3072]{1,0:T(8,128)(2,1)}, bf16[32,3072]{1,0:T(8,128)(2,1)S(1)}, u32[]{:S(2)}, u32[]{:S(2)}) %collective-permute-start.7) | collective-permute-done | bytes 196640 | tf_op jit(solution)/shard_map/ppermute | solution.py:39
  8.9 0.5 collective-permute-start
  9.4 2.9 %collective-permute-done.1.refs_2_ = bf16[768,128]{1,0:T(8,128)(2,1)S(1)} collective-permute-done((bf16[768,128]{1,0:T(8,128)(2,1)}, bf16[768,128]{1,0:T(8,128)(2,1)S(1)}, u32[]{:S(2)}, u32[]{:S(2)}) %collective-permute-start.1) | collective-permute-done | bytes 196640 | tf_op jit(solution)/shard_map/ppermute | solution.py:39
  12.9 1.6 %shard_map.82.refs_0_ = f32[50,128]{1,0:T(8,128)S(1)} custom-call(s32[1]{0:T(128)S(6)} %copy.9.time_ref, bf16[256,2304]{1,0:T(8,128)(2,1)} %weight_hbm.1, f32[32,128]{1,0:T(8,128)} %start_hbm.1), custom_call_target="tpu_custom_call" | custom-call | bytes 4194304 | tf_op jit(solution)/shard_map/pallas_call | solution.py:266
  14.5 1.9 %collective-permute-start.3 = (f32[50,128]{1,0:T(8,128)S(1)}, f32[50,128]{1,0:T(8,128)S(1)}, u32[]{:S(2)}, u32[]{:S(2)}) collective-permute-start(f32[50,128]{1,0:T(8,128)S(1)} %shard_map.82.refs_0_), channel_id=1, source_target_pairs={{0,1},{1,0},{2,3},{3,2},{4,5},{5,4},{6,7},{7,6},{8,9},{9,8},{10,11... | collective-permute-start | bytes 76808 | tf_op jit(solution)/shard_map/ppermute | solution.py:39
  16.4 2.0 %collective-permute-done.3.refs_1_ = f32[50,128]{1,0:T(8,128)S(1)} collective-permute-done((f32[50,128]{1,0:T(8,128)S(1)}, f32[50,128]{1,0:T(8,128)S(1)}, u32[]{:S(2)}, u32[]{:S(2)}) %collective-permute-start.3) | collective-permute-done | bytes 25632 | tf_op jit(solution)/shard_map/ppermute | solution.py:39
  18.5 2.8 %collective-permute-start.4 = (f32[50,128]{1,0:T(8,128)S(1)}, f32[50,128]{1,0:T(8,128)S(1)}, u32[]{:S(2)}, u32[]{:S(2)}) collective-permute-start(f32[50,128]{1,0:T(8,128)S(1)} %shard_map.82.refs_0_), channel_id=1, source_target_pairs={{0,2},{1,3},{2,0},{3,1},{4,6},{5,7},{6,4},{7,5},{8,10},{9,11},{10,... | collective-permute-start | bytes 76808 | tf_op jit(solution)/shard_map/ppermute | solution.py:39
  21.3 1.9 %collective-permute-done.4.refs_2_ = f32[50,128]{1,0:T(8,128)S(1)} collective-permute-done((f32[50,128]{1,0:T(8,128)S(1)}, f32[50,128]{1,0:T(8,128)S(1)}, u32[]{:S(2)}, u32[]{:S(2)}) %collective-permute-start.4) | collective-permute-done | bytes 25632 | tf_op jit(solution)/shard_map/ppermute | solution.py:39
  23.2 4.0 %collective-permute-start.5 = (f32[50,128]{1,0:T(8,128)S(1)}, f32[50,128]{1,0:T(8,128)S(1)}, u32[]{:S(2)}, u32[]{:S(2)}) collective-permute-start(f32[50,128]{1,0:T(8,128)S(1)} %shard_map.82.refs_0_), channel_id=1, source_target_pairs={{0,3},{1,2},{2,1},{3,0},{4,7},{5,6},{6,5},{7,4},{8,11},{9,10},{10,... | collective-permute-start | bytes 76808 | tf_op jit(solution)/shard_map/ppermute | solution.py:39
  27.9 1.2 %collective-permute-done.5.refs_3_ = f32[50,128]{1,0:T(8,128)S(1)} collective-permute-done((f32[50,128]{1,0:T(8,128)S(1)}, f32[50,128]{1,0:T(8,128)S(1)}, u32[]{:S(2)}, u32[]{:S(2)}) %collective-permute-start.5) | collective-permute-done | bytes 25632 | tf_op jit(solution)/shard_map/ppermute | solution.py:39
  29.1 4.9 %shard_map.83 = (bf16[256,1536]{1,0:T(8,128)(2,1)S(1)}, f32[8,1536]{1,0:T(8,128)S(1)}, bf16[384,128]{1,0:T(8,128)(2,1)S(1)}, f32[128,128]{1,0:T(8,128)S(1)}, bf1...) custom-call(f32[50,128]{1,0:T(8,128)S(1)} %shard_map.82.refs_0_, ...), custom_call_target="tpu_custom_call" | custom-call | bytes 4194304 | tf_op jit(solution)/shard_map/pallas_call | solution.py:266
  34.0 2.2 %shard_map.84 = (bf16[128,512]{1,0:T(8,128)(2,1)S(1)}, bf16[512,3072]{1,0:T(8,128)(2,1)S(1)}) custom-call(f32[128,128]{1,0:T(8,128)S(1)} %get-tuple-element.21.refs_0_.refs_8_.refs_5_, bf16[256,1536]{1,0:T(8,128)(2,1)S(1)} %get-tuple-element.22.refs_1_.refs_6_, f32[8,1536]{1,0:T(8,128)S(1)} %get-tuple-element.23.refs_2_.refs_7_, ...), custom_call_target="tpu_custom_call" | custom-call | bytes 4194304 | tf_op jit(solution)/shard_map/pallas_call | solution.py:266
  36.3 1.4 %shard_map.85 = (bf16[512,128]{1,0:T(8,128)(2,1)S(1)}, bf16[256,128]{1,0:T(8,128)(2,1)S(1)}, bf16[128,128]{1,0:T(8,128)(2,1)S(1)}) custom-call(bf16[768,128]{1,0:T(8,128)(2,1)S(1)} %copy-done, bf16[768,128]{1,0:T(8,128)(2,1)S(1)} %collective-permute-done.refs_1_, bf16[768,128]{1,0:T(8,128)(2,1)S(1)} %collective-permute-done.1.refs_2_, ...), custom_call_target="tpu_custom_call" | custom-call | bytes 4194304 | tf_op jit(solution)/shard_map/pallas_call | solution.py:266
  37.8 1.6 %collective-permute-start.10 = (bf16[128,128]{1,0:T(8,128)(2,1)S(1)}, bf16[128,128]{1,0:T(8,128)(2,1)S(1)}, u32[]{:S(2)}, u32[]{:S(2)}) collective-permute-start(bf16[128,128]{1,0:T(8,128)(2,1)S(1)} %get-tuple-element.30), channel_id=1, source_target_pairs={{0,8},{4,12},{8,0},{12,4},{1,9},{5,13},{9,1},{13,5},{2,10},{6,14},... | collective-permute-start | bytes 98312 | tf_op jit(solution)/shard_map/ppermute | solution.py:39
  39.4 0.6 collective-permute-start.9
  40.0 1.8 %collective-permute-done.10 = bf16[128,128]{1,0:T(8,128)(2,1)S(1)} collective-permute-done((bf16[128,128]{1,0:T(8,128)(2,1)S(1)}, bf16[128,128]{1,0:T(8,128)(2,1)S(1)}, u32[]{:S(2)}, u32[]{:S(2)}) %collective-permute-start.10) | collective-permute-done | bytes 32800 | tf_op jit(solution)/shard_map/ppermute | solution.py:39
  41.7 0.9 %collective-permute-done.11 = bf16[128,128]{1,0:T(8,128)(2,1)S(1)} collective-permute-done((bf16[128,128]{1,0:T(8,128)(2,1)S(1)}, bf16[128,128]{1,0:T(8,128)(2,1)S(1)}, u32[]{:S(2)}, u32[]{:S(2)}) %collective-permute-start.11) | collective-permute-done | bytes 32800 | tf_op jit(solution)/shard_map/ppermute | solution.py:39
  42.7 0.1 collective-permute-start.12
  42.8 4.3 %collective-permute-start.13 = (bf16[128,128]{1,0:T(8,128)(2,1)S(1)}, bf16[128,128]{1,0:T(8,128)(2,1)S(1)}, u32[]{:S(2)}, u32[]{:S(2)}) collective-permute-start(bf16[128,128]{1,0:T(8,128)(2,1)S(1)} %add_convert_fusion.refs_0_), channel_id=1, source_target_pairs={{0,2},{1,3},{2,0},{3,1},{4,6},{5,7},{6,4},{7,5},{8,10},{9,11},{10,... | collective-permute-start | bytes 98312 | tf_op jit(solution)/shard_map/ppermute | solution.py:39
  47.2 2.2 %collective-permute-done.13.refs_2_ = bf16[128,128]{1,0:T(8,128)(2,1)S(1)} collective-permute-done((bf16[128,128]{1,0:T(8,128)(2,1)S(1)}, bf16[128,128]{1,0:T(8,128)(2,1)S(1)}, u32[]{:S(2)}, u32[]{:S(2)}) %collective-permute-start.13) | collective-permute-done | bytes 32800 | tf_op jit(solution)/shard_map/ppermute | solution.py:39
  49.4 3.5 %collective-permute-done.14.refs_3_ = bf16[128,128]{1,0:T(8,128)(2,1)S(1)} collective-permute-done((bf16[128,128]{1,0:T(8,128)(2,1)S(1)}, bf16[128,128]{1,0:T(8,128)(2,1)S(1)}, u32[]{:S(2)}, u32[]{:S(2)}) %collective-permute-start.14) | collective-permute-done | bytes 32800 | tf_op jit(solution)/shard_map/ppermute | solution.py:39
  52.9 0.9 %shard_map.86 = (f32[32,128]{1,0:T(8,128)S(1)}, f32[32,128]{1,0:T(8,128)S(1)}, f32[32,128]{1,0:T(8,128)S(1)}, f32[32,128]{1,0:T(8,128)S(1)}) custom-call(bf16[128,128]{1,0:T(8,128)(2,1)S(1)} %add_convert_fusion.refs_0_, bf16[128,128]{1,0:T(8,128)(2,1)S(1)} %collective-permute-done.12.refs_1_, bf16[128,128]{1,0:T(8,128)(2,1)S(1)} %collective-permute-done.13.refs_2_, ...), custom_call_target="tpu_custom_call" | custom-call | bytes 4194304 | tf_op jit(solution)/shard_map/pallas_call | solution.py:266
  53.8 0.9 %collective-permute-start.16 = (f32[32,128]{1,0:T(8,128)S(1)}, f32[32,128]{1,0:T(8,128)S(1)}, u32[]{:S(2)}, u32[]{:S(2)}) collective-permute-start(f32[32,128]{1,0:T(8,128)S(1)} %get-tuple-element.35), channel_id=1, source_target_pairs={{0,2},{1,3},{2,0},{3,1},{4,6},{5,7},{6,4},{7,5},{8,10},{9,11},{10,... | collective-permute-start | bytes 49160 | tf_op jit(solution)/shard_map/ppermute | solution.py:39
  54.7 3.5 %collective-permute-start.17 = (f32[32,128]{1,0:T(8,128)S(1)}, f32[32,128]{1,0:T(8,128)S(1)}, u32[]{:S(2)}, u32[]{:S(2)}) collective-permute-start(f32[32,128]{1,0:T(8,128)S(1)} %get-tuple-element.36), channel_id=1, source_target_pairs={{0,3},{1,2},{2,1},{3,0},{4,7},{5,6},{6,5},{7,4},{8,11},{9,10},{10,... | collective-permute-start | bytes 49160 | tf_op jit(solution)/shard_map/ppermute | solution.py:39
  58.2 0.3 collective-permute-done.16
  58.5 1.7 %collective-permute-done.17 = f32[32,128]{1,0:T(8,128)S(1)} collective-permute-done((f32[32,128]{1,0:T(8,128)S(1)}, f32[32,128]{1,0:T(8,128)S(1)}, u32[]{:S(2)}, u32[]{:S(2)}) %collective-permute-start.17) | collective-permute-done | bytes 16416 | tf_op jit(solution)/shard_map/ppermute | solution.py:39
  60.3 1.0 %collective-permute-start.19 = (f32[32,128]{1,0:T(8,128)S(1)}, f32[32,128]{1,0:T(8,128)S(1)}, u32[]{:S(2)}, u32[]{:S(2)}) collective-permute-start(f32[32,128]{1,0:T(8,128)S(1)} %add_add_fusion), channel_id=1, source_target_pairs={{0,8},{4,12},{8,0},{12,4},{1,9},{5,13},{9,1},{13,5},{2,10},{6,14},... | collective-permute-start | bytes 49160 | tf_op jit(solution)/shard_map/ppermute | solution.py:39
  61.3 0.9 %collective-permute-start.20 = (f32[32,128]{1,0:T(8,128)S(1)}, f32[32,128]{1,0:T(8,128)S(1)}, u32[]{:S(2)}, u32[]{:S(2)}) collective-permute-start(f32[32,128]{1,0:T(8,128)S(1)} %add_add_fusion), channel_id=1, source_target_pairs={{0,12},{4,8},{8,4},{12,0},{1,13},{5,9},{9,5},{13,1},{2,14},{6,10},... | collective-permute-start | bytes 49160 | tf_op jit(solution)/shard_map/ppermute | solution.py:39
  62.2 1.9 %collective-permute-done.19 = f32[32,128]{1,0:T(8,128)S(1)} collective-permute-done((f32[32,128]{1,0:T(8,128)S(1)}, f32[32,128]{1,0:T(8,128)S(1)}, u32[]{:S(2)}, u32[]{:S(2)}) %collective-permute-start.19) | collective-permute-done | bytes 16416 | tf_op jit(solution)/shard_map/ppermute | solution.py:39
  64.1 0.3 collective-permute-done.20
  64.4 0.6 add_bitcast_fusion
  (22 shorter events, 0.2 us)
Async XLA Ops:
  0.0 8.9 %collective-permute-start.7 = (bf16[32,3072]{1,0:T(8,128)(2,1)}, bf16[32,3072]{1,0:T(8,128)(2,1)S(1)}, u32[]{:S(2)}, u32[]{:S(2)}) collective-permute-start(bf16[32,3072]{1,0:T(8,128)(2,1)} %refs_4_.3), channel_id=1, source_target_pairs={{0,8},{4,12},{8,0},{12,4},{1,9},{5,13},{9,1},{13,5},{2,10},{6,14},... | collective-permute-start | bytes 589832 | tf_op jit(solution)/shard_map/ppermute | solution.py:39
  3.0 9.3 %collective-permute-start.1 = (bf16[768,128]{1,0:T(8,128)(2,1)}, bf16[768,128]{1,0:T(8,128)(2,1)S(1)}, u32[]{:S(2)}, u32[]{:S(2)}) collective-permute-start(bf16[768,128]{1,0:T(8,128)(2,1)} %refs_0_.1), channel_id=1, source_target_pairs={{0,8},{4,12},{8,0},{12,4},{1,9},{5,13},{9,1},{13,5},{2,10},{6,14},... | collective-permute-start | bytes 589832 | tf_op jit(solution)/shard_map/ppermute | solution.py:39
  3.0 26.1 %collective-permute-start.6 = (bf16[32,3072]{1,0:T(8,128)(2,1)}, bf16[32,3072]{1,0:T(8,128)(2,1)S(1)}, u32[]{:S(2)}, u32[]{:S(2)}) collective-permute-start(bf16[32,3072]{1,0:T(8,128)(2,1)} %refs_4_.3), channel_id=1, source_target_pairs={{0,4},{4,0},{8,12},{12,8},{1,5},{5,1},{9,13},{13,9},{2,6},{6,2},{1... | collective-permute-start | bytes 589832 | tf_op jit(solution)/shard_map/ppermute | solution.py:39
  8.9 20.2 %collective-permute-start.8 = (bf16[32,3072]{1,0:T(8,128)(2,1)S(1)}, bf16[32,3072]{1,0:T(8,128)(2,1)S(1)}, u32[]{:S(2)}, u32[]{:S(2)}) collective-permute-start(bf16[32,3072]{1,0:T(8,128)(2,1)S(1)} %collective-permute-done.7.refs_6_), channel_id=1, source_target_pairs={{0,4},{4,0},{8,12},{12,8},{1,5},{5,1},{9,13},{13,9},{2,6},{6,2},{1... | collective-permute-start | bytes 589832 | tf_op jit(solution)/shard_map/ppermute | solution.py:39
  8.9 27.4 %collective-permute-start = (bf16[768,128]{1,0:T(8,128)(2,1)}, bf16[768,128]{1,0:T(8,128)(2,1)S(1)}, u32[]{:S(2)}, u32[]{:S(2)}) collective-permute-start(bf16[768,128]{1,0:T(8,128)(2,1)} %refs_0_.1), channel_id=1, source_target_pairs={{0,4},{4,0},{8,12},{12,8},{1,5},{5,1},{9,13},{13,9},{2,6},{6,2},{1... | collective-permute-start | bytes 589832 | tf_op jit(solution)/shard_map/ppermute | solution.py:39
  12.3 24.0 %collective-permute-start.2 = (bf16[768,128]{1,0:T(8,128)(2,1)S(1)}, bf16[768,128]{1,0:T(8,128)(2,1)S(1)}, u32[]{:S(2)}, u32[]{:S(2)}) collective-permute-start(bf16[768,128]{1,0:T(8,128)(2,1)S(1)} %collective-permute-done.1.refs_2_), channel_id=1, source_target_pairs={{0,4},{4,0},{8,12},{12,8},{1,5},{5,1},{9,13},{13,9},{2,6},{6,2},{1... | collective-permute-start | bytes 589832 | tf_op jit(solution)/shard_map/ppermute | solution.py:39
  14.5 3.9 %collective-permute-start.3 = (f32[50,128]{1,0:T(8,128)S(1)}, f32[50,128]{1,0:T(8,128)S(1)}, u32[]{:S(2)}, u32[]{:S(2)}) collective-permute-start(f32[50,128]{1,0:T(8,128)S(1)} %shard_map.82.refs_0_), channel_id=1, source_target_pairs={{0,1},{1,0},{2,3},{3,2},{4,5},{5,4},{6,7},{7,6},{8,9},{9,8},{10,11... | collective-permute-start | bytes 76808 | tf_op jit(solution)/shard_map/ppermute | solution.py:39
  18.5 4.8 %collective-permute-start.4 = (f32[50,128]{1,0:T(8,128)S(1)}, f32[50,128]{1,0:T(8,128)S(1)}, u32[]{:S(2)}, u32[]{:S(2)}) collective-permute-start(f32[50,128]{1,0:T(8,128)S(1)} %shard_map.82.refs_0_), channel_id=1, source_target_pairs={{0,2},{1,3},{2,0},{3,1},{4,6},{5,7},{6,4},{7,5},{8,10},{9,11},{10,... | collective-permute-start | bytes 76808 | tf_op jit(solution)/shard_map/ppermute | solution.py:39
  23.2 5.9 %collective-permute-start.5 = (f32[50,128]{1,0:T(8,128)S(1)}, f32[50,128]{1,0:T(8,128)S(1)}, u32[]{:S(2)}, u32[]{:S(2)}) collective-permute-start(f32[50,128]{1,0:T(8,128)S(1)} %shard_map.82.refs_0_), channel_id=1, source_target_pairs={{0,3},{1,2},{2,1},{3,0},{4,7},{5,6},{6,5},{7,4},{8,11},{9,10},{10,... | collective-permute-start | bytes 76808 | tf_op jit(solution)/shard_map/ppermute | solution.py:39
  34.0 2.3 %copy-start = (bf16[768,128]{1,0:T(8,128)(2,1)S(1)}, bf16[768,128]{1,0:T(8,128)(2,1)}, u32[]{:S(2)}) copy-start(bf16[768,128]{1,0:T(8,128)(2,1)} %refs_0_.1) | copy-start | bytes 589828
  36.3 28.1 %copy-start.1 = (f32[32,128]{1,0:T(8,128)S(1)}, f32[32,128]{1,0:T(8,128)}, u32[]{:S(2)}) copy-start(f32[32,128]{1,0:T(8,128)} %start_hbm.1) | copy-start | bytes 49156
  37.8 4.0 %collective-permute-start.10 = (bf16[128,128]{1,0:T(8,128)(2,1)S(1)}, bf16[128,128]{1,0:T(8,128)(2,1)S(1)}, u32[]{:S(2)}, u32[]{:S(2)}) collective-permute-start(bf16[128,128]{1,0:T(8,128)(2,1)S(1)} %get-tuple-element.30), channel_id=1, source_target_pairs={{0,8},{4,12},{8,0},{12,4},{1,9},{5,13},{9,1},{13,5},{2,10},{6,14},... | collective-permute-start | bytes 98312 | tf_op jit(solution)/shard_map/ppermute | solution.py:39
  39.4 3.3 %collective-permute-start.11 = (bf16[128,128]{1,0:T(8,128)(2,1)S(1)}, bf16[128,128]{1,0:T(8,128)(2,1)S(1)}, u32[]{:S(2)}, u32[]{:S(2)}) collective-permute-start(bf16[128,128]{1,0:T(8,128)(2,1)S(1)} %get-tuple-element.30), channel_id=1, source_target_pairs={{0,12},{4,8},{8,4},{12,0},{1,13},{5,9},{9,5},{13,1},{2,14},{6,10},... | collective-permute-start | bytes 98312 | tf_op jit(solution)/shard_map/ppermute | solution.py:39
  39.4 3.3 %collective-permute-start.9 = (bf16[128,128]{1,0:T(8,128)(2,1)S(1)}, bf16[128,128]{1,0:T(8,128)(2,1)S(1)}, u32[]{:S(2)}, u32[]{:S(2)}) collective-permute-start(bf16[128,128]{1,0:T(8,128)(2,1)S(1)} %get-tuple-element.30), channel_id=1, source_target_pairs={{0,4},{4,0},{8,12},{12,8},{1,5},{5,1},{9,13},{13,9},{2,6},{6,2},{1... | collective-permute-start | bytes 98312 | tf_op jit(solution)/shard_map/ppermute | solution.py:39
  42.7 4.5 %collective-permute-start.12 = (bf16[128,128]{1,0:T(8,128)(2,1)S(1)}, bf16[128,128]{1,0:T(8,128)(2,1)S(1)}, u32[]{:S(2)}, u32[]{:S(2)}) collective-permute-start(bf16[128,128]{1,0:T(8,128)(2,1)S(1)} %add_convert_fusion.refs_0_), channel_id=1, source_target_pairs={{0,1},{1,0},{2,3},{3,2},{4,5},{5,4},{6,7},{7,6},{8,9},{9,8},{10,11... | collective-permute-start | bytes 98312 | tf_op jit(solution)/shard_map/ppermute | solution.py:39
  42.8 6.6 %collective-permute-start.13 = (bf16[128,128]{1,0:T(8,128)(2,1)S(1)}, bf16[128,128]{1,0:T(8,128)(2,1)S(1)}, u32[]{:S(2)}, u32[]{:S(2)}) collective-permute-start(bf16[128,128]{1,0:T(8,128)(2,1)S(1)} %add_convert_fusion.refs_0_), channel_id=1, source_target_pairs={{0,2},{1,3},{2,0},{3,1},{4,6},{5,7},{6,4},{7,5},{8,10},{9,11},{10,... | collective-permute-start | bytes 98312 | tf_op jit(solution)/shard_map/ppermute | solution.py:39
  47.1 5.7 %collective-permute-start.14 = (bf16[128,128]{1,0:T(8,128)(2,1)S(1)}, bf16[128,128]{1,0:T(8,128)(2,1)S(1)}, u32[]{:S(2)}, u32[]{:S(2)}) collective-permute-start(bf16[128,128]{1,0:T(8,128)(2,1)S(1)} %add_convert_fusion.refs_0_), channel_id=1, source_target_pairs={{0,3},{1,2},{2,1},{3,0},{4,7},{5,6},{6,5},{7,4},{8,11},{9,10},{10,... | collective-permute-start | bytes 98312 | tf_op jit(solution)/shard_map/ppermute | solution.py:39
  53.8 4.5 %collective-permute-start.15 = (f32[32,128]{1,0:T(8,128)S(1)}, f32[32,128]{1,0:T(8,128)S(1)}, u32[]{:S(2)}, u32[]{:S(2)}) collective-permute-start(f32[32,128]{1,0:T(8,128)S(1)} %get-tuple-element.34), channel_id=1, source_target_pairs={{0,1},{1,0},{2,3},{3,2},{4,5},{5,4},{6,7},{7,6},{8,9},{9,8},{10,11... | collective-permute-start | bytes 49160 | tf_op jit(solution)/shard_map/ppermute | solution.py:39
  53.8 4.7 %collective-permute-start.16 = (f32[32,128]{1,0:T(8,128)S(1)}, f32[32,128]{1,0:T(8,128)S(1)}, u32[]{:S(2)}, u32[]{:S(2)}) collective-permute-start(f32[32,128]{1,0:T(8,128)S(1)} %get-tuple-element.35), channel_id=1, source_target_pairs={{0,2},{1,3},{2,0},{3,1},{4,6},{5,7},{6,4},{7,5},{8,10},{9,11},{10,... | collective-permute-start | bytes 49160 | tf_op jit(solution)/shard_map/ppermute | solution.py:39
  54.7 5.5 %collective-permute-start.17 = (f32[32,128]{1,0:T(8,128)S(1)}, f32[32,128]{1,0:T(8,128)S(1)}, u32[]{:S(2)}, u32[]{:S(2)}) collective-permute-start(f32[32,128]{1,0:T(8,128)S(1)} %get-tuple-element.36), channel_id=1, source_target_pairs={{0,3},{1,2},{2,1},{3,0},{4,7},{5,6},{6,5},{7,4},{8,11},{9,10},{10,... | collective-permute-start | bytes 49160 | tf_op jit(solution)/shard_map/ppermute | solution.py:39
  60.3 1.9 %collective-permute-start.18 = (f32[32,128]{1,0:T(8,128)S(1)}, f32[32,128]{1,0:T(8,128)S(1)}, u32[]{:S(2)}, u32[]{:S(2)}) collective-permute-start(f32[32,128]{1,0:T(8,128)S(1)} %add_add_fusion), channel_id=1, source_target_pairs={{0,4},{4,0},{8,12},{12,8},{1,5},{5,1},{9,13},{13,9},{2,6},{6,2},{1... | collective-permute-start | bytes 49160 | tf_op jit(solution)/shard_map/ppermute | solution.py:39
  60.3 3.8 %collective-permute-start.19 = (f32[32,128]{1,0:T(8,128)S(1)}, f32[32,128]{1,0:T(8,128)S(1)}, u32[]{:S(2)}, u32[]{:S(2)}) collective-permute-start(f32[32,128]{1,0:T(8,128)S(1)} %add_add_fusion), channel_id=1, source_target_pairs={{0,8},{4,12},{8,0},{12,4},{1,9},{5,13},{9,1},{13,5},{2,10},{6,14},... | collective-permute-start | bytes 49160 | tf_op jit(solution)/shard_map/ppermute | solution.py:39
  61.3 3.2 %collective-permute-start.20 = (f32[32,128]{1,0:T(8,128)S(1)}, f32[32,128]{1,0:T(8,128)S(1)}, u32[]{:S(2)}, u32[]{:S(2)}) collective-permute-start(f32[32,128]{1,0:T(8,128)S(1)} %add_add_fusion), channel_id=1, source_target_pairs={{0,12},{4,8},{8,4},{12,0},{1,13},{5,9},{9,5},{13,1},{2,14},{6,10},... | collective-permute-start | bytes 49160 | tf_op jit(solution)/shard_map/ppermute | solution.py:39

commit v4 on v3

--- a/solution.py
+++ b/solution.py
@@ -17,7 +17,6 @@
 F32 = jnp.float32
 BF16 = jnp.bfloat16
 VMEM = pl.BlockSpec(memory_space=pltpu.VMEM)
-SMEM = pl.BlockSpec(memory_space=pltpu.SMEM)
 HBM = pl.BlockSpec(memory_space=pltpu.HBM)
 
 
@@ -88,23 +87,39 @@
         copy.wait()
 
 
-def modulation_kernel(time_ref, weight_hbm, start_hbm, out_ref, weight_ref, start_ref, sems):
+def modulation_kernel(
+    time_ref, weight_step_ref, weight_hbm, start_hbm, out_ref, step_ref, weight_ref, start_ref, sems
+):
     rows = start_ref.shape[0]
     half = weight_ref.shape[0] // 2
+    pairs = ((weight_hbm, weight_ref), (start_hbm, start_ref))
     copies = run_copies(
-        [
-            pltpu.make_async_copy(weight_hbm, weight_ref, sems.at[0]),
-            pltpu.make_async_copy(start_hbm, start_ref, sems.at[1]),
-        ]
+        [pltpu.make_async_copy(a, b, sems.at[i]) for i, (a, b) in enumerate(pairs)]
     )
     index = lax.broadcasted_iota(jnp.int32, (16, half), 1).astype(F32)
-    angles = time_ref[0].astype(F32) * jnp.exp(-math.log(10000.0) * index / half)
+    frequency = jnp.exp(-math.log(10000.0) * index / half)
+    time = jnp.broadcast_to(time_ref[...].astype(F32), frequency.shape)
+    angles = time * frequency
     embedding = jnp.concatenate([jnp.cos(angles), jnp.sin(angles)], axis=1).astype(BF16)
+    step = weight_step_ref[...].astype(F32) * (1.0 / STEP_DIVISOR)
+    step_ref[...] = jnp.broadcast_to(step, step_ref.shape)
     wait_copies(copies)
     result = bdot(embedding, weight_ref[...])
     out_ref[0:rows, :] = start_ref[...]
     for r in range(weight_ref.shape[1] // LANES):
         out_ref[rows + r : rows + r + 1, :] = result[0:1, r * LANES : (r + 1) * LANES]
+
+
+def load_kernel(qkv_hbm, inw_hbm, qkv_ref, inw_ref, sems):
+    cols = qkv_ref.shape[1]
+    wait_copies(
+        run_copies(
+            [
+                pltpu.make_async_copy(inw_hbm, inw_ref, sems.at[0]),
+                pltpu.make_async_copy(qkv_hbm.at[:, pl.ds(0, cols)], qkv_ref, sems.at[1]),
+            ]
+        )
+    )
 
 
 def attend(x, factors, base, gram, head_count):
@@ -128,44 +143,37 @@
 def setup_kernel(nt, nm, head_count, *refs):
     msgs, refs = refs[:nt], refs[nt:]
     inws, refs = refs[:nm], refs[nm:]
-    qkv_hbm, out_w_hbm, refs = refs[0], refs[1], refs[2:]
-    factor_ref, base_ref, gram_ref, start_ref, inw_ref, gate_ref, out_w_ref = refs[:7]
-    start_s, mod_s, inw_s, z_s, qkv_s, sems = refs[7:]
+    near_ref, qkv_hbm, out_w_hbm, refs = refs[0], refs[1], refs[2], refs[3:]
+    factor_ref, base_ref, gram_ref, start_ref, inw_ref, scaled_ref = refs[:6]
+    start_s, mod_s, inw_s, z_s, qkv_s, out_w_s, sems = refs[6:]
     block = 3 * HD
-    own = run_copies(
-        [
-            pltpu.make_async_copy(
-                inws[0], inw_s.at[place("tm", nm, 0)], sems.at[head_count + 1]
-            )
-        ]
-    )
+    near = near_ref.shape[1] // block
     copies = run_copies(
-        [
+        [pltpu.make_async_copy(out_w_hbm, out_w_s, sems.at[0])]
+        + [
             pltpu.make_async_copy(
                 qkv_hbm.at[:, pl.ds(h * block, block)],
-                qkv_s.at[:, pl.ds(h * block, block)],
-                sems.at[h],
+                qkv_s.at[:, pl.ds((h - near) * block, block)],
+                sems.at[1 + h - near],
             )
-            for h in range(head_count)
+            for h in range(near, head_count)
         ]
-        + [pltpu.make_async_copy(out_w_hbm, out_w_ref, sems.at[head_count])]
-    )
-    wait_copies(own)
+    )
     for k, msg in enumerate(msgs):
         at = place("tensor", nt, k)
         start_s[at] = msg[0 : start_s.shape[1], :]
         mod_s[at, 0 : msg.shape[0] - start_s.shape[1], :] = msg[start_s.shape[1] :, :]
-    for k in range(1, nm):
+    for k in range(nm):
         inw_s[place("tm", nm, k)] = inws[k][...]
-    channels, width = inw_ref.shape
+    channels, width = inw_ref.shape[1], z_s.shape[1]
     chunks = width // LANES
+    per_part = chunks // nm
     per = 3 * chunks // nt
 
     def mod_row(r):
         return mod_s[r // per, r % per : r % per + 1, :]
 
     inw = inw_s[...].reshape(channels, width)
-    inw_ref[...] = inw
     total = jnp.zeros((channels, LANES), F32)
     for c in range(chunks):
         total = total + inw[:, c * LANES : (c + 1) * LANES].astype(F32)
@@ -175,7 +183,8 @@
         centered = inw[:, cols].astype(F32) - mean
         z_s[0:channels, cols] = (centered * (1.0 + mod_row(chunks + c))).astype(BF16)
         z_s[channels : channels + 16, cols] = jnp.broadcast_to(mod_row(c), (16, LANES)).astype(BF16)
-        gate_ref[c : c + 1, :] = mod_row(2 * chunks + c)
+        at = slice(c % per_part * LANES, (c % per_part + 1) * LANES)
+        inw_ref[c // per_part, :, at] = inw[:, cols]
     mean_b = jnp.broadcast_to(mean, (channels, channels))
     gram = bdot_t(inw, inw) * (1.0 / width) - mean_b * mean_b.T
     for i, piece in enumerate(split_terms(gram, 3)):
@@ -183,24 +192,46 @@
     start = start_s[...].reshape(start_ref.shape)
     start_ref[...] = start
 
-    for h in range(head_count):
+    def scale_chunks(first, last):
+        for c in range(first, last):
+            at = slice(c % per_part * LANES, (c % per_part + 1) * LANES)
+            scaled = out_w_s[:, c * LANES : (c + 1) * LANES].astype(F32) * mod_row(2 * chunks + c)
+            scaled_ref[c // per_part, :, at] = scaled.astype(BF16)
+
+    def project(h, weight):
         at = slice(h * block, (h + 1) * block)
-        copies[h].wait()
-        result = bdot(z_s[...], qkv_s[:, at])
+        result = bdot(z_s[...], weight)
         high, low = split_terms(result[0:channels], 2)
         factor_ref[0:channels, at] = high
         factor_ref[channels : 2 * channels, at] = low
         base_ref[:, at] = result[channels : channels + 8]
-    copies[head_count].wait()
-
-
-def attend_kernel(head_count, *refs):
-    start_ref, factor_ref, base_ref, gram_ref, out_w_ref, gate_ref, att_ref, scaled_ref = refs
+
+    for h in range(near):
+        project(h, near_ref[:, h * block : (h + 1) * block])
+    copies[0].wait()
+    far = head_count - near
+    for h in range(far):
+        copies[1 + h].wait()
+        project(near + h, qkv_s[:, h * block : (h + 1) * block])
+        scale_chunks(h * chunks // far, (h + 1) * chunks // far)
+    if far == 0:
+        scale_chunks(0, chunks)
+
+
+def attend_kernel(nm, early, head_count, *refs):
+    heads, refs = refs[:early], refs[early:]
+    start_ref, factor_ref, base_ref, gram_ref, scaled_ref, inw_ref = refs[:6]
+    att_ref, fold_ref, resid_ref = refs[6:]
     x = start_ref[...].astype(BF16)
+    folded = jnp.zeros(fold_ref.shape, F32)
+    resid = jnp.zeros(resid_ref.shape, F32)
+    for k in range(early):
+        at = place("tm", nm, k)
+        folded = folded + bdot(scaled_ref[at], heads[k][...])
+        resid = resid + bdot(inw_ref[at], heads[k][...])
+    fold_ref[...] = folded
+    resid_ref[...] = resid
     att_ref[...] = attend(x, factor_ref, base_ref, gram_ref, head_count)
-    for c in range(out_w_ref.shape[1] // LANES):
-        cols = slice(c * LANES, (c + 1) * LANES)
-        scaled_ref[:, cols] = (out_w_ref[:, cols].astype(F32) * gate_ref[c : c + 1, :]).astype(BF16)
 
 
 def add_own_rows(result, residual, rows):
@@ -209,28 +240,24 @@
     return result + jnp.where((at >= first) & (at < first + rows), residual, 0.0)
 
 
-def step_size(step_ref):
-    return step_ref[0].astype(F32) * (1.0 / STEP_DIVISOR)
-
-
-def fold_kernel(nm, rows, *refs):
-    heads, refs = refs[:nm], refs[nm:]
-    step_ref, scaled_ref, inw_ref, att_ref, start_ref = refs[:5]
-    fold_ref, resid_ref, vel_ref, head_s = refs[5:]
-    for k in range(nm):
-        head_s[place("tm", nm, k)] = heads[k][...]
-    _, width = scaled_ref.shape
-    channels = inw_ref.shape[0]
-    head = head_s[...].reshape(width, head_s.shape[2])
-    resid = bdot(inw_ref[...], head)
-    folded = bdot(scaled_ref[...], head).astype(BF16)
+def fold_kernel(nm, late, rows, *refs):
+    heads, refs = refs[:late], refs[late:]
+    step_ref, scaled_ref, inw_ref, fold_in, resid_in, att_ref, start_ref = refs[:7]
+    fold_ref, resid_ref, vel_ref = refs[7:]
+    channels = inw_ref.shape[1]
+    total, resid = fold_in[...], resid_in[...]
+    for k in range(late):
+        at = place("tm", nm, nm - late + k)
+        total = total + bdot(scaled_ref[at], heads[k][...])
+        resid = resid + bdot(inw_ref[at], heads[k][...])
+    folded = total.astype(BF16)
     fold_ref[...] = folded
     for i, term in enumerate(split_terms(resid, 2)):
         resid_ref[i * channels : (i + 1) * channels, :] = term
     x = start_ref[...].astype(BF16)
     vel = bdot(att_ref[...], folded)
     residual = bdot(jnp.concatenate([x, x], axis=1), resid_ref[...])
-    vel_ref[...] = (add_own_rows(vel, residual, rows) * step_size(step_ref)).astype(vel_ref.dtype)
+    vel_ref[...] = (add_own_rows(vel, residual, rows) * step_ref[0:1, :]).astype(vel_ref.dtype)
 
 
 def iterate_kernel(nparts, rows, head_count, split, *refs):
@@ -245,7 +272,7 @@
     attended = attend(x, factor_ref, base_ref, gram_ref, head_count)
     vel = bdot(attended, fold_ref[...])
     residual = bdot(jnp.concatenate([x, x], axis=1), resid_ref[...])
-    vel = add_own_rows(vel, residual, rows) * step_size(step_ref)
+    vel = add_own_rows(vel, residual, rows) * step_ref[0:1, :]
     if not split:
         outs[0][...] = vel.astype(outs[0].dtype)
         return
@@ -306,7 +333,6 @@
     n_tensor = lax.axis_size("tensor")
     tokens = rows * n_tensor
     width = in_weight.shape[1]
-    chunks = width // LANES
     head_count = qkv_weight.shape[1] // (3 * HD)
     span = out_weight.shape[0]
 
@@ -314,23 +340,24 @@
     small = is_small("tensor") and mod_weight.shape[1] % LANES == 0
     if small:
         mod_rows = mod_weight.shape[1] // LANES
-        message = call(
+        message, step = call(
             modulation_kernel,
-            [shape_of((rows + mod_rows, LANES), F32)],
-            [SMEM, HBM, HBM],
+            [shape_of((rows + mod_rows, LANES), F32), shape_of((8, LANES), F32)],
+            [VMEM, VMEM, HBM, HBM],
             [
                 pltpu.VMEM(mod_weight.shape, BF16),
                 pltpu.VMEM(start_latent.shape, F32),
                 pltpu.SemaphoreType.DMA((2,)),
             ],
-            time_index,
+            time_index.reshape(1, 1),
+            step_weight.reshape(1, 1),
             mod_weight,
             start_latent,
-            limit=8,
-        )[0]
+        )
         messages = gather_parts(message, "tensor")
         block_rows = rows
     else:
+        step = jnp.full((8, LANES), step_weight[0].astype(F32) / STEP_DIVISOR)
         embedding = embedding_of(time_index, mod_weight.shape[0]).astype(BF16)
         mod_part = jnp.dot(embedding, mod_weight, preferred_element_type=F32)
         modulation = lax.all_gather(mod_part, "tensor", axis=1, tiled=True)
@@ -340,62 +367,83 @@
     nt, nm = len(messages), len(inw_parts)
     mod_rows = messages[0].shape[0] - block_rows
     padded = -(-mod_rows // 8) * 8
-    factor, base, gram, start_all, inw_all, gate, out_near = call(
+    near = max(1, head_count // 2)
+    far = max(1, head_count - near)
+    qkv_near, inw_parts[0] = call(
+        load_kernel,
+        [shape_of((width, near * 3 * HD), BF16), shape_of(inw_parts[0].shape, BF16)],
+        [HBM, HBM],
+        [pltpu.SemaphoreType.DMA((2,))],
+        qkv_weight,
+        inw_parts[0],
+    )
+    scaled_shape = (nm, span, width // nm)
+    factor, base, gram, start_all, inw_all, scaled = call(
         functools.partial(setup_kernel, nt, nm, head_count),
         [
             shape_of((2 * channels, qkv_weight.shape[1]), BF16),
             shape_of((8, qkv_weight.shape[1]), F32),
             shape_of((3 * channels, channels), BF16),
             shape_of((tokens, channels), F32),
-            shape_of((channels, width), BF16),
-            shape_of((chunks, LANES), F32),
-            shape_of(out_weight.shape, BF16),
+            shape_of((nm, channels, width // nm), BF16),
+            shape_of(scaled_shape, BF16),
         ],
-        [VMEM] * nt + [HBM] + [VMEM] * (nm - 1) + [HBM, HBM],
+        [VMEM] * (nt + nm + 1) + [HBM, HBM],
         [
             pltpu.VMEM((nt, block_rows, channels), F32),
             pltpu.VMEM((nt, padded, LANES), F32),
             pltpu.VMEM((nm, channels // nm, width), BF16),
             pltpu.VMEM((channels + 16, width), BF16),
-            pltpu.VMEM(qkv_weight.shape, BF16),
-            pltpu.SemaphoreType.DMA((head_count + 2,)),
+            pltpu.VMEM((width, far * 3 * HD), BF16),
+            pltpu.VMEM(out_weight.shape, BF16),
+            pltpu.SemaphoreType.DMA((far + 1,)),
         ],
         *messages,
         *inw_parts,
+        qkv_near,
         qkv_weight,
         out_weight,
         limit=32,
     )
-    attended, scaled = call(
-        functools.partial(attend_kernel, head_count),
-        [shape_of((tokens, head_count * HD), BF16), shape_of(out_weight.shape, BF16)],
-        [VMEM] * 6,
+    head_parts = gather_weight_parts(head_weight, "tm")
+    late = 1 if nm > 1 else 0
+    early = nm - late
+    attended, fold_part, resid_part = call(
+        functools.partial(attend_kernel, nm, early, head_count),
+        [
+            shape_of((tokens, head_count * HD), BF16),
+            shape_of((span, channels), F32),
+            shape_of((channels, channels), F32),
+        ],
+        [VMEM] * (early + 6),
         [],
+        *head_parts[:early],
         start_all,
         factor,
         base,
         gram,
-        out_near,
-        gate,
+        scaled,
+        inw_all,
         limit=16,
     )
-    head_parts = gather_weight_parts(head_weight, "tm")
     folded, resid, vel = call(
-        functools.partial(fold_kernel, nm, rows),
+        functools.partial(fold_kernel, nm, late, rows),
         [
             shape_of((span, channels), BF16),
             shape_of((2 * channels, channels), BF16),
             shape_of((tokens, channels), BF16),
         ],
-        [VMEM] * nm + [SMEM] + [VMEM] * 4,
-        [pltpu.VMEM((nm, width // nm, channels), BF16)],
-        *head_parts,
-        step_weight,
+        [VMEM] * (late + 7),
+        [],
+        *head_parts[early:],
+        step,
         scaled,
         inw_all,
+        fold_part,
+        resid_part,
         attended,
         start_all,
-        limit=24,
+        limit=16,
     )
     small = is_small("tensor")
     for iteration in range(1, ITERS):
@@ -413,10 +461,10 @@
         vels = call(
             functools.partial(iterate_kernel, len(pieces), rows, head_count, split),
             outs,
-            [VMEM] * len(pieces) + [SMEM] + [VMEM] * 6,
+            [VMEM] * (len(pieces) + 7),
             [pltpu.VMEM((n_tensor, rows, channels), F32)],
             *pieces,
-            step_weight,
+            step,
             start_all,
             factor,
             base,

time: 65.2 us -> 65 us (level)
  waiting for transfers between devices: 26.7 us -> 25.1 us
  Pallas kernels: 11 us -> 12.4 us
    ppermute x21, waiting for transfers between devices: 26.7 us -> 25.1 us  [swap(): return lax.ppermute(value, axis, [(i, i ^ k) for i in range(n)])]
    pallas_call x5 -> x6, Pallas kernels: 11 us -> 12.4 us  [call(): pl.pallas_call(kernel, out_shape=outs, in_specs=in_specs, out_specs=[VMEM...]
  transfers between devices with their start and end apart: 21 -> 21, of which waited for: 13 -> 12; matrix products, arithmetic and copies ran while one was open for 0% -> 0% of each run, Pallas kernels for 13% -> 17%
where the time goes in v4:
time: 65 us; the launch traced here: 64.9 us
  starting transfers between devices  25.2 us (39%)
  waiting for transfers between devices  25.1 us (39%)
  Pallas kernels  12.4 us (19%)
  between operations  1.45 us (2%)
  other arithmetic  0.65 us (1%)
    ppermute x21, starting transfers between devices, swap(): return lax.ppermute(value, axis, [(i, i ^ k) for i in range(n)])  25.2 us
    ppermute x21, waiting for transfers between devices, swap(): return lax.ppermute(value, axis, [(i, i ^ k) for i in range(n)])  25.1 us
    pallas_call x6, Pallas kernels, call(): pl.pallas_call(kernel, out_shape=outs, in_specs=in_specs, out_specs=[VMEM...  12.4 us
  transfers between devices with their start and end apart: 21, of which 12 were waited for; matrix products, arithmetic and copies ran while one was open for 0% of the time, Pallas kernels for 17%

profile of v4, /device:TPU:0, one launch (start us, length us, event | category | flops | bytes accessed | tf_op | source)
XLA Modules:
  0.0 64.9 jit_solution(6827894288176896213)
XLA Ops:
  0.0 3.0 %collective-permute-start.6 = (bf16[32,3072]{1,0:T(8,128)(2,1)}, bf16[32,3072]{1,0:T(8,128)(2,1)S(1)}, u32[]{:S(2)}, u32[]{:S(2)}) collective-permute-start(bf16[32,3072]{1,0:T(8,128)(2,1)} %inw_hbm.1), channel_id=1, source_target_pairs={{0,8},{4,12},{8,0},{12,4},{1,9},{5,13},{9,1},{13,5},{2,10},{6,14},... | collective-permute-start | bytes 589832 | tf_op jit(solution)/shard_map/ppermute | solution.py:38
  3.0 5.9 %collective-permute-done.6.refs_6_ = bf16[32,3072]{1,0:T(8,128)(2,1)S(1)} collective-permute-done((bf16[32,3072]{1,0:T(8,128)(2,1)}, bf16[32,3072]{1,0:T(8,128)(2,1)S(1)}, u32[]{:S(2)}, u32[]{:S(2)}) %collective-permute-start.6) | collective-permute-done | bytes 196640 | tf_op jit(solution)/shard_map/ppermute | solution.py:38
  8.9 0.5 collective-permute-start.8
  9.4 2.9 %collective-permute-done.refs_2_ = bf16[768,128]{1,0:T(8,128)(2,1)S(1)} collective-permute-done((bf16[768,128]{1,0:T(8,128)(2,1)}, bf16[768,128]{1,0:T(8,128)(2,1)S(1)}, u32[]{:S(2)}, u32[]{:S(2)}) %collective-permute-start) | collective-permute-done | bytes 196640 | tf_op jit(solution)/shard_map/ppermute | solution.py:38
  13.6 1.6 %shard_map.82 = (f32[50,128]{1,0:T(8,128)S(1)}, f32[8,128]{1,0:T(8,128)S(1)}) custom-call(s32[1,1]{1,0:T(1,128)} %bitcast.4.time_ref, s32[1,1]{1,0:T(1,128)} %bitcast.5.weight_step_ref, bf16[256,2304]{1,0:T(8,128)(2,1)} %weight_hbm.1, f32[32,128]{1,0:T(8,128)} %start_hbm.1), custom_call_target="tpu_custom_call" | custom-call | bytes 4194304 | tf_op jit(solution)/shard_map/pallas_call | solution.py:293
  15.2 1.9 %collective-permute-start.2 = (f32[50,128]{1,0:T(8,128)S(1)}, f32[50,128]{1,0:T(8,128)S(1)}, u32[]{:S(2)}, u32[]{:S(2)}) collective-permute-start(f32[50,128]{1,0:T(8,128)S(1)} %get-tuple-element.26.refs_0_), channel_id=1, source_target_pairs={{0,1},{1,0},{2,3},{3,2},{4,5},{5,4},{6,7},{7,6},{8,9},{9,8},{10,11... | collective-permute-start | bytes 76808 | tf_op jit(solution)/shard_map/ppermute | solution.py:38
  17.1 2.0 %collective-permute-done.2.refs_1_ = f32[50,128]{1,0:T(8,128)S(1)} collective-permute-done((f32[50,128]{1,0:T(8,128)S(1)}, f32[50,128]{1,0:T(8,128)S(1)}, u32[]{:S(2)}, u32[]{:S(2)}) %collective-permute-start.2) | collective-permute-done | bytes 25632 | tf_op jit(solution)/shard_map/ppermute | solution.py:38
  19.1 2.8 %collective-permute-start.3 = (f32[50,128]{1,0:T(8,128)S(1)}, f32[50,128]{1,0:T(8,128)S(1)}, u32[]{:S(2)}, u32[]{:S(2)}) collective-permute-start(f32[50,128]{1,0:T(8,128)S(1)} %get-tuple-element.26.refs_0_), channel_id=1, source_target_pairs={{0,2},{1,3},{2,0},{3,1},{4,6},{5,7},{6,4},{7,5},{8,10},{9,11},{10,... | collective-permute-start | bytes 76808 | tf_op jit(solution)/shard_map/ppermute | solution.py:38
  22.0 1.9 %collective-permute-done.3.refs_2_ = f32[50,128]{1,0:T(8,128)S(1)} collective-permute-done((f32[50,128]{1,0:T(8,128)S(1)}, f32[50,128]{1,0:T(8,128)S(1)}, u32[]{:S(2)}, u32[]{:S(2)}) %collective-permute-start.3) | collective-permute-done | bytes 25632 | tf_op jit(solution)/shard_map/ppermute | solution.py:38
  23.9 4.0 %collective-permute-start.4 = (f32[50,128]{1,0:T(8,128)S(1)}, f32[50,128]{1,0:T(8,128)S(1)}, u32[]{:S(2)}, u32[]{:S(2)}) collective-permute-start(f32[50,128]{1,0:T(8,128)S(1)} %get-tuple-element.26.refs_0_), channel_id=1, source_target_pairs={{0,3},{1,2},{2,1},{3,0},{4,7},{5,6},{6,5},{7,4},{8,11},{9,10},{10,... | collective-permute-start | bytes 76808 | tf_op jit(solution)/shard_map/ppermute | solution.py:38
  27.9 2.5 %shard_map.83 = (bf16[3072,768]{1,0:T(8,128)(2,1)S(1)}, bf16[32,3072]{1,0:T(8,128)(2,1)S(1)}) custom-call(bf16[3072,1536]{1,0:T(8,128)(2,1)} %refs_9_.1, bf16[32,3072]{1,0:T(8,128)(2,1)} %inw_hbm.1), custom_call_target="tpu_custom_call" | custom-call | bytes 4194304 | tf_op jit(solution)/shard_map/pallas_call | solution.py:293
  30.4 5.4 %shard_map.84 = (bf16[256,1536]{1,0:T(8,128)(2,1)S(1)}, f32[8,1536]{1,0:T(8,128)S(1)}, bf16[384,128]{1,0:T(8,128)(2,1)S(1)}, f32[128,128]{1,0:T(8,128)S(1)}, bf1...) custom-call(f32[50,128]{1,0:T(8,128)S(1)} %get-tuple-element.26.refs_0_, ...), custom_call_target="tpu_custom_call" | custom-call | bytes 4194304 | tf_op jit(solution)/shard_map/pallas_call | solution.py:293
  35.8 1.4 %shard_map.85 = (bf16[128,512]{1,0:T(8,128)(2,1)S(1)}, f32[512,128]{1,0:T(8,128)S(1)}, f32[128,128]{1,0:T(8,128)S(1)}) custom-call(bf16[768,128]{1,0:T(8,128)(2,1)S(1)} %copy-done, bf16[768,128]{1,0:T(8,128)(2,1)S(1)} %collective-permute-done.8.refs_1_, bf16[768,128]{1,0:T(8,128)(2,1)S(1)} %collective-permute-done.refs_2_, ...), custom_call_target="tpu_custom_call" | custom-call | bytes 4194304 | tf_op jit(solution)/shard_map/pallas_call | solution.py:293
  37.3 0.6 shard_map.86
  37.9 1.5 %collective-permute-start.10 = (bf16[128,128]{1,0:T(8,128)(2,1)S(1)}, bf16[128,128]{1,0:T(8,128)(2,1)S(1)}, u32[]{:S(2)}, u32[]{:S(2)}) collective-permute-start(bf16[128,128]{1,0:T(8,128)(2,1)S(1)} %get-tuple-element.38), channel_id=1, source_target_pairs={{0,8},{4,12},{8,0},{12,4},{1,9},{5,13},{9,1},{13,5},{2,10},{6,14},... | collective-permute-start | bytes 98312 | tf_op jit(solution)/shard_map/ppermute | solution.py:38
  39.5 0.7 %collective-permute-start.9 = (bf16[128,128]{1,0:T(8,128)(2,1)S(1)}, bf16[128,128]{1,0:T(8,128)(2,1)S(1)}, u32[]{:S(2)}, u32[]{:S(2)}) collective-permute-start(bf16[128,128]{1,0:T(8,128)(2,1)S(1)} %get-tuple-element.38), channel_id=1, source_target_pairs={{0,4},{4,0},{8,12},{12,8},{1,5},{5,1},{9,13},{13,9},{2,6},{6,2},{1... | collective-permute-start | bytes 98312 | tf_op jit(solution)/shard_map/ppermute | solution.py:38
  40.1 1.8 %collective-permute-done.10 = bf16[128,128]{1,0:T(8,128)(2,1)S(1)} collective-permute-done((bf16[128,128]{1,0:T(8,128)(2,1)S(1)}, bf16[128,128]{1,0:T(8,128)(2,1)S(1)}, u32[]{:S(2)}, u32[]{:S(2)}) %collective-permute-start.10) | collective-permute-done | bytes 32800 | tf_op jit(solution)/shard_map/ppermute | solution.py:38
  41.9 0.9 %collective-permute-done.11 = bf16[128,128]{1,0:T(8,128)(2,1)S(1)} collective-permute-done((bf16[128,128]{1,0:T(8,128)(2,1)S(1)}, bf16[128,128]{1,0:T(8,128)(2,1)S(1)}, u32[]{:S(2)}, u32[]{:S(2)}) %collective-permute-start.11) | collective-permute-done | bytes 32800 | tf_op jit(solution)/shard_map/ppermute | solution.py:38
  42.9 3.7 %collective-permute-start.13 = (bf16[128,128]{1,0:T(8,128)(2,1)S(1)}, bf16[128,128]{1,0:T(8,128)(2,1)S(1)}, u32[]{:S(2)}, u32[]{:S(2)}) collective-permute-start(bf16[128,128]{1,0:T(8,128)(2,1)S(1)} %add_convert_fusion.refs_0_), channel_id=1, source_target_pairs={{0,2},{1,3},{2,0},{3,1},{4,6},{5,7},{6,4},{7,5},{8,10},{9,11},{10,... | collective-permute-start | bytes 98312 | tf_op jit(solution)/shard_map/ppermute | solution.py:38
  46.6 0.7 %collective-permute-start.14 = (bf16[128,128]{1,0:T(8,128)(2,1)S(1)}, bf16[128,128]{1,0:T(8,128)(2,1)S(1)}, u32[]{:S(2)}, u32[]{:S(2)}) collective-permute-start(bf16[128,128]{1,0:T(8,128)(2,1)S(1)} %add_convert_fusion.refs_0_), channel_id=1, source_target_pairs={{0,3},{1,2},{2,1},{3,0},{4,7},{5,6},{6,5},{7,4},{8,11},{9,10},{10,... | collective-permute-start | bytes 98312 | tf_op jit(solution)/shard_map/ppermute | solution.py:38
  47.3 1.2 %collective-permute-done.13.refs_2_ = bf16[128,128]{1,0:T(8,128)(2,1)S(1)} collective-permute-done((bf16[128,128]{1,0:T(8,128)(2,1)S(1)}, bf16[128,128]{1,0:T(8,128)(2,1)S(1)}, u32[]{:S(2)}, u32[]{:S(2)}) %collective-permute-start.13) | collective-permute-done | bytes 32800 | tf_op jit(solution)/shard_map/ppermute | solution.py:38
  48.5 3.8 %collective-permute-done.14.refs_3_ = bf16[128,128]{1,0:T(8,128)(2,1)S(1)} collective-permute-done((bf16[128,128]{1,0:T(8,128)(2,1)S(1)}, bf16[128,128]{1,0:T(8,128)(2,1)S(1)}, u32[]{:S(2)}, u32[]{:S(2)}) %collective-permute-start.14) | collective-permute-done | bytes 32800 | tf_op jit(solution)/shard_map/ppermute | solution.py:38
  52.4 0.9 %shard_map.87 = (f32[32,128]{1,0:T(8,128)S(1)}, f32[32,128]{1,0:T(8,128)S(1)}, f32[32,128]{1,0:T(8,128)S(1)}, f32[32,128]{1,0:T(8,128)S(1)}) custom-call(bf16[128,128]{1,0:T(8,128)(2,1)S(1)} %add_convert_fusion.refs_0_, bf16[128,128]{1,0:T(8,128)(2,1)S(1)} %collective-permute-done.12.refs_1_, bf16[128,128]{1,0:T(8,128)(2,1)S(1)} %collective-permute-done.13.refs_2_, ...), custom_call_target="tpu_custom_call" | custom-call | bytes 4194304 | tf_op jit(solution)/shard_map/pallas_call | solution.py:293
  53.3 1.2 %collective-permute-start.16 = (f32[32,128]{1,0:T(8,128)S(1)}, f32[32,128]{1,0:T(8,128)S(1)}, u32[]{:S(2)}, u32[]{:S(2)}) collective-permute-start(f32[32,128]{1,0:T(8,128)S(1)} %get-tuple-element.43), channel_id=1, source_target_pairs={{0,2},{1,3},{2,0},{3,1},{4,6},{5,7},{6,4},{7,5},{8,10},{9,11},{10,... | collective-permute-start | bytes 49160 | tf_op jit(solution)/shard_map/ppermute | solution.py:38
  54.6 3.2 %collective-permute-start.17 = (f32[32,128]{1,0:T(8,128)S(1)}, f32[32,128]{1,0:T(8,128)S(1)}, u32[]{:S(2)}, u32[]{:S(2)}) collective-permute-start(f32[32,128]{1,0:T(8,128)S(1)} %get-tuple-element.44), channel_id=1, source_target_pairs={{0,3},{1,2},{2,1},{3,0},{4,7},{5,6},{6,5},{7,4},{8,11},{9,10},{10,... | collective-permute-start | bytes 49160 | tf_op jit(solution)/shard_map/ppermute | solution.py:38
  57.7 0.3 collective-permute-done.16
  58.0 2.0 %collective-permute-done.17 = f32[32,128]{1,0:T(8,128)S(1)} collective-permute-done((f32[32,128]{1,0:T(8,128)S(1)}, f32[32,128]{1,0:T(8,128)S(1)}, u32[]{:S(2)}, u32[]{:S(2)}) %collective-permute-start.17) | collective-permute-done | bytes 16416 | tf_op jit(solution)/shard_map/ppermute | solution.py:38
  60.1 1.0 %collective-permute-start.19 = (f32[32,128]{1,0:T(8,128)S(1)}, f32[32,128]{1,0:T(8,128)S(1)}, u32[]{:S(2)}, u32[]{:S(2)}) collective-permute-start(f32[32,128]{1,0:T(8,128)S(1)} %add_add_fusion), channel_id=1, source_target_pairs={{0,8},{4,12},{8,0},{12,4},{1,9},{5,13},{9,1},{13,5},{2,10},{6,14},... | collective-permute-start | bytes 49160 | tf_op jit(solution)/shard_map/ppermute | solution.py:38
  61.1 0.9 %collective-permute-start.20 = (f32[32,128]{1,0:T(8,128)S(1)}, f32[32,128]{1,0:T(8,128)S(1)}, u32[]{:S(2)}, u32[]{:S(2)}) collective-permute-start(f32[32,128]{1,0:T(8,128)S(1)} %add_add_fusion), channel_id=1, source_target_pairs={{0,12},{4,8},{8,4},{12,0},{1,13},{5,9},{9,5},{13,1},{2,14},{6,10},... | collective-permute-start | bytes 49160 | tf_op jit(solution)/shard_map/ppermute | solution.py:38
  62.0 1.9 %collective-permute-done.19 = f32[32,128]{1,0:T(8,128)S(1)} collective-permute-done((f32[32,128]{1,0:T(8,128)S(1)}, f32[32,128]{1,0:T(8,128)S(1)}, u32[]{:S(2)}, u32[]{:S(2)}) %collective-permute-start.19) | collective-permute-done | bytes 16416 | tf_op jit(solution)/shard_map/ppermute | solution.py:38
  63.9 0.3 collective-permute-done.20
  64.2 0.6 add_bitcast_fusion
  (23 shorter events, 0.2 us)
Async XLA Ops:
  0.0 8.9 %collective-permute-start.6 = (bf16[32,3072]{1,0:T(8,128)(2,1)}, bf16[32,3072]{1,0:T(8,128)(2,1)S(1)}, u32[]{:S(2)}, u32[]{:S(2)}) collective-permute-start(bf16[32,3072]{1,0:T(8,128)(2,1)} %inw_hbm.1), channel_id=1, source_target_pairs={{0,8},{4,12},{8,0},{12,4},{1,9},{5,13},{9,1},{13,5},{2,10},{6,14},... | collective-permute-start | bytes 589832 | tf_op jit(solution)/shard_map/ppermute | solution.py:38
  3.0 9.3 %collective-permute-start = (bf16[768,128]{1,0:T(8,128)(2,1)}, bf16[768,128]{1,0:T(8,128)(2,1)S(1)}, u32[]{:S(2)}, u32[]{:S(2)}) collective-permute-start(bf16[768,128]{1,0:T(8,128)(2,1)} %refs_0_.1), channel_id=1, source_target_pairs={{0,8},{4,12},{8,0},{12,4},{1,9},{5,13},{9,1},{13,5},{2,10},{6,14},... | collective-permute-start | bytes 589832 | tf_op jit(solution)/shard_map/ppermute | solution.py:38
  3.0 27.4 %collective-permute-start.5 = (bf16[32,3072]{1,0:T(8,128)(2,1)}, bf16[32,3072]{1,0:T(8,128)(2,1)S(1)}, u32[]{:S(2)}, u32[]{:S(2)}) collective-permute-start(bf16[32,3072]{1,0:T(8,128)(2,1)} %inw_hbm.1), channel_id=1, source_target_pairs={{0,4},{4,0},{8,12},{12,8},{1,5},{5,1},{9,13},{13,9},{2,6},{6,2},{1... | collective-permute-start | bytes 589832 | tf_op jit(solution)/shard_map/ppermute | solution.py:38
  8.9 21.5 %collective-permute-start.7 = (bf16[32,3072]{1,0:T(8,128)(2,1)S(1)}, bf16[32,3072]{1,0:T(8,128)(2,1)S(1)}, u32[]{:S(2)}, u32[]{:S(2)}) collective-permute-start(bf16[32,3072]{1,0:T(8,128)(2,1)S(1)} %collective-permute-done.6.refs_6_), channel_id=1, source_target_pairs={{0,4},{4,0},{8,12},{12,8},{1,5},{5,1},{9,13},{13,9},{2,6},{6,2},{1... | collective-permute-start | bytes 589832 | tf_op jit(solution)/shard_map/ppermute | solution.py:38
  8.9 26.9 %collective-permute-start.8 = (bf16[768,128]{1,0:T(8,128)(2,1)}, bf16[768,128]{1,0:T(8,128)(2,1)S(1)}, u32[]{:S(2)}, u32[]{:S(2)}) collective-permute-start(bf16[768,128]{1,0:T(8,128)(2,1)} %refs_0_.1), channel_id=1, source_target_pairs={{0,4},{4,0},{8,12},{12,8},{1,5},{5,1},{9,13},{13,9},{2,6},{6,2},{1... | collective-permute-start | bytes 589832 | tf_op jit(solution)/shard_map/ppermute | solution.py:38
  12.3 25.0 %collective-permute-start.1 = (bf16[768,128]{1,0:T(8,128)(2,1)S(1)}, bf16[768,128]{1,0:T(8,128)(2,1)S(1)}, u32[]{:S(2)}, u32[]{:S(2)}) collective-permute-start(bf16[768,128]{1,0:T(8,128)(2,1)S(1)} %collective-permute-done.refs_2_), channel_id=1, source_target_pairs={{0,4},{4,0},{8,12},{12,8},{1,5},{5,1},{9,13},{13,9},{2,6},{6,2},{1... | collective-permute-start | bytes 589832 | tf_op jit(solution)/shard_map/ppermute | solution.py:38
  15.2 3.9 %collective-permute-start.2 = (f32[50,128]{1,0:T(8,128)S(1)}, f32[50,128]{1,0:T(8,128)S(1)}, u32[]{:S(2)}, u32[]{:S(2)}) collective-permute-start(f32[50,128]{1,0:T(8,128)S(1)} %get-tuple-element.26.refs_0_), channel_id=1, source_target_pairs={{0,1},{1,0},{2,3},{3,2},{4,5},{5,4},{6,7},{7,6},{8,9},{9,8},{10,11... | collective-permute-start | bytes 76808 | tf_op jit(solution)/shard_map/ppermute | solution.py:38
  19.1 4.8 %collective-permute-start.3 = (f32[50,128]{1,0:T(8,128)S(1)}, f32[50,128]{1,0:T(8,128)S(1)}, u32[]{:S(2)}, u32[]{:S(2)}) collective-permute-start(f32[50,128]{1,0:T(8,128)S(1)} %get-tuple-element.26.refs_0_), channel_id=1, source_target_pairs={{0,2},{1,3},{2,0},{3,1},{4,6},{5,7},{6,4},{7,5},{8,10},{9,11},{10,... | collective-permute-start | bytes 76808 | tf_op jit(solution)/shard_map/ppermute | solution.py:38
  23.9 6.5 %collective-permute-start.4 = (f32[50,128]{1,0:T(8,128)S(1)}, f32[50,128]{1,0:T(8,128)S(1)}, u32[]{:S(2)}, u32[]{:S(2)}) collective-permute-start(f32[50,128]{1,0:T(8,128)S(1)} %get-tuple-element.26.refs_0_), channel_id=1, source_target_pairs={{0,3},{1,2},{2,1},{3,0},{4,7},{5,6},{6,5},{7,4},{8,11},{9,10},{10,... | collective-permute-start | bytes 76808 | tf_op jit(solution)/shard_map/ppermute | solution.py:38
  30.4 5.4 %copy-start = (bf16[768,128]{1,0:T(8,128)(2,1)S(1)}, bf16[768,128]{1,0:T(8,128)(2,1)}, u32[]{:S(2)}) copy-start(bf16[768,128]{1,0:T(8,128)(2,1)} %refs_0_.1) | copy-start | bytes 589828
  37.3 26.9 %copy-start.1 = (f32[32,128]{1,0:T(8,128)S(1)}, f32[32,128]{1,0:T(8,128)}, u32[]{:S(2)}) copy-start(f32[32,128]{1,0:T(8,128)} %start_hbm.1) | copy-start | bytes 49156
  37.9 4.0 %collective-permute-start.10 = (bf16[128,128]{1,0:T(8,128)(2,1)S(1)}, bf16[128,128]{1,0:T(8,128)(2,1)S(1)}, u32[]{:S(2)}, u32[]{:S(2)}) collective-permute-start(bf16[128,128]{1,0:T(8,128)(2,1)S(1)} %get-tuple-element.38), channel_id=1, source_target_pairs={{0,8},{4,12},{8,0},{12,4},{1,9},{5,13},{9,1},{13,5},{2,10},{6,14},... | collective-permute-start | bytes 98312 | tf_op jit(solution)/shard_map/ppermute | solution.py:38
  39.5 3.3 %collective-permute-start.11 = (bf16[128,128]{1,0:T(8,128)(2,1)S(1)}, bf16[128,128]{1,0:T(8,128)(2,1)S(1)}, u32[]{:S(2)}, u32[]{:S(2)}) collective-permute-start(bf16[128,128]{1,0:T(8,128)(2,1)S(1)} %get-tuple-element.38), channel_id=1, source_target_pairs={{0,12},{4,8},{8,4},{12,0},{1,13},{5,9},{9,5},{13,1},{2,14},{6,10},... | collective-permute-start | bytes 98312 | tf_op jit(solution)/shard_map/ppermute | solution.py:38
  39.5 3.3 %collective-permute-start.9 = (bf16[128,128]{1,0:T(8,128)(2,1)S(1)}, bf16[128,128]{1,0:T(8,128)(2,1)S(1)}, u32[]{:S(2)}, u32[]{:S(2)}) collective-permute-start(bf16[128,128]{1,0:T(8,128)(2,1)S(1)} %get-tuple-element.38), channel_id=1, source_target_pairs={{0,4},{4,0},{8,12},{12,8},{1,5},{5,1},{9,13},{13,9},{2,6},{6,2},{1... | collective-permute-start | bytes 98312 | tf_op jit(solution)/shard_map/ppermute | solution.py:38
  42.9 4.5 %collective-permute-start.12 = (bf16[128,128]{1,0:T(8,128)(2,1)S(1)}, bf16[128,128]{1,0:T(8,128)(2,1)S(1)}, u32[]{:S(2)}, u32[]{:S(2)}) collective-permute-start(bf16[128,128]{1,0:T(8,128)(2,1)S(1)} %add_convert_fusion.refs_0_), channel_id=1, source_target_pairs={{0,1},{1,0},{2,3},{3,2},{4,5},{5,4},{6,7},{7,6},{8,9},{9,8},{10,11... | collective-permute-start | bytes 98312 | tf_op jit(solution)/shard_map/ppermute | solution.py:38
  42.9 5.6 %collective-permute-start.13 = (bf16[128,128]{1,0:T(8,128)(2,1)S(1)}, bf16[128,128]{1,0:T(8,128)(2,1)S(1)}, u32[]{:S(2)}, u32[]{:S(2)}) collective-permute-start(bf16[128,128]{1,0:T(8,128)(2,1)S(1)} %add_convert_fusion.refs_0_), channel_id=1, source_target_pairs={{0,2},{1,3},{2,0},{3,1},{4,6},{5,7},{6,4},{7,5},{8,10},{9,11},{10,... | collective-permute-start | bytes 98312 | tf_op jit(solution)/shard_map/ppermute | solution.py:38
  46.6 5.7 %collective-permute-start.14 = (bf16[128,128]{1,0:T(8,128)(2,1)S(1)}, bf16[128,128]{1,0:T(8,128)(2,1)S(1)}, u32[]{:S(2)}, u32[]{:S(2)}) collective-permute-start(bf16[128,128]{1,0:T(8,128)(2,1)S(1)} %add_convert_fusion.refs_0_), channel_id=1, source_target_pairs={{0,3},{1,2},{2,1},{3,0},{4,7},{5,6},{6,5},{7,4},{8,11},{9,10},{10,... | collective-permute-start | bytes 98312 | tf_op jit(solution)/shard_map/ppermute | solution.py:38
  53.3 4.5 %collective-permute-start.15 = (f32[32,128]{1,0:T(8,128)S(1)}, f32[32,128]{1,0:T(8,128)S(1)}, u32[]{:S(2)}, u32[]{:S(2)}) collective-permute-start(f32[32,128]{1,0:T(8,128)S(1)} %get-tuple-element.42), channel_id=1, source_target_pairs={{0,1},{1,0},{2,3},{3,2},{4,5},{5,4},{6,7},{7,6},{8,9},{9,8},{10,11... | collective-permute-start | bytes 49160 | tf_op jit(solution)/shard_map/ppermute | solution.py:38
  53.3 4.7 %collective-permute-start.16 = (f32[32,128]{1,0:T(8,128)S(1)}, f32[32,128]{1,0:T(8,128)S(1)}, u32[]{:S(2)}, u32[]{:S(2)}) collective-permute-start(f32[32,128]{1,0:T(8,128)S(1)} %get-tuple-element.43), channel_id=1, source_target_pairs={{0,2},{1,3},{2,0},{3,1},{4,6},{5,7},{6,4},{7,5},{8,10},{9,11},{10,... | collective-permute-start | bytes 49160 | tf_op jit(solution)/shard_map/ppermute | solution.py:38
  54.6 5.5 %collective-permute-start.17 = (f32[32,128]{1,0:T(8,128)S(1)}, f32[32,128]{1,0:T(8,128)S(1)}, u32[]{:S(2)}, u32[]{:S(2)}) collective-permute-start(f32[32,128]{1,0:T(8,128)S(1)} %get-tuple-element.44), channel_id=1, source_target_pairs={{0,3},{1,2},{2,1},{3,0},{4,7},{5,6},{6,5},{7,4},{8,11},{9,10},{10,... | collective-permute-start | bytes 49160 | tf_op jit(solution)/shard_map/ppermute | solution.py:38
  60.1 1.9 %collective-permute-start.18 = (f32[32,128]{1,0:T(8,128)S(1)}, f32[32,128]{1,0:T(8,128)S(1)}, u32[]{:S(2)}, u32[]{:S(2)}) collective-permute-start(f32[32,128]{1,0:T(8,128)S(1)} %add_add_fusion), channel_id=1, source_target_pairs={{0,4},{4,0},{8,12},{12,8},{1,5},{5,1},{9,13},{13,9},{2,6},{6,2},{1... | collective-permute-start | bytes 49160 | tf_op jit(solution)/shard_map/ppermute | solution.py:38
  60.1 3.8 %collective-permute-start.19 = (f32[32,128]{1,0:T(8,128)S(1)}, f32[32,128]{1,0:T(8,128)S(1)}, u32[]{:S(2)}, u32[]{:S(2)}) collective-permute-start(f32[32,128]{1,0:T(8,128)S(1)} %add_add_fusion), channel_id=1, source_target_pairs={{0,8},{4,12},{8,0},{12,4},{1,9},{5,13},{9,1},{13,5},{2,10},{6,14},... | collective-permute-start | bytes 49160 | tf_op jit(solution)/shard_map/ppermute | solution.py:38
  61.1 3.2 %collective-permute-start.20 = (f32[32,128]{1,0:T(8,128)S(1)}, f32[32,128]{1,0:T(8,128)S(1)}, u32[]{:S(2)}, u32[]{:S(2)}) collective-permute-start(f32[32,128]{1,0:T(8,128)S(1)} %add_add_fusion), channel_id=1, source_target_pairs={{0,12},{4,8},{8,4},{12,0},{1,13},{5,9},{9,5},{13,1},{2,14},{6,10},... | collective-permute-start | bytes 49160 | tf_op jit(solution)/shard_map/ppermute | solution.py:38

commit v5 on v4

--- a/solution.py
+++ b/solution.py
@@ -140,97 +140,102 @@
     return outs[0] if head_count == 1 else jnp.concatenate(outs, axis=1)
 
 
-def setup_kernel(nt, nm, head_count, *refs):
+def setup_kernel(nt, nm, block, *refs):
     msgs, refs = refs[:nt], refs[nt:]
     inws, refs = refs[:nm], refs[nm:]
     near_ref, qkv_hbm, out_w_hbm, refs = refs[0], refs[1], refs[2], refs[3:]
-    factor_ref, base_ref, gram_ref, start_ref, inw_ref, scaled_ref = refs[:6]
-    start_s, mod_s, inw_s, z_s, qkv_s, out_w_s, sems = refs[6:]
-    block = 3 * HD
+    factor_ref, base_ref, gram_ref, start_ref, inw_ref, gate_ref, out_w_ref = refs[:7]
+    start_s, mod_s, gate_s, z_s, qkv_s, sems = refs[7:]
     near = near_ref.shape[1] // block
+    count = factor_ref.shape[1] // block
     copies = run_copies(
-        [pltpu.make_async_copy(out_w_hbm, out_w_s, sems.at[0])]
-        + [
+        [
             pltpu.make_async_copy(
-                qkv_hbm.at[:, pl.ds(h * block, block)],
-                qkv_s.at[:, pl.ds((h - near) * block, block)],
-                sems.at[1 + h - near],
+                qkv_hbm.at[:, pl.ds(n * block, block)],
+                qkv_s.at[:, pl.ds((n - near) * block, block)],
+                sems.at[n - near],
             )
-            for h in range(near, head_count)
+            for n in range(near, count)
         ]
+        + [pltpu.make_async_copy(out_w_hbm, out_w_ref, sems.at[count - near])]
     )
     for k, msg in enumerate(msgs):
         at = place("tensor", nt, k)
         start_s[at] = msg[0 : start_s.shape[1], :]
         mod_s[at, 0 : msg.shape[0] - start_s.shape[1], :] = msg[start_s.shape[1] :, :]
     for k in range(nm):
-        inw_s[place("tm", nm, k)] = inws[k][...]
-    channels, width = inw_ref.shape[1], z_s.shape[1]
+        inw_ref[place("tm", nm, k)] = inws[k][...]
+    channels, width = gram_ref.shape[1], z_s.shape[1]
     chunks = width // LANES
-    per_part = chunks // nm
     per = 3 * chunks // nt
 
     def mod_row(r):
         return mod_s[r // per, r % per : r % per + 1, :]
 
-    inw = inw_s[...].reshape(channels, width)
+    def columns(c, n):
+        return inw_ref[:, :, c * LANES : (c + n) * LANES].reshape(channels, n * LANES)
+
     total = jnp.zeros((channels, LANES), F32)
     for c in range(chunks):
-        total = total + inw[:, c * LANES : (c + 1) * LANES].astype(F32)
+        total = total + columns(c, 1).astype(F32)
     mean = jnp.sum(total, axis=1, keepdims=True) * (1.0 / width)
     for c in range(chunks):
         cols = slice(c * LANES, (c + 1) * LANES)
-        centered = inw[:, cols].astype(F32) - mean
+        centered = columns(c, 1).astype(F32) - mean
         z_s[0:channels, cols] = (centered * (1.0 + mod_row(chunks + c))).astype(BF16)
         z_s[channels : channels + 16, cols] = jnp.broadcast_to(mod_row(c), (16, LANES)).astype(BF16)
-        at = slice(c % per_part * LANES, (c % per_part + 1) * LANES)
-        inw_ref[c // per_part, :, at] = inw[:, cols]
+        gate_s[c // (chunks // nm), c % (chunks // nm) : c % (chunks // nm) + 1, :] = mod_row(
+            2 * chunks + c
+        )
+    for p in range(nm):
+        gate_ref[p] = gate_s[p].T
+    gram = jnp.zeros((channels, channels), F32)
+    for c in range(0, chunks, 6):
+        gram = gram + bdot_t(columns(c, 6), columns(c, 6))
     mean_b = jnp.broadcast_to(mean, (channels, channels))
-    gram = bdot_t(inw, inw) * (1.0 / width) - mean_b * mean_b.T
+    gram = gram * (1.0 / width) - mean_b * mean_b.T
     for i, piece in enumerate(split_terms(gram, 3)):
         gram_ref[i * channels : (i + 1) * channels, :] = piece
-    start = start_s[...].reshape(start_ref.shape)
-    start_ref[...] = start
-
-    def scale_chunks(first, last):
-        for c in range(first, last):
-            at = slice(c % per_part * LANES, (c % per_part + 1) * LANES)
-            scaled = out_w_s[:, c * LANES : (c + 1) * LANES].astype(F32) * mod_row(2 * chunks + c)
-            scaled_ref[c // per_part, :, at] = scaled.astype(BF16)
-
-    def project(h, weight):
-        at = slice(h * block, (h + 1) * block)
+    start_ref[...] = start_s[...].reshape(start_ref.shape)
+
+    for n in range(count):
+        at = slice(n * block, (n + 1) * block)
+        if n < near:
+            weight = near_ref[:, at]
+        else:
+            copies[n - near].wait()
+            weight = qkv_s[:, (n - near) * block : (n - near + 1) * block]
         result = bdot(z_s[...], weight)
         high, low = split_terms(result[0:channels], 2)
         factor_ref[0:channels, at] = high
         factor_ref[channels : 2 * channels, at] = low
         base_ref[:, at] = result[channels : channels + 8]
-
-    for h in range(near):
-        project(h, near_ref[:, h * block : (h + 1) * block])
-    copies[0].wait()
-    far = head_count - near
-    for h in range(far):
-        copies[1 + h].wait()
-        project(near + h, qkv_s[:, h * block : (h + 1) * block])
-        scale_chunks(h * chunks // far, (h + 1) * chunks // far)
-    if far == 0:
-        scale_chunks(0, chunks)
+    copies[count - near].wait()
+
+
+def fold_parts(nm, first, heads, gate_ref, out_w_ref, inw_ref):
+    folded, resid = 0.0, 0.0
+    for i, head_ref in enumerate(heads):
+        size, _ = head_ref.shape
+        at = place("tm", nm, first + i)
+        cols = pl.ds(pl.multiple_of(at * size, LANES), size)
+        gate = gate_ref[at]
+        gated = []
+        for r in range(size // LANES):
+            rows = head_ref[r * LANES : (r + 1) * LANES, :].astype(F32)
+            gated.append((rows * gate[:, r : r + 1]).astype(BF16))
+        folded = folded + bdot(out_w_ref[:, cols], jnp.concatenate(gated, axis=0))
+        inw = inw_ref[:, :, cols].reshape(-1, size)
+        resid = resid + bdot(inw, head_ref[...])
+    return folded, resid
 
 
 def attend_kernel(nm, early, head_count, *refs):
     heads, refs = refs[:early], refs[early:]
-    start_ref, factor_ref, base_ref, gram_ref, scaled_ref, inw_ref = refs[:6]
-    att_ref, fold_ref, resid_ref = refs[6:]
+    start_ref, factor_ref, base_ref, gram_ref, gate_ref, out_w_ref, inw_ref = refs[:7]
+    att_ref, fold_ref, resid_ref = refs[7:]
     x = start_ref[...].astype(BF16)
-    folded = jnp.zeros(fold_ref.shape, F32)
-    resid = jnp.zeros(resid_ref.shape, F32)
-    for k in range(early):
-        at = place("tm", nm, k)
-        folded = folded + bdot(scaled_ref[at], heads[k][...])
-        resid = resid + bdot(inw_ref[at], heads[k][...])
-    fold_ref[...] = folded
-    resid_ref[...] = resid
+    fold_ref[...], resid_ref[...] = fold_parts(nm, 0, heads, gate_ref, out_w_ref, inw_ref)
     att_ref[...] = attend(x, factor_ref, base_ref, gram_ref, head_count)
 
 
@@ -242,14 +247,13 @@
 
 def fold_kernel(nm, late, rows, *refs):
     heads, refs = refs[:late], refs[late:]
-    step_ref, scaled_ref, inw_ref, fold_in, resid_in, att_ref, start_ref = refs[:7]
-    fold_ref, resid_ref, vel_ref = refs[7:]
-    channels = inw_ref.shape[1]
+    step_ref, gate_ref, out_w_ref, inw_ref, fold_in, resid_in, att_ref, start_ref = refs[:8]
+    fold_ref, resid_ref, vel_ref = refs[8:]
+    channels = resid_in.shape[0]
     total, resid = fold_in[...], resid_in[...]
-    for k in range(late):
-        at = place("tm", nm, nm - late + k)
-        total = total + bdot(scaled_ref[at], heads[k][...])
-        resid = resid + bdot(inw_ref[at], heads[k][...])
+    if late:
+        more = fold_parts(nm, nm - late, heads, gate_ref, out_w_ref, inw_ref)
+        total, resid = total + more[0], resid + more[1]
     folded = total.astype(BF16)
     fold_ref[...] = folded
     for i, term in enumerate(split_terms(resid, 2)):
@@ -333,6 +337,7 @@
     n_tensor = lax.axis_size("tensor")
     tokens = rows * n_tensor
     width = in_weight.shape[1]
+    chunks = width // LANES
     head_count = qkv_weight.shape[1] // (3 * HD)
     span = out_weight.shape[0]
 
@@ -367,35 +372,37 @@
     nt, nm = len(messages), len(inw_parts)
     mod_rows = messages[0].shape[0] - block_rows
     padded = -(-mod_rows // 8) * 8
-    near = max(1, head_count // 2)
-    far = max(1, head_count - near)
+    span_cols = qkv_weight.shape[1]
+    gate_rows = -(-(chunks // nm) // 8) * 8
+    block = 4 * LANES if span_cols % (4 * LANES) == 0 else span_cols
+    near = max(1, span_cols // block * 2 // 3)
+    far = max(1, span_cols // block - near)
     qkv_near, inw_parts[0] = call(
         load_kernel,
-        [shape_of((width, near * 3 * HD), BF16), shape_of(inw_parts[0].shape, BF16)],
+        [shape_of((width, near * block), BF16), shape_of(inw_parts[0].shape, BF16)],
         [HBM, HBM],
         [pltpu.SemaphoreType.DMA((2,))],
         qkv_weight,
         inw_parts[0],
     )
-    scaled_shape = (nm, span, width // nm)
-    factor, base, gram, start_all, inw_all, scaled = call(
-        functools.partial(setup_kernel, nt, nm, head_count),
+    factor, base, gram, start_all, inw_all, gate, out_near = call(
+        functools.partial(setup_kernel, nt, nm, block),
         [
-            shape_of((2 * channels, qkv_weight.shape[1]), BF16),
-            shape_of((8, qkv_weight.shape[1]), F32),
+            shape_of((2 * channels, span_cols), BF16),
+            shape_of((8, span_cols), F32),
             shape_of((3 * channels, channels), BF16),
             shape_of((tokens, channels), F32),
-            shape_of((nm, channels, width // nm), BF16),
-            shape_of(scaled_shape, BF16),
+            shape_of((nm, channels // nm, width), BF16),
+            shape_of((nm, LANES, gate_rows), F32),
+            shape_of(out_weight.shape, BF16),
         ],
         [VMEM] * (nt + nm + 1) + [HBM, HBM],
         [
             pltpu.VMEM((nt, block_rows, channels), F32),
             pltpu.VMEM((nt, padded, LANES), F32),
-            pltpu.VMEM((nm, channels // nm, width), BF16),
+            pltpu.VMEM((nm, gate_rows, LANES), F32),
             pltpu.VMEM((channels + 16, width), BF16),
-            pltpu.VMEM((width, far * 3 * HD), BF16),
-            pltpu.VMEM(out_weight.shape, BF16),
+            pltpu.VMEM((width, far * block), BF16),
             pltpu.SemaphoreType.DMA((far + 1,)),
         ],
         *messages,
@@ -415,14 +422,15 @@
             shape_of((span, channels), F32),
             shape_of((channels, channels), F32),
         ],
-        [VMEM] * (early + 6),
+        [VMEM] * (early + 7),
         [],
         *head_parts[:early],
         start_all,
         factor,
         base,
         gram,
-        scaled,
+        gate,
+        out_near,
         inw_all,
         limit=16,
     )
@@ -433,11 +441,12 @@
             shape_of((2 * channels, channels), BF16),
             shape_of((tokens, channels), BF16),
         ],
-        [VMEM] * (late + 7),
+        [VMEM] * (late + 8),
         [],
         *head_parts[early:],
         step,
-        scaled,
+        gate,
+        out_near,
         inw_all,
         fold_part,
         resid_part,

time: 65 us -> 64.6 us (level)
  transfers between devices with their start and end apart: 21 -> 21, of which waited for: 12 -> 12; matrix products, arithmetic and copies ran while one was open for 0% -> 0% of each run, Pallas kernels for 17% -> 16%
where the time goes in v5:
time: 64.6 us; the launch traced here: 64.4 us
  starting transfers between devices  25.2 us (39%)
  waiting for transfers between devices  25.1 us (39%)
  Pallas kernels  12 us (19%)
  between operations  1.45 us (2%)
  other arithmetic  0.65 us (1%)
    ppermute x21, starting transfers between devices, swap(): return lax.ppermute(value, axis, [(i, i ^ k) for i in range(n)])  25.2 us
    ppermute x21, waiting for transfers between devices, swap(): return lax.ppermute(value, axis, [(i, i ^ k) for i in range(n)])  25.1 us
    pallas_call x6, Pallas kernels, call(): pl.pallas_call(kernel, out_shape=outs, in_specs=in_specs, out_specs=[VMEM...  12 us
  transfers between devices with their start and end apart: 21, of which 12 were waited for; matrix products, arithmetic and copies ran while one was open for 0% of the time, Pallas kernels for 16%

profile of v5, /device:TPU:0, one launch (start us, length us, event | category | flops | bytes accessed | tf_op | source)
XLA Modules:
  0.0 64.4 jit_solution(17050018669125561014)
XLA Ops:
  0.0 3.0 %collective-permute-start.6 = (bf16[32,3072]{1,0:T(8,128)(2,1)}, bf16[32,3072]{1,0:T(8,128)(2,1)S(1)}, u32[]{:S(2)}, u32[]{:S(2)}) collective-permute-start(bf16[32,3072]{1,0:T(8,128)(2,1)} %inw_hbm.1), channel_id=1, source_target_pairs={{0,8},{4,12},{8,0},{12,4},{1,9},{5,13},{9,1},{13,5},{2,10},{6,14},... | collective-permute-start | bytes 589832 | tf_op jit(solution)/shard_map/ppermute | solution.py:38
  3.0 5.9 %collective-permute-done.6.refs_6_ = bf16[32,3072]{1,0:T(8,128)(2,1)S(1)} collective-permute-done((bf16[32,3072]{1,0:T(8,128)(2,1)}, bf16[32,3072]{1,0:T(8,128)(2,1)S(1)}, u32[]{:S(2)}, u32[]{:S(2)}) %collective-permute-start.6) | collective-permute-done | bytes 196640 | tf_op jit(solution)/shard_map/ppermute | solution.py:38
  8.9 0.5 collective-permute-start.8
  9.4 2.9 %collective-permute-done.refs_2_ = bf16[768,128]{1,0:T(8,128)(2,1)S(1)} collective-permute-done((bf16[768,128]{1,0:T(8,128)(2,1)}, bf16[768,128]{1,0:T(8,128)(2,1)S(1)}, u32[]{:S(2)}, u32[]{:S(2)}) %collective-permute-start) | collective-permute-done | bytes 196640 | tf_op jit(solution)/shard_map/ppermute | solution.py:38
  13.6 1.6 %shard_map.82 = (f32[50,128]{1,0:T(8,128)S(1)}, f32[8,128]{1,0:T(8,128)S(1)}) custom-call(s32[1,1]{1,0:T(1,128)} %bitcast.4.time_ref, s32[1,1]{1,0:T(1,128)} %bitcast.5.weight_step_ref, bf16[256,2304]{1,0:T(8,128)(2,1)} %weight_hbm.1, f32[32,128]{1,0:T(8,128)} %start_hbm.1), custom_call_target="tpu_custom_call" | custom-call | bytes 4194304 | tf_op jit(solution)/shard_map/pallas_call | solution.py:297
  15.2 1.9 %collective-permute-start.2 = (f32[50,128]{1,0:T(8,128)S(1)}, f32[50,128]{1,0:T(8,128)S(1)}, u32[]{:S(2)}, u32[]{:S(2)}) collective-permute-start(f32[50,128]{1,0:T(8,128)S(1)} %get-tuple-element.27.refs_0_), channel_id=1, source_target_pairs={{0,1},{1,0},{2,3},{3,2},{4,5},{5,4},{6,7},{7,6},{8,9},{9,8},{10,11... | collective-permute-start | bytes 76808 | tf_op jit(solution)/shard_map/ppermute | solution.py:38
  17.1 2.0 %collective-permute-done.2.refs_1_ = f32[50,128]{1,0:T(8,128)S(1)} collective-permute-done((f32[50,128]{1,0:T(8,128)S(1)}, f32[50,128]{1,0:T(8,128)S(1)}, u32[]{:S(2)}, u32[]{:S(2)}) %collective-permute-start.2) | collective-permute-done | bytes 25632 | tf_op jit(solution)/shard_map/ppermute | solution.py:38
  19.1 2.8 %collective-permute-start.3 = (f32[50,128]{1,0:T(8,128)S(1)}, f32[50,128]{1,0:T(8,128)S(1)}, u32[]{:S(2)}, u32[]{:S(2)}) collective-permute-start(f32[50,128]{1,0:T(8,128)S(1)} %get-tuple-element.27.refs_0_), channel_id=1, source_target_pairs={{0,2},{1,3},{2,0},{3,1},{4,6},{5,7},{6,4},{7,5},{8,10},{9,11},{10,... | collective-permute-start | bytes 76808 | tf_op jit(solution)/shard_map/ppermute | solution.py:38
  22.0 1.9 %collective-permute-done.3.refs_2_ = f32[50,128]{1,0:T(8,128)S(1)} collective-permute-done((f32[50,128]{1,0:T(8,128)S(1)}, f32[50,128]{1,0:T(8,128)S(1)}, u32[]{:S(2)}, u32[]{:S(2)}) %collective-permute-start.3) | collective-permute-done | bytes 25632 | tf_op jit(solution)/shard_map/ppermute | solution.py:38
  23.9 4.0 %collective-permute-start.4 = (f32[50,128]{1,0:T(8,128)S(1)}, f32[50,128]{1,0:T(8,128)S(1)}, u32[]{:S(2)}, u32[]{:S(2)}) collective-permute-start(f32[50,128]{1,0:T(8,128)S(1)} %get-tuple-element.27.refs_0_), channel_id=1, source_target_pairs={{0,3},{1,2},{2,1},{3,0},{4,7},{5,6},{6,5},{7,4},{8,11},{9,10},{10,... | collective-permute-start | bytes 76808 | tf_op jit(solution)/shard_map/ppermute | solution.py:38
  27.9 2.9 %shard_map.83 = (bf16[3072,1024]{1,0:T(8,128)(2,1)S(1)}, bf16[32,3072]{1,0:T(8,128)(2,1)S(1)}) custom-call(bf16[3072,1536]{1,0:T(8,128)(2,1)} %refs_9_.1, bf16[32,3072]{1,0:T(8,128)(2,1)} %inw_hbm.1), custom_call_target="tpu_custom_call" | custom-call | bytes 4194304 | tf_op jit(solution)/shard_map/pallas_call | solution.py:297
  30.9 4.3 %shard_map.84 = (bf16[256,1536]{1,0:T(8,128)(2,1)S(1)}, f32[8,1536]{1,0:T(8,128)S(1)}, bf16[384,128]{1,0:T(8,128)(2,1)S(1)}, f32[128,128]{1,0:T(8,128)S(1)}, bf1...) custom-call(f32[50,128]{1,0:T(8,128)S(1)} %get-tuple-element.27.refs_0_, ...), custom_call_target="tpu_custom_call" | custom-call | bytes 4194304 | tf_op jit(solution)/shard_map/pallas_call | solution.py:297
  35.2 1.5 %shard_map.85 = (bf16[128,512]{1,0:T(8,128)(2,1)S(1)}, f32[512,128]{1,0:T(8,128)S(1)}, f32[128,128]{1,0:T(8,128)S(1)}) custom-call(bf16[768,128]{1,0:T(8,128)(2,1)S(1)} %copy-done, bf16[768,128]{1,0:T(8,128)(2,1)S(1)} %collective-permute-done.8.refs_1_, bf16[768,128]{1,0:T(8,128)(2,1)S(1)} %collective-permute-done.refs_2_, ...), custom_call_target="tpu_custom_call" | custom-call | bytes 4194304 | tf_op jit(solution)/shard_map/pallas_call | solution.py:297
  36.8 0.7 %shard_map.86 = (bf16[512,128]{1,0:T(8,128)(2,1)S(1)}, bf16[256,128]{1,0:T(8,128)(2,1)S(1)}, bf16[128,128]{1,0:T(8,128)(2,1)S(1)}) custom-call(bf16[768,128]{1,0:T(8,128)(2,1)S(1)} %collective-permute-done.1.refs_0_, f32[8,128]{1,0:T(8,128)S(1)} %get-tuple-element.26.refs_1_.refs_4_, f32[4,128,8]{2,1,0:T(8,128)S(1)} %get-tuple-element.30.refs_7_.refs_2_, ...), custom_call_target="tpu_custom_call" | custom-call | bytes 4194304 | tf_op jit(solution)/shard_map/pallas_call | solution.py:297
  37.5 1.6 %collective-permute-start.10 = (bf16[128,128]{1,0:T(8,128)(2,1)S(1)}, bf16[128,128]{1,0:T(8,128)(2,1)S(1)}, u32[]{:S(2)}, u32[]{:S(2)}) collective-permute-start(bf16[128,128]{1,0:T(8,128)(2,1)S(1)} %get-tuple-element.40), channel_id=1, source_target_pairs={{0,8},{4,12},{8,0},{12,4},{1,9},{5,13},{9,1},{13,5},{2,10},{6,14},... | collective-permute-start | bytes 98312 | tf_op jit(solution)/shard_map/ppermute | solution.py:38
  39.1 0.6 collective-permute-start.9
  39.7 1.8 %collective-permute-done.10 = bf16[128,128]{1,0:T(8,128)(2,1)S(1)} collective-permute-done((bf16[128,128]{1,0:T(8,128)(2,1)S(1)}, bf16[128,128]{1,0:T(8,128)(2,1)S(1)}, u32[]{:S(2)}, u32[]{:S(2)}) %collective-permute-start.10) | collective-permute-done | bytes 32800 | tf_op jit(solution)/shard_map/ppermute | solution.py:38
  41.5 0.9 %collective-permute-done.11 = bf16[128,128]{1,0:T(8,128)(2,1)S(1)} collective-permute-done((bf16[128,128]{1,0:T(8,128)(2,1)S(1)}, bf16[128,128]{1,0:T(8,128)(2,1)S(1)}, u32[]{:S(2)}, u32[]{:S(2)}) %collective-permute-start.11) | collective-permute-done | bytes 32800 | tf_op jit(solution)/shard_map/ppermute | solution.py:38
  42.5 3.3 %collective-permute-start.13 = (bf16[128,128]{1,0:T(8,128)(2,1)S(1)}, bf16[128,128]{1,0:T(8,128)(2,1)S(1)}, u32[]{:S(2)}, u32[]{:S(2)}) collective-permute-start(bf16[128,128]{1,0:T(8,128)(2,1)S(1)} %add_convert_fusion.refs_0_), channel_id=1, source_target_pairs={{0,2},{1,3},{2,0},{3,1},{4,6},{5,7},{6,4},{7,5},{8,10},{9,11},{10,... | collective-permute-start | bytes 98312 | tf_op jit(solution)/shard_map/ppermute | solution.py:38
  45.8 1.1 %collective-permute-start.14 = (bf16[128,128]{1,0:T(8,128)(2,1)S(1)}, bf16[128,128]{1,0:T(8,128)(2,1)S(1)}, u32[]{:S(2)}, u32[]{:S(2)}) collective-permute-start(bf16[128,128]{1,0:T(8,128)(2,1)S(1)} %add_convert_fusion.refs_0_), channel_id=1, source_target_pairs={{0,3},{1,2},{2,1},{3,0},{4,7},{5,6},{6,5},{7,4},{8,11},{9,10},{10,... | collective-permute-start | bytes 98312 | tf_op jit(solution)/shard_map/ppermute | solution.py:38
  46.9 0.8 %collective-permute-done.13.refs_2_ = bf16[128,128]{1,0:T(8,128)(2,1)S(1)} collective-permute-done((bf16[128,128]{1,0:T(8,128)(2,1)S(1)}, bf16[128,128]{1,0:T(8,128)(2,1)S(1)}, u32[]{:S(2)}, u32[]{:S(2)}) %collective-permute-start.13) | collective-permute-done | bytes 32800 | tf_op jit(solution)/shard_map/ppermute | solution.py:38
  47.7 3.8 %collective-permute-done.14.refs_3_ = bf16[128,128]{1,0:T(8,128)(2,1)S(1)} collective-permute-done((bf16[128,128]{1,0:T(8,128)(2,1)S(1)}, bf16[128,128]{1,0:T(8,128)(2,1)S(1)}, u32[]{:S(2)}, u32[]{:S(2)}) %collective-permute-start.14) | collective-permute-done | bytes 32800 | tf_op jit(solution)/shard_map/ppermute | solution.py:38
  51.5 0.9 %shard_map.87 = (f32[32,128]{1,0:T(8,128)S(1)}, f32[32,128]{1,0:T(8,128)S(1)}, f32[32,128]{1,0:T(8,128)S(1)}, f32[32,128]{1,0:T(8,128)S(1)}) custom-call(bf16[128,128]{1,0:T(8,128)(2,1)S(1)} %add_convert_fusion.refs_0_, bf16[128,128]{1,0:T(8,128)(2,1)S(1)} %collective-permute-done.12.refs_1_, bf16[128,128]{1,0:T(8,128)(2,1)S(1)} %collective-permute-done.13.refs_2_, ...), custom_call_target="tpu_custom_call" | custom-call | bytes 4194304 | tf_op jit(solution)/shard_map/pallas_call | solution.py:297
  52.5 1.7 %collective-permute-start.16 = (f32[32,128]{1,0:T(8,128)S(1)}, f32[32,128]{1,0:T(8,128)S(1)}, u32[]{:S(2)}, u32[]{:S(2)}) collective-permute-start(f32[32,128]{1,0:T(8,128)S(1)} %get-tuple-element.45), channel_id=1, source_target_pairs={{0,2},{1,3},{2,0},{3,1},{4,6},{5,7},{6,4},{7,5},{8,10},{9,11},{10,... | collective-permute-start | bytes 49160 | tf_op jit(solution)/shard_map/ppermute | solution.py:38
  54.2 2.7 %collective-permute-start.17 = (f32[32,128]{1,0:T(8,128)S(1)}, f32[32,128]{1,0:T(8,128)S(1)}, u32[]{:S(2)}, u32[]{:S(2)}) collective-permute-start(f32[32,128]{1,0:T(8,128)S(1)} %get-tuple-element.46), channel_id=1, source_target_pairs={{0,3},{1,2},{2,1},{3,0},{4,7},{5,6},{6,5},{7,4},{8,11},{9,10},{10,... | collective-permute-start | bytes 49160 | tf_op jit(solution)/shard_map/ppermute | solution.py:38
  56.9 0.3 collective-permute-done.16
  57.2 2.5 %collective-permute-done.17 = f32[32,128]{1,0:T(8,128)S(1)} collective-permute-done((f32[32,128]{1,0:T(8,128)S(1)}, f32[32,128]{1,0:T(8,128)S(1)}, u32[]{:S(2)}, u32[]{:S(2)}) %collective-permute-start.17) | collective-permute-done | bytes 16416 | tf_op jit(solution)/shard_map/ppermute | solution.py:38
  59.7 0.9 %collective-permute-start.19 = (f32[32,128]{1,0:T(8,128)S(1)}, f32[32,128]{1,0:T(8,128)S(1)}, u32[]{:S(2)}, u32[]{:S(2)}) collective-permute-start(f32[32,128]{1,0:T(8,128)S(1)} %add_add_fusion), channel_id=1, source_target_pairs={{0,8},{4,12},{8,0},{12,4},{1,9},{5,13},{9,1},{13,5},{2,10},{6,14},... | collective-permute-start | bytes 49160 | tf_op jit(solution)/shard_map/ppermute | solution.py:38
  60.7 0.9 %collective-permute-start.20 = (f32[32,128]{1,0:T(8,128)S(1)}, f32[32,128]{1,0:T(8,128)S(1)}, u32[]{:S(2)}, u32[]{:S(2)}) collective-permute-start(f32[32,128]{1,0:T(8,128)S(1)} %add_add_fusion), channel_id=1, source_target_pairs={{0,12},{4,8},{8,4},{12,0},{1,13},{5,9},{9,5},{13,1},{2,14},{6,10},... | collective-permute-start | bytes 49160 | tf_op jit(solution)/shard_map/ppermute | solution.py:38
  61.6 1.9 %collective-permute-done.19 = f32[32,128]{1,0:T(8,128)S(1)} collective-permute-done((f32[32,128]{1,0:T(8,128)S(1)}, f32[32,128]{1,0:T(8,128)S(1)}, u32[]{:S(2)}, u32[]{:S(2)}) %collective-permute-start.19) | collective-permute-done | bytes 16416 | tf_op jit(solution)/shard_map/ppermute | solution.py:38
  63.5 0.3 collective-permute-done.20
  63.8 0.6 add_bitcast_fusion
  (23 shorter events, 0.2 us)
Async XLA Ops:
  0.0 8.9 %collective-permute-start.6 = (bf16[32,3072]{1,0:T(8,128)(2,1)}, bf16[32,3072]{1,0:T(8,128)(2,1)S(1)}, u32[]{:S(2)}, u32[]{:S(2)}) collective-permute-start(bf16[32,3072]{1,0:T(8,128)(2,1)} %inw_hbm.1), channel_id=1, source_target_pairs={{0,8},{4,12},{8,0},{12,4},{1,9},{5,13},{9,1},{13,5},{2,10},{6,14},... | collective-permute-start | bytes 589832 | tf_op jit(solution)/shard_map/ppermute | solution.py:38
  3.0 9.3 %collective-permute-start = (bf16[768,128]{1,0:T(8,128)(2,1)}, bf16[768,128]{1,0:T(8,128)(2,1)S(1)}, u32[]{:S(2)}, u32[]{:S(2)}) collective-permute-start(bf16[768,128]{1,0:T(8,128)(2,1)} %refs_0_.1), channel_id=1, source_target_pairs={{0,8},{4,12},{8,0},{12,4},{1,9},{5,13},{9,1},{13,5},{2,10},{6,14},... | collective-permute-start | bytes 589832 | tf_op jit(solution)/shard_map/ppermute | solution.py:38
  3.0 27.9 %collective-permute-start.5 = (bf16[32,3072]{1,0:T(8,128)(2,1)}, bf16[32,3072]{1,0:T(8,128)(2,1)S(1)}, u32[]{:S(2)}, u32[]{:S(2)}) collective-permute-start(bf16[32,3072]{1,0:T(8,128)(2,1)} %inw_hbm.1), channel_id=1, source_target_pairs={{0,4},{4,0},{8,12},{12,8},{1,5},{5,1},{9,13},{13,9},{2,6},{6,2},{1... | collective-permute-start | bytes 589832 | tf_op jit(solution)/shard_map/ppermute | solution.py:38
  8.9 22.0 %collective-permute-start.7 = (bf16[32,3072]{1,0:T(8,128)(2,1)S(1)}, bf16[32,3072]{1,0:T(8,128)(2,1)S(1)}, u32[]{:S(2)}, u32[]{:S(2)}) collective-permute-start(bf16[32,3072]{1,0:T(8,128)(2,1)S(1)} %collective-permute-done.6.refs_6_), channel_id=1, source_target_pairs={{0,4},{4,0},{8,12},{12,8},{1,5},{5,1},{9,13},{13,9},{2,6},{6,2},{1... | collective-permute-start | bytes 589832 | tf_op jit(solution)/shard_map/ppermute | solution.py:38
  8.9 26.3 %collective-permute-start.8 = (bf16[768,128]{1,0:T(8,128)(2,1)}, bf16[768,128]{1,0:T(8,128)(2,1)S(1)}, u32[]{:S(2)}, u32[]{:S(2)}) collective-permute-start(bf16[768,128]{1,0:T(8,128)(2,1)} %refs_0_.1), channel_id=1, source_target_pairs={{0,4},{4,0},{8,12},{12,8},{1,5},{5,1},{9,13},{13,9},{2,6},{6,2},{1... | collective-permute-start | bytes 589832 | tf_op jit(solution)/shard_map/ppermute | solution.py:38
  12.3 24.5 %collective-permute-start.1 = (bf16[768,128]{1,0:T(8,128)(2,1)S(1)}, bf16[768,128]{1,0:T(8,128)(2,1)S(1)}, u32[]{:S(2)}, u32[]{:S(2)}) collective-permute-start(bf16[768,128]{1,0:T(8,128)(2,1)S(1)} %collective-permute-done.refs_2_), channel_id=1, source_target_pairs={{0,4},{4,0},{8,12},{12,8},{1,5},{5,1},{9,13},{13,9},{2,6},{6,2},{1... | collective-permute-start | bytes 589832 | tf_op jit(solution)/shard_map/ppermute | solution.py:38
  15.2 3.9 %collective-permute-start.2 = (f32[50,128]{1,0:T(8,128)S(1)}, f32[50,128]{1,0:T(8,128)S(1)}, u32[]{:S(2)}, u32[]{:S(2)}) collective-permute-start(f32[50,128]{1,0:T(8,128)S(1)} %get-tuple-element.27.refs_0_), channel_id=1, source_target_pairs={{0,1},{1,0},{2,3},{3,2},{4,5},{5,4},{6,7},{7,6},{8,9},{9,8},{10,11... | collective-permute-start | bytes 76808 | tf_op jit(solution)/shard_map/ppermute | solution.py:38
  19.1 4.8 %collective-permute-start.3 = (f32[50,128]{1,0:T(8,128)S(1)}, f32[50,128]{1,0:T(8,128)S(1)}, u32[]{:S(2)}, u32[]{:S(2)}) collective-permute-start(f32[50,128]{1,0:T(8,128)S(1)} %get-tuple-element.27.refs_0_), channel_id=1, source_target_pairs={{0,2},{1,3},{2,0},{3,1},{4,6},{5,7},{6,4},{7,5},{8,10},{9,11},{10,... | collective-permute-start | bytes 76808 | tf_op jit(solution)/shard_map/ppermute | solution.py:38
  23.9 7.0 %collective-permute-start.4 = (f32[50,128]{1,0:T(8,128)S(1)}, f32[50,128]{1,0:T(8,128)S(1)}, u32[]{:S(2)}, u32[]{:S(2)}) collective-permute-start(f32[50,128]{1,0:T(8,128)S(1)} %get-tuple-element.27.refs_0_), channel_id=1, source_target_pairs={{0,3},{1,2},{2,1},{3,0},{4,7},{5,6},{6,5},{7,4},{8,11},{9,10},{10,... | collective-permute-start | bytes 76808 | tf_op jit(solution)/shard_map/ppermute | solution.py:38
  30.9 4.3 %copy-start = (bf16[768,128]{1,0:T(8,128)(2,1)S(1)}, bf16[768,128]{1,0:T(8,128)(2,1)}, u32[]{:S(2)}) copy-start(bf16[768,128]{1,0:T(8,128)(2,1)} %refs_0_.1) | copy-start | bytes 589828
  36.8 27.1 %copy-start.1 = (f32[32,128]{1,0:T(8,128)S(1)}, f32[32,128]{1,0:T(8,128)}, u32[]{:S(2)}) copy-start(f32[32,128]{1,0:T(8,128)} %start_hbm.1) | copy-start | bytes 49156
  37.5 4.0 %collective-permute-start.10 = (bf16[128,128]{1,0:T(8,128)(2,1)S(1)}, bf16[128,128]{1,0:T(8,128)(2,1)S(1)}, u32[]{:S(2)}, u32[]{:S(2)}) collective-permute-start(bf16[128,128]{1,0:T(8,128)(2,1)S(1)} %get-tuple-element.40), channel_id=1, source_target_pairs={{0,8},{4,12},{8,0},{12,4},{1,9},{5,13},{9,1},{13,5},{2,10},{6,14},... | collective-permute-start | bytes 98312 | tf_op jit(solution)/shard_map/ppermute | solution.py:38
  39.1 3.3 %collective-permute-start.11 = (bf16[128,128]{1,0:T(8,128)(2,1)S(1)}, bf16[128,128]{1,0:T(8,128)(2,1)S(1)}, u32[]{:S(2)}, u32[]{:S(2)}) collective-permute-start(bf16[128,128]{1,0:T(8,128)(2,1)S(1)} %get-tuple-element.40), channel_id=1, source_target_pairs={{0,12},{4,8},{8,4},{12,0},{1,13},{5,9},{9,5},{13,1},{2,14},{6,10},... | collective-permute-start | bytes 98312 | tf_op jit(solution)/shard_map/ppermute | solution.py:38
  39.1 3.3 %collective-permute-start.9 = (bf16[128,128]{1,0:T(8,128)(2,1)S(1)}, bf16[128,128]{1,0:T(8,128)(2,1)S(1)}, u32[]{:S(2)}, u32[]{:S(2)}) collective-permute-start(bf16[128,128]{1,0:T(8,128)(2,1)S(1)} %get-tuple-element.40), channel_id=1, source_target_pairs={{0,4},{4,0},{8,12},{12,8},{1,5},{5,1},{9,13},{13,9},{2,6},{6,2},{1... | collective-permute-start | bytes 98312 | tf_op jit(solution)/shard_map/ppermute | solution.py:38
  42.5 4.5 %collective-permute-start.12 = (bf16[128,128]{1,0:T(8,128)(2,1)S(1)}, bf16[128,128]{1,0:T(8,128)(2,1)S(1)}, u32[]{:S(2)}, u32[]{:S(2)}) collective-permute-start(bf16[128,128]{1,0:T(8,128)(2,1)S(1)} %add_convert_fusion.refs_0_), channel_id=1, source_target_pairs={{0,1},{1,0},{2,3},{3,2},{4,5},{5,4},{6,7},{7,6},{8,9},{9,8},{10,11... | collective-permute-start | bytes 98312 | tf_op jit(solution)/shard_map/ppermute | solution.py:38
  42.5 5.2 %collective-permute-start.13 = (bf16[128,128]{1,0:T(8,128)(2,1)S(1)}, bf16[128,128]{1,0:T(8,128)(2,1)S(1)}, u32[]{:S(2)}, u32[]{:S(2)}) collective-permute-start(bf16[128,128]{1,0:T(8,128)(2,1)S(1)} %add_convert_fusion.refs_0_), channel_id=1, source_target_pairs={{0,2},{1,3},{2,0},{3,1},{4,6},{5,7},{6,4},{7,5},{8,10},{9,11},{10,... | collective-permute-start | bytes 98312 | tf_op jit(solution)/shard_map/ppermute | solution.py:38
  45.8 5.7 %collective-permute-start.14 = (bf16[128,128]{1,0:T(8,128)(2,1)S(1)}, bf16[128,128]{1,0:T(8,128)(2,1)S(1)}, u32[]{:S(2)}, u32[]{:S(2)}) collective-permute-start(bf16[128,128]{1,0:T(8,128)(2,1)S(1)} %add_convert_fusion.refs_0_), channel_id=1, source_target_pairs={{0,3},{1,2},{2,1},{3,0},{4,7},{5,6},{6,5},{7,4},{8,11},{9,10},{10,... | collective-permute-start | bytes 98312 | tf_op jit(solution)/shard_map/ppermute | solution.py:38
  52.4 4.5 %collective-permute-start.15 = (f32[32,128]{1,0:T(8,128)S(1)}, f32[32,128]{1,0:T(8,128)S(1)}, u32[]{:S(2)}, u32[]{:S(2)}) collective-permute-start(f32[32,128]{1,0:T(8,128)S(1)} %get-tuple-element.44), channel_id=1, source_target_pairs={{0,1},{1,0},{2,3},{3,2},{4,5},{5,4},{6,7},{7,6},{8,9},{9,8},{10,11... | collective-permute-start | bytes 49160 | tf_op jit(solution)/shard_map/ppermute | solution.py:38
  52.5 4.7 %collective-permute-start.16 = (f32[32,128]{1,0:T(8,128)S(1)}, f32[32,128]{1,0:T(8,128)S(1)}, u32[]{:S(2)}, u32[]{:S(2)}) collective-permute-start(f32[32,128]{1,0:T(8,128)S(1)} %get-tuple-element.45), channel_id=1, source_target_pairs={{0,2},{1,3},{2,0},{3,1},{4,6},{5,7},{6,4},{7,5},{8,10},{9,11},{10,... | collective-permute-start | bytes 49160 | tf_op jit(solution)/shard_map/ppermute | solution.py:38
  54.2 5.5 %collective-permute-start.17 = (f32[32,128]{1,0:T(8,128)S(1)}, f32[32,128]{1,0:T(8,128)S(1)}, u32[]{:S(2)}, u32[]{:S(2)}) collective-permute-start(f32[32,128]{1,0:T(8,128)S(1)} %get-tuple-element.46), channel_id=1, source_target_pairs={{0,3},{1,2},{2,1},{3,0},{4,7},{5,6},{6,5},{7,4},{8,11},{9,10},{10,... | collective-permute-start | bytes 49160 | tf_op jit(solution)/shard_map/ppermute | solution.py:38
  59.7 1.9 %collective-permute-start.18 = (f32[32,128]{1,0:T(8,128)S(1)}, f32[32,128]{1,0:T(8,128)S(1)}, u32[]{:S(2)}, u32[]{:S(2)}) collective-permute-start(f32[32,128]{1,0:T(8,128)S(1)} %add_add_fusion), channel_id=1, source_target_pairs={{0,4},{4,0},{8,12},{12,8},{1,5},{5,1},{9,13},{13,9},{2,6},{6,2},{1... | collective-permute-start | bytes 49160 | tf_op jit(solution)/shard_map/ppermute | solution.py:38
  59.7 3.8 %collective-permute-start.19 = (f32[32,128]{1,0:T(8,128)S(1)}, f32[32,128]{1,0:T(8,128)S(1)}, u32[]{:S(2)}, u32[]{:S(2)}) collective-permute-start(f32[32,128]{1,0:T(8,128)S(1)} %add_add_fusion), channel_id=1, source_target_pairs={{0,8},{4,12},{8,0},{12,4},{1,9},{5,13},{9,1},{13,5},{2,10},{6,14},... | collective-permute-start | bytes 49160 | tf_op jit(solution)/shard_map/ppermute | solution.py:38
  60.7 3.2 %collective-permute-start.20 = (f32[32,128]{1,0:T(8,128)S(1)}, f32[32,128]{1,0:T(8,128)S(1)}, u32[]{:S(2)}, u32[]{:S(2)}) collective-permute-start(f32[32,128]{1,0:T(8,128)S(1)} %add_add_fusion), channel_id=1, source_target_pairs={{0,12},{4,8},{8,4},{12,0},{1,13},{5,9},{9,5},{13,1},{2,14},{6,10},... | collective-permute-start | bytes 49160 | tf_op jit(solution)/shard_map/ppermute | solution.py:38

commit v6 on v5

--- a/solution.py
+++ b/solution.py
@@ -17,6 +17,7 @@
 F32 = jnp.float32
 BF16 = jnp.bfloat16
 VMEM = pl.BlockSpec(memory_space=pltpu.VMEM)
+SMEM = pl.BlockSpec(memory_space=pltpu.SMEM)
 HBM = pl.BlockSpec(memory_space=pltpu.HBM)
 
 
@@ -87,9 +88,7 @@
         copy.wait()
 
 
-def modulation_kernel(
-    time_ref, weight_step_ref, weight_hbm, start_hbm, out_ref, step_ref, weight_ref, start_ref, sems
-):
+def modulation_kernel(time_ref, weight_hbm, start_hbm, out_ref, weight_ref, start_ref, sems):
     rows = start_ref.shape[0]
     half = weight_ref.shape[0] // 2
     pairs = ((weight_hbm, weight_ref), (start_hbm, start_ref))
@@ -97,12 +96,8 @@
         [pltpu.make_async_copy(a, b, sems.at[i]) for i, (a, b) in enumerate(pairs)]
     )
     index = lax.broadcasted_iota(jnp.int32, (16, half), 1).astype(F32)
-    frequency = jnp.exp(-math.log(10000.0) * index / half)
-    time = jnp.broadcast_to(time_ref[...].astype(F32), frequency.shape)
-    angles = time * frequency
+    angles = time_ref[0].astype(F32) * jnp.exp(-math.log(10000.0) * index / half)
     embedding = jnp.concatenate([jnp.cos(angles), jnp.sin(angles)], axis=1).astype(BF16)
-    step = weight_step_ref[...].astype(F32) * (1.0 / STEP_DIVISOR)
-    step_ref[...] = jnp.broadcast_to(step, step_ref.shape)
     wait_copies(copies)
     result = bdot(embedding, weight_ref[...])
     out_ref[0:rows, :] = start_ref[...]
@@ -110,16 +105,16 @@
         out_ref[rows + r : rows + r + 1, :] = result[0:1, r * LANES : (r + 1) * LANES]
 
 
-def load_kernel(qkv_hbm, inw_hbm, qkv_ref, inw_ref, sems):
+def load_kernel(weight_ref, qkv_hbm, inw_hbm, qkv_ref, inw_ref, step_ref, sems):
     cols = qkv_ref.shape[1]
-    wait_copies(
-        run_copies(
-            [
-                pltpu.make_async_copy(inw_hbm, inw_ref, sems.at[0]),
-                pltpu.make_async_copy(qkv_hbm.at[:, pl.ds(0, cols)], qkv_ref, sems.at[1]),
-            ]
-        )
-    )
+    copies = run_copies(
+        [
+            pltpu.make_async_copy(inw_hbm, inw_ref, sems.at[0]),
+            pltpu.make_async_copy(qkv_hbm.at[:, pl.ds(0, cols)], qkv_ref, sems.at[1]),
+        ]
+    )
+    step_ref[...] = jnp.full(step_ref.shape, weight_ref[0].astype(F32) * (1.0 / STEP_DIVISOR))
+    wait_copies(copies)
 
 
 def attend(x, factors, base, gram, head_count):
@@ -145,7 +140,7 @@
     inws, refs = refs[:nm], refs[nm:]
     near_ref, qkv_hbm, out_w_hbm, refs = refs[0], refs[1], refs[2], refs[3:]
     factor_ref, base_ref, gram_ref, start_ref, inw_ref, gate_ref, out_w_ref = refs[:7]
-    start_s, mod_s, gate_s, z_s, qkv_s, sems = refs[7:]
+    start_s, mod_s, z_s, qkv_s, sems = refs[7:]
     near = near_ref.shape[1] // block
     count = factor_ref.shape[1] // block
     copies = run_copies(
@@ -179,16 +174,29 @@
     for c in range(chunks):
         total = total + columns(c, 1).astype(F32)
     mean = jnp.sum(total, axis=1, keepdims=True) * (1.0 / width)
-    for c in range(chunks):
-        cols = slice(c * LANES, (c + 1) * LANES)
-        centered = columns(c, 1).astype(F32) - mean
-        z_s[0:channels, cols] = (centered * (1.0 + mod_row(chunks + c))).astype(BF16)
-        z_s[channels : channels + 16, cols] = jnp.broadcast_to(mod_row(c), (16, LANES)).astype(BF16)
-        gate_s[c // (chunks // nm), c % (chunks // nm) : c % (chunks // nm) + 1, :] = mod_row(
-            2 * chunks + c
-        )
+    first = jnp.zeros((channels + 16, block), F32)
+    group = 6
+    for g in range(0, chunks, group):
+        for c in range(g, g + group):
+            cols = slice(c * LANES, (c + 1) * LANES)
+            centered = columns(c, 1).astype(F32) - mean
+            z_s[0:channels, cols] = (centered * (1.0 + mod_row(chunks + c))).astype(BF16)
+            shift = jnp.broadcast_to(mod_row(c), (16, LANES)).astype(BF16)
+            z_s[channels : channels + 16, cols] = shift
+        cols = slice(g * LANES, (g + group) * LANES)
+        first = first + bdot(z_s[:, cols], near_ref[cols, 0:block])
+
+    def keep(result, n):
+        at = slice(n * block, (n + 1) * block)
+        high, low = split_terms(result[0:channels], 2)
+        factor_ref[0:channels, at] = high
+        factor_ref[channels : 2 * channels, at] = low
+        base_ref[:, at] = result[channels : channels + 8]
+
+    keep(first, 0)
     for p in range(nm):
-        gate_ref[p] = gate_s[p].T
+        for r in range(chunks // nm):
+            gate_ref[p, r : r + 1, :] = mod_row(2 * chunks + p * (chunks // nm) + r)
     gram = jnp.zeros((channels, channels), F32)
     for c in range(0, chunks, 6):
         gram = gram + bdot_t(columns(c, 6), columns(c, 6))
@@ -198,33 +206,28 @@
         gram_ref[i * channels : (i + 1) * channels, :] = piece
     start_ref[...] = start_s[...].reshape(start_ref.shape)
 
-    for n in range(count):
-        at = slice(n * block, (n + 1) * block)
+    for n in range(1, count):
         if n < near:
-            weight = near_ref[:, at]
+            weight = near_ref[:, n * block : (n + 1) * block]
         else:
             copies[n - near].wait()
             weight = qkv_s[:, (n - near) * block : (n - near + 1) * block]
-        result = bdot(z_s[...], weight)
-        high, low = split_terms(result[0:channels], 2)
-        factor_ref[0:channels, at] = high
-        factor_ref[channels : 2 * channels, at] = low
-        base_ref[:, at] = result[channels : channels + 8]
+        keep(bdot(z_s[...], weight), n)
     copies[count - near].wait()
 
 
 def fold_parts(nm, first, heads, gate_ref, out_w_ref, inw_ref):
     folded, resid = 0.0, 0.0
     for i, head_ref in enumerate(heads):
-        size, _ = head_ref.shape
+        size = head_ref.shape[0]
         at = place("tm", nm, first + i)
         cols = pl.ds(pl.multiple_of(at * size, LANES), size)
         gate = gate_ref[at]
         gated = []
         for r in range(size // LANES):
-            rows = head_ref[r * LANES : (r + 1) * LANES, :].astype(F32)
-            gated.append((rows * gate[:, r : r + 1]).astype(BF16))
-        folded = folded + bdot(out_w_ref[:, cols], jnp.concatenate(gated, axis=0))
+            turned = head_ref[r * LANES : (r + 1) * LANES, :].astype(F32).T
+            gated.append((turned * gate[r : r + 1, :]).astype(BF16))
+        folded = folded + bdot_t(jnp.concatenate(gated, axis=1), out_w_ref[:, cols])
         inw = inw_ref[:, :, cols].reshape(-1, size)
         resid = resid + bdot(inw, head_ref[...])
     return folded, resid
@@ -259,7 +262,7 @@
     for i, term in enumerate(split_terms(resid, 2)):
         resid_ref[i * channels : (i + 1) * channels, :] = term
     x = start_ref[...].astype(BF16)
-    vel = bdot(att_ref[...], folded)
+    vel = bdot_t(att_ref[...], folded)
     residual = bdot(jnp.concatenate([x, x], axis=1), resid_ref[...])
     vel_ref[...] = (add_own_rows(vel, residual, rows) * step_ref[0:1, :]).astype(vel_ref.dtype)
 
@@ -274,7 +277,7 @@
         guess = guess + part[...].astype(F32)
     x = guess.astype(BF16)
     attended = attend(x, factor_ref, base_ref, gram_ref, head_count)
-    vel = bdot(attended, fold_ref[...])
+    vel = bdot_t(attended, fold_ref[...])
     residual = bdot(jnp.concatenate([x, x], axis=1), resid_ref[...])
     vel = add_own_rows(vel, residual, rows) * step_ref[0:1, :]
     if not split:
@@ -345,24 +348,22 @@
     small = is_small("tensor") and mod_weight.shape[1] % LANES == 0
     if small:
         mod_rows = mod_weight.shape[1] // LANES
-        message, step = call(
+        message = call(
             modulation_kernel,
-            [shape_of((rows + mod_rows, LANES), F32), shape_of((8, LANES), F32)],
-            [VMEM, VMEM, HBM, HBM],
+            [shape_of((rows + mod_rows, LANES), F32)],
+            [SMEM, HBM, HBM],
             [
                 pltpu.VMEM(mod_weight.shape, BF16),
                 pltpu.VMEM(start_latent.shape, F32),
                 pltpu.SemaphoreType.DMA((2,)),
             ],
-            time_index.reshape(1, 1),
-            step_weight.reshape(1, 1),
+            time_index,
             mod_weight,
             start_latent,
-        )
+        )[0]
         messages = gather_parts(message, "tensor")
         block_rows = rows
     else:
-        step = jnp.full((8, LANES), step_weight[0].astype(F32) / STEP_DIVISOR)
         embedding = embedding_of(time_index, mod_weight.shape[0]).astype(BF16)
         mod_part = jnp.dot(embedding, mod_weight, preferred_element_type=F32)
         modulation = lax.all_gather(mod_part, "tensor", axis=1, tiled=True)
@@ -375,13 +376,18 @@
     span_cols = qkv_weight.shape[1]
     gate_rows = -(-(chunks // nm) // 8) * 8
     block = 4 * LANES if span_cols % (4 * LANES) == 0 else span_cols
-    near = max(1, span_cols // block * 2 // 3)
+    near = max(1, span_cols // block // 3)
     far = max(1, span_cols // block - near)
-    qkv_near, inw_parts[0] = call(
+    qkv_near, inw_parts[0], step = call(
         load_kernel,
-        [shape_of((width, near * block), BF16), shape_of(inw_parts[0].shape, BF16)],
-        [HBM, HBM],
+        [
+            shape_of((width, near * block), BF16),
+            shape_of(inw_parts[0].shape, BF16),
+            shape_of((8, LANES), F32),
+        ],
+        [SMEM, HBM, HBM],
         [pltpu.SemaphoreType.DMA((2,))],
+        step_weight,
         qkv_weight,
         inw_parts[0],
     )
@@ -393,14 +399,13 @@
             shape_of((3 * channels, channels), BF16),
             shape_of((tokens, channels), F32),
             shape_of((nm, channels // nm, width), BF16),
-            shape_of((nm, LANES, gate_rows), F32),
+            shape_of((nm, gate_rows, LANES), F32),
             shape_of(out_weight.shape, BF16),
         ],
         [VMEM] * (nt + nm + 1) + [HBM, HBM],
         [
             pltpu.VMEM((nt, block_rows, channels), F32),
             pltpu.VMEM((nt, padded, LANES), F32),
-            pltpu.VMEM((nm, gate_rows, LANES), F32),
             pltpu.VMEM((channels + 16, width), BF16),
             pltpu.VMEM((width, far * block), BF16),
             pltpu.SemaphoreType.DMA((far + 1,)),
@@ -419,7 +424,7 @@
         functools.partial(attend_kernel, nm, early, head_count),
         [
             shape_of((tokens, head_count * HD), BF16),
-            shape_of((span, channels), F32),
+            shape_of((channels, span), F32),
             shape_of((channels, channels), F32),
         ],
         [VMEM] * (early + 7),
@@ -437,7 +442,7 @@
     folded, resid, vel = call(
         functools.partial(fold_kernel, nm, late, rows),
         [
-            shape_of((span, channels), BF16),
+            shape_of((channels, span), BF16),
             shape_of((2 * channels, channels), BF16),
             shape_of((tokens, channels), BF16),
         ],

time: 64.6 us -> 63.6 us (0.985)
  Pallas kernels: 12 us -> 10.9 us
    pallas_call x6, Pallas kernels: 12 us -> 10.9 us  [call(): pl.pallas_call(kernel, out_shape=outs, in_specs=in_specs, out_specs=[VMEM...]
  transfers between devices with their start and end apart: 21 -> 21, of which waited for: 12 -> 12; matrix products, arithmetic and copies ran while one was open for 0% -> 0% of each run, Pallas kernels for 16% -> 15%
where the time goes in v6:
time: 63.6 us; the launch traced here: 63.4 us
  starting transfers between devices  25.2 us (40%)
  waiting for transfers between devices  25.1 us (39%)
  Pallas kernels  10.9 us (17%)
  between operations  1.46 us (2%)
  other arithmetic  0.65 us (1%)
    ppermute x21, starting transfers between devices, swap(): return lax.ppermute(value, axis, [(i, i ^ k) for i in range(n)])  25.2 us
    ppermute x21, waiting for transfers between devices, swap(): return lax.ppermute(value, axis, [(i, i ^ k) for i in range(n)])  25.1 us
    pallas_call x6, Pallas kernels, call(): pl.pallas_call(kernel, out_shape=outs, in_specs=in_specs, out_specs=[VMEM...  10.9 us
  transfers between devices with their start and end apart: 21, of which 12 were waited for; matrix products, arithmetic and copies ran while one was open for 0% of the time, Pallas kernels for 15%

profile of v6, /device:TPU:0, one launch (start us, length us, event | category | flops | bytes accessed | tf_op | source)
XLA Modules:
  0.0 63.4 jit_solution(4347148148020715840)
XLA Ops:
  0.0 3.0 %collective-permute-start.6 = (bf16[32,3072]{1,0:T(8,128)(2,1)}, bf16[32,3072]{1,0:T(8,128)(2,1)S(1)}, u32[]{:S(2)}, u32[]{:S(2)}) collective-permute-start(bf16[32,3072]{1,0:T(8,128)(2,1)} %inw_hbm.1), channel_id=1, source_target_pairs={{0,8},{4,12},{8,0},{12,4},{1,9},{5,13},{9,1},{13,5},{2,10},{6,14},... | collective-permute-start | bytes 589832 | tf_op jit(solution)/shard_map/ppermute | solution.py:39
  3.0 5.9 %collective-permute-done.6.refs_6_ = bf16[32,3072]{1,0:T(8,128)(2,1)S(1)} collective-permute-done((bf16[32,3072]{1,0:T(8,128)(2,1)}, bf16[32,3072]{1,0:T(8,128)(2,1)S(1)}, u32[]{:S(2)}, u32[]{:S(2)}) %collective-permute-start.6) | collective-permute-done | bytes 196640 | tf_op jit(solution)/shard_map/ppermute | solution.py:39
  8.9 0.5 collective-permute-start.8
  9.4 2.9 %collective-permute-done.refs_2_ = bf16[768,128]{1,0:T(8,128)(2,1)S(1)} collective-permute-done((bf16[768,128]{1,0:T(8,128)(2,1)}, bf16[768,128]{1,0:T(8,128)(2,1)S(1)}, u32[]{:S(2)}, u32[]{:S(2)}) %collective-permute-start) | collective-permute-done | bytes 196640 | tf_op jit(solution)/shard_map/ppermute | solution.py:39
  12.9 1.6 %shard_map.83.refs_0_ = f32[50,128]{1,0:T(8,128)S(1)} custom-call(s32[1]{0:T(128)S(6)} %copy.9.time_ref, bf16[256,2304]{1,0:T(8,128)(2,1)} %weight_hbm.1, f32[32,128]{1,0:T(8,128)} %start_hbm.1), custom_call_target="tpu_custom_call" | custom-call | bytes 4194304 | tf_op jit(solution)/shard_map/pallas_call | solution.py:300
  14.5 1.9 %collective-permute-start.2 = (f32[50,128]{1,0:T(8,128)S(1)}, f32[50,128]{1,0:T(8,128)S(1)}, u32[]{:S(2)}, u32[]{:S(2)}) collective-permute-start(f32[50,128]{1,0:T(8,128)S(1)} %shard_map.83.refs_0_), channel_id=1, source_target_pairs={{0,1},{1,0},{2,3},{3,2},{4,5},{5,4},{6,7},{7,6},{8,9},{9,8},{10,11... | collective-permute-start | bytes 76808 | tf_op jit(solution)/shard_map/ppermute | solution.py:39
  16.4 2.0 %collective-permute-done.2.refs_1_ = f32[50,128]{1,0:T(8,128)S(1)} collective-permute-done((f32[50,128]{1,0:T(8,128)S(1)}, f32[50,128]{1,0:T(8,128)S(1)}, u32[]{:S(2)}, u32[]{:S(2)}) %collective-permute-start.2) | collective-permute-done | bytes 25632 | tf_op jit(solution)/shard_map/ppermute | solution.py:39
  18.5 2.8 %collective-permute-start.3 = (f32[50,128]{1,0:T(8,128)S(1)}, f32[50,128]{1,0:T(8,128)S(1)}, u32[]{:S(2)}, u32[]{:S(2)}) collective-permute-start(f32[50,128]{1,0:T(8,128)S(1)} %shard_map.83.refs_0_), channel_id=1, source_target_pairs={{0,2},{1,3},{2,0},{3,1},{4,6},{5,7},{6,4},{7,5},{8,10},{9,11},{10,... | collective-permute-start | bytes 76808 | tf_op jit(solution)/shard_map/ppermute | solution.py:39
  21.3 1.9 %collective-permute-done.3.refs_2_ = f32[50,128]{1,0:T(8,128)S(1)} collective-permute-done((f32[50,128]{1,0:T(8,128)S(1)}, f32[50,128]{1,0:T(8,128)S(1)}, u32[]{:S(2)}, u32[]{:S(2)}) %collective-permute-start.3) | collective-permute-done | bytes 25632 | tf_op jit(solution)/shard_map/ppermute | solution.py:39
  23.2 4.0 %collective-permute-start.4 = (f32[50,128]{1,0:T(8,128)S(1)}, f32[50,128]{1,0:T(8,128)S(1)}, u32[]{:S(2)}, u32[]{:S(2)}) collective-permute-start(f32[50,128]{1,0:T(8,128)S(1)} %shard_map.83.refs_0_), channel_id=1, source_target_pairs={{0,3},{1,2},{2,1},{3,0},{4,7},{5,6},{6,5},{7,4},{8,11},{9,10},{10,... | collective-permute-start | bytes 76808 | tf_op jit(solution)/shard_map/ppermute | solution.py:39
  27.9 2.0 %shard_map.82 = (bf16[3072,512]{1,0:T(8,128)(2,1)S(1)}, bf16[32,3072]{1,0:T(8,128)(2,1)S(1)}, f32[8,128]{1,0:T(8,128)S(1)}) custom-call(s32[1]{0:T(128)S(6)} %copy.10.weight_ref, bf16[3072,1536]{1,0:T(8,128)(2,1)} %refs_9_.1, bf16[32,3072]{1,0:T(8,128)(2,1)} %inw_hbm.1), custom_call_target="tpu_custom_call" | custom-call | bytes 4194304 | tf_op jit(solution)/shard_map/pallas_call | solution.py:300
  30.0 4.0 %shard_map.84 = (bf16[256,1536]{1,0:T(8,128)(2,1)S(1)}, f32[8,1536]{1,0:T(8,128)S(1)}, bf16[384,128]{1,0:T(8,128)(2,1)S(1)}, f32[128,128]{1,0:T(8,128)S(1)}, bf1...) custom-call(f32[50,128]{1,0:T(8,128)S(1)} %shard_map.83.refs_0_, ...), custom_call_target="tpu_custom_call" | custom-call | bytes 4194304 | tf_op jit(solution)/shard_map/pallas_call | solution.py:300
  34.0 1.8 %shard_map.85 = (bf16[128,512]{1,0:T(8,128)(2,1)S(1)}, f32[128,512]{1,0:T(8,128)S(1)}, f32[128,128]{1,0:T(8,128)S(1)}) custom-call(bf16[768,128]{1,0:T(8,128)(2,1)S(1)} %copy-done, bf16[768,128]{1,0:T(8,128)(2,1)S(1)} %collective-permute-done.8.refs_1_, bf16[768,128]{1,0:T(8,128)(2,1)S(1)} %collective-permute-done.refs_2_, ...), custom_call_target="tpu_custom_call" | custom-call | bytes 4194304 | tf_op jit(solution)/shard_map/pallas_call | solution.py:300
  35.8 0.7 %shard_map.86 = (bf16[128,512]{1,0:T(8,128)(2,1)S(1)}, bf16[256,128]{1,0:T(8,128)(2,1)S(1)}, bf16[128,128]{1,0:T(8,128)(2,1)S(1)}) custom-call(bf16[768,128]{1,0:T(8,128)(2,1)S(1)} %collective-permute-done.1.refs_0_, f32[8,128]{1,0:T(8,128)S(1)} %get-tuple-element.25.refs_1_.refs_4_, f32[4,8,128]{2,1,0:T(8,128)S(1)} %get-tuple-element.28.refs_7_.refs_2_, ...), custom_call_target="tpu_custom_call" | custom-call | bytes 4194304 | tf_op jit(solution)/shard_map/pallas_call | solution.py:300
  36.5 1.6 %collective-permute-start.10 = (bf16[128,128]{1,0:T(8,128)(2,1)S(1)}, bf16[128,128]{1,0:T(8,128)(2,1)S(1)}, u32[]{:S(2)}, u32[]{:S(2)}) collective-permute-start(bf16[128,128]{1,0:T(8,128)(2,1)S(1)} %get-tuple-element.38), channel_id=1, source_target_pairs={{0,8},{4,12},{8,0},{12,4},{1,9},{5,13},{9,1},{13,5},{2,10},{6,14},... | collective-permute-start | bytes 98312 | tf_op jit(solution)/shard_map/ppermute | solution.py:39
  38.0 0.7 %collective-permute-start.9 = (bf16[128,128]{1,0:T(8,128)(2,1)S(1)}, bf16[128,128]{1,0:T(8,128)(2,1)S(1)}, u32[]{:S(2)}, u32[]{:S(2)}) collective-permute-start(bf16[128,128]{1,0:T(8,128)(2,1)S(1)} %get-tuple-element.38), channel_id=1, source_target_pairs={{0,4},{4,0},{8,12},{12,8},{1,5},{5,1},{9,13},{13,9},{2,6},{6,2},{1... | collective-permute-start | bytes 98312 | tf_op jit(solution)/shard_map/ppermute | solution.py:39
  38.7 1.8 %collective-permute-done.10 = bf16[128,128]{1,0:T(8,128)(2,1)S(1)} collective-permute-done((bf16[128,128]{1,0:T(8,128)(2,1)S(1)}, bf16[128,128]{1,0:T(8,128)(2,1)S(1)}, u32[]{:S(2)}, u32[]{:S(2)}) %collective-permute-start.10) | collective-permute-done | bytes 32800 | tf_op jit(solution)/shard_map/ppermute | solution.py:39
  40.5 0.9 %collective-permute-done.11 = bf16[128,128]{1,0:T(8,128)(2,1)S(1)} collective-permute-done((bf16[128,128]{1,0:T(8,128)(2,1)S(1)}, bf16[128,128]{1,0:T(8,128)(2,1)S(1)}, u32[]{:S(2)}, u32[]{:S(2)}) %collective-permute-start.11) | collective-permute-done | bytes 32800 | tf_op jit(solution)/shard_map/ppermute | solution.py:39
  41.5 3.5 %collective-permute-start.13 = (bf16[128,128]{1,0:T(8,128)(2,1)S(1)}, bf16[128,128]{1,0:T(8,128)(2,1)S(1)}, u32[]{:S(2)}, u32[]{:S(2)}) collective-permute-start(bf16[128,128]{1,0:T(8,128)(2,1)S(1)} %add_convert_fusion.refs_0_), channel_id=1, source_target_pairs={{0,2},{1,3},{2,0},{3,1},{4,6},{5,7},{6,4},{7,5},{8,10},{9,11},{10,... | collective-permute-start | bytes 98312 | tf_op jit(solution)/shard_map/ppermute | solution.py:39
  45.0 0.9 %collective-permute-start.14 = (bf16[128,128]{1,0:T(8,128)(2,1)S(1)}, bf16[128,128]{1,0:T(8,128)(2,1)S(1)}, u32[]{:S(2)}, u32[]{:S(2)}) collective-permute-start(bf16[128,128]{1,0:T(8,128)(2,1)S(1)} %add_convert_fusion.refs_0_), channel_id=1, source_target_pairs={{0,3},{1,2},{2,1},{3,0},{4,7},{5,6},{6,5},{7,4},{8,11},{9,10},{10,... | collective-permute-start | bytes 98312 | tf_op jit(solution)/shard_map/ppermute | solution.py:39
  45.9 1.0 %collective-permute-done.13.refs_2_ = bf16[128,128]{1,0:T(8,128)(2,1)S(1)} collective-permute-done((bf16[128,128]{1,0:T(8,128)(2,1)S(1)}, bf16[128,128]{1,0:T(8,128)(2,1)S(1)}, u32[]{:S(2)}, u32[]{:S(2)}) %collective-permute-start.13) | collective-permute-done | bytes 32800 | tf_op jit(solution)/shard_map/ppermute | solution.py:39
  46.9 3.8 %collective-permute-done.14.refs_3_ = bf16[128,128]{1,0:T(8,128)(2,1)S(1)} collective-permute-done((bf16[128,128]{1,0:T(8,128)(2,1)S(1)}, bf16[128,128]{1,0:T(8,128)(2,1)S(1)}, u32[]{:S(2)}, u32[]{:S(2)}) %collective-permute-start.14) | collective-permute-done | bytes 32800 | tf_op jit(solution)/shard_map/ppermute | solution.py:39
  50.7 0.9 %shard_map.87 = (f32[32,128]{1,0:T(8,128)S(1)}, f32[32,128]{1,0:T(8,128)S(1)}, f32[32,128]{1,0:T(8,128)S(1)}, f32[32,128]{1,0:T(8,128)S(1)}) custom-call(bf16[128,128]{1,0:T(8,128)(2,1)S(1)} %add_convert_fusion.refs_0_, bf16[128,128]{1,0:T(8,128)(2,1)S(1)} %collective-permute-done.12.refs_1_, bf16[128,128]{1,0:T(8,128)(2,1)S(1)} %collective-permute-done.13.refs_2_, ...), custom_call_target="tpu_custom_call" | custom-call | bytes 4194304 | tf_op jit(solution)/shard_map/pallas_call | solution.py:300
  51.7 1.4 %collective-permute-start.16 = (f32[32,128]{1,0:T(8,128)S(1)}, f32[32,128]{1,0:T(8,128)S(1)}, u32[]{:S(2)}, u32[]{:S(2)}) collective-permute-start(f32[32,128]{1,0:T(8,128)S(1)} %get-tuple-element.43), channel_id=1, source_target_pairs={{0,2},{1,3},{2,0},{3,1},{4,6},{5,7},{6,4},{7,5},{8,10},{9,11},{10,... | collective-permute-start | bytes 49160 | tf_op jit(solution)/shard_map/ppermute | solution.py:39
  53.1 2.9 %collective-permute-start.17 = (f32[32,128]{1,0:T(8,128)S(1)}, f32[32,128]{1,0:T(8,128)S(1)}, u32[]{:S(2)}, u32[]{:S(2)}) collective-permute-start(f32[32,128]{1,0:T(8,128)S(1)} %get-tuple-element.44), channel_id=1, source_target_pairs={{0,3},{1,2},{2,1},{3,0},{4,7},{5,6},{6,5},{7,4},{8,11},{9,10},{10,... | collective-permute-start | bytes 49160 | tf_op jit(solution)/shard_map/ppermute | solution.py:39
  56.1 0.3 collective-permute-done.16
  56.4 2.3 %collective-permute-done.17 = f32[32,128]{1,0:T(8,128)S(1)} collective-permute-done((f32[32,128]{1,0:T(8,128)S(1)}, f32[32,128]{1,0:T(8,128)S(1)}, u32[]{:S(2)}, u32[]{:S(2)}) %collective-permute-start.17) | collective-permute-done | bytes 16416 | tf_op jit(solution)/shard_map/ppermute | solution.py:39
  58.7 1.0 %collective-permute-start.19 = (f32[32,128]{1,0:T(8,128)S(1)}, f32[32,128]{1,0:T(8,128)S(1)}, u32[]{:S(2)}, u32[]{:S(2)}) collective-permute-start(f32[32,128]{1,0:T(8,128)S(1)} %add_add_fusion), channel_id=1, source_target_pairs={{0,8},{4,12},{8,0},{12,4},{1,9},{5,13},{9,1},{13,5},{2,10},{6,14},... | collective-permute-start | bytes 49160 | tf_op jit(solution)/shard_map/ppermute | solution.py:39
  59.7 0.9 %collective-permute-start.20 = (f32[32,128]{1,0:T(8,128)S(1)}, f32[32,128]{1,0:T(8,128)S(1)}, u32[]{:S(2)}, u32[]{:S(2)}) collective-permute-start(f32[32,128]{1,0:T(8,128)S(1)} %add_add_fusion), channel_id=1, source_target_pairs={{0,12},{4,8},{8,4},{12,0},{1,13},{5,9},{9,5},{13,1},{2,14},{6,10},... | collective-permute-start | bytes 49160 | tf_op jit(solution)/shard_map/ppermute | solution.py:39
  60.5 1.9 %collective-permute-done.19 = f32[32,128]{1,0:T(8,128)S(1)} collective-permute-done((f32[32,128]{1,0:T(8,128)S(1)}, f32[32,128]{1,0:T(8,128)S(1)}, u32[]{:S(2)}, u32[]{:S(2)}) %collective-permute-start.19) | collective-permute-done | bytes 16416 | tf_op jit(solution)/shard_map/ppermute | solution.py:39
  62.5 0.3 collective-permute-done.20
  62.8 0.6 add_bitcast_fusion
  (23 shorter events, 0.2 us)
Async XLA Ops:
  0.0 8.9 %collective-permute-start.6 = (bf16[32,3072]{1,0:T(8,128)(2,1)}, bf16[32,3072]{1,0:T(8,128)(2,1)S(1)}, u32[]{:S(2)}, u32[]{:S(2)}) collective-permute-start(bf16[32,3072]{1,0:T(8,128)(2,1)} %inw_hbm.1), channel_id=1, source_target_pairs={{0,8},{4,12},{8,0},{12,4},{1,9},{5,13},{9,1},{13,5},{2,10},{6,14},... | collective-permute-start | bytes 589832 | tf_op jit(solution)/shard_map/ppermute | solution.py:39
  3.0 9.3 %collective-permute-start = (bf16[768,128]{1,0:T(8,128)(2,1)}, bf16[768,128]{1,0:T(8,128)(2,1)S(1)}, u32[]{:S(2)}, u32[]{:S(2)}) collective-permute-start(bf16[768,128]{1,0:T(8,128)(2,1)} %refs_0_.1), channel_id=1, source_target_pairs={{0,8},{4,12},{8,0},{12,4},{1,9},{5,13},{9,1},{13,5},{2,10},{6,14},... | collective-permute-start | bytes 589832 | tf_op jit(solution)/shard_map/ppermute | solution.py:39
  3.0 27.0 %collective-permute-start.5 = (bf16[32,3072]{1,0:T(8,128)(2,1)}, bf16[32,3072]{1,0:T(8,128)(2,1)S(1)}, u32[]{:S(2)}, u32[]{:S(2)}) collective-permute-start(bf16[32,3072]{1,0:T(8,128)(2,1)} %inw_hbm.1), channel_id=1, source_target_pairs={{0,4},{4,0},{8,12},{12,8},{1,5},{5,1},{9,13},{13,9},{2,6},{6,2},{1... | collective-permute-start | bytes 589832 | tf_op jit(solution)/shard_map/ppermute | solution.py:39
  8.9 21.1 %collective-permute-start.7 = (bf16[32,3072]{1,0:T(8,128)(2,1)S(1)}, bf16[32,3072]{1,0:T(8,128)(2,1)S(1)}, u32[]{:S(2)}, u32[]{:S(2)}) collective-permute-start(bf16[32,3072]{1,0:T(8,128)(2,1)S(1)} %collective-permute-done.6.refs_6_), channel_id=1, source_target_pairs={{0,4},{4,0},{8,12},{12,8},{1,5},{5,1},{9,13},{13,9},{2,6},{6,2},{1... | collective-permute-start | bytes 589832 | tf_op jit(solution)/shard_map/ppermute | solution.py:39
  8.9 25.1 %collective-permute-start.8 = (bf16[768,128]{1,0:T(8,128)(2,1)}, bf16[768,128]{1,0:T(8,128)(2,1)S(1)}, u32[]{:S(2)}, u32[]{:S(2)}) collective-permute-start(bf16[768,128]{1,0:T(8,128)(2,1)} %refs_0_.1), channel_id=1, source_target_pairs={{0,4},{4,0},{8,12},{12,8},{1,5},{5,1},{9,13},{13,9},{2,6},{6,2},{1... | collective-permute-start | bytes 589832 | tf_op jit(solution)/shard_map/ppermute | solution.py:39
  12.3 23.5 %collective-permute-start.1 = (bf16[768,128]{1,0:T(8,128)(2,1)S(1)}, bf16[768,128]{1,0:T(8,128)(2,1)S(1)}, u32[]{:S(2)}, u32[]{:S(2)}) collective-permute-start(bf16[768,128]{1,0:T(8,128)(2,1)S(1)} %collective-permute-done.refs_2_), channel_id=1, source_target_pairs={{0,4},{4,0},{8,12},{12,8},{1,5},{5,1},{9,13},{13,9},{2,6},{6,2},{1... | collective-permute-start | bytes 589832 | tf_op jit(solution)/shard_map/ppermute | solution.py:39
  14.5 3.9 %collective-permute-start.2 = (f32[50,128]{1,0:T(8,128)S(1)}, f32[50,128]{1,0:T(8,128)S(1)}, u32[]{:S(2)}, u32[]{:S(2)}) collective-permute-start(f32[50,128]{1,0:T(8,128)S(1)} %shard_map.83.refs_0_), channel_id=1, source_target_pairs={{0,1},{1,0},{2,3},{3,2},{4,5},{5,4},{6,7},{7,6},{8,9},{9,8},{10,11... | collective-permute-start | bytes 76808 | tf_op jit(solution)/shard_map/ppermute | solution.py:39
  18.5 4.8 %collective-permute-start.3 = (f32[50,128]{1,0:T(8,128)S(1)}, f32[50,128]{1,0:T(8,128)S(1)}, u32[]{:S(2)}, u32[]{:S(2)}) collective-permute-start(f32[50,128]{1,0:T(8,128)S(1)} %shard_map.83.refs_0_), channel_id=1, source_target_pairs={{0,2},{1,3},{2,0},{3,1},{4,6},{5,7},{6,4},{7,5},{8,10},{9,11},{10,... | collective-permute-start | bytes 76808 | tf_op jit(solution)/shard_map/ppermute | solution.py:39
  23.2 6.7 %collective-permute-start.4 = (f32[50,128]{1,0:T(8,128)S(1)}, f32[50,128]{1,0:T(8,128)S(1)}, u32[]{:S(2)}, u32[]{:S(2)}) collective-permute-start(f32[50,128]{1,0:T(8,128)S(1)} %shard_map.83.refs_0_), channel_id=1, source_target_pairs={{0,3},{1,2},{2,1},{3,0},{4,7},{5,6},{6,5},{7,4},{8,11},{9,10},{10,... | collective-permute-start | bytes 76808 | tf_op jit(solution)/shard_map/ppermute | solution.py:39
  30.0 4.0 %copy-start = (bf16[768,128]{1,0:T(8,128)(2,1)S(1)}, bf16[768,128]{1,0:T(8,128)(2,1)}, u32[]{:S(2)}) copy-start(bf16[768,128]{1,0:T(8,128)(2,1)} %refs_0_.1) | copy-start | bytes 589828
  35.8 27.0 %copy-start.1 = (f32[32,128]{1,0:T(8,128)S(1)}, f32[32,128]{1,0:T(8,128)}, u32[]{:S(2)}) copy-start(f32[32,128]{1,0:T(8,128)} %start_hbm.1) | copy-start | bytes 49156
  36.5 4.0 %collective-permute-start.10 = (bf16[128,128]{1,0:T(8,128)(2,1)S(1)}, bf16[128,128]{1,0:T(8,128)(2,1)S(1)}, u32[]{:S(2)}, u32[]{:S(2)}) collective-permute-start(bf16[128,128]{1,0:T(8,128)(2,1)S(1)} %get-tuple-element.38), channel_id=1, source_target_pairs={{0,8},{4,12},{8,0},{12,4},{1,9},{5,13},{9,1},{13,5},{2,10},{6,14},... | collective-permute-start | bytes 98312 | tf_op jit(solution)/shard_map/ppermute | solution.py:39
  38.0 3.3 %collective-permute-start.11 = (bf16[128,128]{1,0:T(8,128)(2,1)S(1)}, bf16[128,128]{1,0:T(8,128)(2,1)S(1)}, u32[]{:S(2)}, u32[]{:S(2)}) collective-permute-start(bf16[128,128]{1,0:T(8,128)(2,1)S(1)} %get-tuple-element.38), channel_id=1, source_target_pairs={{0,12},{4,8},{8,4},{12,0},{1,13},{5,9},{9,5},{13,1},{2,14},{6,10},... | collective-permute-start | bytes 98312 | tf_op jit(solution)/shard_map/ppermute | solution.py:39
  38.0 3.3 %collective-permute-start.9 = (bf16[128,128]{1,0:T(8,128)(2,1)S(1)}, bf16[128,128]{1,0:T(8,128)(2,1)S(1)}, u32[]{:S(2)}, u32[]{:S(2)}) collective-permute-start(bf16[128,128]{1,0:T(8,128)(2,1)S(1)} %get-tuple-element.38), channel_id=1, source_target_pairs={{0,4},{4,0},{8,12},{12,8},{1,5},{5,1},{9,13},{13,9},{2,6},{6,2},{1... | collective-permute-start | bytes 98312 | tf_op jit(solution)/shard_map/ppermute | solution.py:39
  41.4 4.5 %collective-permute-start.12 = (bf16[128,128]{1,0:T(8,128)(2,1)S(1)}, bf16[128,128]{1,0:T(8,128)(2,1)S(1)}, u32[]{:S(2)}, u32[]{:S(2)}) collective-permute-start(bf16[128,128]{1,0:T(8,128)(2,1)S(1)} %add_convert_fusion.refs_0_), channel_id=1, source_target_pairs={{0,1},{1,0},{2,3},{3,2},{4,5},{5,4},{6,7},{7,6},{8,9},{9,8},{10,11... | collective-permute-start | bytes 98312 | tf_op jit(solution)/shard_map/ppermute | solution.py:39
  41.5 5.4 %collective-permute-start.13 = (bf16[128,128]{1,0:T(8,128)(2,1)S(1)}, bf16[128,128]{1,0:T(8,128)(2,1)S(1)}, u32[]{:S(2)}, u32[]{:S(2)}) collective-permute-start(bf16[128,128]{1,0:T(8,128)(2,1)S(1)} %add_convert_fusion.refs_0_), channel_id=1, source_target_pairs={{0,2},{1,3},{2,0},{3,1},{4,6},{5,7},{6,4},{7,5},{8,10},{9,11},{10,... | collective-permute-start | bytes 98312 | tf_op jit(solution)/shard_map/ppermute | solution.py:39
  45.0 5.7 %collective-permute-start.14 = (bf16[128,128]{1,0:T(8,128)(2,1)S(1)}, bf16[128,128]{1,0:T(8,128)(2,1)S(1)}, u32[]{:S(2)}, u32[]{:S(2)}) collective-permute-start(bf16[128,128]{1,0:T(8,128)(2,1)S(1)} %add_convert_fusion.refs_0_), channel_id=1, source_target_pairs={{0,3},{1,2},{2,1},{3,0},{4,7},{5,6},{6,5},{7,4},{8,11},{9,10},{10,... | collective-permute-start | bytes 98312 | tf_op jit(solution)/shard_map/ppermute | solution.py:39
  51.6 4.5 %collective-permute-start.15 = (f32[32,128]{1,0:T(8,128)S(1)}, f32[32,128]{1,0:T(8,128)S(1)}, u32[]{:S(2)}, u32[]{:S(2)}) collective-permute-start(f32[32,128]{1,0:T(8,128)S(1)} %get-tuple-element.42), channel_id=1, source_target_pairs={{0,1},{1,0},{2,3},{3,2},{4,5},{5,4},{6,7},{7,6},{8,9},{9,8},{10,11... | collective-permute-start | bytes 49160 | tf_op jit(solution)/shard_map/ppermute | solution.py:39
  51.7 4.7 %collective-permute-start.16 = (f32[32,128]{1,0:T(8,128)S(1)}, f32[32,128]{1,0:T(8,128)S(1)}, u32[]{:S(2)}, u32[]{:S(2)}) collective-permute-start(f32[32,128]{1,0:T(8,128)S(1)} %get-tuple-element.43), channel_id=1, source_target_pairs={{0,2},{1,3},{2,0},{3,1},{4,6},{5,7},{6,4},{7,5},{8,10},{9,11},{10,... | collective-permute-start | bytes 49160 | tf_op jit(solution)/shard_map/ppermute | solution.py:39
  53.1 5.5 %collective-permute-start.17 = (f32[32,128]{1,0:T(8,128)S(1)}, f32[32,128]{1,0:T(8,128)S(1)}, u32[]{:S(2)}, u32[]{:S(2)}) collective-permute-start(f32[32,128]{1,0:T(8,128)S(1)} %get-tuple-element.44), channel_id=1, source_target_pairs={{0,3},{1,2},{2,1},{3,0},{4,7},{5,6},{6,5},{7,4},{8,11},{9,10},{10,... | collective-permute-start | bytes 49160 | tf_op jit(solution)/shard_map/ppermute | solution.py:39
  58.7 1.9 %collective-permute-start.18 = (f32[32,128]{1,0:T(8,128)S(1)}, f32[32,128]{1,0:T(8,128)S(1)}, u32[]{:S(2)}, u32[]{:S(2)}) collective-permute-start(f32[32,128]{1,0:T(8,128)S(1)} %add_add_fusion), channel_id=1, source_target_pairs={{0,4},{4,0},{8,12},{12,8},{1,5},{5,1},{9,13},{13,9},{2,6},{6,2},{1... | collective-permute-start | bytes 49160 | tf_op jit(solution)/shard_map/ppermute | solution.py:39
  58.7 3.8 %collective-permute-start.19 = (f32[32,128]{1,0:T(8,128)S(1)}, f32[32,128]{1,0:T(8,128)S(1)}, u32[]{:S(2)}, u32[]{:S(2)}) collective-permute-start(f32[32,128]{1,0:T(8,128)S(1)} %add_add_fusion), channel_id=1, source_target_pairs={{0,8},{4,12},{8,0},{12,4},{1,9},{5,13},{9,1},{13,5},{2,10},{6,14},... | collective-permute-start | bytes 49160 | tf_op jit(solution)/shard_map/ppermute | solution.py:39
  59.7 3.2 %collective-permute-start.20 = (f32[32,128]{1,0:T(8,128)S(1)}, f32[32,128]{1,0:T(8,128)S(1)}, u32[]{:S(2)}, u32[]{:S(2)}) collective-permute-start(f32[32,128]{1,0:T(8,128)S(1)} %add_add_fusion), channel_id=1, source_target_pairs={{0,12},{4,8},{8,4},{12,0},{1,13},{5,9},{9,5},{13,1},{2,14},{6,10},... | collective-permute-start | bytes 49160 | tf_op jit(solution)/shard_map/ppermute | solution.py:39

commit v7 on v6

--- a/solution.py
+++ b/solution.py
@@ -105,16 +105,41 @@
         out_ref[rows + r : rows + r + 1, :] = result[0:1, r * LANES : (r + 1) * LANES]
 
 
-def load_kernel(weight_ref, qkv_hbm, inw_hbm, qkv_ref, inw_ref, step_ref, sems):
+def channel_columns(inw_ref, c, n):
+    return inw_ref[:, :, c * LANES : (c + n) * LANES].reshape(-1, n * LANES)
+
+
+def load_kernel(nm, weight_ref, qkv_hbm, inw_hbm, *refs):
+    inws, refs = refs[: nm - 1], refs[nm - 1 :]
+    qkv_ref, inw_ref, mean_ref, gram_ref, step_ref, sems = refs
     cols = qkv_ref.shape[1]
     copies = run_copies(
         [
-            pltpu.make_async_copy(inw_hbm, inw_ref, sems.at[0]),
+            pltpu.make_async_copy(inw_hbm, inw_ref.at[place("tm", nm, 0)], sems.at[0]),
             pltpu.make_async_copy(qkv_hbm.at[:, pl.ds(0, cols)], qkv_ref, sems.at[1]),
         ]
     )
     step_ref[...] = jnp.full(step_ref.shape, weight_ref[0].astype(F32) * (1.0 / STEP_DIVISOR))
-    wait_copies(copies)
+    for k in range(1, nm):
+        inw_ref[place("tm", nm, k)] = inws[k - 1][...]
+    copies[0].wait()
+    channels, width = mean_ref.shape[0], inw_ref.shape[2]
+    chunks = width // LANES
+    total = jnp.zeros((channels, LANES), F32)
+    for c in range(chunks):
+        total = total + channel_columns(inw_ref, c, 1).astype(F32)
+    mean = jnp.sum(total, axis=1, keepdims=True) * (1.0 / width)
+    mean_b = jnp.broadcast_to(mean, mean_ref.shape)
+    mean_ref[...] = mean_b
+    gram = jnp.zeros((channels, channels), F32)
+    for c in range(0, chunks, 6):
+        piece = channel_columns(inw_ref, c, 6)
+        gram = gram + bdot_t(piece, piece)
+    mean_c = jnp.broadcast_to(mean, (channels, channels))
+    gram = gram * (1.0 / width) - mean_c * mean_c.T
+    for i, term in enumerate(split_terms(gram, 3)):
+        gram_ref[i * channels : (i + 1) * channels, :] = term
+    copies[1].wait()
 
 
 def attend(x, factors, base, gram, head_count):
@@ -137,10 +162,10 @@
 
 def setup_kernel(nt, nm, block, *refs):
     msgs, refs = refs[:nt], refs[nt:]
-    inws, refs = refs[:nm], refs[nm:]
-    near_ref, qkv_hbm, out_w_hbm, refs = refs[0], refs[1], refs[2], refs[3:]
-    factor_ref, base_ref, gram_ref, start_ref, inw_ref, gate_ref, out_w_ref = refs[:7]
-    start_s, mod_s, z_s, qkv_s, sems = refs[7:]
+    inw_ref, mean_ref, near_ref, qkv_hbm, out_w_hbm = refs[:5]
+    refs = refs[5:]
+    factor_ref, base_ref, start_ref, gate_ref, out_w_ref = refs[:5]
+    start_s, mod_s, gate_s, z_s, qkv_s, sems = refs[5:]
     near = near_ref.shape[1] // block
     count = factor_ref.shape[1] // block
     copies = run_copies(
@@ -158,28 +183,20 @@
         at = place("tensor", nt, k)
         start_s[at] = msg[0 : start_s.shape[1], :]
         mod_s[at, 0 : msg.shape[0] - start_s.shape[1], :] = msg[start_s.shape[1] :, :]
-    for k in range(nm):
-        inw_ref[place("tm", nm, k)] = inws[k][...]
-    channels, width = gram_ref.shape[1], z_s.shape[1]
+    channels, width = mean_ref.shape[0], z_s.shape[1]
     chunks = width // LANES
     per = 3 * chunks // nt
 
     def mod_row(r):
         return mod_s[r // per, r % per : r % per + 1, :]
 
-    def columns(c, n):
-        return inw_ref[:, :, c * LANES : (c + n) * LANES].reshape(channels, n * LANES)
-
-    total = jnp.zeros((channels, LANES), F32)
-    for c in range(chunks):
-        total = total + columns(c, 1).astype(F32)
-    mean = jnp.sum(total, axis=1, keepdims=True) * (1.0 / width)
+    mean = mean_ref[...]
     first = jnp.zeros((channels + 16, block), F32)
     group = 6
     for g in range(0, chunks, group):
         for c in range(g, g + group):
             cols = slice(c * LANES, (c + 1) * LANES)
-            centered = columns(c, 1).astype(F32) - mean
+            centered = channel_columns(inw_ref, c, 1).astype(F32) - mean
             z_s[0:channels, cols] = (centered * (1.0 + mod_row(chunks + c))).astype(BF16)
             shift = jnp.broadcast_to(mod_row(c), (16, LANES)).astype(BF16)
             z_s[channels : channels + 16, cols] = shift
@@ -196,14 +213,8 @@
     keep(first, 0)
     for p in range(nm):
         for r in range(chunks // nm):
-            gate_ref[p, r : r + 1, :] = mod_row(2 * chunks + p * (chunks // nm) + r)
-    gram = jnp.zeros((channels, channels), F32)
-    for c in range(0, chunks, 6):
-        gram = gram + bdot_t(columns(c, 6), columns(c, 6))
-    mean_b = jnp.broadcast_to(mean, (channels, channels))
-    gram = gram * (1.0 / width) - mean_b * mean_b.T
-    for i, piece in enumerate(split_terms(gram, 3)):
-        gram_ref[i * channels : (i + 1) * channels, :] = piece
+            gate_s[p, r : r + 1, :] = mod_row(2 * chunks + p * (chunks // nm) + r)
+        gate_ref[p] = gate_s[p].T
     start_ref[...] = start_s[...].reshape(start_ref.shape)
 
     for n in range(1, count):
@@ -219,15 +230,15 @@
 def fold_parts(nm, first, heads, gate_ref, out_w_ref, inw_ref):
     folded, resid = 0.0, 0.0
     for i, head_ref in enumerate(heads):
-        size = head_ref.shape[0]
+        size, _ = head_ref.shape
         at = place("tm", nm, first + i)
         cols = pl.ds(pl.multiple_of(at * size, LANES), size)
         gate = gate_ref[at]
         gated = []
         for r in range(size // LANES):
-            turned = head_ref[r * LANES : (r + 1) * LANES, :].astype(F32).T
-            gated.append((turned * gate[r : r + 1, :]).astype(BF16))
-        folded = folded + bdot_t(jnp.concatenate(gated, axis=1), out_w_ref[:, cols])
+            rows = head_ref[r * LANES : (r + 1) * LANES, :].astype(F32)
+            gated.append((rows * gate[:, r : r + 1]).astype(BF16))
+        folded = folded + bdot(out_w_ref[:, cols], jnp.concatenate(gated, axis=0))
         inw = inw_ref[:, :, cols].reshape(-1, size)
         resid = resid + bdot(inw, head_ref[...])
     return folded, resid
@@ -262,7 +273,7 @@
     for i, term in enumerate(split_terms(resid, 2)):
         resid_ref[i * channels : (i + 1) * channels, :] = term
     x = start_ref[...].astype(BF16)
-    vel = bdot_t(att_ref[...], folded)
+    vel = bdot(att_ref[...], folded)
     residual = bdot(jnp.concatenate([x, x], axis=1), resid_ref[...])
     vel_ref[...] = (add_own_rows(vel, residual, rows) * step_ref[0:1, :]).astype(vel_ref.dtype)
 
@@ -277,7 +288,7 @@
         guess = guess + part[...].astype(F32)
     x = guess.astype(BF16)
     attended = attend(x, factor_ref, base_ref, gram_ref, head_count)
-    vel = bdot_t(attended, fold_ref[...])
+    vel = bdot(attended, fold_ref[...])
     residual = bdot(jnp.concatenate([x, x], axis=1), resid_ref[...])
     vel = add_own_rows(vel, residual, rows) * step_ref[0:1, :]
     if not split:
@@ -378,40 +389,43 @@
     block = 4 * LANES if span_cols % (4 * LANES) == 0 else span_cols
     near = max(1, span_cols // block // 3)
     far = max(1, span_cols // block - near)
-    qkv_near, inw_parts[0], step = call(
-        load_kernel,
+    qkv_near, inw_all, mean, gram, step = call(
+        functools.partial(load_kernel, nm),
         [
             shape_of((width, near * block), BF16),
-            shape_of(inw_parts[0].shape, BF16),
+            shape_of((nm, channels // nm, width), BF16),
+            shape_of((channels, LANES), F32),
+            shape_of((3 * channels, channels), BF16),
             shape_of((8, LANES), F32),
         ],
-        [SMEM, HBM, HBM],
+        [SMEM, HBM, HBM] + [VMEM] * (nm - 1),
         [pltpu.SemaphoreType.DMA((2,))],
         step_weight,
         qkv_weight,
-        inw_parts[0],
-    )
-    factor, base, gram, start_all, inw_all, gate, out_near = call(
+        *inw_parts,
+        limit=16,
+    )
+    factor, base, start_all, gate, out_near = call(
         functools.partial(setup_kernel, nt, nm, block),
         [
             shape_of((2 * channels, span_cols), BF16),
             shape_of((8, span_cols), F32),
-            shape_of((3 * channels, channels), BF16),
             shape_of((tokens, channels), F32),
-            shape_of((nm, channels // nm, width), BF16),
-            shape_of((nm, gate_rows, LANES), F32),
+            shape_of((nm, LANES, gate_rows), F32),
             shape_of(out_weight.shape, BF16),
         ],
-        [VMEM] * (nt + nm + 1) + [HBM, HBM],
+        [VMEM] * (nt + 3) + [HBM, HBM],
         [
             pltpu.VMEM((nt, block_rows, channels), F32),
             pltpu.VMEM((nt, padded, LANES), F32),
+            pltpu.VMEM((nm, gate_rows, LANES), F32),
             pltpu.VMEM((channels + 16, width), BF16),
             pltpu.VMEM((width, far * block), BF16),
             pltpu.SemaphoreType.DMA((far + 1,)),
         ],
         *messages,
-        *inw_parts,
+        inw_all,
+        mean,
         qkv_near,
         qkv_weight,
         out_weight,
@@ -424,7 +438,7 @@
         functools.partial(attend_kernel, nm, early, head_count),
         [
             shape_of((tokens, head_count * HD), BF16),
-            shape_of((channels, span), F32),
+            shape_of((span, channels), F32),
             shape_of((channels, channels), F32),
         ],
         [VMEM] * (early + 7),
@@ -442,7 +456,7 @@
     folded, resid, vel = call(
         functools.partial(fold_kernel, nm, late, rows),
         [
-            shape_of((channels, span), BF16),
+            shape_of((span, channels), BF16),
             shape_of((2 * channels, channels), BF16),
             shape_of((tokens, channels), BF16),
         ],

time: 63.6 us -> 58.3 us (0.917)
  starting transfers between devices: 25.2 us -> 20.9 us
  waiting for transfers between devices: 25.1 us -> 24.1 us
    ppermute x21, starting transfers between devices: 25.2 us -> 20.9 us  [swap(): return lax.ppermute(value, axis, [(i, i ^ k) for i in range(n)])]
    ppermute x21, waiting for transfers between devices: 25.1 us -> 24.1 us  [swap(): return lax.ppermute(value, axis, [(i, i ^ k) for i in range(n)])]
  transfers between devices with their start and end apart: 21 -> 21, of which waited for: 12 -> 11; matrix products, arithmetic and copies ran while one was open for 0% -> 0% of each run, Pallas kernels for 15% -> 16%
where the time goes in v7:
time: 58.3 us; the launch traced here: 58.2 us
  waiting for transfers between devices  24.1 us (41%)
  starting transfers between devices  20.9 us (36%)
  Pallas kernels  11 us (19%)
  between operations  1.44 us (2%)
  other arithmetic  0.65 us (1%)
    ppermute x21, waiting for transfers between devices, swap(): return lax.ppermute(value, axis, [(i, i ^ k) for i in range(n)])  24.1 us
    ppermute x21, starting transfers between devices, swap(): return lax.ppermute(value, axis, [(i, i ^ k) for i in range(n)])  20.9 us
    pallas_call x6, Pallas kernels, call(): pl.pallas_call(kernel, out_shape=outs, in_specs=in_specs, out_specs=[VMEM...  11 us
  transfers between devices with their start and end apart: 21, of which 11 were waited for; matrix products, arithmetic and copies ran while one was open for 0% of the time, Pallas kernels for 16%

profile of v7, /device:TPU:0, one launch (start us, length us, event | category | flops | bytes accessed | tf_op | source)
XLA Modules:
  0.0 58.2 jit_solution(2732002092959979677)
XLA Ops:
  0.0 3.0 %collective-permute-start.3 = (bf16[32,3072]{1,0:T(8,128)(2,1)}, bf16[32,3072]{1,0:T(8,128)(2,1)S(1)}, u32[]{:S(2)}, u32[]{:S(2)}) collective-permute-start(bf16[32,3072]{1,0:T(8,128)(2,1)} %inw_hbm.1), channel_id=1, source_target_pairs={{0,8},{4,12},{8,0},{12,4},{1,9},{5,13},{9,1},{13,5},{2,10},{6,14},... | collective-permute-start | bytes 589832 | tf_op jit(solution)/shard_map/ppermute | solution.py:39
  3.0 5.9 %collective-permute-done.3.refs_1_ = bf16[32,3072]{1,0:T(8,128)(2,1)S(1)} collective-permute-done((bf16[32,3072]{1,0:T(8,128)(2,1)}, bf16[32,3072]{1,0:T(8,128)(2,1)S(1)}, u32[]{:S(2)}, u32[]{:S(2)}) %collective-permute-start.3) | collective-permute-done | bytes 196640 | tf_op jit(solution)/shard_map/ppermute | solution.py:39
  8.9 0.5 collective-permute-start.8
  9.4 2.9 %collective-permute-done.refs_2_ = bf16[768,128]{1,0:T(8,128)(2,1)S(1)} collective-permute-done((bf16[768,128]{1,0:T(8,128)(2,1)}, bf16[768,128]{1,0:T(8,128)(2,1)S(1)}, u32[]{:S(2)}, u32[]{:S(2)}) %collective-permute-start) | collective-permute-done | bytes 196640 | tf_op jit(solution)/shard_map/ppermute | solution.py:39
  12.9 1.6 %shard_map.83.refs_0_ = f32[50,128]{1,0:T(8,128)S(1)} custom-call(s32[1]{0:T(128)S(6)} %copy.9.time_ref, bf16[256,2304]{1,0:T(8,128)(2,1)} %weight_hbm.1, f32[32,128]{1,0:T(8,128)} %start_hbm.1), custom_call_target="tpu_custom_call" | custom-call | bytes 4194304 | tf_op jit(solution)/shard_map/pallas_call | solution.py:311
  14.5 1.9 %collective-permute-start.5 = (f32[50,128]{1,0:T(8,128)S(1)}, f32[50,128]{1,0:T(8,128)S(1)}, u32[]{:S(2)}, u32[]{:S(2)}) collective-permute-start(f32[50,128]{1,0:T(8,128)S(1)} %shard_map.83.refs_0_), channel_id=1, source_target_pairs={{0,1},{1,0},{2,3},{3,2},{4,5},{5,4},{6,7},{7,6},{8,9},{9,8},{10,11... | collective-permute-start | bytes 76808 | tf_op jit(solution)/shard_map/ppermute | solution.py:39
  16.4 2.6 %collective-permute-start.6 = (f32[50,128]{1,0:T(8,128)S(1)}, f32[50,128]{1,0:T(8,128)S(1)}, u32[]{:S(2)}, u32[]{:S(2)}) collective-permute-start(f32[50,128]{1,0:T(8,128)S(1)} %shard_map.83.refs_0_), channel_id=1, source_target_pairs={{0,2},{1,3},{2,0},{3,1},{4,6},{5,7},{6,4},{7,5},{8,10},{9,11},{10,... | collective-permute-start | bytes 76808 | tf_op jit(solution)/shard_map/ppermute | solution.py:39
  19.7 2.0 %shard_map.82 = (bf16[3072,512]{1,0:T(8,128)(2,1)S(1)}, bf16[4,32,3072]{2,1,0:T(8,128)(2,1)S(1)}, f32[128,128]{1,0:T(8,128)S(1)}, bf16[384,128]{1,0:T(8,128)(2,1)S(1)}, f32[8,128]{1,0:T(8,128)S(1)}) custom-call(s32[1]{0:T(128)S(6)} %copy.10.weight_ref, bf16[3072,1536]{1,0:T(8,128)(2,1)} %refs_7_.1, bf16[32,3072]{1,0:T(8,128)(2,1)} %inw_hbm.1, ...), custom_call_target="tpu_custom_call" | custom-call | bytes 4194304 | tf_op jit(solution)/shard_map/pallas_call | solution.py:311
  21.7 2.9 %collective-permute-done.7.refs_3_ = f32[50,128]{1,0:T(8,128)S(1)} collective-permute-done((f32[50,128]{1,0:T(8,128)S(1)}, f32[50,128]{1,0:T(8,128)S(1)}, u32[]{:S(2)}, u32[]{:S(2)}) %collective-permute-start.7) | collective-permute-done | bytes 25632 | tf_op jit(solution)/shard_map/ppermute | solution.py:39
  24.7 4.2 %shard_map.84 = (bf16[256,1536]{1,0:T(8,128)(2,1)S(1)}, f32[8,1536]{1,0:T(8,128)S(1)}, f32[128,128]{1,0:T(8,128)S(1)}, f32[4,128,8]{2,1,0:T(8,128)S(1)}, bf16[512,3072]{1,0:T(8,128)(2,1)S(1)}) custom-call(f32[50,128]{1,0:T(8,128)S(1)} %shard_map.83.refs_0_, f32[50,128]{1,0:T(8,128)S(1)} %collective-permute-done.5.refs_1_, ...), custom_call_target="tpu_custom_call" | custom-call | bytes 4194304 | tf_op jit(solution)/shard_map/pallas_call | solution.py:311
  29.0 1.5 %shard_map.85 = (bf16[128,512]{1,0:T(8,128)(2,1)S(1)}, f32[512,128]{1,0:T(8,128)S(1)}, f32[128,128]{1,0:T(8,128)S(1)}) custom-call(bf16[768,128]{1,0:T(8,128)(2,1)S(1)} %copy-done, bf16[768,128]{1,0:T(8,128)(2,1)S(1)} %collective-permute-done.8.refs_1_, bf16[768,128]{1,0:T(8,128)(2,1)S(1)} %collective-permute-done.refs_2_, ...), custom_call_target="tpu_custom_call" | custom-call | bytes 4194304 | tf_op jit(solution)/shard_map/pallas_call | solution.py:311
  30.5 0.7 %shard_map.86 = (bf16[512,128]{1,0:T(8,128)(2,1)S(1)}, bf16[256,128]{1,0:T(8,128)(2,1)S(1)}, bf16[128,128]{1,0:T(8,128)(2,1)S(1)}) custom-call(bf16[768,128]{1,0:T(8,128)(2,1)S(1)} %collective-permute-done.1.refs_0_, f32[8,128]{1,0:T(8,128)S(1)} %get-tuple-element.25.refs_1_.refs_4_, f32[4,128,8]{2,1,0:T(8,128)S(1)} %get-tuple-element.29.refs_7_.refs_2_, ...), custom_call_target="tpu_custom_call" | custom-call | bytes 4194304 | tf_op jit(solution)/shard_map/pallas_call | solution.py:311
  31.3 1.6 %collective-permute-start.10 = (bf16[128,128]{1,0:T(8,128)(2,1)S(1)}, bf16[128,128]{1,0:T(8,128)(2,1)S(1)}, u32[]{:S(2)}, u32[]{:S(2)}) collective-permute-start(bf16[128,128]{1,0:T(8,128)(2,1)S(1)} %get-tuple-element.38), channel_id=1, source_target_pairs={{0,8},{4,12},{8,0},{12,4},{1,9},{5,13},{9,1},{13,5},{2,10},{6,14},... | collective-permute-start | bytes 98312 | tf_op jit(solution)/shard_map/ppermute | solution.py:39
  32.8 0.6 %collective-permute-start.9 = (bf16[128,128]{1,0:T(8,128)(2,1)S(1)}, bf16[128,128]{1,0:T(8,128)(2,1)S(1)}, u32[]{:S(2)}, u32[]{:S(2)}) collective-permute-start(bf16[128,128]{1,0:T(8,128)(2,1)S(1)} %get-tuple-element.38), channel_id=1, source_target_pairs={{0,4},{4,0},{8,12},{12,8},{1,5},{5,1},{9,13},{13,9},{2,6},{6,2},{1... | collective-permute-start | bytes 98312 | tf_op jit(solution)/shard_map/ppermute | solution.py:39
  33.5 1.8 %collective-permute-done.10 = bf16[128,128]{1,0:T(8,128)(2,1)S(1)} collective-permute-done((bf16[128,128]{1,0:T(8,128)(2,1)S(1)}, bf16[128,128]{1,0:T(8,128)(2,1)S(1)}, u32[]{:S(2)}, u32[]{:S(2)}) %collective-permute-start.10) | collective-permute-done | bytes 32800 | tf_op jit(solution)/shard_map/ppermute | solution.py:39
  35.2 0.9 %collective-permute-done.11 = bf16[128,128]{1,0:T(8,128)(2,1)S(1)} collective-permute-done((bf16[128,128]{1,0:T(8,128)(2,1)S(1)}, bf16[128,128]{1,0:T(8,128)(2,1)S(1)}, u32[]{:S(2)}, u32[]{:S(2)}) %collective-permute-start.11) | collective-permute-done | bytes 32800 | tf_op jit(solution)/shard_map/ppermute | solution.py:39
  36.2 0.1 collective-permute-start.12
  36.3 1.4 %collective-permute-start.13 = (bf16[128,128]{1,0:T(8,128)(2,1)S(1)}, bf16[128,128]{1,0:T(8,128)(2,1)S(1)}, u32[]{:S(2)}, u32[]{:S(2)}) collective-permute-start(bf16[128,128]{1,0:T(8,128)(2,1)S(1)} %add_convert_fusion.refs_0_), channel_id=1, source_target_pairs={{0,2},{1,3},{2,0},{3,1},{4,6},{5,7},{6,4},{7,5},{8,10},{9,11},{10,... | collective-permute-start | bytes 98312 | tf_op jit(solution)/shard_map/ppermute | solution.py:39
  37.7 2.9 %collective-permute-start.14 = (bf16[128,128]{1,0:T(8,128)(2,1)S(1)}, bf16[128,128]{1,0:T(8,128)(2,1)S(1)}, u32[]{:S(2)}, u32[]{:S(2)}) collective-permute-start(bf16[128,128]{1,0:T(8,128)(2,1)S(1)} %add_convert_fusion.refs_0_), channel_id=1, source_target_pairs={{0,3},{1,2},{2,1},{3,0},{4,7},{5,6},{6,5},{7,4},{8,11},{9,10},{10,... | collective-permute-start | bytes 98312 | tf_op jit(solution)/shard_map/ppermute | solution.py:39
  40.7 0.9 %collective-permute-done.13.refs_2_ = bf16[128,128]{1,0:T(8,128)(2,1)S(1)} collective-permute-done((bf16[128,128]{1,0:T(8,128)(2,1)S(1)}, bf16[128,128]{1,0:T(8,128)(2,1)S(1)}, u32[]{:S(2)}, u32[]{:S(2)}) %collective-permute-start.13) | collective-permute-done | bytes 32800 | tf_op jit(solution)/shard_map/ppermute | solution.py:39
  41.5 1.9 %collective-permute-done.14.refs_3_ = bf16[128,128]{1,0:T(8,128)(2,1)S(1)} collective-permute-done((bf16[128,128]{1,0:T(8,128)(2,1)S(1)}, bf16[128,128]{1,0:T(8,128)(2,1)S(1)}, u32[]{:S(2)}, u32[]{:S(2)}) %collective-permute-start.14) | collective-permute-done | bytes 32800 | tf_op jit(solution)/shard_map/ppermute | solution.py:39
  43.4 0.9 %shard_map.87 = (f32[32,128]{1,0:T(8,128)S(1)}, f32[32,128]{1,0:T(8,128)S(1)}, f32[32,128]{1,0:T(8,128)S(1)}, f32[32,128]{1,0:T(8,128)S(1)}) custom-call(bf16[128,128]{1,0:T(8,128)(2,1)S(1)} %add_convert_fusion.refs_0_, bf16[128,128]{1,0:T(8,128)(2,1)S(1)} %collective-permute-done.12.refs_1_, bf16[128,128]{1,0:T(8,128)(2,1)S(1)} %collective-permute-done.13.refs_2_, ...), custom_call_target="tpu_custom_call" | custom-call | bytes 4194304 | tf_op jit(solution)/shard_map/pallas_call | solution.py:311
  44.3 0.1 collective-permute-start.15
  44.4 3.5 %collective-permute-start.16 = (f32[32,128]{1,0:T(8,128)S(1)}, f32[32,128]{1,0:T(8,128)S(1)}, u32[]{:S(2)}, u32[]{:S(2)}) collective-permute-start(f32[32,128]{1,0:T(8,128)S(1)} %get-tuple-element.43), channel_id=1, source_target_pairs={{0,2},{1,3},{2,0},{3,1},{4,6},{5,7},{6,4},{7,5},{8,10},{9,11},{10,... | collective-permute-start | bytes 49160 | tf_op jit(solution)/shard_map/ppermute | solution.py:39
  47.9 0.9 %collective-permute-start.17 = (f32[32,128]{1,0:T(8,128)S(1)}, f32[32,128]{1,0:T(8,128)S(1)}, u32[]{:S(2)}, u32[]{:S(2)}) collective-permute-start(f32[32,128]{1,0:T(8,128)S(1)} %get-tuple-element.44), channel_id=1, source_target_pairs={{0,3},{1,2},{2,1},{3,0},{4,7},{5,6},{6,5},{7,4},{8,11},{9,10},{10,... | collective-permute-start | bytes 49160 | tf_op jit(solution)/shard_map/ppermute | solution.py:39
  48.8 0.9 %collective-permute-done.16 = f32[32,128]{1,0:T(8,128)S(1)} collective-permute-done((f32[32,128]{1,0:T(8,128)S(1)}, f32[32,128]{1,0:T(8,128)S(1)}, u32[]{:S(2)}, u32[]{:S(2)}) %collective-permute-start.16) | collective-permute-done | bytes 16416 | tf_op jit(solution)/shard_map/ppermute | solution.py:39
  49.6 3.8 %collective-permute-done.17 = f32[32,128]{1,0:T(8,128)S(1)} collective-permute-done((f32[32,128]{1,0:T(8,128)S(1)}, f32[32,128]{1,0:T(8,128)S(1)}, u32[]{:S(2)}, u32[]{:S(2)}) %collective-permute-start.17) | collective-permute-done | bytes 16416 | tf_op jit(solution)/shard_map/ppermute | solution.py:39
  53.4 0.9 %collective-permute-start.19 = (f32[32,128]{1,0:T(8,128)S(1)}, f32[32,128]{1,0:T(8,128)S(1)}, u32[]{:S(2)}, u32[]{:S(2)}) collective-permute-start(f32[32,128]{1,0:T(8,128)S(1)} %add_add_fusion), channel_id=1, source_target_pairs={{0,8},{4,12},{8,0},{12,4},{1,9},{5,13},{9,1},{13,5},{2,10},{6,14},... | collective-permute-start | bytes 49160 | tf_op jit(solution)/shard_map/ppermute | solution.py:39
  54.4 0.9 %collective-permute-start.20 = (f32[32,128]{1,0:T(8,128)S(1)}, f32[32,128]{1,0:T(8,128)S(1)}, u32[]{:S(2)}, u32[]{:S(2)}) collective-permute-start(f32[32,128]{1,0:T(8,128)S(1)} %add_add_fusion), channel_id=1, source_target_pairs={{0,12},{4,8},{8,4},{12,0},{1,13},{5,9},{9,5},{13,1},{2,14},{6,10},... | collective-permute-start | bytes 49160 | tf_op jit(solution)/shard_map/ppermute | solution.py:39
  55.3 1.9 %collective-permute-done.19 = f32[32,128]{1,0:T(8,128)S(1)} collective-permute-done((f32[32,128]{1,0:T(8,128)S(1)}, f32[32,128]{1,0:T(8,128)S(1)}, u32[]{:S(2)}, u32[]{:S(2)}) %collective-permute-start.19) | collective-permute-done | bytes 16416 | tf_op jit(solution)/shard_map/ppermute | solution.py:39
  57.2 0.3 collective-permute-done.20
  57.6 0.6 %add_bitcast_fusion = f32[1,32,128]{2,1,0:T(8,128)} fusion(f32[32,128]{1,0:T(8,128)S(1)} %copy-done.1, f32[32,128]{1,0:T(8,128)S(1)} %collective-permute-done.20, f32[32,128]{1,0:T(8,128)S(1)} %collective-permute-done.19, f32[32,128]{1,0:T(8,128)S(1)} %add_add_fusion, f32[32,128]{1,0:T(8,128)S(1)} %collective-permute-done.18, pred[]{:T(512)S(6)} %lt.14, ...), kind=kLoop, calls=%fused_computation.1 | loop fusion | flops 28672 | bytes 98307 | tf_op jit(solution)/shard_map/broadcast_in_dim | solution.py:510
  (23 shorter events, 0.1 us)
Async XLA Ops:
  0.0 8.9 %collective-permute-start.3 = (bf16[32,3072]{1,0:T(8,128)(2,1)}, bf16[32,3072]{1,0:T(8,128)(2,1)S(1)}, u32[]{:S(2)}, u32[]{:S(2)}) collective-permute-start(bf16[32,3072]{1,0:T(8,128)(2,1)} %inw_hbm.1), channel_id=1, source_target_pairs={{0,8},{4,12},{8,0},{12,4},{1,9},{5,13},{9,1},{13,5},{2,10},{6,14},... | collective-permute-start | bytes 589832 | tf_op jit(solution)/shard_map/ppermute | solution.py:39
  3.0 9.3 %collective-permute-start = (bf16[768,128]{1,0:T(8,128)(2,1)}, bf16[768,128]{1,0:T(8,128)(2,1)S(1)}, u32[]{:S(2)}, u32[]{:S(2)}) collective-permute-start(bf16[768,128]{1,0:T(8,128)(2,1)} %refs_0_.1), channel_id=1, source_target_pairs={{0,8},{4,12},{8,0},{12,4},{1,9},{5,13},{9,1},{13,5},{2,10},{6,14},... | collective-permute-start | bytes 589832 | tf_op jit(solution)/shard_map/ppermute | solution.py:39
  3.0 13.4 %collective-permute-start.2 = (bf16[32,3072]{1,0:T(8,128)(2,1)}, bf16[32,3072]{1,0:T(8,128)(2,1)S(1)}, u32[]{:S(2)}, u32[]{:S(2)}) collective-permute-start(bf16[32,3072]{1,0:T(8,128)(2,1)} %inw_hbm.1), channel_id=1, source_target_pairs={{0,4},{4,0},{8,12},{12,8},{1,5},{5,1},{9,13},{13,9},{2,6},{6,2},{1... | collective-permute-start | bytes 589832 | tf_op jit(solution)/shard_map/ppermute | solution.py:39
  8.9 10.1 %collective-permute-start.4 = (bf16[32,3072]{1,0:T(8,128)(2,1)S(1)}, bf16[32,3072]{1,0:T(8,128)(2,1)S(1)}, u32[]{:S(2)}, u32[]{:S(2)}) collective-permute-start(bf16[32,3072]{1,0:T(8,128)(2,1)S(1)} %collective-permute-done.3.refs_1_), channel_id=1, source_target_pairs={{0,4},{4,0},{8,12},{12,8},{1,5},{5,1},{9,13},{13,9},{2,6},{6,2},{1... | collective-permute-start | bytes 589832 | tf_op jit(solution)/shard_map/ppermute | solution.py:39
  8.9 20.0 %collective-permute-start.8 = (bf16[768,128]{1,0:T(8,128)(2,1)}, bf16[768,128]{1,0:T(8,128)(2,1)S(1)}, u32[]{:S(2)}, u32[]{:S(2)}) collective-permute-start(bf16[768,128]{1,0:T(8,128)(2,1)} %refs_0_.1), channel_id=1, source_target_pairs={{0,4},{4,0},{8,12},{12,8},{1,5},{5,1},{9,13},{13,9},{2,6},{6,2},{1... | collective-permute-start | bytes 589832 | tf_op jit(solution)/shard_map/ppermute | solution.py:39
  12.3 18.2 %collective-permute-start.1 = (bf16[768,128]{1,0:T(8,128)(2,1)S(1)}, bf16[768,128]{1,0:T(8,128)(2,1)S(1)}, u32[]{:S(2)}, u32[]{:S(2)}) collective-permute-start(bf16[768,128]{1,0:T(8,128)(2,1)S(1)} %collective-permute-done.refs_2_), channel_id=1, source_target_pairs={{0,4},{4,0},{8,12},{12,8},{1,5},{5,1},{9,13},{13,9},{2,6},{6,2},{1... | collective-permute-start | bytes 589832 | tf_op jit(solution)/shard_map/ppermute | solution.py:39
  14.5 7.2 %collective-permute-start.5 = (f32[50,128]{1,0:T(8,128)S(1)}, f32[50,128]{1,0:T(8,128)S(1)}, u32[]{:S(2)}, u32[]{:S(2)}) collective-permute-start(f32[50,128]{1,0:T(8,128)S(1)} %shard_map.83.refs_0_), channel_id=1, source_target_pairs={{0,1},{1,0},{2,3},{3,2},{4,5},{5,4},{6,7},{7,6},{8,9},{9,8},{10,11... | collective-permute-start | bytes 76808 | tf_op jit(solution)/shard_map/ppermute | solution.py:39
  16.4 5.3 %collective-permute-start.6 = (f32[50,128]{1,0:T(8,128)S(1)}, f32[50,128]{1,0:T(8,128)S(1)}, u32[]{:S(2)}, u32[]{:S(2)}) collective-permute-start(f32[50,128]{1,0:T(8,128)S(1)} %shard_map.83.refs_0_), channel_id=1, source_target_pairs={{0,2},{1,3},{2,0},{3,1},{4,6},{5,7},{6,4},{7,5},{8,10},{9,11},{10,... | collective-permute-start | bytes 76808 | tf_op jit(solution)/shard_map/ppermute | solution.py:39
  19.0 5.7 %collective-permute-start.7 = (f32[50,128]{1,0:T(8,128)S(1)}, f32[50,128]{1,0:T(8,128)S(1)}, u32[]{:S(2)}, u32[]{:S(2)}) collective-permute-start(f32[50,128]{1,0:T(8,128)S(1)} %shard_map.83.refs_0_), channel_id=1, source_target_pairs={{0,3},{1,2},{2,1},{3,0},{4,7},{5,6},{6,5},{7,4},{8,11},{9,10},{10,... | collective-permute-start | bytes 76808 | tf_op jit(solution)/shard_map/ppermute | solution.py:39
  24.7 4.3 %copy-start = (bf16[768,128]{1,0:T(8,128)(2,1)S(1)}, bf16[768,128]{1,0:T(8,128)(2,1)}, u32[]{:S(2)}) copy-start(bf16[768,128]{1,0:T(8,128)(2,1)} %refs_0_.1) | copy-start | bytes 589828
  30.5 27.1 %copy-start.1 = (f32[32,128]{1,0:T(8,128)S(1)}, f32[32,128]{1,0:T(8,128)}, u32[]{:S(2)}) copy-start(f32[32,128]{1,0:T(8,128)} %start_hbm.1) | copy-start | bytes 49156
  31.3 4.0 %collective-permute-start.10 = (bf16[128,128]{1,0:T(8,128)(2,1)S(1)}, bf16[128,128]{1,0:T(8,128)(2,1)S(1)}, u32[]{:S(2)}, u32[]{:S(2)}) collective-permute-start(bf16[128,128]{1,0:T(8,128)(2,1)S(1)} %get-tuple-element.38), channel_id=1, source_target_pairs={{0,8},{4,12},{8,0},{12,4},{1,9},{5,13},{9,1},{13,5},{2,10},{6,14},... | collective-permute-start | bytes 98312 | tf_op jit(solution)/shard_map/ppermute | solution.py:39
  32.8 3.3 %collective-permute-start.11 = (bf16[128,128]{1,0:T(8,128)(2,1)S(1)}, bf16[128,128]{1,0:T(8,128)(2,1)S(1)}, u32[]{:S(2)}, u32[]{:S(2)}) collective-permute-start(bf16[128,128]{1,0:T(8,128)(2,1)S(1)} %get-tuple-element.38), channel_id=1, source_target_pairs={{0,12},{4,8},{8,4},{12,0},{1,13},{5,9},{9,5},{13,1},{2,14},{6,10},... | collective-permute-start | bytes 98312 | tf_op jit(solution)/shard_map/ppermute | solution.py:39
  32.8 3.3 %collective-permute-start.9 = (bf16[128,128]{1,0:T(8,128)(2,1)S(1)}, bf16[128,128]{1,0:T(8,128)(2,1)S(1)}, u32[]{:S(2)}, u32[]{:S(2)}) collective-permute-start(bf16[128,128]{1,0:T(8,128)(2,1)S(1)} %get-tuple-element.38), channel_id=1, source_target_pairs={{0,4},{4,0},{8,12},{12,8},{1,5},{5,1},{9,13},{13,9},{2,6},{6,2},{1... | collective-permute-start | bytes 98312 | tf_op jit(solution)/shard_map/ppermute | solution.py:39
  36.2 4.5 %collective-permute-start.12 = (bf16[128,128]{1,0:T(8,128)(2,1)S(1)}, bf16[128,128]{1,0:T(8,128)(2,1)S(1)}, u32[]{:S(2)}, u32[]{:S(2)}) collective-permute-start(bf16[128,128]{1,0:T(8,128)(2,1)S(1)} %add_convert_fusion.refs_0_), channel_id=1, source_target_pairs={{0,1},{1,0},{2,3},{3,2},{4,5},{5,4},{6,7},{7,6},{8,9},{9,8},{10,11... | collective-permute-start | bytes 98312 | tf_op jit(solution)/shard_map/ppermute | solution.py:39
  36.3 5.2 %collective-permute-start.13 = (bf16[128,128]{1,0:T(8,128)(2,1)S(1)}, bf16[128,128]{1,0:T(8,128)(2,1)S(1)}, u32[]{:S(2)}, u32[]{:S(2)}) collective-permute-start(bf16[128,128]{1,0:T(8,128)(2,1)S(1)} %add_convert_fusion.refs_0_), channel_id=1, source_target_pairs={{0,2},{1,3},{2,0},{3,1},{4,6},{5,7},{6,4},{7,5},{8,10},{9,11},{10,... | collective-permute-start | bytes 98312 | tf_op jit(solution)/shard_map/ppermute | solution.py:39
  37.7 5.7 %collective-permute-start.14 = (bf16[128,128]{1,0:T(8,128)(2,1)S(1)}, bf16[128,128]{1,0:T(8,128)(2,1)S(1)}, u32[]{:S(2)}, u32[]{:S(2)}) collective-permute-start(bf16[128,128]{1,0:T(8,128)(2,1)S(1)} %add_convert_fusion.refs_0_), channel_id=1, source_target_pairs={{0,3},{1,2},{2,1},{3,0},{4,7},{5,6},{6,5},{7,4},{8,11},{9,10},{10,... | collective-permute-start | bytes 98312 | tf_op jit(solution)/shard_map/ppermute | solution.py:39
  44.3 4.5 %collective-permute-start.15 = (f32[32,128]{1,0:T(8,128)S(1)}, f32[32,128]{1,0:T(8,128)S(1)}, u32[]{:S(2)}, u32[]{:S(2)}) collective-permute-start(f32[32,128]{1,0:T(8,128)S(1)} %get-tuple-element.42), channel_id=1, source_target_pairs={{0,1},{1,0},{2,3},{3,2},{4,5},{5,4},{6,7},{7,6},{8,9},{9,8},{10,11... | collective-permute-start | bytes 49160 | tf_op jit(solution)/shard_map/ppermute | solution.py:39
  44.4 5.2 %collective-permute-start.16 = (f32[32,128]{1,0:T(8,128)S(1)}, f32[32,128]{1,0:T(8,128)S(1)}, u32[]{:S(2)}, u32[]{:S(2)}) collective-permute-start(f32[32,128]{1,0:T(8,128)S(1)} %get-tuple-element.43), channel_id=1, source_target_pairs={{0,2},{1,3},{2,0},{3,1},{4,6},{5,7},{6,4},{7,5},{8,10},{9,11},{10,... | collective-permute-start | bytes 49160 | tf_op jit(solution)/shard_map/ppermute | solution.py:39
  47.9 5.5 %collective-permute-start.17 = (f32[32,128]{1,0:T(8,128)S(1)}, f32[32,128]{1,0:T(8,128)S(1)}, u32[]{:S(2)}, u32[]{:S(2)}) collective-permute-start(f32[32,128]{1,0:T(8,128)S(1)} %get-tuple-element.44), channel_id=1, source_target_pairs={{0,3},{1,2},{2,1},{3,0},{4,7},{5,6},{6,5},{7,4},{8,11},{9,10},{10,... | collective-permute-start | bytes 49160 | tf_op jit(solution)/shard_map/ppermute | solution.py:39
  53.4 1.9 %collective-permute-start.18 = (f32[32,128]{1,0:T(8,128)S(1)}, f32[32,128]{1,0:T(8,128)S(1)}, u32[]{:S(2)}, u32[]{:S(2)}) collective-permute-start(f32[32,128]{1,0:T(8,128)S(1)} %add_add_fusion), channel_id=1, source_target_pairs={{0,4},{4,0},{8,12},{12,8},{1,5},{5,1},{9,13},{13,9},{2,6},{6,2},{1... | collective-permute-start | bytes 49160 | tf_op jit(solution)/shard_map/ppermute | solution.py:39
  53.4 3.8 %collective-permute-start.19 = (f32[32,128]{1,0:T(8,128)S(1)}, f32[32,128]{1,0:T(8,128)S(1)}, u32[]{:S(2)}, u32[]{:S(2)}) collective-permute-start(f32[32,128]{1,0:T(8,128)S(1)} %add_add_fusion), channel_id=1, source_target_pairs={{0,8},{4,12},{8,0},{12,4},{1,9},{5,13},{9,1},{13,5},{2,10},{6,14},... | collective-permute-start | bytes 49160 | tf_op jit(solution)/shard_map/ppermute | solution.py:39
  54.4 3.2 %collective-permute-start.20 = (f32[32,128]{1,0:T(8,128)S(1)}, f32[32,128]{1,0:T(8,128)S(1)}, u32[]{:S(2)}, u32[]{:S(2)}) collective-permute-start(f32[32,128]{1,0:T(8,128)S(1)} %add_add_fusion), channel_id=1, source_target_pairs={{0,12},{4,8},{8,4},{12,0},{1,13},{5,9},{9,5},{13,1},{2,14},{6,10},... | collective-permute-start | bytes 49160 | tf_op jit(solution)/shard_map/ppermute | solution.py:39

commit v8 on v7

--- a/solution.py
+++ b/solution.py
@@ -37,6 +37,29 @@
 def swap(value, axis, k):
     n = lax.axis_size(axis)
     return lax.ppermute(value, axis, [(i, i ^ k) for i in range(n)])
+
+
+def hub_route(value, k):
+    n = lax.axis_size("tensor")
+    pairs = [
+        (t * n + z, t * n + (z ^ k) if t % 2 else (t ^ 2) * n + z)
+        for t in range(lax.axis_size("tm"))
+        for z in range(n)
+    ]
+    return lax.ppermute(value, ("tm", "tensor"), pairs)
+
+
+def hub_earlier_sum(value):
+    stacked = jnp.stack([swap(value, "tm", 1), value])
+    total = stacked.astype(F32)
+    for k in (2, 3, 1):
+        total = total + hub_route(stacked, k).astype(F32)
+    pair = (total[0] + total[1]).astype(BF16)
+    straight, crossed = swap(pair, "tm", 2), swap(pair, "tm", 3)
+    me = lax.axis_index("tm")
+    odd, high = me % 2 == 1, me >= 2
+    far = jnp.where(odd, straight, crossed).astype(F32)
+    return jnp.where(high, far, 0.0) + jnp.where(odd, total[0], 0.0)
 
 
 def gather_parts(value, axis):
@@ -476,8 +499,11 @@
     small = is_small("tensor")
     for iteration in range(1, ITERS):
         last = iteration + 1 == ITERS
-        earlier = earlier_sum(vel, False)
-        if small:
+        hub = lax.axis_size("tm") == 4 and lax.axis_size("tensor") == 4
+        earlier = None if hub else earlier_sum(vel, False)
+        if hub:
+            pieces = [hub_earlier_sum(vel)]
+        elif small:
             pieces = gather_parts(earlier.astype(BF16), "tensor")
         else:
             pieces = [lax.psum(earlier, "tensor")]

time: 58.3 us -> 57 us (0.978)
  starting transfers between devices: 20.9 us -> 19.3 us
    ppermute x21 -> x18, starting transfers between devices: 20.9 us -> 15.8 us  [swap(): return lax.ppermute(value, axis, [(i, i ^ k) for i in range(n)])]
    ppermute x0 -> x3, starting transfers between devices: none -> 3.59 us  [hub_route(): return lax.ppermute(value, ('tm', 'tensor'), pairs)]
    ppermute x0 -> x3, waiting for transfers between devices: none -> 2.94 us  [hub_route(): return lax.ppermute(value, ('tm', 'tensor'), pairs)]
    ppermute x21 -> x18, waiting for transfers between devices: 24.1 us -> 21.3 us  [swap(): return lax.ppermute(value, axis, [(i, i ^ k) for i in range(n)])]
  transfers between devices with their start and end apart: 21 -> 21, of which waited for: 11 -> 13; matrix products, arithmetic and copies ran while one was open for 0% -> 0% of each run, Pallas kernels for 16% -> 17%
where the time goes in v8:
time: 57 us; the launch traced here: 56.8 us
  waiting for transfers between devices  24.3 us (43%)
  starting transfers between devices  19.3 us (34%)
  Pallas kernels  11 us (19%)
  between operations  1.45 us (3%)
  other arithmetic  0.69 us (1%)
    ppermute x18, waiting for transfers between devices, swap(): return lax.ppermute(value, axis, [(i, i ^ k) for i in range(n)])  21.3 us
    ppermute x18, starting transfers between devices, swap(): return lax.ppermute(value, axis, [(i, i ^ k) for i in range(n)])  15.8 us
    pallas_call x6, Pallas kernels, call(): pl.pallas_call(kernel, out_shape=outs, in_specs=in_specs, out_specs=[VMEM...  11 us
    ppermute x3, starting transfers between devices, hub_route(): return lax.ppermute(value, ('tm', 'tensor'), pairs)  3.59 us
    ppermute x3, waiting for transfers between devices, hub_route(): return lax.ppermute(value, ('tm', 'tensor'), pairs)  2.94 us
  transfers between devices with their start and end apart: 21, of which 13 were waited for; matrix products, arithmetic and copies ran while one was open for 0% of the time, Pallas kernels for 17%

profile of v8, /device:TPU:0, one launch (start us, length us, event | category | flops | bytes accessed | tf_op | source)
XLA Modules:
  0.0 56.8 jit_solution(9049537894775701814)
XLA Ops:
  0.0 3.0 %collective-permute-start.3 = (bf16[32,3072]{1,0:T(8,128)(2,1)}, bf16[32,3072]{1,0:T(8,128)(2,1)S(1)}, u32[]{:S(2)}, u32[]{:S(2)}) collective-permute-start(bf16[32,3072]{1,0:T(8,128)(2,1)} %inw_hbm.1), channel_id=1, source_target_pairs={{0,8},{4,12},{8,0},{12,4},{1,9},{5,13},{9,1},{13,5},{2,10},{6,14},... | collective-permute-start | bytes 589832 | tf_op jit(solution)/shard_map/ppermute | solution.py:39
  3.0 5.9 %collective-permute-done.3.refs_1_ = bf16[32,3072]{1,0:T(8,128)(2,1)S(1)} collective-permute-done((bf16[32,3072]{1,0:T(8,128)(2,1)}, bf16[32,3072]{1,0:T(8,128)(2,1)S(1)}, u32[]{:S(2)}, u32[]{:S(2)}) %collective-permute-start.3) | collective-permute-done | bytes 196640 | tf_op jit(solution)/shard_map/ppermute | solution.py:39
  8.9 0.5 collective-permute-start.8
  9.4 2.9 %collective-permute-done.refs_2_ = bf16[768,128]{1,0:T(8,128)(2,1)S(1)} collective-permute-done((bf16[768,128]{1,0:T(8,128)(2,1)}, bf16[768,128]{1,0:T(8,128)(2,1)S(1)}, u32[]{:S(2)}, u32[]{:S(2)}) %collective-permute-start) | collective-permute-done | bytes 196640 | tf_op jit(solution)/shard_map/ppermute | solution.py:39
  12.9 1.6 %shard_map.83.refs_0_ = f32[50,128]{1,0:T(8,128)S(1)} custom-call(s32[1]{0:T(128)S(6)} %copy.9.time_ref, bf16[256,2304]{1,0:T(8,128)(2,1)} %weight_hbm.1, f32[32,128]{1,0:T(8,128)} %start_hbm.1), custom_call_target="tpu_custom_call" | custom-call | bytes 4194304 | tf_op jit(solution)/shard_map/pallas_call | solution.py:334
  14.5 1.9 %collective-permute-start.5 = (f32[50,128]{1,0:T(8,128)S(1)}, f32[50,128]{1,0:T(8,128)S(1)}, u32[]{:S(2)}, u32[]{:S(2)}) collective-permute-start(f32[50,128]{1,0:T(8,128)S(1)} %shard_map.83.refs_0_), channel_id=1, source_target_pairs={{0,1},{1,0},{2,3},{3,2},{4,5},{5,4},{6,7},{7,6},{8,9},{9,8},{10,11... | collective-permute-start | bytes 76808 | tf_op jit(solution)/shard_map/ppermute | solution.py:39
  16.4 2.6 %collective-permute-start.6 = (f32[50,128]{1,0:T(8,128)S(1)}, f32[50,128]{1,0:T(8,128)S(1)}, u32[]{:S(2)}, u32[]{:S(2)}) collective-permute-start(f32[50,128]{1,0:T(8,128)S(1)} %shard_map.83.refs_0_), channel_id=1, source_target_pairs={{0,2},{1,3},{2,0},{3,1},{4,6},{5,7},{6,4},{7,5},{8,10},{9,11},{10,... | collective-permute-start | bytes 76808 | tf_op jit(solution)/shard_map/ppermute | solution.py:39
  19.7 2.0 %shard_map.82 = (bf16[3072,512]{1,0:T(8,128)(2,1)S(1)}, bf16[4,32,3072]{2,1,0:T(8,128)(2,1)S(1)}, f32[128,128]{1,0:T(8,128)S(1)}, bf16[384,128]{1,0:T(8,128)(2,1)S(1)}, f32[8,128]{1,0:T(8,128)S(1)}) custom-call(s32[1]{0:T(128)S(6)} %copy.10.weight_ref, bf16[3072,1536]{1,0:T(8,128)(2,1)} %refs_7_.1, bf16[32,3072]{1,0:T(8,128)(2,1)} %inw_hbm.1, ...), custom_call_target="tpu_custom_call" | custom-call | bytes 4194304 | tf_op jit(solution)/shard_map/pallas_call | solution.py:334
  21.7 2.9 %collective-permute-done.7.refs_3_ = f32[50,128]{1,0:T(8,128)S(1)} collective-permute-done((f32[50,128]{1,0:T(8,128)S(1)}, f32[50,128]{1,0:T(8,128)S(1)}, u32[]{:S(2)}, u32[]{:S(2)}) %collective-permute-start.7) | collective-permute-done | bytes 25632 | tf_op jit(solution)/shard_map/ppermute | solution.py:39
  24.7 4.2 %shard_map.84 = (bf16[256,1536]{1,0:T(8,128)(2,1)S(1)}, f32[8,1536]{1,0:T(8,128)S(1)}, f32[128,128]{1,0:T(8,128)S(1)}, f32[4,128,8]{2,1,0:T(8,128)S(1)}, bf16[512,3072]{1,0:T(8,128)(2,1)S(1)}) custom-call(f32[50,128]{1,0:T(8,128)S(1)} %shard_map.83.refs_0_, f32[50,128]{1,0:T(8,128)S(1)} %collective-permute-done.5.refs_1_, ...), custom_call_target="tpu_custom_call" | custom-call | bytes 4194304 | tf_op jit(solution)/shard_map/pallas_call | solution.py:334
  29.0 1.5 %shard_map.85 = (bf16[128,512]{1,0:T(8,128)(2,1)S(1)}, f32[512,128]{1,0:T(8,128)S(1)}, f32[128,128]{1,0:T(8,128)S(1)}) custom-call(bf16[768,128]{1,0:T(8,128)(2,1)S(1)} %copy-done, bf16[768,128]{1,0:T(8,128)(2,1)S(1)} %collective-permute-done.8.refs_1_, bf16[768,128]{1,0:T(8,128)(2,1)S(1)} %collective-permute-done.refs_2_, ...), custom_call_target="tpu_custom_call" | custom-call | bytes 4194304 | tf_op jit(solution)/shard_map/pallas_call | solution.py:334
  30.5 0.7 %shard_map.86 = (bf16[512,128]{1,0:T(8,128)(2,1)S(1)}, bf16[256,128]{1,0:T(8,128)(2,1)S(1)}, bf16[128,128]{1,0:T(8,128)(2,1)S(1)}) custom-call(bf16[768,128]{1,0:T(8,128)(2,1)S(1)} %collective-permute-done.1.refs_0_, f32[8,128]{1,0:T(8,128)S(1)} %get-tuple-element.25.refs_1_, f32[4,128,8]{2,1,0:T(8,128)S(1)} %get-tuple-element.29.refs_7_.refs_2_, ...), custom_call_target="tpu_custom_call" | custom-call | bytes 4194304 | tf_op jit(solution)/shard_map/pallas_call | solution.py:334
  31.3 1.2 %collective-permute-done.9 = bf16[128,128]{1,0:T(8,128)(2,1)S(1)} collective-permute-done((bf16[128,128]{1,0:T(8,128)(2,1)S(1)}, bf16[128,128]{1,0:T(8,128)(2,1)S(1)}, u32[]{:S(2)}, u32[]{:S(2)}) %collective-permute-start.9) | collective-permute-done | bytes 32800 | tf_op jit(solution)/shard_map/ppermute | solution.py:39
  32.5 1.6 %collective-permute-start.10 = (bf16[2,128,128]{2,1,0:T(8,128)(2,1)S(1)}, bf16[2,128,128]{2,1,0:T(8,128)(2,1)S(1)}, u32[]{:S(2)}, u32[]{:S(2)}) collective-permute-start(bf16[2,128,128]{2,1,0:T(8,128)(2,1)S(1)} %pad_maximum_fusion), channel_id=1, source_target_pairs={{0,8},{1,9},{2,10},{3,11},{4,6},{5,7},{6,4},{7,5},{8,0},{9,1},{10,... | collective-permute-start | bytes 196616 | tf_op jit(solution)/shard_map/ppermute | solution.py:49
  34.1 0.5 collective-permute-start.11
  34.6 1.5 %collective-permute-start.12 = (bf16[2,128,128]{2,1,0:T(8,128)(2,1)S(1)}, bf16[2,128,128]{2,1,0:T(8,128)(2,1)S(1)}, u32[]{:S(2)}, u32[]{:S(2)}) collective-permute-start(bf16[2,128,128]{2,1,0:T(8,128)(2,1)S(1)} %pad_maximum_fusion), channel_id=1, source_target_pairs={{0,8},{1,9},{2,10},{3,11},{4,5},{5,4},{6,7},{7,6},{8,0},{9,1},{10,... | collective-permute-start | bytes 196616 | tf_op jit(solution)/shard_map/ppermute | solution.py:49
  36.1 0.7 %collective-permute-done.10 = bf16[2,128,128]{2,1,0:T(8,128)(2,1)S(1)} collective-permute-done((bf16[2,128,128]{2,1,0:T(8,128)(2,1)S(1)}, bf16[2,128,128]{2,1,0:T(8,128)(2,1)S(1)}, u32[]{:S(2)}, u32[]{:S(2)}) %collective-permute-start.10) | collective-permute-done | bytes 65568 | tf_op jit(solution)/shard_map/ppermute | solution.py:49
  36.9 1.5 %collective-permute-done.11 = bf16[2,128,128]{2,1,0:T(8,128)(2,1)S(1)} collective-permute-done((bf16[2,128,128]{2,1,0:T(8,128)(2,1)S(1)}, bf16[2,128,128]{2,1,0:T(8,128)(2,1)S(1)}, u32[]{:S(2)}, u32[]{:S(2)}) %collective-permute-start.11) | collective-permute-done | bytes 65568 | tf_op jit(solution)/shard_map/ppermute | solution.py:49
  38.4 0.7 %collective-permute-done.12 = bf16[2,128,128]{2,1,0:T(8,128)(2,1)S(1)} collective-permute-done((bf16[2,128,128]{2,1,0:T(8,128)(2,1)S(1)}, bf16[2,128,128]{2,1,0:T(8,128)(2,1)S(1)}, u32[]{:S(2)}, u32[]{:S(2)}) %collective-permute-start.12) | collective-permute-done | bytes 65568 | tf_op jit(solution)/shard_map/ppermute | solution.py:49
  39.1 1.4 %collective-permute-start.13 = (bf16[128,128]{1,0:T(8,128)(2,1)S(1)}, bf16[128,128]{1,0:T(8,128)(2,1)S(1)}, u32[]{:S(2)}, u32[]{:S(2)}) collective-permute-start(bf16[128,128]{1,0:T(8,128)(2,1)S(1)} %fusion.1), channel_id=1, source_target_pairs={{0,8},{4,12},{8,0},{12,4},{1,9},{5,13},{9,1},{13,5},{2,10},{6,14},... | collective-permute-start | bytes 98312 | tf_op jit(solution)/shard_map/ppermute | solution.py:39
  40.5 2.6 %collective-permute-done.13 = bf16[128,128]{1,0:T(8,128)(2,1)S(1)} collective-permute-done((bf16[128,128]{1,0:T(8,128)(2,1)S(1)}, bf16[128,128]{1,0:T(8,128)(2,1)S(1)}, u32[]{:S(2)}, u32[]{:S(2)}) %collective-permute-start.13) | collective-permute-done | bytes 32800 | tf_op jit(solution)/shard_map/ppermute | solution.py:39
  43.1 0.7 %collective-permute-done.14 = bf16[128,128]{1,0:T(8,128)(2,1)S(1)} collective-permute-done((bf16[128,128]{1,0:T(8,128)(2,1)S(1)}, bf16[128,128]{1,0:T(8,128)(2,1)S(1)}, u32[]{:S(2)}, u32[]{:S(2)}) %collective-permute-start.14) | collective-permute-done | bytes 32800 | tf_op jit(solution)/shard_map/ppermute | solution.py:39
  43.9 0.9 %shard_map.87 = (f32[32,128]{1,0:T(8,128)S(1)}, f32[32,128]{1,0:T(8,128)S(1)}, f32[32,128]{1,0:T(8,128)S(1)}, f32[32,128]{1,0:T(8,128)S(1)}) custom-call(f32[128,128]{1,0:T(8,128)S(1)} %bitcast_add_fusion.refs_0_, f32[8,128]{1,0:T(8,128)S(1)} %get-tuple-element.25.refs_1_, f32[128,128]{1,0:T(8,128)S(1)} %get-tuple-element.31.refs_3_.refs_8_.refs_2_, ...), custom_call_target="tpu_custom_call" | custom-call | bytes 4194304 | tf_op jit(solution)/shard_map/pallas_call | solution.py:334
  44.9 1.8 %collective-permute-start.16 = (f32[32,128]{1,0:T(8,128)S(1)}, f32[32,128]{1,0:T(8,128)S(1)}, u32[]{:S(2)}, u32[]{:S(2)}) collective-permute-start(f32[32,128]{1,0:T(8,128)S(1)} %get-tuple-element.43), channel_id=1, source_target_pairs={{0,2},{1,3},{2,0},{3,1},{4,6},{5,7},{6,4},{7,5},{8,10},{9,11},{10,... | collective-permute-start | bytes 49160 | tf_op jit(solution)/shard_map/ppermute | solution.py:39
  46.7 2.6 %collective-permute-start.17 = (f32[32,128]{1,0:T(8,128)S(1)}, f32[32,128]{1,0:T(8,128)S(1)}, u32[]{:S(2)}, u32[]{:S(2)}) collective-permute-start(f32[32,128]{1,0:T(8,128)S(1)} %get-tuple-element.44), channel_id=1, source_target_pairs={{0,3},{1,2},{2,1},{3,0},{4,7},{5,6},{6,5},{7,4},{8,11},{9,10},{10,... | collective-permute-start | bytes 49160 | tf_op jit(solution)/shard_map/ppermute | solution.py:39
  49.3 0.3 collective-permute-done.16
  49.6 2.6 %collective-permute-done.17 = f32[32,128]{1,0:T(8,128)S(1)} collective-permute-done((f32[32,128]{1,0:T(8,128)S(1)}, f32[32,128]{1,0:T(8,128)S(1)}, u32[]{:S(2)}, u32[]{:S(2)}) %collective-permute-start.17) | collective-permute-done | bytes 16416 | tf_op jit(solution)/shard_map/ppermute | solution.py:39
  52.2 0.8 %collective-permute-start.19 = (f32[32,128]{1,0:T(8,128)S(1)}, f32[32,128]{1,0:T(8,128)S(1)}, u32[]{:S(2)}, u32[]{:S(2)}) collective-permute-start(f32[32,128]{1,0:T(8,128)S(1)} %add_add_fusion), channel_id=1, source_target_pairs={{0,8},{4,12},{8,0},{12,4},{1,9},{5,13},{9,1},{13,5},{2,10},{6,14},... | collective-permute-start | bytes 49160 | tf_op jit(solution)/shard_map/ppermute | solution.py:39
  53.0 1.1 %collective-permute-start.20 = (f32[32,128]{1,0:T(8,128)S(1)}, f32[32,128]{1,0:T(8,128)S(1)}, u32[]{:S(2)}, u32[]{:S(2)}) collective-permute-start(f32[32,128]{1,0:T(8,128)S(1)} %add_add_fusion), channel_id=1, source_target_pairs={{0,12},{4,8},{8,4},{12,0},{1,13},{5,9},{9,5},{13,1},{2,14},{6,10},... | collective-permute-start | bytes 49160 | tf_op jit(solution)/shard_map/ppermute | solution.py:39
  54.1 2.0 %collective-permute-done.19 = f32[32,128]{1,0:T(8,128)S(1)} collective-permute-done((f32[32,128]{1,0:T(8,128)S(1)}, f32[32,128]{1,0:T(8,128)S(1)}, u32[]{:S(2)}, u32[]{:S(2)}) %collective-permute-start.19) | collective-permute-done | bytes 16416 | tf_op jit(solution)/shard_map/ppermute | solution.py:39
  56.0 0.1 collective-permute-done.20
  56.2 0.6 %add_bitcast_fusion = f32[1,32,128]{2,1,0:T(8,128)} fusion(f32[32,128]{1,0:T(8,128)S(1)} %copy-done.1, f32[32,128]{1,0:T(8,128)S(1)} %collective-permute-done.20, f32[32,128]{1,0:T(8,128)S(1)} %collective-permute-done.19, f32[32,128]{1,0:T(8,128)S(1)} %add_add_fusion, f32[32,128]{1,0:T(8,128)S(1)} %collective-permute-done.18, pred[]{:T(512)S(6)} %lt.18, ...), kind=kLoop, calls=%fused_computation.6 | loop fusion | flops 28672 | bytes 98307 | tf_op jit(solution)/shard_map/broadcast_in_dim | solution.py:536
  (26 shorter events, 0.3 us)
Async XLA Ops:
  0.0 8.9 %collective-permute-start.3 = (bf16[32,3072]{1,0:T(8,128)(2,1)}, bf16[32,3072]{1,0:T(8,128)(2,1)S(1)}, u32[]{:S(2)}, u32[]{:S(2)}) collective-permute-start(bf16[32,3072]{1,0:T(8,128)(2,1)} %inw_hbm.1), channel_id=1, source_target_pairs={{0,8},{4,12},{8,0},{12,4},{1,9},{5,13},{9,1},{13,5},{2,10},{6,14},... | collective-permute-start | bytes 589832 | tf_op jit(solution)/shard_map/ppermute | solution.py:39
  3.0 9.3 %collective-permute-start = (bf16[768,128]{1,0:T(8,128)(2,1)}, bf16[768,128]{1,0:T(8,128)(2,1)S(1)}, u32[]{:S(2)}, u32[]{:S(2)}) collective-permute-start(bf16[768,128]{1,0:T(8,128)(2,1)} %refs_0_.1), channel_id=1, source_target_pairs={{0,8},{4,12},{8,0},{12,4},{1,9},{5,13},{9,1},{13,5},{2,10},{6,14},... | collective-permute-start | bytes 589832 | tf_op jit(solution)/shard_map/ppermute | solution.py:39
  3.0 13.4 %collective-permute-start.2 = (bf16[32,3072]{1,0:T(8,128)(2,1)}, bf16[32,3072]{1,0:T(8,128)(2,1)S(1)}, u32[]{:S(2)}, u32[]{:S(2)}) collective-permute-start(bf16[32,3072]{1,0:T(8,128)(2,1)} %inw_hbm.1), channel_id=1, source_target_pairs={{0,4},{4,0},{8,12},{12,8},{1,5},{5,1},{9,13},{13,9},{2,6},{6,2},{1... | collective-permute-start | bytes 589832 | tf_op jit(solution)/shard_map/ppermute | solution.py:39
  8.9 10.1 %collective-permute-start.4 = (bf16[32,3072]{1,0:T(8,128)(2,1)S(1)}, bf16[32,3072]{1,0:T(8,128)(2,1)S(1)}, u32[]{:S(2)}, u32[]{:S(2)}) collective-permute-start(bf16[32,3072]{1,0:T(8,128)(2,1)S(1)} %collective-permute-done.3.refs_1_), channel_id=1, source_target_pairs={{0,4},{4,0},{8,12},{12,8},{1,5},{5,1},{9,13},{13,9},{2,6},{6,2},{1... | collective-permute-start | bytes 589832 | tf_op jit(solution)/shard_map/ppermute | solution.py:39
  8.9 20.0 %collective-permute-start.8 = (bf16[768,128]{1,0:T(8,128)(2,1)}, bf16[768,128]{1,0:T(8,128)(2,1)S(1)}, u32[]{:S(2)}, u32[]{:S(2)}) collective-permute-start(bf16[768,128]{1,0:T(8,128)(2,1)} %refs_0_.1), channel_id=1, source_target_pairs={{0,4},{4,0},{8,12},{12,8},{1,5},{5,1},{9,13},{13,9},{2,6},{6,2},{1... | collective-permute-start | bytes 589832 | tf_op jit(solution)/shard_map/ppermute | solution.py:39
  12.3 18.2 %collective-permute-start.1 = (bf16[768,128]{1,0:T(8,128)(2,1)S(1)}, bf16[768,128]{1,0:T(8,128)(2,1)S(1)}, u32[]{:S(2)}, u32[]{:S(2)}) collective-permute-start(bf16[768,128]{1,0:T(8,128)(2,1)S(1)} %collective-permute-done.refs_2_), channel_id=1, source_target_pairs={{0,4},{4,0},{8,12},{12,8},{1,5},{5,1},{9,13},{13,9},{2,6},{6,2},{1... | collective-permute-start | bytes 589832 | tf_op jit(solution)/shard_map/ppermute | solution.py:39
  14.5 7.2 %collective-permute-start.5 = (f32[50,128]{1,0:T(8,128)S(1)}, f32[50,128]{1,0:T(8,128)S(1)}, u32[]{:S(2)}, u32[]{:S(2)}) collective-permute-start(f32[50,128]{1,0:T(8,128)S(1)} %shard_map.83.refs_0_), channel_id=1, source_target_pairs={{0,1},{1,0},{2,3},{3,2},{4,5},{5,4},{6,7},{7,6},{8,9},{9,8},{10,11... | collective-permute-start | bytes 76808 | tf_op jit(solution)/shard_map/ppermute | solution.py:39
  16.4 5.3 %collective-permute-start.6 = (f32[50,128]{1,0:T(8,128)S(1)}, f32[50,128]{1,0:T(8,128)S(1)}, u32[]{:S(2)}, u32[]{:S(2)}) collective-permute-start(f32[50,128]{1,0:T(8,128)S(1)} %shard_map.83.refs_0_), channel_id=1, source_target_pairs={{0,2},{1,3},{2,0},{3,1},{4,6},{5,7},{6,4},{7,5},{8,10},{9,11},{10,... | collective-permute-start | bytes 76808 | tf_op jit(solution)/shard_map/ppermute | solution.py:39
  19.0 5.7 %collective-permute-start.7 = (f32[50,128]{1,0:T(8,128)S(1)}, f32[50,128]{1,0:T(8,128)S(1)}, u32[]{:S(2)}, u32[]{:S(2)}) collective-permute-start(f32[50,128]{1,0:T(8,128)S(1)} %shard_map.83.refs_0_), channel_id=1, source_target_pairs={{0,3},{1,2},{2,1},{3,0},{4,7},{5,6},{6,5},{7,4},{8,11},{9,10},{10,... | collective-permute-start | bytes 76808 | tf_op jit(solution)/shard_map/ppermute | solution.py:39
  24.7 4.3 %copy-start = (bf16[768,128]{1,0:T(8,128)(2,1)S(1)}, bf16[768,128]{1,0:T(8,128)(2,1)}, u32[]{:S(2)}) copy-start(bf16[768,128]{1,0:T(8,128)(2,1)} %refs_0_.1) | copy-start | bytes 589828
  30.5 25.7 %copy-start.1 = (f32[32,128]{1,0:T(8,128)S(1)}, f32[32,128]{1,0:T(8,128)}, u32[]{:S(2)}) copy-start(f32[32,128]{1,0:T(8,128)} %start_hbm.1) | copy-start | bytes 49156
  31.3 1.3 %collective-permute-start.9 = (bf16[128,128]{1,0:T(8,128)(2,1)S(1)}, bf16[128,128]{1,0:T(8,128)(2,1)S(1)}, u32[]{:S(2)}, u32[]{:S(2)}) collective-permute-start(bf16[128,128]{1,0:T(8,128)(2,1)S(1)} %get-tuple-element.38), channel_id=1, source_target_pairs={{0,4},{4,0},{8,12},{12,8},{1,5},{5,1},{9,13},{13,9},{2,6},{6,2},{1... | collective-permute-start | bytes 98312 | tf_op jit(solution)/shard_map/ppermute | solution.py:39
  32.5 4.3 %collective-permute-start.10 = (bf16[2,128,128]{2,1,0:T(8,128)(2,1)S(1)}, bf16[2,128,128]{2,1,0:T(8,128)(2,1)S(1)}, u32[]{:S(2)}, u32[]{:S(2)}) collective-permute-start(bf16[2,128,128]{2,1,0:T(8,128)(2,1)S(1)} %pad_maximum_fusion), channel_id=1, source_target_pairs={{0,8},{1,9},{2,10},{3,11},{4,6},{5,7},{6,4},{7,5},{8,0},{9,1},{10,... | collective-permute-start | bytes 196616 | tf_op jit(solution)/shard_map/ppermute | solution.py:49
  34.1 4.3 %collective-permute-start.11 = (bf16[2,128,128]{2,1,0:T(8,128)(2,1)S(1)}, bf16[2,128,128]{2,1,0:T(8,128)(2,1)S(1)}, u32[]{:S(2)}, u32[]{:S(2)}) collective-permute-start(bf16[2,128,128]{2,1,0:T(8,128)(2,1)S(1)} %pad_maximum_fusion), channel_id=1, source_target_pairs={{0,8},{1,9},{2,10},{3,11},{4,7},{5,6},{6,5},{7,4},{8,0},{9,1},{10,... | collective-permute-start | bytes 196616 | tf_op jit(solution)/shard_map/ppermute | solution.py:49
  34.6 4.4 %collective-permute-start.12 = (bf16[2,128,128]{2,1,0:T(8,128)(2,1)S(1)}, bf16[2,128,128]{2,1,0:T(8,128)(2,1)S(1)}, u32[]{:S(2)}, u32[]{:S(2)}) collective-permute-start(bf16[2,128,128]{2,1,0:T(8,128)(2,1)S(1)} %pad_maximum_fusion), channel_id=1, source_target_pairs={{0,8},{1,9},{2,10},{3,11},{4,5},{5,4},{6,7},{7,6},{8,0},{9,1},{10,... | collective-permute-start | bytes 196616 | tf_op jit(solution)/shard_map/ppermute | solution.py:49
  39.1 4.0 %collective-permute-start.13 = (bf16[128,128]{1,0:T(8,128)(2,1)S(1)}, bf16[128,128]{1,0:T(8,128)(2,1)S(1)}, u32[]{:S(2)}, u32[]{:S(2)}) collective-permute-start(bf16[128,128]{1,0:T(8,128)(2,1)S(1)} %fusion.1), channel_id=1, source_target_pairs={{0,8},{4,12},{8,0},{12,4},{1,9},{5,13},{9,1},{13,5},{2,10},{6,14},... | collective-permute-start | bytes 98312 | tf_op jit(solution)/shard_map/ppermute | solution.py:39
  40.5 3.3 %collective-permute-start.14 = (bf16[128,128]{1,0:T(8,128)(2,1)S(1)}, bf16[128,128]{1,0:T(8,128)(2,1)S(1)}, u32[]{:S(2)}, u32[]{:S(2)}) collective-permute-start(bf16[128,128]{1,0:T(8,128)(2,1)S(1)} %fusion.1), channel_id=1, source_target_pairs={{0,12},{4,8},{8,4},{12,0},{1,13},{5,9},{9,5},{13,1},{2,14},{6,10},... | collective-permute-start | bytes 98312 | tf_op jit(solution)/shard_map/ppermute | solution.py:39
  44.8 4.5 %collective-permute-start.15 = (f32[32,128]{1,0:T(8,128)S(1)}, f32[32,128]{1,0:T(8,128)S(1)}, u32[]{:S(2)}, u32[]{:S(2)}) collective-permute-start(f32[32,128]{1,0:T(8,128)S(1)} %get-tuple-element.42), channel_id=1, source_target_pairs={{0,1},{1,0},{2,3},{3,2},{4,5},{5,4},{6,7},{7,6},{8,9},{9,8},{10,11... | collective-permute-start | bytes 49160 | tf_op jit(solution)/shard_map/ppermute | solution.py:39
  44.9 4.7 %collective-permute-start.16 = (f32[32,128]{1,0:T(8,128)S(1)}, f32[32,128]{1,0:T(8,128)S(1)}, u32[]{:S(2)}, u32[]{:S(2)}) collective-permute-start(f32[32,128]{1,0:T(8,128)S(1)} %get-tuple-element.43), channel_id=1, source_target_pairs={{0,2},{1,3},{2,0},{3,1},{4,6},{5,7},{6,4},{7,5},{8,10},{9,11},{10,... | collective-permute-start | bytes 49160 | tf_op jit(solution)/shard_map/ppermute | solution.py:39
  46.7 5.5 %collective-permute-start.17 = (f32[32,128]{1,0:T(8,128)S(1)}, f32[32,128]{1,0:T(8,128)S(1)}, u32[]{:S(2)}, u32[]{:S(2)}) collective-permute-start(f32[32,128]{1,0:T(8,128)S(1)} %get-tuple-element.44), channel_id=1, source_target_pairs={{0,3},{1,2},{2,1},{3,0},{4,7},{5,6},{6,5},{7,4},{8,11},{9,10},{10,... | collective-permute-start | bytes 49160 | tf_op jit(solution)/shard_map/ppermute | solution.py:39
  52.2 1.9 %collective-permute-start.18 = (f32[32,128]{1,0:T(8,128)S(1)}, f32[32,128]{1,0:T(8,128)S(1)}, u32[]{:S(2)}, u32[]{:S(2)}) collective-permute-start(f32[32,128]{1,0:T(8,128)S(1)} %add_add_fusion), channel_id=1, source_target_pairs={{0,4},{4,0},{8,12},{12,8},{1,5},{5,1},{9,13},{13,9},{2,6},{6,2},{1... | collective-permute-start | bytes 49160 | tf_op jit(solution)/shard_map/ppermute | solution.py:39
  52.2 3.8 %collective-permute-start.19 = (f32[32,128]{1,0:T(8,128)S(1)}, f32[32,128]{1,0:T(8,128)S(1)}, u32[]{:S(2)}, u32[]{:S(2)}) collective-permute-start(f32[32,128]{1,0:T(8,128)S(1)} %add_add_fusion), channel_id=1, source_target_pairs={{0,8},{4,12},{8,0},{12,4},{1,9},{5,13},{9,1},{13,5},{2,10},{6,14},... | collective-permute-start | bytes 49160 | tf_op jit(solution)/shard_map/ppermute | solution.py:39
  53.0 3.2 %collective-permute-start.20 = (f32[32,128]{1,0:T(8,128)S(1)}, f32[32,128]{1,0:T(8,128)S(1)}, u32[]{:S(2)}, u32[]{:S(2)}) collective-permute-start(f32[32,128]{1,0:T(8,128)S(1)} %add_add_fusion), channel_id=1, source_target_pairs={{0,12},{4,8},{8,4},{12,0},{1,13},{5,9},{9,5},{13,1},{2,14},{6,10},... | collective-permute-start | bytes 49160 | tf_op jit(solution)/shard_map/ppermute | solution.py:39

commit v9 on v7

--- a/solution.py
+++ b/solution.py
@@ -88,41 +88,41 @@
         copy.wait()
 
 
-def modulation_kernel(time_ref, weight_hbm, start_hbm, out_ref, weight_ref, start_ref, sems):
+def modulation_kernel(
+    time_ref, weight_hbm, start_hbm, qkv_hbm, inw_hbm, out_ref, qkv_ref, inw_ref, weight_ref, start_ref, sems
+):
     rows = start_ref.shape[0]
     half = weight_ref.shape[0] // 2
-    pairs = ((weight_hbm, weight_ref), (start_hbm, start_ref))
+    pairs = (
+        (weight_hbm, weight_ref),
+        (start_hbm, start_ref),
+        (inw_hbm, inw_ref),
+        (qkv_hbm.at[:, pl.ds(0, qkv_ref.shape[1])], qkv_ref),
+    )
     copies = run_copies(
         [pltpu.make_async_copy(a, b, sems.at[i]) for i, (a, b) in enumerate(pairs)]
     )
     index = lax.broadcasted_iota(jnp.int32, (16, half), 1).astype(F32)
     angles = time_ref[0].astype(F32) * jnp.exp(-math.log(10000.0) * index / half)
     embedding = jnp.concatenate([jnp.cos(angles), jnp.sin(angles)], axis=1).astype(BF16)
-    wait_copies(copies)
+    wait_copies(copies[:2])
     result = bdot(embedding, weight_ref[...])
     out_ref[0:rows, :] = start_ref[...]
     for r in range(weight_ref.shape[1] // LANES):
         out_ref[rows + r : rows + r + 1, :] = result[0:1, r * LANES : (r + 1) * LANES]
+    wait_copies(copies[2:])
 
 
 def channel_columns(inw_ref, c, n):
     return inw_ref[:, :, c * LANES : (c + n) * LANES].reshape(-1, n * LANES)
 
 
-def load_kernel(nm, weight_ref, qkv_hbm, inw_hbm, *refs):
-    inws, refs = refs[: nm - 1], refs[nm - 1 :]
-    qkv_ref, inw_ref, mean_ref, gram_ref, step_ref, sems = refs
-    cols = qkv_ref.shape[1]
-    copies = run_copies(
-        [
-            pltpu.make_async_copy(inw_hbm, inw_ref.at[place("tm", nm, 0)], sems.at[0]),
-            pltpu.make_async_copy(qkv_hbm.at[:, pl.ds(0, cols)], qkv_ref, sems.at[1]),
-        ]
-    )
+def prepare_kernel(nm, weight_ref, *refs):
+    inws, refs = refs[:nm], refs[nm:]
+    inw_ref, mean_ref, gram_ref, step_ref = refs
     step_ref[...] = jnp.full(step_ref.shape, weight_ref[0].astype(F32) * (1.0 / STEP_DIVISOR))
-    for k in range(1, nm):
-        inw_ref[place("tm", nm, k)] = inws[k - 1][...]
-    copies[0].wait()
+    for k in range(nm):
+        inw_ref[place("tm", nm, k)] = inws[k][...]
     channels, width = mean_ref.shape[0], inw_ref.shape[2]
     chunks = width // LANES
     total = jnp.zeros((channels, LANES), F32)
@@ -139,7 +139,6 @@
     gram = gram * (1.0 / width) - mean_c * mean_c.T
     for i, term in enumerate(split_terms(gram, 3)):
         gram_ref[i * channels : (i + 1) * channels, :] = term
-    copies[1].wait()
 
 
 def attend(x, factors, base, gram, head_count):
@@ -244,36 +243,25 @@
     return folded, resid
 
 
-def attend_kernel(nm, early, head_count, *refs):
-    heads, refs = refs[:early], refs[early:]
-    start_ref, factor_ref, base_ref, gram_ref, gate_ref, out_w_ref, inw_ref = refs[:7]
-    att_ref, fold_ref, resid_ref = refs[7:]
-    x = start_ref[...].astype(BF16)
-    fold_ref[...], resid_ref[...] = fold_parts(nm, 0, heads, gate_ref, out_w_ref, inw_ref)
-    att_ref[...] = attend(x, factor_ref, base_ref, gram_ref, head_count)
-
-
 def add_own_rows(result, residual, rows):
     first = lax.axis_index("tensor") * rows
     at = lax.broadcasted_iota(jnp.int32, result.shape, 0)
     return result + jnp.where((at >= first) & (at < first + rows), residual, 0.0)
 
 
-def fold_kernel(nm, late, rows, *refs):
-    heads, refs = refs[:late], refs[late:]
-    step_ref, gate_ref, out_w_ref, inw_ref, fold_in, resid_in, att_ref, start_ref = refs[:8]
+def first_kernel(nm, rows, head_count, *refs):
+    heads, refs = refs[:nm], refs[nm:]
+    step_ref, start_ref, factor_ref, base_ref, gram_ref, gate_ref, out_w_ref, inw_ref = refs[:8]
     fold_ref, resid_ref, vel_ref = refs[8:]
-    channels = resid_in.shape[0]
-    total, resid = fold_in[...], resid_in[...]
-    if late:
-        more = fold_parts(nm, nm - late, heads, gate_ref, out_w_ref, inw_ref)
-        total, resid = total + more[0], resid + more[1]
+    x = start_ref[...].astype(BF16)
+    total, resid = fold_parts(nm, 0, heads, gate_ref, out_w_ref, inw_ref)
+    attended = attend(x, factor_ref, base_ref, gram_ref, head_count)
+    channels = resid.shape[0]
     folded = total.astype(BF16)
     fold_ref[...] = folded
     for i, term in enumerate(split_terms(resid, 2)):
         resid_ref[i * channels : (i + 1) * channels, :] = term
-    x = start_ref[...].astype(BF16)
-    vel = bdot(att_ref[...], folded)
+    vel = bdot(attended, folded)
     residual = bdot(jnp.concatenate([x, x], axis=1), resid_ref[...])
     vel_ref[...] = (add_own_rows(vel, residual, rows) * step_ref[0:1, :]).astype(vel_ref.dtype)
 
@@ -356,26 +344,37 @@
     span = out_weight.shape[0]
 
     inw_parts = gather_weight_parts(in_weight, "tm")
+    span_cols = qkv_weight.shape[1]
+    block = 4 * LANES if span_cols % (4 * LANES) == 0 else span_cols
+    near = max(1, span_cols // block // 3)
+    far = max(1, span_cols // block - near)
     small = is_small("tensor") and mod_weight.shape[1] % LANES == 0
     if small:
         mod_rows = mod_weight.shape[1] // LANES
-        message = call(
+        message, qkv_near, inw_parts[0] = call(
             modulation_kernel,
-            [shape_of((rows + mod_rows, LANES), F32)],
-            [SMEM, HBM, HBM],
+            [
+                shape_of((rows + mod_rows, LANES), F32),
+                shape_of((width, near * block), BF16),
+                shape_of(inw_parts[0].shape, BF16),
+            ],
+            [SMEM, HBM, HBM, HBM, HBM],
             [
                 pltpu.VMEM(mod_weight.shape, BF16),
                 pltpu.VMEM(start_latent.shape, F32),
-                pltpu.SemaphoreType.DMA((2,)),
+                pltpu.SemaphoreType.DMA((4,)),
             ],
             time_index,
             mod_weight,
             start_latent,
-        )[0]
+            qkv_weight,
+            inw_parts[0],
+        )
         messages = gather_parts(message, "tensor")
         block_rows = rows
     else:
         embedding = embedding_of(time_index, mod_weight.shape[0]).astype(BF16)
+        qkv_near = qkv_weight[:, : near * block]
         mod_part = jnp.dot(embedding, mod_weight, preferred_element_type=F32)
         modulation = lax.all_gather(mod_part, "tensor", axis=1, tiled=True)
         start_all = lax.all_gather(start_latent, "tensor", axis=0, tiled=True)
@@ -384,24 +383,18 @@
     nt, nm = len(messages), len(inw_parts)
     mod_rows = messages[0].shape[0] - block_rows
     padded = -(-mod_rows // 8) * 8
-    span_cols = qkv_weight.shape[1]
     gate_rows = -(-(chunks // nm) // 8) * 8
-    block = 4 * LANES if span_cols % (4 * LANES) == 0 else span_cols
-    near = max(1, span_cols // block // 3)
-    far = max(1, span_cols // block - near)
-    qkv_near, inw_all, mean, gram, step = call(
-        functools.partial(load_kernel, nm),
+    inw_all, mean, gram, step = call(
+        functools.partial(prepare_kernel, nm),
         [
-            shape_of((width, near * block), BF16),
             shape_of((nm, channels // nm, width), BF16),
             shape_of((channels, LANES), F32),
             shape_of((3 * channels, channels), BF16),
             shape_of((8, LANES), F32),
         ],
-        [SMEM, HBM, HBM] + [VMEM] * (nm - 1),
-        [pltpu.SemaphoreType.DMA((2,))],
+        [SMEM] + [VMEM] * nm,
+        [],
         step_weight,
-        qkv_weight,
         *inw_parts,
         limit=16,
     )
@@ -432,18 +425,17 @@
         limit=32,
     )
     head_parts = gather_weight_parts(head_weight, "tm")
-    late = 1 if nm > 1 else 0
-    early = nm - late
-    attended, fold_part, resid_part = call(
-        functools.partial(attend_kernel, nm, early, head_count),
+    folded, resid, vel = call(
+        functools.partial(first_kernel, nm, rows, head_count),
         [
-            shape_of((tokens, head_count * HD), BF16),
-            shape_of((span, channels), F32),
-            shape_of((channels, channels), F32),
+            shape_of((span, channels), BF16),
+            shape_of((2 * channels, channels), BF16),
+            shape_of((tokens, channels), BF16),
         ],
-        [VMEM] * (early + 7),
+        [VMEM] * (nm + 8),
         [],
-        *head_parts[:early],
+        *head_parts,
+        step,
         start_all,
         factor,
         base,
@@ -451,26 +443,6 @@
         gate,
         out_near,
         inw_all,
-        limit=16,
-    )
-    folded, resid, vel = call(
-        functools.partial(fold_kernel, nm, late, rows),
-        [
-            shape_of((span, channels), BF16),
-            shape_of((2 * channels, channels), BF16),
-            shape_of((tokens, channels), BF16),
-        ],
-        [VMEM] * (late + 8),
-        [],
-        *head_parts[early:],
-        step,
-        gate,
-        out_near,
-        inw_all,
-        fold_part,
-        resid_part,
-        attended,
-        start_all,
         limit=16,
     )
     small = is_small("tensor")

time: 58.3 us -> 58.8 us (level)
  waiting for transfers between devices: 24.1 us -> 25.7 us
  Pallas kernels: 11 us -> 9.92 us
    ppermute x21, waiting for transfers between devices: 24.1 us -> 25.7 us  [swap(): return lax.ppermute(value, axis, [(i, i ^ k) for i in range(n)])]
    pallas_call x6 -> x5, Pallas kernels: 11 us -> 9.92 us  [call(): pl.pallas_call(kernel, out_shape=outs, in_specs=in_specs, out_specs=[VMEM...]
  transfers between devices with their start and end apart: 21 -> 21, of which waited for: 11 -> 12; matrix products, arithmetic and copies ran while one was open for 0% -> 0% of each run, Pallas kernels for 16% -> 12%
where the time goes in v9:
time: 58.8 us; the launch traced here: 58.6 us
  waiting for transfers between devices  25.7 us (44%)
  starting transfers between devices  21 us (36%)
  Pallas kernels  9.92 us (17%)
  between operations  1.42 us (2%)
  other arithmetic  0.65 us (1%)
    ppermute x21, waiting for transfers between devices, swap(): return lax.ppermute(value, axis, [(i, i ^ k) for i in range(n)])  25.7 us
    ppermute x21, starting transfers between devices, swap(): return lax.ppermute(value, axis, [(i, i ^ k) for i in range(n)])  21 us
    pallas_call x5, Pallas kernels, call(): pl.pallas_call(kernel, out_shape=outs, in_specs=in_specs, out_specs=[VMEM...  9.92 us
  transfers between devices with their start and end apart: 21, of which 12 were waited for; matrix products, arithmetic and copies ran while one was open for 0% of the time, Pallas kernels for 12%

profile of v9, /device:TPU:0, one launch (start us, length us, event | category | flops | bytes accessed | tf_op | source)
XLA Modules:
  0.0 58.6 jit_solution(3111057592508592749)
XLA Ops:
  0.0 3.0 %collective-permute-start.4 = (bf16[32,3072]{1,0:T(8,128)(2,1)}, bf16[32,3072]{1,0:T(8,128)(2,1)S(1)}, u32[]{:S(2)}, u32[]{:S(2)}) collective-permute-start(bf16[32,3072]{1,0:T(8,128)(2,1)} %inw_hbm.1), channel_id=1, source_target_pairs={{0,8},{4,12},{8,0},{12,4},{1,9},{5,13},{9,1},{13,5},{2,10},{6,14},... | collective-permute-start | bytes 589832 | tf_op jit(solution)/shard_map/ppermute | solution.py:39
  3.0 5.9 %collective-permute-done.4.refs_2_ = bf16[32,3072]{1,0:T(8,128)(2,1)S(1)} collective-permute-done((bf16[32,3072]{1,0:T(8,128)(2,1)}, bf16[32,3072]{1,0:T(8,128)(2,1)S(1)}, u32[]{:S(2)}, u32[]{:S(2)}) %collective-permute-start.4) | collective-permute-done | bytes 196640 | tf_op jit(solution)/shard_map/ppermute | solution.py:39
  8.9 0.5 collective-permute-start
  9.4 2.9 %collective-permute-done.1.refs_2_ = bf16[768,128]{1,0:T(8,128)(2,1)S(1)} collective-permute-done((bf16[768,128]{1,0:T(8,128)(2,1)}, bf16[768,128]{1,0:T(8,128)(2,1)S(1)}, u32[]{:S(2)}, u32[]{:S(2)}) %collective-permute-start.1) | collective-permute-done | bytes 196640 | tf_op jit(solution)/shard_map/ppermute | solution.py:39
  12.9 2.4 %shard_map.82 = (f32[50,128]{1,0:T(8,128)S(1)}, bf16[3072,512]{1,0:T(8,128)(2,1)S(1)}, bf16[32,3072]{1,0:T(8,128)(2,1)S(1)}) custom-call(s32[1]{0:T(128)S(6)} %copy.9.time_ref, bf16[256,2304]{1,0:T(8,128)(2,1)} %weight_hbm.1, f32[32,128]{1,0:T(8,128)} %start_hbm.1, bf16[3072,1536]{1,0:T(8,128)(2,1)} %refs_7_.1, bf16[32,3072]{1,0:T(8,128)(2,1)} %inw_hbm.1), custom_call_target="tpu_custom_call" | custom-call | bytes 4194304 | tf_op jit(solution)/shard_map/pallas_call | solution.py:299
  15.3 1.9 %collective-permute-start.6 = (f32[50,128]{1,0:T(8,128)S(1)}, f32[50,128]{1,0:T(8,128)S(1)}, u32[]{:S(2)}, u32[]{:S(2)}) collective-permute-start(f32[50,128]{1,0:T(8,128)S(1)} %get-tuple-element.26.refs_0_), channel_id=1, source_target_pairs={{0,1},{1,0},{2,3},{3,2},{4,5},{5,4},{6,7},{7,6},{8,9},{9,8},{10,11... | collective-permute-start | bytes 76808 | tf_op jit(solution)/shard_map/ppermute | solution.py:39
  17.2 2.6 %collective-permute-start.7 = (f32[50,128]{1,0:T(8,128)S(1)}, f32[50,128]{1,0:T(8,128)S(1)}, u32[]{:S(2)}, u32[]{:S(2)}) collective-permute-start(f32[50,128]{1,0:T(8,128)S(1)} %get-tuple-element.26.refs_0_), channel_id=1, source_target_pairs={{0,2},{1,3},{2,0},{3,1},{4,6},{5,7},{6,4},{7,5},{8,10},{9,11},{10,... | collective-permute-start | bytes 76808 | tf_op jit(solution)/shard_map/ppermute | solution.py:39
  20.5 0.5 shard_map.83
  20.9 1.4 %collective-permute-done.7.refs_2_ = f32[50,128]{1,0:T(8,128)S(1)} collective-permute-done((f32[50,128]{1,0:T(8,128)S(1)}, f32[50,128]{1,0:T(8,128)S(1)}, u32[]{:S(2)}, u32[]{:S(2)}) %collective-permute-start.7) | collective-permute-done | bytes 25632 | tf_op jit(solution)/shard_map/ppermute | solution.py:39
  22.3 3.1 %collective-permute-done.8.refs_3_ = f32[50,128]{1,0:T(8,128)S(1)} collective-permute-done((f32[50,128]{1,0:T(8,128)S(1)}, f32[50,128]{1,0:T(8,128)S(1)}, u32[]{:S(2)}, u32[]{:S(2)}) %collective-permute-start.8) | collective-permute-done | bytes 25632 | tf_op jit(solution)/shard_map/ppermute | solution.py:39
  25.5 4.3 %shard_map.84 = (bf16[256,1536]{1,0:T(8,128)(2,1)S(1)}, f32[8,1536]{1,0:T(8,128)S(1)}, f32[128,128]{1,0:T(8,128)S(1)}, f32[4,128,8]{2,1,0:T(8,128)S(1)}, bf16[512,3072]{1,0:T(8,128)(2,1)S(1)}) custom-call(f32[50,128]{1,0:T(8,128)S(1)} %get-tuple-element.26.refs_0_, f32[50,128]{1,0:T(8,128)S(1)} %collective-permute-done.6.refs_1_, ...), custom_call_target="tpu_custom_call" | custom-call | bytes 4194304 | tf_op jit(solution)/shard_map/pallas_call | solution.py:299
  29.8 1.9 %shard_map.85 = (bf16[512,128]{1,0:T(8,128)(2,1)S(1)}, bf16[256,128]{1,0:T(8,128)(2,1)S(1)}, bf16[128,128]{1,0:T(8,128)(2,1)S(1)}) custom-call(bf16[768,128]{1,0:T(8,128)(2,1)S(1)} %copy-done, bf16[768,128]{1,0:T(8,128)(2,1)S(1)} %collective-permute-done.refs_1_, bf16[768,128]{1,0:T(8,128)(2,1)S(1)} %collective-permute-done.1.refs_2_, ...), custom_call_target="tpu_custom_call" | custom-call | bytes 4194304 | tf_op jit(solution)/shard_map/pallas_call | solution.py:299
  31.7 1.6 %collective-permute-start.10 = (bf16[128,128]{1,0:T(8,128)(2,1)S(1)}, bf16[128,128]{1,0:T(8,128)(2,1)S(1)}, u32[]{:S(2)}, u32[]{:S(2)}) collective-permute-start(bf16[128,128]{1,0:T(8,128)(2,1)S(1)} %get-tuple-element.36), channel_id=1, source_target_pairs={{0,8},{4,12},{8,0},{12,4},{1,9},{5,13},{9,1},{13,5},{2,10},{6,14},... | collective-permute-start | bytes 98312 | tf_op jit(solution)/shard_map/ppermute | solution.py:39
  33.3 0.6 %collective-permute-start.9 = (bf16[128,128]{1,0:T(8,128)(2,1)S(1)}, bf16[128,128]{1,0:T(8,128)(2,1)S(1)}, u32[]{:S(2)}, u32[]{:S(2)}) collective-permute-start(bf16[128,128]{1,0:T(8,128)(2,1)S(1)} %get-tuple-element.36), channel_id=1, source_target_pairs={{0,4},{4,0},{8,12},{12,8},{1,5},{5,1},{9,13},{13,9},{2,6},{6,2},{1... | collective-permute-start | bytes 98312 | tf_op jit(solution)/shard_map/ppermute | solution.py:39
  33.9 1.8 %collective-permute-done.10 = bf16[128,128]{1,0:T(8,128)(2,1)S(1)} collective-permute-done((bf16[128,128]{1,0:T(8,128)(2,1)S(1)}, bf16[128,128]{1,0:T(8,128)(2,1)S(1)}, u32[]{:S(2)}, u32[]{:S(2)}) %collective-permute-start.10) | collective-permute-done | bytes 32800 | tf_op jit(solution)/shard_map/ppermute | solution.py:39
  35.7 0.9 %collective-permute-done.11 = bf16[128,128]{1,0:T(8,128)(2,1)S(1)} collective-permute-done((bf16[128,128]{1,0:T(8,128)(2,1)S(1)}, bf16[128,128]{1,0:T(8,128)(2,1)S(1)}, u32[]{:S(2)}, u32[]{:S(2)}) %collective-permute-start.11) | collective-permute-done | bytes 32800 | tf_op jit(solution)/shard_map/ppermute | solution.py:39
  36.7 0.1 collective-permute-start.12
  36.8 0.9 %collective-permute-start.13 = (bf16[128,128]{1,0:T(8,128)(2,1)S(1)}, bf16[128,128]{1,0:T(8,128)(2,1)S(1)}, u32[]{:S(2)}, u32[]{:S(2)}) collective-permute-start(bf16[128,128]{1,0:T(8,128)(2,1)S(1)} %add_convert_fusion.refs_0_), channel_id=1, source_target_pairs={{0,2},{1,3},{2,0},{3,1},{4,6},{5,7},{6,4},{7,5},{8,10},{9,11},{10,... | collective-permute-start | bytes 98312 | tf_op jit(solution)/shard_map/ppermute | solution.py:39
  37.6 3.5 %collective-permute-start.14 = (bf16[128,128]{1,0:T(8,128)(2,1)S(1)}, bf16[128,128]{1,0:T(8,128)(2,1)S(1)}, u32[]{:S(2)}, u32[]{:S(2)}) collective-permute-start(bf16[128,128]{1,0:T(8,128)(2,1)S(1)} %add_convert_fusion.refs_0_), channel_id=1, source_target_pairs={{0,3},{1,2},{2,1},{3,0},{4,7},{5,6},{6,5},{7,4},{8,11},{9,10},{10,... | collective-permute-start | bytes 98312 | tf_op jit(solution)/shard_map/ppermute | solution.py:39
  41.1 0.6 collective-permute-done.13.refs_2_
  41.7 1.7 %collective-permute-done.14.refs_3_ = bf16[128,128]{1,0:T(8,128)(2,1)S(1)} collective-permute-done((bf16[128,128]{1,0:T(8,128)(2,1)S(1)}, bf16[128,128]{1,0:T(8,128)(2,1)S(1)}, u32[]{:S(2)}, u32[]{:S(2)}) %collective-permute-start.14) | collective-permute-done | bytes 32800 | tf_op jit(solution)/shard_map/ppermute | solution.py:39
  43.4 0.9 %shard_map.86 = (f32[32,128]{1,0:T(8,128)S(1)}, f32[32,128]{1,0:T(8,128)S(1)}, f32[32,128]{1,0:T(8,128)S(1)}, f32[32,128]{1,0:T(8,128)S(1)}) custom-call(bf16[128,128]{1,0:T(8,128)(2,1)S(1)} %add_convert_fusion.refs_0_, bf16[128,128]{1,0:T(8,128)(2,1)S(1)} %collective-permute-done.12.refs_1_, bf16[128,128]{1,0:T(8,128)(2,1)S(1)} %collective-permute-done.13.refs_2_, ...), custom_call_target="tpu_custom_call" | custom-call | bytes 4194304 | tf_op jit(solution)/shard_map/pallas_call | solution.py:299
  44.3 0.3 collective-permute-start.15
  44.5 3.8 %collective-permute-start.16 = (f32[32,128]{1,0:T(8,128)S(1)}, f32[32,128]{1,0:T(8,128)S(1)}, u32[]{:S(2)}, u32[]{:S(2)}) collective-permute-start(f32[32,128]{1,0:T(8,128)S(1)} %get-tuple-element.41), channel_id=1, source_target_pairs={{0,2},{1,3},{2,0},{3,1},{4,6},{5,7},{6,4},{7,5},{8,10},{9,11},{10,... | collective-permute-start | bytes 49160 | tf_op jit(solution)/shard_map/ppermute | solution.py:39
  48.4 0.3 collective-permute-start.17
  48.7 1.4 %collective-permute-done.16 = f32[32,128]{1,0:T(8,128)S(1)} collective-permute-done((f32[32,128]{1,0:T(8,128)S(1)}, f32[32,128]{1,0:T(8,128)S(1)}, u32[]{:S(2)}, u32[]{:S(2)}) %collective-permute-start.16) | collective-permute-done | bytes 16416 | tf_op jit(solution)/shard_map/ppermute | solution.py:39
  50.1 3.8 %collective-permute-done.17 = f32[32,128]{1,0:T(8,128)S(1)} collective-permute-done((f32[32,128]{1,0:T(8,128)S(1)}, f32[32,128]{1,0:T(8,128)S(1)}, u32[]{:S(2)}, u32[]{:S(2)}) %collective-permute-start.17) | collective-permute-done | bytes 16416 | tf_op jit(solution)/shard_map/ppermute | solution.py:39
  53.9 0.9 %collective-permute-start.19 = (f32[32,128]{1,0:T(8,128)S(1)}, f32[32,128]{1,0:T(8,128)S(1)}, u32[]{:S(2)}, u32[]{:S(2)}) collective-permute-start(f32[32,128]{1,0:T(8,128)S(1)} %add_add_fusion), channel_id=1, source_target_pairs={{0,8},{4,12},{8,0},{12,4},{1,9},{5,13},{9,1},{13,5},{2,10},{6,14},... | collective-permute-start | bytes 49160 | tf_op jit(solution)/shard_map/ppermute | solution.py:39
  54.9 0.9 %collective-permute-start.20 = (f32[32,128]{1,0:T(8,128)S(1)}, f32[32,128]{1,0:T(8,128)S(1)}, u32[]{:S(2)}, u32[]{:S(2)}) collective-permute-start(f32[32,128]{1,0:T(8,128)S(1)} %add_add_fusion), channel_id=1, source_target_pairs={{0,12},{4,8},{8,4},{12,0},{1,13},{5,9},{9,5},{13,1},{2,14},{6,10},... | collective-permute-start | bytes 49160 | tf_op jit(solution)/shard_map/ppermute | solution.py:39
  55.8 1.9 %collective-permute-done.19 = f32[32,128]{1,0:T(8,128)S(1)} collective-permute-done((f32[32,128]{1,0:T(8,128)S(1)}, f32[32,128]{1,0:T(8,128)S(1)}, u32[]{:S(2)}, u32[]{:S(2)}) %collective-permute-start.19) | collective-permute-done | bytes 16416 | tf_op jit(solution)/shard_map/ppermute | solution.py:39
  57.7 0.3 collective-permute-done.20
  58.0 0.6 %add_bitcast_fusion = f32[1,32,128]{2,1,0:T(8,128)} fusion(f32[32,128]{1,0:T(8,128)S(1)} %copy-done.1, f32[32,128]{1,0:T(8,128)S(1)} %collective-permute-done.20, f32[32,128]{1,0:T(8,128)S(1)} %collective-permute-done.19, f32[32,128]{1,0:T(8,128)S(1)} %add_add_fusion, f32[32,128]{1,0:T(8,128)S(1)} %collective-permute-done.18, pred[]{:T(512)S(6)} %lt.14, ...), kind=kLoop, calls=%fused_computation.1 | loop fusion | flops 28672 | bytes 98307 | tf_op jit(solution)/shard_map/broadcast_in_dim | solution.py:482
  (22 shorter events, 0.1 us)
Async XLA Ops:
  0.0 8.9 %collective-permute-start.4 = (bf16[32,3072]{1,0:T(8,128)(2,1)}, bf16[32,3072]{1,0:T(8,128)(2,1)S(1)}, u32[]{:S(2)}, u32[]{:S(2)}) collective-permute-start(bf16[32,3072]{1,0:T(8,128)(2,1)} %inw_hbm.1), channel_id=1, source_target_pairs={{0,8},{4,12},{8,0},{12,4},{1,9},{5,13},{9,1},{13,5},{2,10},{6,14},... | collective-permute-start | bytes 589832 | tf_op jit(solution)/shard_map/ppermute | solution.py:39
  3.0 9.3 %collective-permute-start.1 = (bf16[768,128]{1,0:T(8,128)(2,1)}, bf16[768,128]{1,0:T(8,128)(2,1)S(1)}, u32[]{:S(2)}, u32[]{:S(2)}) collective-permute-start(bf16[768,128]{1,0:T(8,128)(2,1)} %refs_0_.1), channel_id=1, source_target_pairs={{0,8},{4,12},{8,0},{12,4},{1,9},{5,13},{9,1},{13,5},{2,10},{6,14},... | collective-permute-start | bytes 589832 | tf_op jit(solution)/shard_map/ppermute | solution.py:39
  3.0 14.2 %collective-permute-start.3 = (bf16[32,3072]{1,0:T(8,128)(2,1)}, bf16[32,3072]{1,0:T(8,128)(2,1)S(1)}, u32[]{:S(2)}, u32[]{:S(2)}) collective-permute-start(bf16[32,3072]{1,0:T(8,128)(2,1)} %inw_hbm.1), channel_id=1, source_target_pairs={{0,4},{4,0},{8,12},{12,8},{1,5},{5,1},{9,13},{13,9},{2,6},{6,2},{1... | collective-permute-start | bytes 589832 | tf_op jit(solution)/shard_map/ppermute | solution.py:39
  8.9 10.9 %collective-permute-start.5 = (bf16[32,3072]{1,0:T(8,128)(2,1)S(1)}, bf16[32,3072]{1,0:T(8,128)(2,1)S(1)}, u32[]{:S(2)}, u32[]{:S(2)}) collective-permute-start(bf16[32,3072]{1,0:T(8,128)(2,1)S(1)} %collective-permute-done.4.refs_2_), channel_id=1, source_target_pairs={{0,4},{4,0},{8,12},{12,8},{1,5},{5,1},{9,13},{13,9},{2,6},{6,2},{1... | collective-permute-start | bytes 589832 | tf_op jit(solution)/shard_map/ppermute | solution.py:39
  8.9 20.9 %collective-permute-start = (bf16[768,128]{1,0:T(8,128)(2,1)}, bf16[768,128]{1,0:T(8,128)(2,1)S(1)}, u32[]{:S(2)}, u32[]{:S(2)}) collective-permute-start(bf16[768,128]{1,0:T(8,128)(2,1)} %refs_0_.1), channel_id=1, source_target_pairs={{0,4},{4,0},{8,12},{12,8},{1,5},{5,1},{9,13},{13,9},{2,6},{6,2},{1... | collective-permute-start | bytes 589832 | tf_op jit(solution)/shard_map/ppermute | solution.py:39
  12.3 17.5 %collective-permute-start.2 = (bf16[768,128]{1,0:T(8,128)(2,1)S(1)}, bf16[768,128]{1,0:T(8,128)(2,1)S(1)}, u32[]{:S(2)}, u32[]{:S(2)}) collective-permute-start(bf16[768,128]{1,0:T(8,128)(2,1)S(1)} %collective-permute-done.1.refs_2_), channel_id=1, source_target_pairs={{0,4},{4,0},{8,12},{12,8},{1,5},{5,1},{9,13},{13,9},{2,6},{6,2},{1... | collective-permute-start | bytes 589832 | tf_op jit(solution)/shard_map/ppermute | solution.py:39
  15.3 5.6 %collective-permute-start.6 = (f32[50,128]{1,0:T(8,128)S(1)}, f32[50,128]{1,0:T(8,128)S(1)}, u32[]{:S(2)}, u32[]{:S(2)}) collective-permute-start(f32[50,128]{1,0:T(8,128)S(1)} %get-tuple-element.26.refs_0_), channel_id=1, source_target_pairs={{0,1},{1,0},{2,3},{3,2},{4,5},{5,4},{6,7},{7,6},{8,9},{9,8},{10,11... | collective-permute-start | bytes 76808 | tf_op jit(solution)/shard_map/ppermute | solution.py:39
  17.2 5.1 %collective-permute-start.7 = (f32[50,128]{1,0:T(8,128)S(1)}, f32[50,128]{1,0:T(8,128)S(1)}, u32[]{:S(2)}, u32[]{:S(2)}) collective-permute-start(f32[50,128]{1,0:T(8,128)S(1)} %get-tuple-element.26.refs_0_), channel_id=1, source_target_pairs={{0,2},{1,3},{2,0},{3,1},{4,6},{5,7},{6,4},{7,5},{8,10},{9,11},{10,... | collective-permute-start | bytes 76808 | tf_op jit(solution)/shard_map/ppermute | solution.py:39
  19.8 5.7 %collective-permute-start.8 = (f32[50,128]{1,0:T(8,128)S(1)}, f32[50,128]{1,0:T(8,128)S(1)}, u32[]{:S(2)}, u32[]{:S(2)}) collective-permute-start(f32[50,128]{1,0:T(8,128)S(1)} %get-tuple-element.26.refs_0_), channel_id=1, source_target_pairs={{0,3},{1,2},{2,1},{3,0},{4,7},{5,6},{6,5},{7,4},{8,11},{9,10},{10,... | collective-permute-start | bytes 76808 | tf_op jit(solution)/shard_map/ppermute | solution.py:39
  25.5 4.3 %copy-start = (bf16[768,128]{1,0:T(8,128)(2,1)S(1)}, bf16[768,128]{1,0:T(8,128)(2,1)}, u32[]{:S(2)}) copy-start(bf16[768,128]{1,0:T(8,128)(2,1)} %refs_0_.1) | copy-start | bytes 589828
  29.8 28.2 %copy-start.1 = (f32[32,128]{1,0:T(8,128)S(1)}, f32[32,128]{1,0:T(8,128)}, u32[]{:S(2)}) copy-start(f32[32,128]{1,0:T(8,128)} %start_hbm.1) | copy-start | bytes 49156
  31.7 4.0 %collective-permute-start.10 = (bf16[128,128]{1,0:T(8,128)(2,1)S(1)}, bf16[128,128]{1,0:T(8,128)(2,1)S(1)}, u32[]{:S(2)}, u32[]{:S(2)}) collective-permute-start(bf16[128,128]{1,0:T(8,128)(2,1)S(1)} %get-tuple-element.36), channel_id=1, source_target_pairs={{0,8},{4,12},{8,0},{12,4},{1,9},{5,13},{9,1},{13,5},{2,10},{6,14},... | collective-permute-start | bytes 98312 | tf_op jit(solution)/shard_map/ppermute | solution.py:39
  33.3 3.3 %collective-permute-start.11 = (bf16[128,128]{1,0:T(8,128)(2,1)S(1)}, bf16[128,128]{1,0:T(8,128)(2,1)S(1)}, u32[]{:S(2)}, u32[]{:S(2)}) collective-permute-start(bf16[128,128]{1,0:T(8,128)(2,1)S(1)} %get-tuple-element.36), channel_id=1, source_target_pairs={{0,12},{4,8},{8,4},{12,0},{1,13},{5,9},{9,5},{13,1},{2,14},{6,10},... | collective-permute-start | bytes 98312 | tf_op jit(solution)/shard_map/ppermute | solution.py:39
  33.3 3.3 %collective-permute-start.9 = (bf16[128,128]{1,0:T(8,128)(2,1)S(1)}, bf16[128,128]{1,0:T(8,128)(2,1)S(1)}, u32[]{:S(2)}, u32[]{:S(2)}) collective-permute-start(bf16[128,128]{1,0:T(8,128)(2,1)S(1)} %get-tuple-element.36), channel_id=1, source_target_pairs={{0,4},{4,0},{8,12},{12,8},{1,5},{5,1},{9,13},{13,9},{2,6},{6,2},{1... | collective-permute-start | bytes 98312 | tf_op jit(solution)/shard_map/ppermute | solution.py:39
  36.7 4.5 %collective-permute-start.12 = (bf16[128,128]{1,0:T(8,128)(2,1)S(1)}, bf16[128,128]{1,0:T(8,128)(2,1)S(1)}, u32[]{:S(2)}, u32[]{:S(2)}) collective-permute-start(bf16[128,128]{1,0:T(8,128)(2,1)S(1)} %add_convert_fusion.refs_0_), channel_id=1, source_target_pairs={{0,1},{1,0},{2,3},{3,2},{4,5},{5,4},{6,7},{7,6},{8,9},{9,8},{10,11... | collective-permute-start | bytes 98312 | tf_op jit(solution)/shard_map/ppermute | solution.py:39
  36.8 5.0 %collective-permute-start.13 = (bf16[128,128]{1,0:T(8,128)(2,1)S(1)}, bf16[128,128]{1,0:T(8,128)(2,1)S(1)}, u32[]{:S(2)}, u32[]{:S(2)}) collective-permute-start(bf16[128,128]{1,0:T(8,128)(2,1)S(1)} %add_convert_fusion.refs_0_), channel_id=1, source_target_pairs={{0,2},{1,3},{2,0},{3,1},{4,6},{5,7},{6,4},{7,5},{8,10},{9,11},{10,... | collective-permute-start | bytes 98312 | tf_op jit(solution)/shard_map/ppermute | solution.py:39
  37.6 5.8 %collective-permute-start.14 = (bf16[128,128]{1,0:T(8,128)(2,1)S(1)}, bf16[128,128]{1,0:T(8,128)(2,1)S(1)}, u32[]{:S(2)}, u32[]{:S(2)}) collective-permute-start(bf16[128,128]{1,0:T(8,128)(2,1)S(1)} %add_convert_fusion.refs_0_), channel_id=1, source_target_pairs={{0,3},{1,2},{2,1},{3,0},{4,7},{5,6},{6,5},{7,4},{8,11},{9,10},{10,... | collective-permute-start | bytes 98312 | tf_op jit(solution)/shard_map/ppermute | solution.py:39
  44.3 4.5 %collective-permute-start.15 = (f32[32,128]{1,0:T(8,128)S(1)}, f32[32,128]{1,0:T(8,128)S(1)}, u32[]{:S(2)}, u32[]{:S(2)}) collective-permute-start(f32[32,128]{1,0:T(8,128)S(1)} %get-tuple-element.40), channel_id=1, source_target_pairs={{0,1},{1,0},{2,3},{3,2},{4,5},{5,4},{6,7},{7,6},{8,9},{9,8},{10,11... | collective-permute-start | bytes 49160 | tf_op jit(solution)/shard_map/ppermute | solution.py:39
  44.5 5.6 %collective-permute-start.16 = (f32[32,128]{1,0:T(8,128)S(1)}, f32[32,128]{1,0:T(8,128)S(1)}, u32[]{:S(2)}, u32[]{:S(2)}) collective-permute-start(f32[32,128]{1,0:T(8,128)S(1)} %get-tuple-element.41), channel_id=1, source_target_pairs={{0,2},{1,3},{2,0},{3,1},{4,6},{5,7},{6,4},{7,5},{8,10},{9,11},{10,... | collective-permute-start | bytes 49160 | tf_op jit(solution)/shard_map/ppermute | solution.py:39
  48.4 5.5 %collective-permute-start.17 = (f32[32,128]{1,0:T(8,128)S(1)}, f32[32,128]{1,0:T(8,128)S(1)}, u32[]{:S(2)}, u32[]{:S(2)}) collective-permute-start(f32[32,128]{1,0:T(8,128)S(1)} %get-tuple-element.42), channel_id=1, source_target_pairs={{0,3},{1,2},{2,1},{3,0},{4,7},{5,6},{6,5},{7,4},{8,11},{9,10},{10,... | collective-permute-start | bytes 49160 | tf_op jit(solution)/shard_map/ppermute | solution.py:39
  53.9 1.9 %collective-permute-start.18 = (f32[32,128]{1,0:T(8,128)S(1)}, f32[32,128]{1,0:T(8,128)S(1)}, u32[]{:S(2)}, u32[]{:S(2)}) collective-permute-start(f32[32,128]{1,0:T(8,128)S(1)} %add_add_fusion), channel_id=1, source_target_pairs={{0,4},{4,0},{8,12},{12,8},{1,5},{5,1},{9,13},{13,9},{2,6},{6,2},{1... | collective-permute-start | bytes 49160 | tf_op jit(solution)/shard_map/ppermute | solution.py:39
  53.9 3.8 %collective-permute-start.19 = (f32[32,128]{1,0:T(8,128)S(1)}, f32[32,128]{1,0:T(8,128)S(1)}, u32[]{:S(2)}, u32[]{:S(2)}) collective-permute-start(f32[32,128]{1,0:T(8,128)S(1)} %add_add_fusion), channel_id=1, source_target_pairs={{0,8},{4,12},{8,0},{12,4},{1,9},{5,13},{9,1},{13,5},{2,10},{6,14},... | collective-permute-start | bytes 49160 | tf_op jit(solution)/shard_map/ppermute | solution.py:39
  54.9 3.2 %collective-permute-start.20 = (f32[32,128]{1,0:T(8,128)S(1)}, f32[32,128]{1,0:T(8,128)S(1)}, u32[]{:S(2)}, u32[]{:S(2)}) collective-permute-start(f32[32,128]{1,0:T(8,128)S(1)} %add_add_fusion), channel_id=1, source_target_pairs={{0,12},{4,8},{8,4},{12,0},{1,13},{5,9},{9,5},{13,1},{2,14},{6,10},... | collective-permute-start | bytes 49160 | tf_op jit(solution)/shard_map/ppermute | solution.py:39

commit v10 on v9

--- a/solution.py
+++ b/solution.py
@@ -89,7 +89,7 @@
 
 
 def modulation_kernel(
-    time_ref, weight_hbm, start_hbm, qkv_hbm, inw_hbm, out_ref, qkv_ref, inw_ref, weight_ref, start_ref, sems
+    time_ref, weight_hbm, start_hbm, qkv_hbm, inw_hbm, out_ref, qkv_ref, inw_ref, weight_ref, start_ref, out_s, sems
 ):
     rows = start_ref.shape[0]
     half = weight_ref.shape[0] // 2
@@ -107,9 +107,10 @@
     embedding = jnp.concatenate([jnp.cos(angles), jnp.sin(angles)], axis=1).astype(BF16)
     wait_copies(copies[:2])
     result = bdot(embedding, weight_ref[...])
-    out_ref[0:rows, :] = start_ref[...]
+    out_s[0:rows, :] = start_ref[...]
     for r in range(weight_ref.shape[1] // LANES):
-        out_ref[rows + r : rows + r + 1, :] = result[0:1, r * LANES : (r + 1) * LANES]
+        out_s[rows + r : rows + r + 1, :] = result[0:1, r * LANES : (r + 1) * LANES]
+    out_ref[...] = out_s[...].astype(BF16)
     wait_copies(copies[2:])
 
 
@@ -180,8 +181,8 @@
     )
     for k, msg in enumerate(msgs):
         at = place("tensor", nt, k)
-        start_s[at] = msg[0 : start_s.shape[1], :]
-        mod_s[at, 0 : msg.shape[0] - start_s.shape[1], :] = msg[start_s.shape[1] :, :]
+        start_s[at] = msg[0 : start_s.shape[1], :].astype(F32)
+        mod_s[at, 0 : msg.shape[0] - start_s.shape[1], :] = msg[start_s.shape[1] :, :].astype(F32)
     channels, width = mean_ref.shape[0], z_s.shape[1]
     chunks = width // LANES
     per = 3 * chunks // nt
@@ -243,25 +244,36 @@
     return folded, resid
 
 
+def attend_kernel(nm, early, head_count, *refs):
+    heads, refs = refs[:early], refs[early:]
+    start_ref, factor_ref, base_ref, gram_ref, gate_ref, out_w_ref, inw_ref = refs[:7]
+    att_ref, fold_ref, resid_ref = refs[7:]
+    x = start_ref[...].astype(BF16)
+    fold_ref[...], resid_ref[...] = fold_parts(nm, 0, heads, gate_ref, out_w_ref, inw_ref)
+    att_ref[...] = attend(x, factor_ref, base_ref, gram_ref, head_count)
+
+
 def add_own_rows(result, residual, rows):
     first = lax.axis_index("tensor") * rows
     at = lax.broadcasted_iota(jnp.int32, result.shape, 0)
     return result + jnp.where((at >= first) & (at < first + rows), residual, 0.0)
 
 
-def first_kernel(nm, rows, head_count, *refs):
-    heads, refs = refs[:nm], refs[nm:]
-    step_ref, start_ref, factor_ref, base_ref, gram_ref, gate_ref, out_w_ref, inw_ref = refs[:8]
+def fold_kernel(nm, late, rows, *refs):
+    heads, refs = refs[:late], refs[late:]
+    step_ref, gate_ref, out_w_ref, inw_ref, fold_in, resid_in, att_ref, start_ref = refs[:8]
     fold_ref, resid_ref, vel_ref = refs[8:]
-    x = start_ref[...].astype(BF16)
-    total, resid = fold_parts(nm, 0, heads, gate_ref, out_w_ref, inw_ref)
-    attended = attend(x, factor_ref, base_ref, gram_ref, head_count)
-    channels = resid.shape[0]
+    channels = resid_in.shape[0]
+    total, resid = fold_in[...], resid_in[...]
+    if late:
+        more = fold_parts(nm, nm - late, heads, gate_ref, out_w_ref, inw_ref)
+        total, resid = total + more[0], resid + more[1]
     folded = total.astype(BF16)
     fold_ref[...] = folded
     for i, term in enumerate(split_terms(resid, 2)):
         resid_ref[i * channels : (i + 1) * channels, :] = term
-    vel = bdot(attended, folded)
+    x = start_ref[...].astype(BF16)
+    vel = bdot(att_ref[...], folded)
     residual = bdot(jnp.concatenate([x, x], axis=1), resid_ref[...])
     vel_ref[...] = (add_own_rows(vel, residual, rows) * step_ref[0:1, :]).astype(vel_ref.dtype)
 
@@ -284,7 +296,7 @@
         return
     vel_s[...] = vel.reshape(vel_s.shape)
     for k in range(len(outs)):
-        outs[k][...] = vel_s[lax.axis_index("tensor") ^ k]
+        outs[k][...] = vel_s[lax.axis_index("tensor") ^ k].astype(outs[k].dtype)
 
 
 def shape_of(shape, dtype):
@@ -317,7 +329,8 @@
 
 def earlier_sum(value, inclusive):
     if is_small("tm"):
-        return sum_earlier(gather_parts(value, "tm"), inclusive)
+        parts = gather_parts(value.astype(BF16), "tm")
+        return sum_earlier([value] + parts[1:], inclusive)
     everything = lax.all_gather(value, "tm").astype(F32)
     index = jnp.arange(everything.shape[0]).reshape((-1,) + (1,) * value.ndim)
     me = lax.axis_index("tm")
@@ -354,7 +367,7 @@
         message, qkv_near, inw_parts[0] = call(
             modulation_kernel,
             [
-                shape_of((rows + mod_rows, LANES), F32),
+                shape_of((rows + mod_rows, LANES), BF16),
                 shape_of((width, near * block), BF16),
                 shape_of(inw_parts[0].shape, BF16),
             ],
@@ -362,6 +375,7 @@
             [
                 pltpu.VMEM(mod_weight.shape, BF16),
                 pltpu.VMEM(start_latent.shape, F32),
+                pltpu.VMEM((rows + mod_rows, LANES), F32),
                 pltpu.SemaphoreType.DMA((4,)),
             ],
             time_index,
@@ -425,17 +439,18 @@
         limit=32,
     )
     head_parts = gather_weight_parts(head_weight, "tm")
-    folded, resid, vel = call(
-        functools.partial(first_kernel, nm, rows, head_count),
+    late = 1 if nm > 1 else 0
+    early = nm - late
+    attended, fold_part, resid_part = call(
+        functools.partial(attend_kernel, nm, early, head_count),
         [
-            shape_of((span, channels), BF16),
-            shape_of((2 * channels, channels), BF16),
-            shape_of((tokens, channels), BF16),
+            shape_of((tokens, head_count * HD), BF16),
+            shape_of((span, channels), F32),
+            shape_of((channels, channels), F32),
         ],
-        [VMEM] * (nm + 8),
+        [VMEM] * (early + 7),
         [],
-        *head_parts,
-        step,
+        *head_parts[:early],
         start_all,
         factor,
         base,
@@ -443,6 +458,26 @@
         gate,
         out_near,
         inw_all,
+        limit=16,
+    )
+    folded, resid, vel = call(
+        functools.partial(fold_kernel, nm, late, rows),
+        [
+            shape_of((span, channels), BF16),
+            shape_of((2 * channels, channels), BF16),
+            shape_of((tokens, channels), BF16),
+        ],
+        [VMEM] * (late + 8),
+        [],
+        *head_parts[early:],
+        step,
+        gate,
+        out_near,
+        inw_all,
+        fold_part,
+        resid_part,
+        attended,
+        start_all,
         limit=16,
     )
     small = is_small("tensor")
@@ -455,7 +490,7 @@
             pieces = [lax.psum(earlier, "tensor")]
         split = last and small
         if split:
-            outs = [shape_of((rows, channels), F32)] * n_tensor
+            outs = [shape_of((rows, channels), BF16 if k else F32) for k in range(n_tensor)]
         else:
             outs = [shape_of((tokens, channels), F32 if last else BF16)]
         vels = call(
@@ -476,7 +511,7 @@
     if small:
         drift = vels[0]
         for k in range(1, n_tensor):
-            drift = drift + swap(vels[k], "tensor", k)
+            drift = drift + swap(vels[k], "tensor", k).astype(F32)
     else:
         drift = lax.psum_scatter(vel, "tensor", scatter_dimension=0, tiled=True)
     return (start_latent + earlier_sum(drift, True))[None]

time: 58.8 us -> 58.9 us (level)
    pallas_call x5 -> x6, Pallas kernels: 9.92 us -> 10.3 us  [call(): pl.pallas_call(kernel, out_shape=outs, in_specs=in_specs, out_specs=[VMEM...]
  transfers between devices with their start and end apart: 21 -> 21, of which waited for: 12 -> 12; matrix products, arithmetic and copies ran while one was open for 0% -> 0% of each run, Pallas kernels for 12% -> 15%
where the time goes in v10:
time: 58.9 us; the launch traced here: 58.8 us
  waiting for transfers between devices  25.4 us (43%)
  starting transfers between devices  21 us (36%)
  Pallas kernels  10.3 us (17%)
  between operations  1.43 us (2%)
  other arithmetic  0.65 us (1%)
    ppermute x21, waiting for transfers between devices, swap(): return lax.ppermute(value, axis, [(i, i ^ k) for i in range(n)])  25.4 us
    ppermute x21, starting transfers between devices, swap(): return lax.ppermute(value, axis, [(i, i ^ k) for i in range(n)])  21 us
    pallas_call x6, Pallas kernels, call(): pl.pallas_call(kernel, out_shape=outs, in_specs=in_specs, out_specs=[VMEM...  10.3 us
  transfers between devices with their start and end apart: 21, of which 12 were waited for; matrix products, arithmetic and copies ran while one was open for 0% of the time, Pallas kernels for 15%

profile of v10, /device:TPU:0, one launch (start us, length us, event | category | flops | bytes accessed | tf_op | source)
XLA Modules:
  0.0 58.8 jit_solution(2357700166571541698)
XLA Ops:
  0.0 3.0 %collective-permute-start.3 = (bf16[32,3072]{1,0:T(8,128)(2,1)}, bf16[32,3072]{1,0:T(8,128)(2,1)S(1)}, u32[]{:S(2)}, u32[]{:S(2)}) collective-permute-start(bf16[32,3072]{1,0:T(8,128)(2,1)} %inw_hbm.1), channel_id=1, source_target_pairs={{0,8},{4,12},{8,0},{12,4},{1,9},{5,13},{9,1},{13,5},{2,10},{6,14},... | collective-permute-start | bytes 589832 | tf_op jit(solution)/shard_map/ppermute | solution.py:39
  3.0 5.9 %collective-permute-done.3.refs_2_ = bf16[32,3072]{1,0:T(8,128)(2,1)S(1)} collective-permute-done((bf16[32,3072]{1,0:T(8,128)(2,1)}, bf16[32,3072]{1,0:T(8,128)(2,1)S(1)}, u32[]{:S(2)}, u32[]{:S(2)}) %collective-permute-start.3) | collective-permute-done | bytes 196640 | tf_op jit(solution)/shard_map/ppermute | solution.py:39
  8.9 0.5 collective-permute-start.8
  9.4 2.9 %collective-permute-done.refs_2_ = bf16[768,128]{1,0:T(8,128)(2,1)S(1)} collective-permute-done((bf16[768,128]{1,0:T(8,128)(2,1)}, bf16[768,128]{1,0:T(8,128)(2,1)S(1)}, u32[]{:S(2)}, u32[]{:S(2)}) %collective-permute-start) | collective-permute-done | bytes 196640 | tf_op jit(solution)/shard_map/ppermute | solution.py:39
  12.9 2.4 %shard_map.82 = (bf16[50,128]{1,0:T(8,128)(2,1)S(1)}, bf16[3072,512]{1,0:T(8,128)(2,1)S(1)}, bf16[32,3072]{1,0:T(8,128)(2,1)S(1)}) custom-call(s32[1]{0:T(128)S(6)} %copy.9.time_ref, bf16[256,2304]{1,0:T(8,128)(2,1)} %weight_hbm.1, f32[32,128]{1,0:T(8,128)} %start_hbm.1, bf16[3072,1536]{1,0:T(8,128)(2,1)} %refs_7_.1, bf16[32,3072]{1,0:T(8,128)(2,1)} %inw_hbm.1), custom_call_target="tpu_custom_call" | custom-call | bytes 4194304 | tf_op jit(solution)/shard_map/pallas_call | solution.py:311
  15.3 1.9 %collective-permute-start.5 = (bf16[50,128]{1,0:T(8,128)(2,1)S(1)}, bf16[50,128]{1,0:T(8,128)(2,1)S(1)}, u32[]{:S(2)}, u32[]{:S(2)}) collective-permute-start(bf16[50,128]{1,0:T(8,128)(2,1)S(1)} %get-tuple-element.29.refs_0_), channel_id=1, source_target_pairs={{0,1},{1,0},{2,3},{3,2},{4,5},{5,4},{6,7},{7,6},{8,9},{9,8},{10,11... | collective-permute-start | bytes 38408 | tf_op jit(solution)/shard_map/ppermute | solution.py:39
  17.2 2.6 %collective-permute-start.6 = (bf16[50,128]{1,0:T(8,128)(2,1)S(1)}, bf16[50,128]{1,0:T(8,128)(2,1)S(1)}, u32[]{:S(2)}, u32[]{:S(2)}) collective-permute-start(bf16[50,128]{1,0:T(8,128)(2,1)S(1)} %get-tuple-element.29.refs_0_), channel_id=1, source_target_pairs={{0,2},{1,3},{2,0},{3,1},{4,6},{5,7},{6,4},{7,5},{8,10},{9,11},{10,... | collective-permute-start | bytes 38408 | tf_op jit(solution)/shard_map/ppermute | solution.py:39
  20.5 0.5 shard_map.83
  20.9 0.9 %collective-permute-done.6.refs_2_ = bf16[50,128]{1,0:T(8,128)(2,1)S(1)} collective-permute-done((bf16[50,128]{1,0:T(8,128)(2,1)S(1)}, bf16[50,128]{1,0:T(8,128)(2,1)S(1)}, u32[]{:S(2)}, u32[]{:S(2)}) %collective-permute-start.6) | collective-permute-done | bytes 12832 | tf_op jit(solution)/shard_map/ppermute | solution.py:39
  21.8 3.5 %collective-permute-done.7.refs_3_ = bf16[50,128]{1,0:T(8,128)(2,1)S(1)} collective-permute-done((bf16[50,128]{1,0:T(8,128)(2,1)S(1)}, bf16[50,128]{1,0:T(8,128)(2,1)S(1)}, u32[]{:S(2)}, u32[]{:S(2)}) %collective-permute-start.7) | collective-permute-done | bytes 12832 | tf_op jit(solution)/shard_map/ppermute | solution.py:39
  25.3 4.3 %shard_map.84 = (bf16[256,1536]{1,0:T(8,128)(2,1)S(1)}, f32[8,1536]{1,0:T(8,128)S(1)}, f32[128,128]{1,0:T(8,128)S(1)}, f32[4,128,8]{2,1,0:T(8,128)S(1)}, bf16[512,3072]{1,0:T(8,128)(2,1)S(1)}) custom-call(bf16[50,128]{1,0:T(8,128)(2,1)S(1)} %get-tuple-element.29.refs_0_, bf16[50,128]{1,0:T(8,128)(2,1)S(1)} %collective-permute-done.5.refs_1_, ...), custom_call_target="tpu_custom_call" | custom-call | bytes 4194304 | tf_op jit(solution)/shard_map/pallas_call | solution.py:311
  29.6 1.5 %shard_map.85 = (bf16[128,512]{1,0:T(8,128)(2,1)S(1)}, f32[512,128]{1,0:T(8,128)S(1)}, f32[128,128]{1,0:T(8,128)S(1)}) custom-call(bf16[768,128]{1,0:T(8,128)(2,1)S(1)} %copy-done, bf16[768,128]{1,0:T(8,128)(2,1)S(1)} %collective-permute-done.8.refs_1_, bf16[768,128]{1,0:T(8,128)(2,1)S(1)} %collective-permute-done.refs_2_, ...), custom_call_target="tpu_custom_call" | custom-call | bytes 4194304 | tf_op jit(solution)/shard_map/pallas_call | solution.py:311
  31.2 0.7 %shard_map.86 = (bf16[512,128]{1,0:T(8,128)(2,1)S(1)}, bf16[256,128]{1,0:T(8,128)(2,1)S(1)}, bf16[128,128]{1,0:T(8,128)(2,1)S(1)}) custom-call(bf16[768,128]{1,0:T(8,128)(2,1)S(1)} %collective-permute-done.1.refs_0_, f32[8,128]{1,0:T(8,128)S(1)} %get-tuple-element.28.refs_1_.refs_4_, f32[4,128,8]{2,1,0:T(8,128)S(1)} %get-tuple-element.33.refs_7_.refs_2_, ...), custom_call_target="tpu_custom_call" | custom-call | bytes 4194304 | tf_op jit(solution)/shard_map/pallas_call | solution.py:311
  31.9 1.5 %collective-permute-start.10 = (bf16[128,128]{1,0:T(8,128)(2,1)S(1)}, bf16[128,128]{1,0:T(8,128)(2,1)S(1)}, u32[]{:S(2)}, u32[]{:S(2)}) collective-permute-start(bf16[128,128]{1,0:T(8,128)(2,1)S(1)} %get-tuple-element.42), channel_id=1, source_target_pairs={{0,8},{4,12},{8,0},{12,4},{1,9},{5,13},{9,1},{13,5},{2,10},{6,14},... | collective-permute-start | bytes 98312 | tf_op jit(solution)/shard_map/ppermute | solution.py:39
  33.5 0.7 %collective-permute-start.9 = (bf16[128,128]{1,0:T(8,128)(2,1)S(1)}, bf16[128,128]{1,0:T(8,128)(2,1)S(1)}, u32[]{:S(2)}, u32[]{:S(2)}) collective-permute-start(bf16[128,128]{1,0:T(8,128)(2,1)S(1)} %get-tuple-element.42), channel_id=1, source_target_pairs={{0,4},{4,0},{8,12},{12,8},{1,5},{5,1},{9,13},{13,9},{2,6},{6,2},{1... | collective-permute-start | bytes 98312 | tf_op jit(solution)/shard_map/ppermute | solution.py:39
  34.1 1.8 %collective-permute-done.10 = bf16[128,128]{1,0:T(8,128)(2,1)S(1)} collective-permute-done((bf16[128,128]{1,0:T(8,128)(2,1)S(1)}, bf16[128,128]{1,0:T(8,128)(2,1)S(1)}, u32[]{:S(2)}, u32[]{:S(2)}) %collective-permute-start.10) | collective-permute-done | bytes 32800 | tf_op jit(solution)/shard_map/ppermute | solution.py:39
  35.9 0.9 %collective-permute-done.11 = bf16[128,128]{1,0:T(8,128)(2,1)S(1)} collective-permute-done((bf16[128,128]{1,0:T(8,128)(2,1)S(1)}, bf16[128,128]{1,0:T(8,128)(2,1)S(1)}, u32[]{:S(2)}, u32[]{:S(2)}) %collective-permute-start.11) | collective-permute-done | bytes 32800 | tf_op jit(solution)/shard_map/ppermute | solution.py:39
  36.9 0.8 %collective-permute-start.13 = (bf16[128,128]{1,0:T(8,128)(2,1)S(1)}, bf16[128,128]{1,0:T(8,128)(2,1)S(1)}, u32[]{:S(2)}, u32[]{:S(2)}) collective-permute-start(bf16[128,128]{1,0:T(8,128)(2,1)S(1)} %add_convert_fusion.refs_0_), channel_id=1, source_target_pairs={{0,2},{1,3},{2,0},{3,1},{4,6},{5,7},{6,4},{7,5},{8,10},{9,11},{10,... | collective-permute-start | bytes 98312 | tf_op jit(solution)/shard_map/ppermute | solution.py:39
  37.7 3.6 %collective-permute-start.14 = (bf16[128,128]{1,0:T(8,128)(2,1)S(1)}, bf16[128,128]{1,0:T(8,128)(2,1)S(1)}, u32[]{:S(2)}, u32[]{:S(2)}) collective-permute-start(bf16[128,128]{1,0:T(8,128)(2,1)S(1)} %add_convert_fusion.refs_0_), channel_id=1, source_target_pairs={{0,3},{1,2},{2,1},{3,0},{4,7},{5,6},{6,5},{7,4},{8,11},{9,10},{10,... | collective-permute-start | bytes 98312 | tf_op jit(solution)/shard_map/ppermute | solution.py:39
  41.3 0.6 %collective-permute-done.13.refs_2_ = bf16[128,128]{1,0:T(8,128)(2,1)S(1)} collective-permute-done((bf16[128,128]{1,0:T(8,128)(2,1)S(1)}, bf16[128,128]{1,0:T(8,128)(2,1)S(1)}, u32[]{:S(2)}, u32[]{:S(2)}) %collective-permute-start.13) | collective-permute-done | bytes 32800 | tf_op jit(solution)/shard_map/ppermute | solution.py:39
  41.9 1.6 %collective-permute-done.14.refs_3_ = bf16[128,128]{1,0:T(8,128)(2,1)S(1)} collective-permute-done((bf16[128,128]{1,0:T(8,128)(2,1)S(1)}, bf16[128,128]{1,0:T(8,128)(2,1)S(1)}, u32[]{:S(2)}, u32[]{:S(2)}) %collective-permute-start.14) | collective-permute-done | bytes 32800 | tf_op jit(solution)/shard_map/ppermute | solution.py:39
  43.5 0.9 %shard_map.87 = (f32[32,128]{1,0:T(8,128)S(1)}, bf16[32,128]{1,0:T(8,128)(2,1)S(1)}, bf16[32,128]{1,0:T(8,128)(2,1)S(1)}, bf16[32,128]{1,0:T(8,128)(2,1)S(1)}) custom-call(bf16[128,128]{1,0:T(8,128)(2,1)S(1)} %add_convert_fusion.refs_0_, bf16[128,128]{1,0:T(8,128)(2,1)S(1)} %collective-permute-done.12.refs_1_, ...), custom_call_target="tpu_custom_call" | custom-call | bytes 4194304 | tf_op jit(solution)/shard_map/pallas_call | solution.py:311
  44.4 0.3 collective-permute-start.15
  44.7 3.8 %collective-permute-start.16 = (bf16[32,128]{1,0:T(8,128)(2,1)S(1)}, bf16[32,128]{1,0:T(8,128)(2,1)S(1)}, u32[]{:S(2)}, u32[]{:S(2)}) collective-permute-start(bf16[32,128]{1,0:T(8,128)(2,1)S(1)} %get-tuple-element.47), channel_id=1, source_target_pairs={{0,2},{1,3},{2,0},{3,1},{4,6},{5,7},{6,4},{7,5},{8,10},{9,11},{10,... | collective-permute-start | bytes 24584 | tf_op jit(solution)/shard_map/ppermute | solution.py:39
  48.5 0.4 collective-permute-start.17
  48.9 1.3 %collective-permute-done.16 = bf16[32,128]{1,0:T(8,128)(2,1)S(1)} collective-permute-done((bf16[32,128]{1,0:T(8,128)(2,1)S(1)}, bf16[32,128]{1,0:T(8,128)(2,1)S(1)}, u32[]{:S(2)}, u32[]{:S(2)}) %collective-permute-start.16) | collective-permute-done | bytes 8224 | tf_op jit(solution)/shard_map/ppermute | solution.py:39
  50.2 3.8 %collective-permute-done.17 = bf16[32,128]{1,0:T(8,128)(2,1)S(1)} collective-permute-done((bf16[32,128]{1,0:T(8,128)(2,1)S(1)}, bf16[32,128]{1,0:T(8,128)(2,1)S(1)}, u32[]{:S(2)}, u32[]{:S(2)}) %collective-permute-start.17) | collective-permute-done | bytes 8224 | tf_op jit(solution)/shard_map/ppermute | solution.py:39
  54.1 1.0 %collective-permute-start.19 = (bf16[32,128]{1,0:T(8,128)(2,1)S(1)}, bf16[32,128]{1,0:T(8,128)(2,1)S(1)}, u32[]{:S(2)}, u32[]{:S(2)}) collective-permute-start(bf16[32,128]{1,0:T(8,128)(2,1)S(1)} %fusion), channel_id=1, source_target_pairs={{0,8},{4,12},{8,0},{12,4},{1,9},{5,13},{9,1},{13,5},{2,10},{6,14},... | collective-permute-start | bytes 24584 | tf_op jit(solution)/shard_map/ppermute | solution.py:39
  55.1 0.9 %collective-permute-start.20 = (bf16[32,128]{1,0:T(8,128)(2,1)S(1)}, bf16[32,128]{1,0:T(8,128)(2,1)S(1)}, u32[]{:S(2)}, u32[]{:S(2)}) collective-permute-start(bf16[32,128]{1,0:T(8,128)(2,1)S(1)} %fusion), channel_id=1, source_target_pairs={{0,12},{4,8},{8,4},{12,0},{1,13},{5,9},{9,5},{13,1},{2,14},{6,10},... | collective-permute-start | bytes 24584 | tf_op jit(solution)/shard_map/ppermute | solution.py:39
  55.9 1.9 %collective-permute-done.19 = bf16[32,128]{1,0:T(8,128)(2,1)S(1)} collective-permute-done((bf16[32,128]{1,0:T(8,128)(2,1)S(1)}, bf16[32,128]{1,0:T(8,128)(2,1)S(1)}, u32[]{:S(2)}, u32[]{:S(2)}) %collective-permute-start.19) | collective-permute-done | bytes 8224 | tf_op jit(solution)/shard_map/ppermute | solution.py:39
  57.8 0.3 collective-permute-done.20
  58.1 0.6 %add_bitcast_fusion = f32[1,32,128]{2,1,0:T(8,128)} fusion(f32[32,128]{1,0:T(8,128)S(1)} %copy-done.1, bf16[32,128]{1,0:T(8,128)(2,1)S(1)} %collective-permute-done.20, bf16[32,128]{1,0:T(8,128)(2,1)S(1)} %collective-permute-done.19, bf16[32,128]{1,0:T(8,128)(2,1)S(1)} %collective-permute-done.18, pred[]{:T(512)S(6)} %lt.14, pred[]{:T(512)S(6)} %lt.13, ...), kind=kLoop, calls=%fused_computation.1 | loop fusion | flops 65536 | bytes 98307 | tf_op jit(solution)/shard_map/broadcast_in_dim | solution.py:517
  (23 shorter events, 0.2 us)
Async XLA Ops:
  0.0 8.9 %collective-permute-start.3 = (bf16[32,3072]{1,0:T(8,128)(2,1)}, bf16[32,3072]{1,0:T(8,128)(2,1)S(1)}, u32[]{:S(2)}, u32[]{:S(2)}) collective-permute-start(bf16[32,3072]{1,0:T(8,128)(2,1)} %inw_hbm.1), channel_id=1, source_target_pairs={{0,8},{4,12},{8,0},{12,4},{1,9},{5,13},{9,1},{13,5},{2,10},{6,14},... | collective-permute-start | bytes 589832 | tf_op jit(solution)/shard_map/ppermute | solution.py:39
  3.0 9.3 %collective-permute-start = (bf16[768,128]{1,0:T(8,128)(2,1)}, bf16[768,128]{1,0:T(8,128)(2,1)S(1)}, u32[]{:S(2)}, u32[]{:S(2)}) collective-permute-start(bf16[768,128]{1,0:T(8,128)(2,1)} %refs_0_.1), channel_id=1, source_target_pairs={{0,8},{4,12},{8,0},{12,4},{1,9},{5,13},{9,1},{13,5},{2,10},{6,14},... | collective-permute-start | bytes 589832 | tf_op jit(solution)/shard_map/ppermute | solution.py:39
  3.0 14.2 %collective-permute-start.2 = (bf16[32,3072]{1,0:T(8,128)(2,1)}, bf16[32,3072]{1,0:T(8,128)(2,1)S(1)}, u32[]{:S(2)}, u32[]{:S(2)}) collective-permute-start(bf16[32,3072]{1,0:T(8,128)(2,1)} %inw_hbm.1), channel_id=1, source_target_pairs={{0,4},{4,0},{8,12},{12,8},{1,5},{5,1},{9,13},{13,9},{2,6},{6,2},{1... | collective-permute-start | bytes 589832 | tf_op jit(solution)/shard_map/ppermute | solution.py:39
  8.9 10.9 %collective-permute-start.4 = (bf16[32,3072]{1,0:T(8,128)(2,1)S(1)}, bf16[32,3072]{1,0:T(8,128)(2,1)S(1)}, u32[]{:S(2)}, u32[]{:S(2)}) collective-permute-start(bf16[32,3072]{1,0:T(8,128)(2,1)S(1)} %collective-permute-done.3.refs_2_), channel_id=1, source_target_pairs={{0,4},{4,0},{8,12},{12,8},{1,5},{5,1},{9,13},{13,9},{2,6},{6,2},{1... | collective-permute-start | bytes 589832 | tf_op jit(solution)/shard_map/ppermute | solution.py:39
  8.9 20.7 %collective-permute-start.8 = (bf16[768,128]{1,0:T(8,128)(2,1)}, bf16[768,128]{1,0:T(8,128)(2,1)S(1)}, u32[]{:S(2)}, u32[]{:S(2)}) collective-permute-start(bf16[768,128]{1,0:T(8,128)(2,1)} %refs_0_.1), channel_id=1, source_target_pairs={{0,4},{4,0},{8,12},{12,8},{1,5},{5,1},{9,13},{13,9},{2,6},{6,2},{1... | collective-permute-start | bytes 589832 | tf_op jit(solution)/shard_map/ppermute | solution.py:39
  12.3 18.9 %collective-permute-start.1 = (bf16[768,128]{1,0:T(8,128)(2,1)S(1)}, bf16[768,128]{1,0:T(8,128)(2,1)S(1)}, u32[]{:S(2)}, u32[]{:S(2)}) collective-permute-start(bf16[768,128]{1,0:T(8,128)(2,1)S(1)} %collective-permute-done.refs_2_), channel_id=1, source_target_pairs={{0,4},{4,0},{8,12},{12,8},{1,5},{5,1},{9,13},{13,9},{2,6},{6,2},{1... | collective-permute-start | bytes 589832 | tf_op jit(solution)/shard_map/ppermute | solution.py:39
  15.3 5.6 %collective-permute-start.5 = (bf16[50,128]{1,0:T(8,128)(2,1)S(1)}, bf16[50,128]{1,0:T(8,128)(2,1)S(1)}, u32[]{:S(2)}, u32[]{:S(2)}) collective-permute-start(bf16[50,128]{1,0:T(8,128)(2,1)S(1)} %get-tuple-element.29.refs_0_), channel_id=1, source_target_pairs={{0,1},{1,0},{2,3},{3,2},{4,5},{5,4},{6,7},{7,6},{8,9},{9,8},{10,11... | collective-permute-start | bytes 38408 | tf_op jit(solution)/shard_map/ppermute | solution.py:39
  17.2 4.6 %collective-permute-start.6 = (bf16[50,128]{1,0:T(8,128)(2,1)S(1)}, bf16[50,128]{1,0:T(8,128)(2,1)S(1)}, u32[]{:S(2)}, u32[]{:S(2)}) collective-permute-start(bf16[50,128]{1,0:T(8,128)(2,1)S(1)} %get-tuple-element.29.refs_0_), channel_id=1, source_target_pairs={{0,2},{1,3},{2,0},{3,1},{4,6},{5,7},{6,4},{7,5},{8,10},{9,11},{10,... | collective-permute-start | bytes 38408 | tf_op jit(solution)/shard_map/ppermute | solution.py:39
  19.8 5.5 %collective-permute-start.7 = (bf16[50,128]{1,0:T(8,128)(2,1)S(1)}, bf16[50,128]{1,0:T(8,128)(2,1)S(1)}, u32[]{:S(2)}, u32[]{:S(2)}) collective-permute-start(bf16[50,128]{1,0:T(8,128)(2,1)S(1)} %get-tuple-element.29.refs_0_), channel_id=1, source_target_pairs={{0,3},{1,2},{2,1},{3,0},{4,7},{5,6},{6,5},{7,4},{8,11},{9,10},{10,... | collective-permute-start | bytes 38408 | tf_op jit(solution)/shard_map/ppermute | solution.py:39
  25.3 4.3 %copy-start = (bf16[768,128]{1,0:T(8,128)(2,1)S(1)}, bf16[768,128]{1,0:T(8,128)(2,1)}, u32[]{:S(2)}) copy-start(bf16[768,128]{1,0:T(8,128)(2,1)} %refs_0_.1) | copy-start | bytes 589828
  31.2 27.0 %copy-start.1 = (f32[32,128]{1,0:T(8,128)S(1)}, f32[32,128]{1,0:T(8,128)}, u32[]{:S(2)}) copy-start(f32[32,128]{1,0:T(8,128)} %start_hbm.1) | copy-start | bytes 49156
  31.9 4.0 %collective-permute-start.10 = (bf16[128,128]{1,0:T(8,128)(2,1)S(1)}, bf16[128,128]{1,0:T(8,128)(2,1)S(1)}, u32[]{:S(2)}, u32[]{:S(2)}) collective-permute-start(bf16[128,128]{1,0:T(8,128)(2,1)S(1)} %get-tuple-element.42), channel_id=1, source_target_pairs={{0,8},{4,12},{8,0},{12,4},{1,9},{5,13},{9,1},{13,5},{2,10},{6,14},... | collective-permute-start | bytes 98312 | tf_op jit(solution)/shard_map/ppermute | solution.py:39
  33.5 3.3 %collective-permute-start.11 = (bf16[128,128]{1,0:T(8,128)(2,1)S(1)}, bf16[128,128]{1,0:T(8,128)(2,1)S(1)}, u32[]{:S(2)}, u32[]{:S(2)}) collective-permute-start(bf16[128,128]{1,0:T(8,128)(2,1)S(1)} %get-tuple-element.42), channel_id=1, source_target_pairs={{0,12},{4,8},{8,4},{12,0},{1,13},{5,9},{9,5},{13,1},{2,14},{6,10},... | collective-permute-start | bytes 98312 | tf_op jit(solution)/shard_map/ppermute | solution.py:39
  33.5 3.3 %collective-permute-start.9 = (bf16[128,128]{1,0:T(8,128)(2,1)S(1)}, bf16[128,128]{1,0:T(8,128)(2,1)S(1)}, u32[]{:S(2)}, u32[]{:S(2)}) collective-permute-start(bf16[128,128]{1,0:T(8,128)(2,1)S(1)} %get-tuple-element.42), channel_id=1, source_target_pairs={{0,4},{4,0},{8,12},{12,8},{1,5},{5,1},{9,13},{13,9},{2,6},{6,2},{1... | collective-permute-start | bytes 98312 | tf_op jit(solution)/shard_map/ppermute | solution.py:39
  36.9 4.5 %collective-permute-start.12 = (bf16[128,128]{1,0:T(8,128)(2,1)S(1)}, bf16[128,128]{1,0:T(8,128)(2,1)S(1)}, u32[]{:S(2)}, u32[]{:S(2)}) collective-permute-start(bf16[128,128]{1,0:T(8,128)(2,1)S(1)} %add_convert_fusion.refs_0_), channel_id=1, source_target_pairs={{0,1},{1,0},{2,3},{3,2},{4,5},{5,4},{6,7},{7,6},{8,9},{9,8},{10,11... | collective-permute-start | bytes 98312 | tf_op jit(solution)/shard_map/ppermute | solution.py:39
  36.9 5.0 %collective-permute-start.13 = (bf16[128,128]{1,0:T(8,128)(2,1)S(1)}, bf16[128,128]{1,0:T(8,128)(2,1)S(1)}, u32[]{:S(2)}, u32[]{:S(2)}) collective-permute-start(bf16[128,128]{1,0:T(8,128)(2,1)S(1)} %add_convert_fusion.refs_0_), channel_id=1, source_target_pairs={{0,2},{1,3},{2,0},{3,1},{4,6},{5,7},{6,4},{7,5},{8,10},{9,11},{10,... | collective-permute-start | bytes 98312 | tf_op jit(solution)/shard_map/ppermute | solution.py:39
  37.7 5.8 %collective-permute-start.14 = (bf16[128,128]{1,0:T(8,128)(2,1)S(1)}, bf16[128,128]{1,0:T(8,128)(2,1)S(1)}, u32[]{:S(2)}, u32[]{:S(2)}) collective-permute-start(bf16[128,128]{1,0:T(8,128)(2,1)S(1)} %add_convert_fusion.refs_0_), channel_id=1, source_target_pairs={{0,3},{1,2},{2,1},{3,0},{4,7},{5,6},{6,5},{7,4},{8,11},{9,10},{10,... | collective-permute-start | bytes 98312 | tf_op jit(solution)/shard_map/ppermute | solution.py:39
  44.4 4.5 %collective-permute-start.15 = (bf16[32,128]{1,0:T(8,128)(2,1)S(1)}, bf16[32,128]{1,0:T(8,128)(2,1)S(1)}, u32[]{:S(2)}, u32[]{:S(2)}) collective-permute-start(bf16[32,128]{1,0:T(8,128)(2,1)S(1)} %get-tuple-element.46), channel_id=1, source_target_pairs={{0,1},{1,0},{2,3},{3,2},{4,5},{5,4},{6,7},{7,6},{8,9},{9,8},{10,11... | collective-permute-start | bytes 24584 | tf_op jit(solution)/shard_map/ppermute | solution.py:39
  44.7 5.5 %collective-permute-start.16 = (bf16[32,128]{1,0:T(8,128)(2,1)S(1)}, bf16[32,128]{1,0:T(8,128)(2,1)S(1)}, u32[]{:S(2)}, u32[]{:S(2)}) collective-permute-start(bf16[32,128]{1,0:T(8,128)(2,1)S(1)} %get-tuple-element.47), channel_id=1, source_target_pairs={{0,2},{1,3},{2,0},{3,1},{4,6},{5,7},{6,4},{7,5},{8,10},{9,11},{10,... | collective-permute-start | bytes 24584 | tf_op jit(solution)/shard_map/ppermute | solution.py:39
  48.5 5.4 %collective-permute-start.17 = (bf16[32,128]{1,0:T(8,128)(2,1)S(1)}, bf16[32,128]{1,0:T(8,128)(2,1)S(1)}, u32[]{:S(2)}, u32[]{:S(2)}) collective-permute-start(bf16[32,128]{1,0:T(8,128)(2,1)S(1)} %get-tuple-element.48), channel_id=1, source_target_pairs={{0,3},{1,2},{2,1},{3,0},{4,7},{5,6},{6,5},{7,4},{8,11},{9,10},{10,... | collective-permute-start | bytes 24584 | tf_op jit(solution)/shard_map/ppermute | solution.py:39
  54.0 1.9 %collective-permute-start.18 = (bf16[32,128]{1,0:T(8,128)(2,1)S(1)}, bf16[32,128]{1,0:T(8,128)(2,1)S(1)}, u32[]{:S(2)}, u32[]{:S(2)}) collective-permute-start(bf16[32,128]{1,0:T(8,128)(2,1)S(1)} %fusion), channel_id=1, source_target_pairs={{0,4},{4,0},{8,12},{12,8},{1,5},{5,1},{9,13},{13,9},{2,6},{6,2},{1... | collective-permute-start | bytes 24584 | tf_op jit(solution)/shard_map/ppermute | solution.py:39
  54.1 3.7 %collective-permute-start.19 = (bf16[32,128]{1,0:T(8,128)(2,1)S(1)}, bf16[32,128]{1,0:T(8,128)(2,1)S(1)}, u32[]{:S(2)}, u32[]{:S(2)}) collective-permute-start(bf16[32,128]{1,0:T(8,128)(2,1)S(1)} %fusion), channel_id=1, source_target_pairs={{0,8},{4,12},{8,0},{12,4},{1,9},{5,13},{9,1},{13,5},{2,10},{6,14},... | collective-permute-start | bytes 24584 | tf_op jit(solution)/shard_map/ppermute | solution.py:39
  55.1 3.1 %collective-permute-start.20 = (bf16[32,128]{1,0:T(8,128)(2,1)S(1)}, bf16[32,128]{1,0:T(8,128)(2,1)S(1)}, u32[]{:S(2)}, u32[]{:S(2)}) collective-permute-start(bf16[32,128]{1,0:T(8,128)(2,1)S(1)} %fusion), channel_id=1, source_target_pairs={{0,12},{4,8},{8,4},{12,0},{1,13},{5,9},{9,5},{13,1},{2,14},{6,10},... | collective-permute-start | bytes 24584 | tf_op jit(solution)/shard_map/ppermute | solution.py:39

commit v11 on v10

--- a/solution.py
+++ b/solution.py
@@ -89,7 +89,7 @@
 
 
 def modulation_kernel(
-    time_ref, weight_hbm, start_hbm, qkv_hbm, inw_hbm, out_ref, qkv_ref, inw_ref, weight_ref, start_ref, out_s, sems
+    time_ref, weight_hbm, start_hbm, qkv_hbm, inw_hbm, out_ref, qkv_ref, inw_ref, weight_ref, start_ref, sems
 ):
     rows = start_ref.shape[0]
     half = weight_ref.shape[0] // 2
@@ -107,10 +107,9 @@
     embedding = jnp.concatenate([jnp.cos(angles), jnp.sin(angles)], axis=1).astype(BF16)
     wait_copies(copies[:2])
     result = bdot(embedding, weight_ref[...])
-    out_s[0:rows, :] = start_ref[...]
+    out_ref[0:rows, :] = start_ref[...]
     for r in range(weight_ref.shape[1] // LANES):
-        out_s[rows + r : rows + r + 1, :] = result[0:1, r * LANES : (r + 1) * LANES]
-    out_ref[...] = out_s[...].astype(BF16)
+        out_ref[rows + r : rows + r + 1, :] = result[0:1, r * LANES : (r + 1) * LANES]
     wait_copies(copies[2:])
 
 
@@ -181,8 +180,8 @@
     )
     for k, msg in enumerate(msgs):
         at = place("tensor", nt, k)
-        start_s[at] = msg[0 : start_s.shape[1], :].astype(F32)
-        mod_s[at, 0 : msg.shape[0] - start_s.shape[1], :] = msg[start_s.shape[1] :, :].astype(F32)
+        start_s[at] = msg[0 : start_s.shape[1], :]
+        mod_s[at, 0 : msg.shape[0] - start_s.shape[1], :] = msg[start_s.shape[1] :, :]
     channels, width = mean_ref.shape[0], z_s.shape[1]
     chunks = width // LANES
     per = 3 * chunks // nt
@@ -296,7 +295,7 @@
         return
     vel_s[...] = vel.reshape(vel_s.shape)
     for k in range(len(outs)):
-        outs[k][...] = vel_s[lax.axis_index("tensor") ^ k].astype(outs[k].dtype)
+        outs[k][...] = vel_s[lax.axis_index("tensor") ^ k]
 
 
 def shape_of(shape, dtype):
@@ -329,8 +328,7 @@
 
 def earlier_sum(value, inclusive):
     if is_small("tm"):
-        parts = gather_parts(value.astype(BF16), "tm")
-        return sum_earlier([value] + parts[1:], inclusive)
+        return sum_earlier(gather_parts(value, "tm"), inclusive)
     everything = lax.all_gather(value, "tm").astype(F32)
     index = jnp.arange(everything.shape[0]).reshape((-1,) + (1,) * value.ndim)
     me = lax.axis_index("tm")
@@ -367,7 +365,7 @@
         message, qkv_near, inw_parts[0] = call(
             modulation_kernel,
             [
-                shape_of((rows + mod_rows, LANES), BF16),
+                shape_of((rows + mod_rows, LANES), F32),
                 shape_of((width, near * block), BF16),
                 shape_of(inw_parts[0].shape, BF16),
             ],
@@ -375,7 +373,6 @@
             [
                 pltpu.VMEM(mod_weight.shape, BF16),
                 pltpu.VMEM(start_latent.shape, F32),
-                pltpu.VMEM((rows + mod_rows, LANES), F32),
                 pltpu.SemaphoreType.DMA((4,)),
             ],
             time_index,
@@ -490,7 +487,7 @@
             pieces = [lax.psum(earlier, "tensor")]
         split = last and small
         if split:
-            outs = [shape_of((rows, channels), BF16 if k else F32) for k in range(n_tensor)]
+            outs = [shape_of((rows, channels), F32)] * n_tensor
         else:
             outs = [shape_of((tokens, channels), F32 if last else BF16)]
         vels = call(
@@ -511,7 +508,7 @@
     if small:
         drift = vels[0]
         for k in range(1, n_tensor):
-            drift = drift + swap(vels[k], "tensor", k).astype(F32)
+            drift = drift + swap(vels[k], "tensor", k)
     else:
         drift = lax.psum_scatter(vel, "tensor", scatter_dimension=0, tiled=True)
     return (start_latent + earlier_sum(drift, True))[None]

time: 58.9 us -> 59.2 us (level)
  no operation moved by 1% of the time
where the time goes in v11:
time: 59.2 us; the launch traced here: 59 us
  waiting for transfers between devices  25.7 us (43%)
  starting transfers between devices  21 us (35%)
  Pallas kernels  10.3 us (17%)
  between operations  1.42 us (2%)
  other arithmetic  0.65 us (1%)
    ppermute x21, waiting for transfers between devices, swap(): return lax.ppermute(value, axis, [(i, i ^ k) for i in range(n)])  25.7 us
    ppermute x21, starting transfers between devices, swap(): return lax.ppermute(value, axis, [(i, i ^ k) for i in range(n)])  21 us
    pallas_call x6, Pallas kernels, call(): pl.pallas_call(kernel, out_shape=outs, in_specs=in_specs, out_specs=[VMEM...  10.3 us
  transfers between devices with their start and end apart: 21, of which 12 were waited for; matrix products, arithmetic and copies ran while one was open for 0% of the time, Pallas kernels for 15%

profile of v11, /device:TPU:0, one launch (start us, length us, event | category | flops | bytes accessed | tf_op | source)
XLA Modules:
  0.0 59.0 jit_solution(14230990221568816954)
XLA Ops:
  0.0 3.0 %collective-permute-start.3 = (bf16[32,3072]{1,0:T(8,128)(2,1)}, bf16[32,3072]{1,0:T(8,128)(2,1)S(1)}, u32[]{:S(2)}, u32[]{:S(2)}) collective-permute-start(bf16[32,3072]{1,0:T(8,128)(2,1)} %inw_hbm.1), channel_id=1, source_target_pairs={{0,8},{4,12},{8,0},{12,4},{1,9},{5,13},{9,1},{13,5},{2,10},{6,14},... | collective-permute-start | bytes 589832 | tf_op jit(solution)/shard_map/ppermute | solution.py:39
  3.0 5.9 %collective-permute-done.3.refs_2_ = bf16[32,3072]{1,0:T(8,128)(2,1)S(1)} collective-permute-done((bf16[32,3072]{1,0:T(8,128)(2,1)}, bf16[32,3072]{1,0:T(8,128)(2,1)S(1)}, u32[]{:S(2)}, u32[]{:S(2)}) %collective-permute-start.3) | collective-permute-done | bytes 196640 | tf_op jit(solution)/shard_map/ppermute | solution.py:39
  8.9 0.5 collective-permute-start.8
  9.4 2.9 %collective-permute-done.refs_2_ = bf16[768,128]{1,0:T(8,128)(2,1)S(1)} collective-permute-done((bf16[768,128]{1,0:T(8,128)(2,1)}, bf16[768,128]{1,0:T(8,128)(2,1)S(1)}, u32[]{:S(2)}, u32[]{:S(2)}) %collective-permute-start) | collective-permute-done | bytes 196640 | tf_op jit(solution)/shard_map/ppermute | solution.py:39
  12.9 2.4 %shard_map.82 = (f32[50,128]{1,0:T(8,128)S(1)}, bf16[3072,512]{1,0:T(8,128)(2,1)S(1)}, bf16[32,3072]{1,0:T(8,128)(2,1)S(1)}) custom-call(s32[1]{0:T(128)S(6)} %copy.9.time_ref, bf16[256,2304]{1,0:T(8,128)(2,1)} %weight_hbm.1, f32[32,128]{1,0:T(8,128)} %start_hbm.1, bf16[3072,1536]{1,0:T(8,128)(2,1)} %refs_7_.1, bf16[32,3072]{1,0:T(8,128)(2,1)} %inw_hbm.1), custom_call_target="tpu_custom_call" | custom-call | bytes 4194304 | tf_op jit(solution)/shard_map/pallas_call | solution.py:310
  15.3 1.9 %collective-permute-start.5 = (f32[50,128]{1,0:T(8,128)S(1)}, f32[50,128]{1,0:T(8,128)S(1)}, u32[]{:S(2)}, u32[]{:S(2)}) collective-permute-start(f32[50,128]{1,0:T(8,128)S(1)} %get-tuple-element.29.refs_0_), channel_id=1, source_target_pairs={{0,1},{1,0},{2,3},{3,2},{4,5},{5,4},{6,7},{7,6},{8,9},{9,8},{10,11... | collective-permute-start | bytes 76808 | tf_op jit(solution)/shard_map/ppermute | solution.py:39
  17.2 2.6 %collective-permute-start.6 = (f32[50,128]{1,0:T(8,128)S(1)}, f32[50,128]{1,0:T(8,128)S(1)}, u32[]{:S(2)}, u32[]{:S(2)}) collective-permute-start(f32[50,128]{1,0:T(8,128)S(1)} %get-tuple-element.29.refs_0_), channel_id=1, source_target_pairs={{0,2},{1,3},{2,0},{3,1},{4,6},{5,7},{6,4},{7,5},{8,10},{9,11},{10,... | collective-permute-start | bytes 76808 | tf_op jit(solution)/shard_map/ppermute | solution.py:39
  20.5 0.5 shard_map.83
  20.9 1.4 %collective-permute-done.6.refs_2_ = f32[50,128]{1,0:T(8,128)S(1)} collective-permute-done((f32[50,128]{1,0:T(8,128)S(1)}, f32[50,128]{1,0:T(8,128)S(1)}, u32[]{:S(2)}, u32[]{:S(2)}) %collective-permute-start.6) | collective-permute-done | bytes 25632 | tf_op jit(solution)/shard_map/ppermute | solution.py:39
  22.3 3.1 %collective-permute-done.7.refs_3_ = f32[50,128]{1,0:T(8,128)S(1)} collective-permute-done((f32[50,128]{1,0:T(8,128)S(1)}, f32[50,128]{1,0:T(8,128)S(1)}, u32[]{:S(2)}, u32[]{:S(2)}) %collective-permute-start.7) | collective-permute-done | bytes 25632 | tf_op jit(solution)/shard_map/ppermute | solution.py:39
  25.5 4.3 %shard_map.84 = (bf16[256,1536]{1,0:T(8,128)(2,1)S(1)}, f32[8,1536]{1,0:T(8,128)S(1)}, f32[128,128]{1,0:T(8,128)S(1)}, f32[4,128,8]{2,1,0:T(8,128)S(1)}, bf16[512,3072]{1,0:T(8,128)(2,1)S(1)}) custom-call(f32[50,128]{1,0:T(8,128)S(1)} %get-tuple-element.29.refs_0_, f32[50,128]{1,0:T(8,128)S(1)} %collective-permute-done.5.refs_1_, ...), custom_call_target="tpu_custom_call" | custom-call | bytes 4194304 | tf_op jit(solution)/shard_map/pallas_call | solution.py:310
  29.8 1.5 %shard_map.85 = (bf16[128,512]{1,0:T(8,128)(2,1)S(1)}, f32[512,128]{1,0:T(8,128)S(1)}, f32[128,128]{1,0:T(8,128)S(1)}) custom-call(bf16[768,128]{1,0:T(8,128)(2,1)S(1)} %copy-done, bf16[768,128]{1,0:T(8,128)(2,1)S(1)} %collective-permute-done.8.refs_1_, bf16[768,128]{1,0:T(8,128)(2,1)S(1)} %collective-permute-done.refs_2_, ...), custom_call_target="tpu_custom_call" | custom-call | bytes 4194304 | tf_op jit(solution)/shard_map/pallas_call | solution.py:310
  31.4 0.7 %shard_map.86 = (bf16[512,128]{1,0:T(8,128)(2,1)S(1)}, bf16[256,128]{1,0:T(8,128)(2,1)S(1)}, bf16[128,128]{1,0:T(8,128)(2,1)S(1)}) custom-call(bf16[768,128]{1,0:T(8,128)(2,1)S(1)} %collective-permute-done.1.refs_0_, f32[8,128]{1,0:T(8,128)S(1)} %get-tuple-element.28.refs_1_.refs_4_, f32[4,128,8]{2,1,0:T(8,128)S(1)} %get-tuple-element.33.refs_7_.refs_2_, ...), custom_call_target="tpu_custom_call" | custom-call | bytes 4194304 | tf_op jit(solution)/shard_map/pallas_call | solution.py:310
  32.1 1.6 %collective-permute-start.10 = (bf16[128,128]{1,0:T(8,128)(2,1)S(1)}, bf16[128,128]{1,0:T(8,128)(2,1)S(1)}, u32[]{:S(2)}, u32[]{:S(2)}) collective-permute-start(bf16[128,128]{1,0:T(8,128)(2,1)S(1)} %get-tuple-element.42), channel_id=1, source_target_pairs={{0,8},{4,12},{8,0},{12,4},{1,9},{5,13},{9,1},{13,5},{2,10},{6,14},... | collective-permute-start | bytes 98312 | tf_op jit(solution)/shard_map/ppermute | solution.py:39
  33.7 0.6 %collective-permute-start.9 = (bf16[128,128]{1,0:T(8,128)(2,1)S(1)}, bf16[128,128]{1,0:T(8,128)(2,1)S(1)}, u32[]{:S(2)}, u32[]{:S(2)}) collective-permute-start(bf16[128,128]{1,0:T(8,128)(2,1)S(1)} %get-tuple-element.42), channel_id=1, source_target_pairs={{0,4},{4,0},{8,12},{12,8},{1,5},{5,1},{9,13},{13,9},{2,6},{6,2},{1... | collective-permute-start | bytes 98312 | tf_op jit(solution)/shard_map/ppermute | solution.py:39
  34.3 1.8 %collective-permute-done.10 = bf16[128,128]{1,0:T(8,128)(2,1)S(1)} collective-permute-done((bf16[128,128]{1,0:T(8,128)(2,1)S(1)}, bf16[128,128]{1,0:T(8,128)(2,1)S(1)}, u32[]{:S(2)}, u32[]{:S(2)}) %collective-permute-start.10) | collective-permute-done | bytes 32800 | tf_op jit(solution)/shard_map/ppermute | solution.py:39
  36.1 0.9 %collective-permute-done.11 = bf16[128,128]{1,0:T(8,128)(2,1)S(1)} collective-permute-done((bf16[128,128]{1,0:T(8,128)(2,1)S(1)}, bf16[128,128]{1,0:T(8,128)(2,1)S(1)}, u32[]{:S(2)}, u32[]{:S(2)}) %collective-permute-start.11) | collective-permute-done | bytes 32800 | tf_op jit(solution)/shard_map/ppermute | solution.py:39
  37.1 0.9 %collective-permute-start.13 = (bf16[128,128]{1,0:T(8,128)(2,1)S(1)}, bf16[128,128]{1,0:T(8,128)(2,1)S(1)}, u32[]{:S(2)}, u32[]{:S(2)}) collective-permute-start(bf16[128,128]{1,0:T(8,128)(2,1)S(1)} %add_convert_fusion.refs_0_), channel_id=1, source_target_pairs={{0,2},{1,3},{2,0},{3,1},{4,6},{5,7},{6,4},{7,5},{8,10},{9,11},{10,... | collective-permute-start | bytes 98312 | tf_op jit(solution)/shard_map/ppermute | solution.py:39
  38.0 3.5 %collective-permute-start.14 = (bf16[128,128]{1,0:T(8,128)(2,1)S(1)}, bf16[128,128]{1,0:T(8,128)(2,1)S(1)}, u32[]{:S(2)}, u32[]{:S(2)}) collective-permute-start(bf16[128,128]{1,0:T(8,128)(2,1)S(1)} %add_convert_fusion.refs_0_), channel_id=1, source_target_pairs={{0,3},{1,2},{2,1},{3,0},{4,7},{5,6},{6,5},{7,4},{8,11},{9,10},{10,... | collective-permute-start | bytes 98312 | tf_op jit(solution)/shard_map/ppermute | solution.py:39
  41.5 0.6 collective-permute-done.13.refs_2_
  42.1 1.7 %collective-permute-done.14.refs_3_ = bf16[128,128]{1,0:T(8,128)(2,1)S(1)} collective-permute-done((bf16[128,128]{1,0:T(8,128)(2,1)S(1)}, bf16[128,128]{1,0:T(8,128)(2,1)S(1)}, u32[]{:S(2)}, u32[]{:S(2)}) %collective-permute-start.14) | collective-permute-done | bytes 32800 | tf_op jit(solution)/shard_map/ppermute | solution.py:39
  43.7 0.9 %shard_map.87 = (f32[32,128]{1,0:T(8,128)S(1)}, f32[32,128]{1,0:T(8,128)S(1)}, f32[32,128]{1,0:T(8,128)S(1)}, f32[32,128]{1,0:T(8,128)S(1)}) custom-call(bf16[128,128]{1,0:T(8,128)(2,1)S(1)} %add_convert_fusion.refs_0_, bf16[128,128]{1,0:T(8,128)(2,1)S(1)} %collective-permute-done.12.refs_1_, bf16[128,128]{1,0:T(8,128)(2,1)S(1)} %collective-permute-done.13.refs_2_, ...), custom_call_target="tpu_custom_call" | custom-call | bytes 4194304 | tf_op jit(solution)/shard_map/pallas_call | solution.py:310
  44.6 0.3 collective-permute-start.15
  44.9 3.8 %collective-permute-start.16 = (f32[32,128]{1,0:T(8,128)S(1)}, f32[32,128]{1,0:T(8,128)S(1)}, u32[]{:S(2)}, u32[]{:S(2)}) collective-permute-start(f32[32,128]{1,0:T(8,128)S(1)} %get-tuple-element.47), channel_id=1, source_target_pairs={{0,2},{1,3},{2,0},{3,1},{4,6},{5,7},{6,4},{7,5},{8,10},{9,11},{10,... | collective-permute-start | bytes 49160 | tf_op jit(solution)/shard_map/ppermute | solution.py:39
  48.7 0.3 collective-permute-start.17
  49.1 1.4 %collective-permute-done.16 = f32[32,128]{1,0:T(8,128)S(1)} collective-permute-done((f32[32,128]{1,0:T(8,128)S(1)}, f32[32,128]{1,0:T(8,128)S(1)}, u32[]{:S(2)}, u32[]{:S(2)}) %collective-permute-start.16) | collective-permute-done | bytes 16416 | tf_op jit(solution)/shard_map/ppermute | solution.py:39
  50.5 3.8 %collective-permute-done.17 = f32[32,128]{1,0:T(8,128)S(1)} collective-permute-done((f32[32,128]{1,0:T(8,128)S(1)}, f32[32,128]{1,0:T(8,128)S(1)}, u32[]{:S(2)}, u32[]{:S(2)}) %collective-permute-start.17) | collective-permute-done | bytes 16416 | tf_op jit(solution)/shard_map/ppermute | solution.py:39
  54.3 0.9 %collective-permute-start.19 = (f32[32,128]{1,0:T(8,128)S(1)}, f32[32,128]{1,0:T(8,128)S(1)}, u32[]{:S(2)}, u32[]{:S(2)}) collective-permute-start(f32[32,128]{1,0:T(8,128)S(1)} %add_add_fusion), channel_id=1, source_target_pairs={{0,8},{4,12},{8,0},{12,4},{1,9},{5,13},{9,1},{13,5},{2,10},{6,14},... | collective-permute-start | bytes 49160 | tf_op jit(solution)/shard_map/ppermute | solution.py:39
  55.2 0.9 %collective-permute-start.20 = (f32[32,128]{1,0:T(8,128)S(1)}, f32[32,128]{1,0:T(8,128)S(1)}, u32[]{:S(2)}, u32[]{:S(2)}) collective-permute-start(f32[32,128]{1,0:T(8,128)S(1)} %add_add_fusion), channel_id=1, source_target_pairs={{0,12},{4,8},{8,4},{12,0},{1,13},{5,9},{9,5},{13,1},{2,14},{6,10},... | collective-permute-start | bytes 49160 | tf_op jit(solution)/shard_map/ppermute | solution.py:39
  56.1 1.9 %collective-permute-done.19 = f32[32,128]{1,0:T(8,128)S(1)} collective-permute-done((f32[32,128]{1,0:T(8,128)S(1)}, f32[32,128]{1,0:T(8,128)S(1)}, u32[]{:S(2)}, u32[]{:S(2)}) %collective-permute-start.19) | collective-permute-done | bytes 16416 | tf_op jit(solution)/shard_map/ppermute | solution.py:39
  58.1 0.3 collective-permute-done.20
  58.4 0.6 %add_bitcast_fusion = f32[1,32,128]{2,1,0:T(8,128)} fusion(f32[32,128]{1,0:T(8,128)S(1)} %copy-done.1, f32[32,128]{1,0:T(8,128)S(1)} %collective-permute-done.20, f32[32,128]{1,0:T(8,128)S(1)} %collective-permute-done.19, f32[32,128]{1,0:T(8,128)S(1)} %add_add_fusion, f32[32,128]{1,0:T(8,128)S(1)} %collective-permute-done.18, pred[]{:T(512)S(6)} %lt.14, ...), kind=kLoop, calls=%fused_computation.1 | loop fusion | flops 28672 | bytes 98307 | tf_op jit(solution)/shard_map/broadcast_in_dim | solution.py:514
  (23 shorter events, 0.2 us)
Async XLA Ops:
  0.0 8.9 %collective-permute-start.3 = (bf16[32,3072]{1,0:T(8,128)(2,1)}, bf16[32,3072]{1,0:T(8,128)(2,1)S(1)}, u32[]{:S(2)}, u32[]{:S(2)}) collective-permute-start(bf16[32,3072]{1,0:T(8,128)(2,1)} %inw_hbm.1), channel_id=1, source_target_pairs={{0,8},{4,12},{8,0},{12,4},{1,9},{5,13},{9,1},{13,5},{2,10},{6,14},... | collective-permute-start | bytes 589832 | tf_op jit(solution)/shard_map/ppermute | solution.py:39
  3.0 9.3 %collective-permute-start = (bf16[768,128]{1,0:T(8,128)(2,1)}, bf16[768,128]{1,0:T(8,128)(2,1)S(1)}, u32[]{:S(2)}, u32[]{:S(2)}) collective-permute-start(bf16[768,128]{1,0:T(8,128)(2,1)} %refs_0_.1), channel_id=1, source_target_pairs={{0,8},{4,12},{8,0},{12,4},{1,9},{5,13},{9,1},{13,5},{2,10},{6,14},... | collective-permute-start | bytes 589832 | tf_op jit(solution)/shard_map/ppermute | solution.py:39
  3.0 14.2 %collective-permute-start.2 = (bf16[32,3072]{1,0:T(8,128)(2,1)}, bf16[32,3072]{1,0:T(8,128)(2,1)S(1)}, u32[]{:S(2)}, u32[]{:S(2)}) collective-permute-start(bf16[32,3072]{1,0:T(8,128)(2,1)} %inw_hbm.1), channel_id=1, source_target_pairs={{0,4},{4,0},{8,12},{12,8},{1,5},{5,1},{9,13},{13,9},{2,6},{6,2},{1... | collective-permute-start | bytes 589832 | tf_op jit(solution)/shard_map/ppermute | solution.py:39
  8.9 10.9 %collective-permute-start.4 = (bf16[32,3072]{1,0:T(8,128)(2,1)S(1)}, bf16[32,3072]{1,0:T(8,128)(2,1)S(1)}, u32[]{:S(2)}, u32[]{:S(2)}) collective-permute-start(bf16[32,3072]{1,0:T(8,128)(2,1)S(1)} %collective-permute-done.3.refs_2_), channel_id=1, source_target_pairs={{0,4},{4,0},{8,12},{12,8},{1,5},{5,1},{9,13},{13,9},{2,6},{6,2},{1... | collective-permute-start | bytes 589832 | tf_op jit(solution)/shard_map/ppermute | solution.py:39
  8.9 20.9 %collective-permute-start.8 = (bf16[768,128]{1,0:T(8,128)(2,1)}, bf16[768,128]{1,0:T(8,128)(2,1)S(1)}, u32[]{:S(2)}, u32[]{:S(2)}) collective-permute-start(bf16[768,128]{1,0:T(8,128)(2,1)} %refs_0_.1), channel_id=1, source_target_pairs={{0,4},{4,0},{8,12},{12,8},{1,5},{5,1},{9,13},{13,9},{2,6},{6,2},{1... | collective-permute-start | bytes 589832 | tf_op jit(solution)/shard_map/ppermute | solution.py:39
  12.3 19.0 %collective-permute-start.1 = (bf16[768,128]{1,0:T(8,128)(2,1)S(1)}, bf16[768,128]{1,0:T(8,128)(2,1)S(1)}, u32[]{:S(2)}, u32[]{:S(2)}) collective-permute-start(bf16[768,128]{1,0:T(8,128)(2,1)S(1)} %collective-permute-done.refs_2_), channel_id=1, source_target_pairs={{0,4},{4,0},{8,12},{12,8},{1,5},{5,1},{9,13},{13,9},{2,6},{6,2},{1... | collective-permute-start | bytes 589832 | tf_op jit(solution)/shard_map/ppermute | solution.py:39
  15.3 5.6 %collective-permute-start.5 = (f32[50,128]{1,0:T(8,128)S(1)}, f32[50,128]{1,0:T(8,128)S(1)}, u32[]{:S(2)}, u32[]{:S(2)}) collective-permute-start(f32[50,128]{1,0:T(8,128)S(1)} %get-tuple-element.29.refs_0_), channel_id=1, source_target_pairs={{0,1},{1,0},{2,3},{3,2},{4,5},{5,4},{6,7},{7,6},{8,9},{9,8},{10,11... | collective-permute-start | bytes 76808 | tf_op jit(solution)/shard_map/ppermute | solution.py:39
  17.2 5.1 %collective-permute-start.6 = (f32[50,128]{1,0:T(8,128)S(1)}, f32[50,128]{1,0:T(8,128)S(1)}, u32[]{:S(2)}, u32[]{:S(2)}) collective-permute-start(f32[50,128]{1,0:T(8,128)S(1)} %get-tuple-element.29.refs_0_), channel_id=1, source_target_pairs={{0,2},{1,3},{2,0},{3,1},{4,6},{5,7},{6,4},{7,5},{8,10},{9,11},{10,... | collective-permute-start | bytes 76808 | tf_op jit(solution)/shard_map/ppermute | solution.py:39
  19.8 5.7 %collective-permute-start.7 = (f32[50,128]{1,0:T(8,128)S(1)}, f32[50,128]{1,0:T(8,128)S(1)}, u32[]{:S(2)}, u32[]{:S(2)}) collective-permute-start(f32[50,128]{1,0:T(8,128)S(1)} %get-tuple-element.29.refs_0_), channel_id=1, source_target_pairs={{0,3},{1,2},{2,1},{3,0},{4,7},{5,6},{6,5},{7,4},{8,11},{9,10},{10,... | collective-permute-start | bytes 76808 | tf_op jit(solution)/shard_map/ppermute | solution.py:39
  25.5 4.3 %copy-start = (bf16[768,128]{1,0:T(8,128)(2,1)S(1)}, bf16[768,128]{1,0:T(8,128)(2,1)}, u32[]{:S(2)}) copy-start(bf16[768,128]{1,0:T(8,128)(2,1)} %refs_0_.1) | copy-start | bytes 589828
  31.3 27.1 %copy-start.1 = (f32[32,128]{1,0:T(8,128)S(1)}, f32[32,128]{1,0:T(8,128)}, u32[]{:S(2)}) copy-start(f32[32,128]{1,0:T(8,128)} %start_hbm.1) | copy-start | bytes 49156
  32.1 4.0 %collective-permute-start.10 = (bf16[128,128]{1,0:T(8,128)(2,1)S(1)}, bf16[128,128]{1,0:T(8,128)(2,1)S(1)}, u32[]{:S(2)}, u32[]{:S(2)}) collective-permute-start(bf16[128,128]{1,0:T(8,128)(2,1)S(1)} %get-tuple-element.42), channel_id=1, source_target_pairs={{0,8},{4,12},{8,0},{12,4},{1,9},{5,13},{9,1},{13,5},{2,10},{6,14},... | collective-permute-start | bytes 98312 | tf_op jit(solution)/shard_map/ppermute | solution.py:39
  33.7 3.3 %collective-permute-start.11 = (bf16[128,128]{1,0:T(8,128)(2,1)S(1)}, bf16[128,128]{1,0:T(8,128)(2,1)S(1)}, u32[]{:S(2)}, u32[]{:S(2)}) collective-permute-start(bf16[128,128]{1,0:T(8,128)(2,1)S(1)} %get-tuple-element.42), channel_id=1, source_target_pairs={{0,12},{4,8},{8,4},{12,0},{1,13},{5,9},{9,5},{13,1},{2,14},{6,10},... | collective-permute-start | bytes 98312 | tf_op jit(solution)/shard_map/ppermute | solution.py:39
  33.7 3.3 %collective-permute-start.9 = (bf16[128,128]{1,0:T(8,128)(2,1)S(1)}, bf16[128,128]{1,0:T(8,128)(2,1)S(1)}, u32[]{:S(2)}, u32[]{:S(2)}) collective-permute-start(bf16[128,128]{1,0:T(8,128)(2,1)S(1)} %get-tuple-element.42), channel_id=1, source_target_pairs={{0,4},{4,0},{8,12},{12,8},{1,5},{5,1},{9,13},{13,9},{2,6},{6,2},{1... | collective-permute-start | bytes 98312 | tf_op jit(solution)/shard_map/ppermute | solution.py:39
  37.0 4.5 %collective-permute-start.12 = (bf16[128,128]{1,0:T(8,128)(2,1)S(1)}, bf16[128,128]{1,0:T(8,128)(2,1)S(1)}, u32[]{:S(2)}, u32[]{:S(2)}) collective-permute-start(bf16[128,128]{1,0:T(8,128)(2,1)S(1)} %add_convert_fusion.refs_0_), channel_id=1, source_target_pairs={{0,1},{1,0},{2,3},{3,2},{4,5},{5,4},{6,7},{7,6},{8,9},{9,8},{10,11... | collective-permute-start | bytes 98312 | tf_op jit(solution)/shard_map/ppermute | solution.py:39
  37.1 5.0 %collective-permute-start.13 = (bf16[128,128]{1,0:T(8,128)(2,1)S(1)}, bf16[128,128]{1,0:T(8,128)(2,1)S(1)}, u32[]{:S(2)}, u32[]{:S(2)}) collective-permute-start(bf16[128,128]{1,0:T(8,128)(2,1)S(1)} %add_convert_fusion.refs_0_), channel_id=1, source_target_pairs={{0,2},{1,3},{2,0},{3,1},{4,6},{5,7},{6,4},{7,5},{8,10},{9,11},{10,... | collective-permute-start | bytes 98312 | tf_op jit(solution)/shard_map/ppermute | solution.py:39
  38.0 5.8 %collective-permute-start.14 = (bf16[128,128]{1,0:T(8,128)(2,1)S(1)}, bf16[128,128]{1,0:T(8,128)(2,1)S(1)}, u32[]{:S(2)}, u32[]{:S(2)}) collective-permute-start(bf16[128,128]{1,0:T(8,128)(2,1)S(1)} %add_convert_fusion.refs_0_), channel_id=1, source_target_pairs={{0,3},{1,2},{2,1},{3,0},{4,7},{5,6},{6,5},{7,4},{8,11},{9,10},{10,... | collective-permute-start | bytes 98312 | tf_op jit(solution)/shard_map/ppermute | solution.py:39
  44.6 4.5 %collective-permute-start.15 = (f32[32,128]{1,0:T(8,128)S(1)}, f32[32,128]{1,0:T(8,128)S(1)}, u32[]{:S(2)}, u32[]{:S(2)}) collective-permute-start(f32[32,128]{1,0:T(8,128)S(1)} %get-tuple-element.46), channel_id=1, source_target_pairs={{0,1},{1,0},{2,3},{3,2},{4,5},{5,4},{6,7},{7,6},{8,9},{9,8},{10,11... | collective-permute-start | bytes 49160 | tf_op jit(solution)/shard_map/ppermute | solution.py:39
  44.9 5.6 %collective-permute-start.16 = (f32[32,128]{1,0:T(8,128)S(1)}, f32[32,128]{1,0:T(8,128)S(1)}, u32[]{:S(2)}, u32[]{:S(2)}) collective-permute-start(f32[32,128]{1,0:T(8,128)S(1)} %get-tuple-element.47), channel_id=1, source_target_pairs={{0,2},{1,3},{2,0},{3,1},{4,6},{5,7},{6,4},{7,5},{8,10},{9,11},{10,... | collective-permute-start | bytes 49160 | tf_op jit(solution)/shard_map/ppermute | solution.py:39
  48.7 5.5 %collective-permute-start.17 = (f32[32,128]{1,0:T(8,128)S(1)}, f32[32,128]{1,0:T(8,128)S(1)}, u32[]{:S(2)}, u32[]{:S(2)}) collective-permute-start(f32[32,128]{1,0:T(8,128)S(1)} %get-tuple-element.48), channel_id=1, source_target_pairs={{0,3},{1,2},{2,1},{3,0},{4,7},{5,6},{6,5},{7,4},{8,11},{9,10},{10,... | collective-permute-start | bytes 49160 | tf_op jit(solution)/shard_map/ppermute | solution.py:39
  54.3 1.9 %collective-permute-start.18 = (f32[32,128]{1,0:T(8,128)S(1)}, f32[32,128]{1,0:T(8,128)S(1)}, u32[]{:S(2)}, u32[]{:S(2)}) collective-permute-start(f32[32,128]{1,0:T(8,128)S(1)} %add_add_fusion), channel_id=1, source_target_pairs={{0,4},{4,0},{8,12},{12,8},{1,5},{5,1},{9,13},{13,9},{2,6},{6,2},{1... | collective-permute-start | bytes 49160 | tf_op jit(solution)/shard_map/ppermute | solution.py:39
  54.3 3.8 %collective-permute-start.19 = (f32[32,128]{1,0:T(8,128)S(1)}, f32[32,128]{1,0:T(8,128)S(1)}, u32[]{:S(2)}, u32[]{:S(2)}) collective-permute-start(f32[32,128]{1,0:T(8,128)S(1)} %add_add_fusion), channel_id=1, source_target_pairs={{0,8},{4,12},{8,0},{12,4},{1,9},{5,13},{9,1},{13,5},{2,10},{6,14},... | collective-permute-start | bytes 49160 | tf_op jit(solution)/shard_map/ppermute | solution.py:39
  55.2 3.2 %collective-permute-start.20 = (f32[32,128]{1,0:T(8,128)S(1)}, f32[32,128]{1,0:T(8,128)S(1)}, u32[]{:S(2)}, u32[]{:S(2)}) collective-permute-start(f32[32,128]{1,0:T(8,128)S(1)} %add_add_fusion), channel_id=1, source_target_pairs={{0,12},{4,8},{8,4},{12,0},{1,13},{5,9},{9,5},{13,1},{2,14},{6,10},... | collective-permute-start | bytes 49160 | tf_op jit(solution)/shard_map/ppermute | solution.py:39

commit v12 on v10

--- a/solution.py
+++ b/solution.py
@@ -162,22 +162,23 @@
 
 def setup_kernel(nt, nm, block, *refs):
     msgs, refs = refs[:nt], refs[nt:]
-    inw_ref, mean_ref, near_ref, qkv_hbm, out_w_hbm = refs[:5]
+    inw_ref, mean_ref, near_ref, _, qkv_hbm = refs[:5]
     refs = refs[5:]
-    factor_ref, base_ref, start_ref, gate_ref, out_w_ref = refs[:5]
-    start_s, mod_s, gate_s, z_s, qkv_s, sems = refs[5:]
+    factor_ref, base_ref, start_ref, gate_ref = refs[:4]
+    start_s, mod_s, gate_s, z_s, qkv_s, sems = refs[4:]
     near = near_ref.shape[1] // block
     count = factor_ref.shape[1] // block
+    half = z_s.shape[1] // 2
     copies = run_copies(
         [
             pltpu.make_async_copy(
-                qkv_hbm.at[:, pl.ds(n * block, block)],
-                qkv_s.at[:, pl.ds((n - near) * block, block)],
-                sems.at[n - near],
+                qkv_hbm.at[pl.ds(p * half, half), pl.ds(n * block, block)],
+                qkv_s.at[pl.ds(p * half, half), pl.ds((n - near) * block, block)],
+                sems.at[2 * (n - near) + p],
             )
             for n in range(near, count)
+            for p in range(2)
         ]
-        + [pltpu.make_async_copy(out_w_hbm, out_w_ref, sems.at[count - near])]
     )
     for k, msg in enumerate(msgs):
         at = place("tensor", nt, k)
@@ -218,13 +219,17 @@
     start_ref[...] = start_s[...].reshape(start_ref.shape)
 
     for n in range(1, count):
-        if n < near:
-            weight = near_ref[:, n * block : (n + 1) * block]
-        else:
-            copies[n - near].wait()
-            weight = qkv_s[:, (n - near) * block : (n - near + 1) * block]
-        keep(bdot(z_s[...], weight), n)
-    copies[count - near].wait()
+        at = slice((n - near) * block, (n - near + 1) * block)
+        result = 0.0
+        for p in range(2):
+            rows_at = slice(p * half, (p + 1) * half)
+            if n < near:
+                weight = near_ref[rows_at, n * block : (n + 1) * block]
+            else:
+                copies[2 * (n - near) + p].wait()
+                weight = qkv_s[rows_at, at]
+            result = result + bdot(z_s[:, rows_at], weight)
+        keep(result, n)
 
 
 def fold_parts(nm, first, heads, gate_ref, out_w_ref, inw_ref):
@@ -412,30 +417,29 @@
         *inw_parts,
         limit=16,
     )
-    factor, base, start_all, gate, out_near = call(
+    factor, base, start_all, gate = call(
         functools.partial(setup_kernel, nt, nm, block),
         [
             shape_of((2 * channels, span_cols), BF16),
             shape_of((8, span_cols), F32),
             shape_of((tokens, channels), F32),
             shape_of((nm, LANES, gate_rows), F32),
-            shape_of(out_weight.shape, BF16),
         ],
-        [VMEM] * (nt + 3) + [HBM, HBM],
+        [VMEM] * (nt + 4) + [HBM],
         [
             pltpu.VMEM((nt, block_rows, channels), F32),
             pltpu.VMEM((nt, padded, LANES), F32),
             pltpu.VMEM((nm, gate_rows, LANES), F32),
             pltpu.VMEM((channels + 16, width), BF16),
             pltpu.VMEM((width, far * block), BF16),
-            pltpu.SemaphoreType.DMA((far + 1,)),
+            pltpu.SemaphoreType.DMA((2 * far,)),
         ],
         *messages,
         inw_all,
         mean,
         qkv_near,
+        out_weight,
         qkv_weight,
-        out_weight,
         limit=32,
     )
     head_parts = gather_weight_parts(head_weight, "tm")
@@ -456,7 +460,7 @@
         base,
         gram,
         gate,
-        out_near,
+        out_weight,
         inw_all,
         limit=16,
     )
@@ -472,7 +476,7 @@
         *head_parts[early:],
         step,
         gate,
-        out_near,
+        out_weight,
         inw_all,
         fold_part,
         resid_part,

time: 58.9 us -> 58.5 us (level)
  transfers between devices with their start and end apart: 21 -> 21, of which waited for: 12 -> 12; matrix products, arithmetic and copies ran while one was open for 0% -> 0% of each run, Pallas kernels for 15% -> 14%
where the time goes in v12:
time: 58.5 us; the launch traced here: 58.3 us
  waiting for transfers between devices  25.4 us (43%)
  starting transfers between devices  21 us (36%)
  Pallas kernels  9.81 us (17%)
  between operations  1.44 us (2%)
  other arithmetic  0.65 us (1%)
    ppermute x21, waiting for transfers between devices, swap(): return lax.ppermute(value, axis, [(i, i ^ k) for i in range(n)])  25.4 us
    ppermute x21, starting transfers between devices, swap(): return lax.ppermute(value, axis, [(i, i ^ k) for i in range(n)])  21 us
    pallas_call x6, Pallas kernels, call(): pl.pallas_call(kernel, out_shape=outs, in_specs=in_specs, out_specs=[VMEM...  9.81 us
  transfers between devices with their start and end apart: 21, of which 12 were waited for; matrix products, arithmetic and copies ran while one was open for 0% of the time, Pallas kernels for 14%

profile of v12, /device:TPU:0, one launch (start us, length us, event | category | flops | bytes accessed | tf_op | source)
XLA Modules:
  0.0 58.3 jit_solution(8409933318071511290)
XLA Ops:
  0.0 3.0 %collective-permute-start.3 = (bf16[32,3072]{1,0:T(8,128)(2,1)}, bf16[32,3072]{1,0:T(8,128)(2,1)S(1)}, u32[]{:S(2)}, u32[]{:S(2)}) collective-permute-start(bf16[32,3072]{1,0:T(8,128)(2,1)} %inw_hbm.1), channel_id=1, source_target_pairs={{0,8},{4,12},{8,0},{12,4},{1,9},{5,13},{9,1},{13,5},{2,10},{6,14},... | collective-permute-start | bytes 589832 | tf_op jit(solution)/shard_map/ppermute | solution.py:39
  3.0 5.9 %collective-permute-done.3.refs_2_ = bf16[32,3072]{1,0:T(8,128)(2,1)S(1)} collective-permute-done((bf16[32,3072]{1,0:T(8,128)(2,1)}, bf16[32,3072]{1,0:T(8,128)(2,1)S(1)}, u32[]{:S(2)}, u32[]{:S(2)}) %collective-permute-start.3) | collective-permute-done | bytes 196640 | tf_op jit(solution)/shard_map/ppermute | solution.py:39
  8.9 0.5 collective-permute-start.8
  9.4 2.9 %collective-permute-done.refs_2_ = bf16[768,128]{1,0:T(8,128)(2,1)S(1)} collective-permute-done((bf16[768,128]{1,0:T(8,128)(2,1)}, bf16[768,128]{1,0:T(8,128)(2,1)S(1)}, u32[]{:S(2)}, u32[]{:S(2)}) %collective-permute-start) | collective-permute-done | bytes 196640 | tf_op jit(solution)/shard_map/ppermute | solution.py:39
  13.0 2.5 %shard_map.82 = (bf16[50,128]{1,0:T(8,128)(2,1)S(1)}, bf16[3072,512]{1,0:T(8,128)(2,1)S(1)}, bf16[32,3072]{1,0:T(8,128)(2,1)S(1)}) custom-call(s32[1]{0:T(128)S(6)} %copy.9.time_ref, bf16[256,2304]{1,0:T(8,128)(2,1)} %weight_hbm.1, f32[32,128]{1,0:T(8,128)} %start_hbm.1, bf16[3072,1536]{1,0:T(8,128)(2,1)} %refs_8_.2, bf16[32,3072]{1,0:T(8,128)(2,1)} %inw_hbm.1), custom_call_target="tpu_custom_call" | custom-call | bytes 4194304 | tf_op jit(solution)/shard_map/pallas_call | solution.py:316
  15.5 1.9 %collective-permute-start.5 = (bf16[50,128]{1,0:T(8,128)(2,1)S(1)}, bf16[50,128]{1,0:T(8,128)(2,1)S(1)}, u32[]{:S(2)}, u32[]{:S(2)}) collective-permute-start(bf16[50,128]{1,0:T(8,128)(2,1)S(1)} %get-tuple-element.28.refs_0_), channel_id=1, source_target_pairs={{0,1},{1,0},{2,3},{3,2},{4,5},{5,4},{6,7},{7,6},{8,9},{9,8},{10,11... | collective-permute-start | bytes 38408 | tf_op jit(solution)/shard_map/ppermute | solution.py:39
  17.4 2.6 %collective-permute-start.6 = (bf16[50,128]{1,0:T(8,128)(2,1)S(1)}, bf16[50,128]{1,0:T(8,128)(2,1)S(1)}, u32[]{:S(2)}, u32[]{:S(2)}) collective-permute-start(bf16[50,128]{1,0:T(8,128)(2,1)S(1)} %get-tuple-element.28.refs_0_), channel_id=1, source_target_pairs={{0,2},{1,3},{2,0},{3,1},{4,6},{5,7},{6,4},{7,5},{8,10},{9,11},{10,... | collective-permute-start | bytes 38408 | tf_op jit(solution)/shard_map/ppermute | solution.py:39
  20.6 0.5 shard_map.83
  21.1 0.9 %collective-permute-done.6.refs_2_ = bf16[50,128]{1,0:T(8,128)(2,1)S(1)} collective-permute-done((bf16[50,128]{1,0:T(8,128)(2,1)S(1)}, bf16[50,128]{1,0:T(8,128)(2,1)S(1)}, u32[]{:S(2)}, u32[]{:S(2)}) %collective-permute-start.6) | collective-permute-done | bytes 12832 | tf_op jit(solution)/shard_map/ppermute | solution.py:39
  22.0 3.5 %collective-permute-done.7.refs_3_ = bf16[50,128]{1,0:T(8,128)(2,1)S(1)} collective-permute-done((bf16[50,128]{1,0:T(8,128)(2,1)S(1)}, bf16[50,128]{1,0:T(8,128)(2,1)S(1)}, u32[]{:S(2)}, u32[]{:S(2)}) %collective-permute-start.7) | collective-permute-done | bytes 12832 | tf_op jit(solution)/shard_map/ppermute | solution.py:39
  25.5 3.7 %shard_map.84 = (bf16[256,1536]{1,0:T(8,128)(2,1)S(1)}, f32[8,1536]{1,0:T(8,128)S(1)}, f32[128,128]{1,0:T(8,128)S(1)}, f32[4,128,8]{2,1,0:T(8,128)S(1)}) custom-call(bf16[50,128]{1,0:T(8,128)(2,1)S(1)} %get-tuple-element.28.refs_0_, bf16[50,128]{1,0:T(8,128)(2,1)S(1)} %collective-permute-done.5.refs_1_, bf16[50,128]{1,0:T(8,128)(2,1)S(1)} %collective-permute-done.6.refs_2_, ...), custom_call_target="tpu_custom_call" | custom-call | bytes 4194304 | tf_op jit(solution)/shard_map/pallas_call | solution.py:316
  29.2 1.5 %shard_map.85 = (bf16[128,512]{1,0:T(8,128)(2,1)S(1)}, f32[512,128]{1,0:T(8,128)S(1)}, f32[128,128]{1,0:T(8,128)S(1)}) custom-call(bf16[768,128]{1,0:T(8,128)(2,1)S(1)} %copy-done.1, bf16[768,128]{1,0:T(8,128)(2,1)S(1)} %collective-permute-done.8.refs_1_, bf16[768,128]{1,0:T(8,128)(2,1)S(1)} %collective-permute-done.refs_2_, ...), custom_call_target="tpu_custom_call" | custom-call | bytes 4194304 | tf_op jit(solution)/shard_map/pallas_call | solution.py:316
  30.8 0.7 %shard_map.86 = (bf16[512,128]{1,0:T(8,128)(2,1)S(1)}, bf16[256,128]{1,0:T(8,128)(2,1)S(1)}, bf16[128,128]{1,0:T(8,128)(2,1)S(1)}) custom-call(bf16[768,128]{1,0:T(8,128)(2,1)S(1)} %collective-permute-done.1.refs_0_, f32[8,128]{1,0:T(8,128)S(1)} %get-tuple-element.27.refs_1_.refs_4_, f32[4,128,8]{2,1,0:T(8,128)S(1)} %get-tuple-element.32.refs_7_.refs_2_, ...), custom_call_target="tpu_custom_call" | custom-call | bytes 4194304 | tf_op jit(solution)/shard_map/pallas_call | solution.py:316
  31.5 1.6 %collective-permute-start.10 = (bf16[128,128]{1,0:T(8,128)(2,1)S(1)}, bf16[128,128]{1,0:T(8,128)(2,1)S(1)}, u32[]{:S(2)}, u32[]{:S(2)}) collective-permute-start(bf16[128,128]{1,0:T(8,128)(2,1)S(1)} %get-tuple-element.40), channel_id=1, source_target_pairs={{0,8},{4,12},{8,0},{12,4},{1,9},{5,13},{9,1},{13,5},{2,10},{6,14},... | collective-permute-start | bytes 98312 | tf_op jit(solution)/shard_map/ppermute | solution.py:39
  33.1 0.6 %collective-permute-start.9 = (bf16[128,128]{1,0:T(8,128)(2,1)S(1)}, bf16[128,128]{1,0:T(8,128)(2,1)S(1)}, u32[]{:S(2)}, u32[]{:S(2)}) collective-permute-start(bf16[128,128]{1,0:T(8,128)(2,1)S(1)} %get-tuple-element.40), channel_id=1, source_target_pairs={{0,4},{4,0},{8,12},{12,8},{1,5},{5,1},{9,13},{13,9},{2,6},{6,2},{1... | collective-permute-start | bytes 98312 | tf_op jit(solution)/shard_map/ppermute | solution.py:39
  33.7 1.8 %collective-permute-done.10 = bf16[128,128]{1,0:T(8,128)(2,1)S(1)} collective-permute-done((bf16[128,128]{1,0:T(8,128)(2,1)S(1)}, bf16[128,128]{1,0:T(8,128)(2,1)S(1)}, u32[]{:S(2)}, u32[]{:S(2)}) %collective-permute-start.10) | collective-permute-done | bytes 32800 | tf_op jit(solution)/shard_map/ppermute | solution.py:39
  35.5 0.9 %collective-permute-done.11 = bf16[128,128]{1,0:T(8,128)(2,1)S(1)} collective-permute-done((bf16[128,128]{1,0:T(8,128)(2,1)S(1)}, bf16[128,128]{1,0:T(8,128)(2,1)S(1)}, u32[]{:S(2)}, u32[]{:S(2)}) %collective-permute-start.11) | collective-permute-done | bytes 32800 | tf_op jit(solution)/shard_map/ppermute | solution.py:39
  36.5 0.8 %collective-permute-start.13 = (bf16[128,128]{1,0:T(8,128)(2,1)S(1)}, bf16[128,128]{1,0:T(8,128)(2,1)S(1)}, u32[]{:S(2)}, u32[]{:S(2)}) collective-permute-start(bf16[128,128]{1,0:T(8,128)(2,1)S(1)} %add_convert_fusion.refs_0_), channel_id=1, source_target_pairs={{0,2},{1,3},{2,0},{3,1},{4,6},{5,7},{6,4},{7,5},{8,10},{9,11},{10,... | collective-permute-start | bytes 98312 | tf_op jit(solution)/shard_map/ppermute | solution.py:39
  37.3 3.6 %collective-permute-start.14 = (bf16[128,128]{1,0:T(8,128)(2,1)S(1)}, bf16[128,128]{1,0:T(8,128)(2,1)S(1)}, u32[]{:S(2)}, u32[]{:S(2)}) collective-permute-start(bf16[128,128]{1,0:T(8,128)(2,1)S(1)} %add_convert_fusion.refs_0_), channel_id=1, source_target_pairs={{0,3},{1,2},{2,1},{3,0},{4,7},{5,6},{6,5},{7,4},{8,11},{9,10},{10,... | collective-permute-start | bytes 98312 | tf_op jit(solution)/shard_map/ppermute | solution.py:39
  40.9 0.6 %collective-permute-done.13.refs_2_ = bf16[128,128]{1,0:T(8,128)(2,1)S(1)} collective-permute-done((bf16[128,128]{1,0:T(8,128)(2,1)S(1)}, bf16[128,128]{1,0:T(8,128)(2,1)S(1)}, u32[]{:S(2)}, u32[]{:S(2)}) %collective-permute-start.13) | collective-permute-done | bytes 32800 | tf_op jit(solution)/shard_map/ppermute | solution.py:39
  41.5 1.6 %collective-permute-done.14.refs_3_ = bf16[128,128]{1,0:T(8,128)(2,1)S(1)} collective-permute-done((bf16[128,128]{1,0:T(8,128)(2,1)S(1)}, bf16[128,128]{1,0:T(8,128)(2,1)S(1)}, u32[]{:S(2)}, u32[]{:S(2)}) %collective-permute-start.14) | collective-permute-done | bytes 32800 | tf_op jit(solution)/shard_map/ppermute | solution.py:39
  43.1 0.9 %shard_map.87 = (f32[32,128]{1,0:T(8,128)S(1)}, bf16[32,128]{1,0:T(8,128)(2,1)S(1)}, bf16[32,128]{1,0:T(8,128)(2,1)S(1)}, bf16[32,128]{1,0:T(8,128)(2,1)S(1)}) custom-call(bf16[128,128]{1,0:T(8,128)(2,1)S(1)} %add_convert_fusion.refs_0_, bf16[128,128]{1,0:T(8,128)(2,1)S(1)} %collective-permute-done.12.refs_1_, ...), custom_call_target="tpu_custom_call" | custom-call | bytes 4194304 | tf_op jit(solution)/shard_map/pallas_call | solution.py:316
  44.0 0.3 collective-permute-start.15
  44.3 3.8 %collective-permute-start.16 = (bf16[32,128]{1,0:T(8,128)(2,1)S(1)}, bf16[32,128]{1,0:T(8,128)(2,1)S(1)}, u32[]{:S(2)}, u32[]{:S(2)}) collective-permute-start(bf16[32,128]{1,0:T(8,128)(2,1)S(1)} %get-tuple-element.45), channel_id=1, source_target_pairs={{0,2},{1,3},{2,0},{3,1},{4,6},{5,7},{6,4},{7,5},{8,10},{9,11},{10,... | collective-permute-start | bytes 24584 | tf_op jit(solution)/shard_map/ppermute | solution.py:39
  48.1 0.4 collective-permute-start.17
  48.5 1.3 %collective-permute-done.16 = bf16[32,128]{1,0:T(8,128)(2,1)S(1)} collective-permute-done((bf16[32,128]{1,0:T(8,128)(2,1)S(1)}, bf16[32,128]{1,0:T(8,128)(2,1)S(1)}, u32[]{:S(2)}, u32[]{:S(2)}) %collective-permute-start.16) | collective-permute-done | bytes 8224 | tf_op jit(solution)/shard_map/ppermute | solution.py:39
  49.8 3.8 %collective-permute-done.17 = bf16[32,128]{1,0:T(8,128)(2,1)S(1)} collective-permute-done((bf16[32,128]{1,0:T(8,128)(2,1)S(1)}, bf16[32,128]{1,0:T(8,128)(2,1)S(1)}, u32[]{:S(2)}, u32[]{:S(2)}) %collective-permute-start.17) | collective-permute-done | bytes 8224 | tf_op jit(solution)/shard_map/ppermute | solution.py:39
  53.7 1.0 %collective-permute-start.19 = (bf16[32,128]{1,0:T(8,128)(2,1)S(1)}, bf16[32,128]{1,0:T(8,128)(2,1)S(1)}, u32[]{:S(2)}, u32[]{:S(2)}) collective-permute-start(bf16[32,128]{1,0:T(8,128)(2,1)S(1)} %fusion), channel_id=1, source_target_pairs={{0,8},{4,12},{8,0},{12,4},{1,9},{5,13},{9,1},{13,5},{2,10},{6,14},... | collective-permute-start | bytes 24584 | tf_op jit(solution)/shard_map/ppermute | solution.py:39
  54.6 0.9 %collective-permute-start.20 = (bf16[32,128]{1,0:T(8,128)(2,1)S(1)}, bf16[32,128]{1,0:T(8,128)(2,1)S(1)}, u32[]{:S(2)}, u32[]{:S(2)}) collective-permute-start(bf16[32,128]{1,0:T(8,128)(2,1)S(1)} %fusion), channel_id=1, source_target_pairs={{0,12},{4,8},{8,4},{12,0},{1,13},{5,9},{9,5},{13,1},{2,14},{6,10},... | collective-permute-start | bytes 24584 | tf_op jit(solution)/shard_map/ppermute | solution.py:39
  55.5 1.9 %collective-permute-done.19 = bf16[32,128]{1,0:T(8,128)(2,1)S(1)} collective-permute-done((bf16[32,128]{1,0:T(8,128)(2,1)S(1)}, bf16[32,128]{1,0:T(8,128)(2,1)S(1)}, u32[]{:S(2)}, u32[]{:S(2)}) %collective-permute-start.19) | collective-permute-done | bytes 8224 | tf_op jit(solution)/shard_map/ppermute | solution.py:39
  57.4 0.3 collective-permute-done.20
  57.7 0.6 %add_bitcast_fusion = f32[1,32,128]{2,1,0:T(8,128)} fusion(f32[32,128]{1,0:T(8,128)S(1)} %copy-done.2, bf16[32,128]{1,0:T(8,128)(2,1)S(1)} %collective-permute-done.20, bf16[32,128]{1,0:T(8,128)(2,1)S(1)} %collective-permute-done.19, bf16[32,128]{1,0:T(8,128)(2,1)S(1)} %collective-permute-done.18, pred[]{:T(512)S(6)} %lt.14, pred[]{:T(512)S(6)} %lt.13, ...), kind=kLoop, calls=%fused_computation.1 | loop fusion | flops 65536 | bytes 98307 | tf_op jit(solution)/shard_map/broadcast_in_dim | solution.py:521
  (25 shorter events, 0.3 us)
Async XLA Ops:
  0.0 8.9 %collective-permute-start.3 = (bf16[32,3072]{1,0:T(8,128)(2,1)}, bf16[32,3072]{1,0:T(8,128)(2,1)S(1)}, u32[]{:S(2)}, u32[]{:S(2)}) collective-permute-start(bf16[32,3072]{1,0:T(8,128)(2,1)} %inw_hbm.1), channel_id=1, source_target_pairs={{0,8},{4,12},{8,0},{12,4},{1,9},{5,13},{9,1},{13,5},{2,10},{6,14},... | collective-permute-start | bytes 589832 | tf_op jit(solution)/shard_map/ppermute | solution.py:39
  3.0 9.3 %collective-permute-start = (bf16[768,128]{1,0:T(8,128)(2,1)}, bf16[768,128]{1,0:T(8,128)(2,1)S(1)}, u32[]{:S(2)}, u32[]{:S(2)}) collective-permute-start(bf16[768,128]{1,0:T(8,128)(2,1)} %refs_0_.1), channel_id=1, source_target_pairs={{0,8},{4,12},{8,0},{12,4},{1,9},{5,13},{9,1},{13,5},{2,10},{6,14},... | collective-permute-start | bytes 589832 | tf_op jit(solution)/shard_map/ppermute | solution.py:39
  3.0 14.4 %collective-permute-start.2 = (bf16[32,3072]{1,0:T(8,128)(2,1)}, bf16[32,3072]{1,0:T(8,128)(2,1)S(1)}, u32[]{:S(2)}, u32[]{:S(2)}) collective-permute-start(bf16[32,3072]{1,0:T(8,128)(2,1)} %inw_hbm.1), channel_id=1, source_target_pairs={{0,4},{4,0},{8,12},{12,8},{1,5},{5,1},{9,13},{13,9},{2,6},{6,2},{1... | collective-permute-start | bytes 589832 | tf_op jit(solution)/shard_map/ppermute | solution.py:39
  8.9 11.0 %collective-permute-start.4 = (bf16[32,3072]{1,0:T(8,128)(2,1)S(1)}, bf16[32,3072]{1,0:T(8,128)(2,1)S(1)}, u32[]{:S(2)}, u32[]{:S(2)}) collective-permute-start(bf16[32,3072]{1,0:T(8,128)(2,1)S(1)} %collective-permute-done.3.refs_2_), channel_id=1, source_target_pairs={{0,4},{4,0},{8,12},{12,8},{1,5},{5,1},{9,13},{13,9},{2,6},{6,2},{1... | collective-permute-start | bytes 589832 | tf_op jit(solution)/shard_map/ppermute | solution.py:39
  8.9 20.3 %collective-permute-start.8 = (bf16[768,128]{1,0:T(8,128)(2,1)}, bf16[768,128]{1,0:T(8,128)(2,1)S(1)}, u32[]{:S(2)}, u32[]{:S(2)}) collective-permute-start(bf16[768,128]{1,0:T(8,128)(2,1)} %refs_0_.1), channel_id=1, source_target_pairs={{0,4},{4,0},{8,12},{12,8},{1,5},{5,1},{9,13},{13,9},{2,6},{6,2},{1... | collective-permute-start | bytes 589832 | tf_op jit(solution)/shard_map/ppermute | solution.py:39
  12.3 18.4 %collective-permute-start.1 = (bf16[768,128]{1,0:T(8,128)(2,1)S(1)}, bf16[768,128]{1,0:T(8,128)(2,1)S(1)}, u32[]{:S(2)}, u32[]{:S(2)}) collective-permute-start(bf16[768,128]{1,0:T(8,128)(2,1)S(1)} %collective-permute-done.refs_2_), channel_id=1, source_target_pairs={{0,4},{4,0},{8,12},{12,8},{1,5},{5,1},{9,13},{13,9},{2,6},{6,2},{1... | collective-permute-start | bytes 589832 | tf_op jit(solution)/shard_map/ppermute | solution.py:39
  12.9 12.5 %copy-start = (bf16[512,3072]{1,0:T(8,128)(2,1)S(1)}, bf16[512,3072]{1,0:T(8,128)(2,1)}, u32[]{:S(2)}) copy-start(bf16[512,3072]{1,0:T(8,128)(2,1)} %refs_3_.1) | copy-start | bytes 9437188
  15.5 5.6 %collective-permute-start.5 = (bf16[50,128]{1,0:T(8,128)(2,1)S(1)}, bf16[50,128]{1,0:T(8,128)(2,1)S(1)}, u32[]{:S(2)}, u32[]{:S(2)}) collective-permute-start(bf16[50,128]{1,0:T(8,128)(2,1)S(1)} %get-tuple-element.28.refs_0_), channel_id=1, source_target_pairs={{0,1},{1,0},{2,3},{3,2},{4,5},{5,4},{6,7},{7,6},{8,9},{9,8},{10,11... | collective-permute-start | bytes 38408 | tf_op jit(solution)/shard_map/ppermute | solution.py:39
  17.4 4.6 %collective-permute-start.6 = (bf16[50,128]{1,0:T(8,128)(2,1)S(1)}, bf16[50,128]{1,0:T(8,128)(2,1)S(1)}, u32[]{:S(2)}, u32[]{:S(2)}) collective-permute-start(bf16[50,128]{1,0:T(8,128)(2,1)S(1)} %get-tuple-element.28.refs_0_), channel_id=1, source_target_pairs={{0,2},{1,3},{2,0},{3,1},{4,6},{5,7},{6,4},{7,5},{8,10},{9,11},{10,... | collective-permute-start | bytes 38408 | tf_op jit(solution)/shard_map/ppermute | solution.py:39
  20.0 5.5 %collective-permute-start.7 = (bf16[50,128]{1,0:T(8,128)(2,1)S(1)}, bf16[50,128]{1,0:T(8,128)(2,1)S(1)}, u32[]{:S(2)}, u32[]{:S(2)}) collective-permute-start(bf16[50,128]{1,0:T(8,128)(2,1)S(1)} %get-tuple-element.28.refs_0_), channel_id=1, source_target_pairs={{0,3},{1,2},{2,1},{3,0},{4,7},{5,6},{6,5},{7,4},{8,11},{9,10},{10,... | collective-permute-start | bytes 38408 | tf_op jit(solution)/shard_map/ppermute | solution.py:39
  25.5 3.7 %copy-start.1 = (bf16[768,128]{1,0:T(8,128)(2,1)S(1)}, bf16[768,128]{1,0:T(8,128)(2,1)}, u32[]{:S(2)}) copy-start(bf16[768,128]{1,0:T(8,128)(2,1)} %refs_0_.1) | copy-start | bytes 589828
  30.7 27.0 %copy-start.2 = (f32[32,128]{1,0:T(8,128)S(1)}, f32[32,128]{1,0:T(8,128)}, u32[]{:S(2)}) copy-start(f32[32,128]{1,0:T(8,128)} %start_hbm.1) | copy-start | bytes 49156
  31.5 4.0 %collective-permute-start.10 = (bf16[128,128]{1,0:T(8,128)(2,1)S(1)}, bf16[128,128]{1,0:T(8,128)(2,1)S(1)}, u32[]{:S(2)}, u32[]{:S(2)}) collective-permute-start(bf16[128,128]{1,0:T(8,128)(2,1)S(1)} %get-tuple-element.40), channel_id=1, source_target_pairs={{0,8},{4,12},{8,0},{12,4},{1,9},{5,13},{9,1},{13,5},{2,10},{6,14},... | collective-permute-start | bytes 98312 | tf_op jit(solution)/shard_map/ppermute | solution.py:39
  33.1 3.3 %collective-permute-start.11 = (bf16[128,128]{1,0:T(8,128)(2,1)S(1)}, bf16[128,128]{1,0:T(8,128)(2,1)S(1)}, u32[]{:S(2)}, u32[]{:S(2)}) collective-permute-start(bf16[128,128]{1,0:T(8,128)(2,1)S(1)} %get-tuple-element.40), channel_id=1, source_target_pairs={{0,12},{4,8},{8,4},{12,0},{1,13},{5,9},{9,5},{13,1},{2,14},{6,10},... | collective-permute-start | bytes 98312 | tf_op jit(solution)/shard_map/ppermute | solution.py:39
  33.1 3.3 %collective-permute-start.9 = (bf16[128,128]{1,0:T(8,128)(2,1)S(1)}, bf16[128,128]{1,0:T(8,128)(2,1)S(1)}, u32[]{:S(2)}, u32[]{:S(2)}) collective-permute-start(bf16[128,128]{1,0:T(8,128)(2,1)S(1)} %get-tuple-element.40), channel_id=1, source_target_pairs={{0,4},{4,0},{8,12},{12,8},{1,5},{5,1},{9,13},{13,9},{2,6},{6,2},{1... | collective-permute-start | bytes 98312 | tf_op jit(solution)/shard_map/ppermute | solution.py:39
  36.4 4.5 %collective-permute-start.12 = (bf16[128,128]{1,0:T(8,128)(2,1)S(1)}, bf16[128,128]{1,0:T(8,128)(2,1)S(1)}, u32[]{:S(2)}, u32[]{:S(2)}) collective-permute-start(bf16[128,128]{1,0:T(8,128)(2,1)S(1)} %add_convert_fusion.refs_0_), channel_id=1, source_target_pairs={{0,1},{1,0},{2,3},{3,2},{4,5},{5,4},{6,7},{7,6},{8,9},{9,8},{10,11... | collective-permute-start | bytes 98312 | tf_op jit(solution)/shard_map/ppermute | solution.py:39
  36.5 5.0 %collective-permute-start.13 = (bf16[128,128]{1,0:T(8,128)(2,1)S(1)}, bf16[128,128]{1,0:T(8,128)(2,1)S(1)}, u32[]{:S(2)}, u32[]{:S(2)}) collective-permute-start(bf16[128,128]{1,0:T(8,128)(2,1)S(1)} %add_convert_fusion.refs_0_), channel_id=1, source_target_pairs={{0,2},{1,3},{2,0},{3,1},{4,6},{5,7},{6,4},{7,5},{8,10},{9,11},{10,... | collective-permute-start | bytes 98312 | tf_op jit(solution)/shard_map/ppermute | solution.py:39
  37.3 5.8 %collective-permute-start.14 = (bf16[128,128]{1,0:T(8,128)(2,1)S(1)}, bf16[128,128]{1,0:T(8,128)(2,1)S(1)}, u32[]{:S(2)}, u32[]{:S(2)}) collective-permute-start(bf16[128,128]{1,0:T(8,128)(2,1)S(1)} %add_convert_fusion.refs_0_), channel_id=1, source_target_pairs={{0,3},{1,2},{2,1},{3,0},{4,7},{5,6},{6,5},{7,4},{8,11},{9,10},{10,... | collective-permute-start | bytes 98312 | tf_op jit(solution)/shard_map/ppermute | solution.py:39
  44.0 4.5 %collective-permute-start.15 = (bf16[32,128]{1,0:T(8,128)(2,1)S(1)}, bf16[32,128]{1,0:T(8,128)(2,1)S(1)}, u32[]{:S(2)}, u32[]{:S(2)}) collective-permute-start(bf16[32,128]{1,0:T(8,128)(2,1)S(1)} %get-tuple-element.44), channel_id=1, source_target_pairs={{0,1},{1,0},{2,3},{3,2},{4,5},{5,4},{6,7},{7,6},{8,9},{9,8},{10,11... | collective-permute-start | bytes 24584 | tf_op jit(solution)/shard_map/ppermute | solution.py:39
  44.3 5.5 %collective-permute-start.16 = (bf16[32,128]{1,0:T(8,128)(2,1)S(1)}, bf16[32,128]{1,0:T(8,128)(2,1)S(1)}, u32[]{:S(2)}, u32[]{:S(2)}) collective-permute-start(bf16[32,128]{1,0:T(8,128)(2,1)S(1)} %get-tuple-element.45), channel_id=1, source_target_pairs={{0,2},{1,3},{2,0},{3,1},{4,6},{5,7},{6,4},{7,5},{8,10},{9,11},{10,... | collective-permute-start | bytes 24584 | tf_op jit(solution)/shard_map/ppermute | solution.py:39
  48.1 5.4 %collective-permute-start.17 = (bf16[32,128]{1,0:T(8,128)(2,1)S(1)}, bf16[32,128]{1,0:T(8,128)(2,1)S(1)}, u32[]{:S(2)}, u32[]{:S(2)}) collective-permute-start(bf16[32,128]{1,0:T(8,128)(2,1)S(1)} %get-tuple-element.46), channel_id=1, source_target_pairs={{0,3},{1,2},{2,1},{3,0},{4,7},{5,6},{6,5},{7,4},{8,11},{9,10},{10,... | collective-permute-start | bytes 24584 | tf_op jit(solution)/shard_map/ppermute | solution.py:39
  53.6 1.9 %collective-permute-start.18 = (bf16[32,128]{1,0:T(8,128)(2,1)S(1)}, bf16[32,128]{1,0:T(8,128)(2,1)S(1)}, u32[]{:S(2)}, u32[]{:S(2)}) collective-permute-start(bf16[32,128]{1,0:T(8,128)(2,1)S(1)} %fusion), channel_id=1, source_target_pairs={{0,4},{4,0},{8,12},{12,8},{1,5},{5,1},{9,13},{13,9},{2,6},{6,2},{1... | collective-permute-start | bytes 24584 | tf_op jit(solution)/shard_map/ppermute | solution.py:39
  53.7 3.7 %collective-permute-start.19 = (bf16[32,128]{1,0:T(8,128)(2,1)S(1)}, bf16[32,128]{1,0:T(8,128)(2,1)S(1)}, u32[]{:S(2)}, u32[]{:S(2)}) collective-permute-start(bf16[32,128]{1,0:T(8,128)(2,1)S(1)} %fusion), channel_id=1, source_target_pairs={{0,8},{4,12},{8,0},{12,4},{1,9},{5,13},{9,1},{13,5},{2,10},{6,14},... | collective-permute-start | bytes 24584 | tf_op jit(solution)/shard_map/ppermute | solution.py:39
  54.6 3.1 %collective-permute-start.20 = (bf16[32,128]{1,0:T(8,128)(2,1)S(1)}, bf16[32,128]{1,0:T(8,128)(2,1)S(1)}, u32[]{:S(2)}, u32[]{:S(2)}) collective-permute-start(bf16[32,128]{1,0:T(8,128)(2,1)S(1)} %fusion), channel_id=1, source_target_pairs={{0,12},{4,8},{8,4},{12,0},{1,13},{5,9},{9,5},{13,1},{2,14},{6,10},... | collective-permute-start | bytes 24584 | tf_op jit(solution)/shard_map/ppermute | solution.py:39
